TPU v7x, 32 devices: a whole 2x2x4 slice. The times are simulated.
32 devices in a mesh: dp: 8 (over z, y), tensor: 4 (over x, core).
Axes of the slice: x: 2, y: 2, z: 4, core: 2. Of those that a mesh axis runs over, the one named last changes fastest.
Arguments:
- hidden_in: bfloat16 [16384, 768], P(('dp', 'tensor')), may hold values from -6 to 6
- grad_out: bfloat16 [16384, 768], P(('dp', 'tensor')), may hold values from -6 to 6
- w_query: bfloat16 [768, 768], P('dp', 'tensor'), may hold values from -0.21875 to 0.21875
- b_query: float32 [768], P('tensor'), may hold values from -1.75 to 1.75
- w_key: bfloat16 [768, 768], P('dp', 'tensor'), may hold values from -0.21875 to 0.21875
- w_value: bfloat16 [768, 768], P('dp', 'tensor'), may hold values from -0.21875 to 0.21875
- b_value: float32 [768], P('tensor'), may hold values from -0.3125 to 0.3125
- w_out: bfloat16 [768, 768], P('tensor', 'dp'), may hold values from -3 to 3
- b_out: float32 [768], replicated, may hold values from -1.75 to 1.75
- gain_one: float32 [768], replicated, may hold values from 0.25 to 1.75
- shift_one: float32 [768], replicated, may hold values from -1.75 to 1.75
- w_up: bfloat16 [768, 3072], P('dp', 'tensor'), may hold values from -0.21875 to 0.21875
- b_up: float32 [3072], replicated, may hold values from -1.75 to 1.75
- w_down: bfloat16 [3072, 768], P('tensor', 'dp'), may hold values from -0.109375 to 0.109375
- b_down: float32 [768], replicated, may hold values from -1.75 to 1.75
- gain_two: float32 [768], replicated, may hold values from 0.25 to 1.75
- shift_two: float32 [768], replicated, may hold values from -1.75 to 1.75
- lengths: int32 [8], P('dp'), may hold values from 1024 to 2048, as said below
- global_raw: int32 [8, 2], P('dp'), may hold values from 0 to 65535
- random_raw: int32 [8, 32, 3], P('dp'), may hold values from 0 to 65535
Outputs:
- layer_out: bfloat16 [16384, 768], P(('dp', 'tensor'))
- grad_in: float32 [16384, 768], P(('dp', 'tensor'))
- grad_w_query: float32 [768, 768], P('dp', 'tensor')
- grad_b_query: float32 [768], P('tensor')
- grad_w_key: float32 [768, 768], P('dp', 'tensor')
- grad_w_value: float32 [768, 768], P('dp', 'tensor')
- grad_b_value: float32 [768], P('tensor')
- grad_w_out: float32 [768, 768], P('tensor', 'dp')
- grad_b_out: float32 [768], replicated
- grad_gain_one: float32 [768], replicated
- grad_shift_one: float32 [768], replicated
- grad_w_up: float32 [768, 3072], P('dp', 'tensor')
- grad_b_up: float32 [3072], P('tensor')
- grad_w_down: float32 [3072, 768], P('tensor', 'dp')
- grad_b_down: float32 [768], replicated
- grad_gain_two: float32 [768], replicated
- grad_shift_two: float32 [768], replicated
Inputs may be any that keep to these rules, and one draw needn't show every extreme that they name: `lengths`: the first sequence has 2048 live tokens.
All inputs are finite; a program needn't handle non-finite values.
Results may differ from a plain program's by a relative error of at most 0.015.
Values may be sent and summed in bfloat16 or wider, within the bound.
No kernel may reach another device: no remote copies, remote signals or barrier semaphores. Data moves between devices by JAX's collectives and lax.ppermute only.
A program may use at most 192 MiB of HBM per device.

v0:
```python
from functools import partial

import jax
import jax.numpy as jnp
from jax import lax
from jax.sharding import PartitionSpec as P

D = 768
HD = 64
FF = 3072
BLK = 64
GLOB = 2
RAND = 3
QROWS = 512
LMAX = 2048
NB = 32


masked_score = -1e30
EPSILON = 1e-12


def cut_along(array, dim, length):
    shape = array.shape
    blocks = array.reshape(*shape[:dim], length, shape[dim] // length, *shape[dim + 1 :])
    return jnp.moveaxis(blocks, dim, 0)


def sent_and_summed(array, axis, dim):
    length = lax.axis_size(axis)
    blocks = lax.all_to_all(cut_along(array, dim, length), axis, 0, 0, tiled=True)
    return jnp.sum(blocks.astype(jnp.float32), axis=0)


def layer_norm(values, gain_vec, shift_vec):
    centred = values - jnp.mean(values, axis=-1, keepdims=True)
    inv_std = lax.rsqrt(jnp.mean(centred * centred, axis=-1, keepdims=True) + EPSILON)
    scaled = centred * inv_std
    return (scaled * gain_vec + shift_vec, scaled, inv_std)


def norm_backward(upstream, scaled, inv_std, gain_vec):
    weighted = upstream * gain_vec
    inner_sum = jnp.mean(weighted * scaled, axis=-1, keepdims=True)
    grad_values = inv_std * (
        weighted - jnp.mean(weighted, axis=-1, keepdims=True) - scaled * inner_sum
    )
    return (grad_values, jnp.sum(upstream * scaled, axis=0), jnp.sum(upstream, axis=0))


def block_tables(lengths, global_raw, random_raw):
    seq_count = lengths.shape[0]
    live_count = (lengths + BLK - 1) // BLK
    block_ids = jnp.arange(NB, dtype=jnp.int32)
    left_block = jnp.maximum(block_ids - 1, 0)
    right_block = jnp.minimum(block_ids + 1, NB - 1)
    near_ids = jnp.stack([left_block, block_ids, right_block], axis=1)[None]
    global_ids = jnp.broadcast_to(
        (global_raw % live_count[:, None])[:, None, :], (seq_count, NB, GLOB)
    )
    random_ids = random_raw % live_count[:, None, None]
    key_table = jnp.concatenate([near_ids, global_ids, random_ids], axis=2)
    near_ok = jnp.stack([block_ids >= 1, block_ids >= 0, block_ids + 1 < NB], axis=1)
    block_ok = jnp.concatenate([near_ok, jnp.ones((NB, GLOB + RAND), dtype=jnp.bool_)], axis=1)
    position = key_table[..., None] * BLK + jnp.arange(BLK, dtype=jnp.int32)
    key_valid = block_ok[None, :, :, None] & (position < lengths[:, None, None, None])
    offsets = jnp.arange(seq_count, dtype=jnp.int32)[:, None, None] * NB
    return (
        (key_table + offsets).reshape(seq_count * NB, -1),
        key_valid.reshape(seq_count * NB, -1),
    )


def attend_forward(queries, key_rows, value_rows, key_table, key_valid):
    group_size = QROWS // BLK
    local_heads = queries.shape[2]
    group_count = queries.shape[0] // group_size
    score_scale = HD ** (-0.5)

    def one_group(pieces):
        q_part, table_part, valid_part = pieces
        k_part = key_rows[table_part].reshape(group_size, -1, local_heads, HD)
        v_part = value_rows[table_part].reshape(group_size, -1, local_heads, HD)
        scores = (
            jnp.einsum("gqhd,gkhd->ghqk", q_part, k_part, preferred_element_type=jnp.float32)
            * score_scale
        )
        scores = jnp.where(valid_part[:, None, None, :], scores, masked_score)
        row_max = jnp.max(scores, axis=-1, keepdims=True)
        exp_scores = jnp.exp(scores - row_max)
        row_total = jnp.sum(exp_scores, axis=-1, keepdims=True)
        weights = (exp_scores / row_total).astype(jnp.bfloat16)
        mixed_out = jnp.einsum(
            "ghqk,gkhd->gqhd", weights, v_part, preferred_element_type=jnp.float32
        )
        return (mixed_out, (row_max + jnp.log(row_total))[..., 0])

    return lax.map(
        one_group,
        (
            queries.reshape(group_count, group_size, BLK, local_heads, HD),
            key_table.reshape(group_count, group_size, -1),
            key_valid.reshape(group_count, group_size, -1),
        ),
    )


def attend_backward(queries, key_rows, value_rows, key_table, key_valid, log_total, grad_mixed):
    group_size = QROWS // BLK
    local_heads = queries.shape[2]
    group_count = queries.shape[0] // group_size
    score_scale = HD ** (-0.5)

    def one_group(carried, pieces):
        grad_keys, grad_values = carried
        q_part, table_part, valid_part, total_part, upstream = pieces
        k_part = key_rows[table_part].reshape(group_size, -1, local_heads, HD)
        v_part = value_rows[table_part].reshape(group_size, -1, local_heads, HD)
        scores = (
            jnp.einsum("gqhd,gkhd->ghqk", q_part, k_part, preferred_element_type=jnp.float32)
            * score_scale
        )
        scores = jnp.where(valid_part[:, None, None, :], scores, masked_score)
        probabilities = jnp.exp(scores - total_part[..., None])
        weights = probabilities.astype(jnp.bfloat16)
        grad_probs = jnp.einsum(
            "gqhd,gkhd->ghqk", upstream, v_part, preferred_element_type=jnp.float32
        )
        inner_sum = jnp.sum(probabilities * grad_probs, axis=-1, keepdims=True)
        grad_scores = (probabilities * (grad_probs - inner_sum)).astype(jnp.bfloat16)
        grad_query = (
            jnp.einsum("ghqk,gkhd->gqhd", grad_scores, k_part, preferred_element_type=jnp.float32)
            * score_scale
        )
        key_part = (
            jnp.einsum("ghqk,gqhd->gkhd", grad_scores, q_part, preferred_element_type=jnp.float32)
            * score_scale
        )
        value_part = jnp.einsum(
            "ghqk,gqhd->gkhd", weights, upstream, preferred_element_type=jnp.float32
        )
        flat_ids = table_part.reshape(-1)
        grad_keys = grad_keys.at[flat_ids].add(key_part.reshape(-1, BLK, local_heads, HD))
        grad_values = grad_values.at[flat_ids].add(value_part.reshape(-1, BLK, local_heads, HD))
        return ((grad_keys, grad_values), grad_query)

    empty = jnp.zeros(key_rows.shape, jnp.float32)
    (grad_keys, grad_values), grad_query = lax.scan(
        one_group,
        (empty, empty),
        (
            queries.reshape(group_count, group_size, BLK, local_heads, HD),
            key_table.reshape(group_count, group_size, -1),
            key_valid.reshape(group_count, group_size, -1),
            log_total,
            grad_mixed.reshape(group_count, group_size, BLK, local_heads, HD),
        ),
    )
    return (grad_query, grad_keys, grad_values)


def gather_layer(shards):
    gathered = (
        lax.all_gather(shards[0], "dp", axis=0, tiled=True),
        lax.all_gather(shards[1], "dp", axis=0, tiled=True),
        lax.all_gather(shards[2], "dp", axis=0, tiled=True),
        lax.all_gather(shards[3], "dp", axis=1, tiled=True),
        lax.all_gather(shards[4], "dp", axis=0, tiled=True),
        lax.all_gather(shards[5], "dp", axis=1, tiled=True),
    )
    return (gathered[0], gathered[1], gathered[2], gathered[3], gathered[4], gathered[5])


def layer_forward(hidden_in, weights, biases, key_table, key_valid):
    query_all, key_all, value_all, out_all, up_all, down_all = weights
    b_query, b_value, b_out, gain_one, shift_one, b_up_used, b_down, gain_two, shift_two = biases
    f32 = jnp.float32
    bf16 = jnp.bfloat16
    local_width = query_all.shape[1]
    local_heads = local_width // HD
    full_in = lax.all_gather(hidden_in, "tensor", axis=0, tiled=True)
    group_rows = full_in.shape[0]
    blocks_total = group_rows // BLK
    queries = (jnp.dot(full_in, query_all, preferred_element_type=f32) + b_query).astype(bf16)
    key_rows = jnp.dot(full_in, key_all, preferred_element_type=f32).astype(bf16)
    value_rows = (jnp.dot(full_in, value_all, preferred_element_type=f32) + b_value).astype(bf16)
    queries_blk = queries.reshape(blocks_total, BLK, local_heads, HD)
    keys_blk = key_rows.reshape(blocks_total, BLK, local_heads, HD)
    values_blk = value_rows.reshape(blocks_total, BLK, local_heads, HD)
    mixed_out, log_total = attend_forward(queries_blk, keys_blk, values_blk, key_table, key_valid)
    mixed_low = mixed_out.reshape(group_rows, local_width).astype(bf16)
    after_attn = (
        hidden_in.astype(f32)
        + lax.psum_scatter(
            jnp.dot(mixed_low, out_all, preferred_element_type=f32),
            "tensor",
            scatter_dimension=0,
            tiled=True,
        )
        + b_out
    )
    normed, scaled_one, inv_one = layer_norm(after_attn, gain_one, shift_one)
    normed_low = normed.astype(bf16)
    ffn_rows = lax.all_gather(normed_low, "tensor", axis=0, tiled=True)
    up_pre = jnp.dot(ffn_rows, up_all, preferred_element_type=f32) + b_up_used
    activated = jax.nn.gelu(up_pre, approximate=True).astype(bf16)
    ffn_sum = lax.psum_scatter(
        jnp.dot(activated, down_all, preferred_element_type=f32),
        "tensor",
        scatter_dimension=0,
        tiled=True,
    )
    summed = normed + ffn_sum + b_down
    layer_out, scaled_two, inv_two = layer_norm(summed, gain_two, shift_two)
    return (
        layer_out,
        full_in,
        (queries_blk, keys_blk, values_blk, log_total),
        mixed_low,
        (scaled_one, inv_one),
        ffn_rows,
        up_pre,
        activated,
        (scaled_two, inv_two),
    )


def per_device(
    hidden_in,
    grad_out,
    w_query,
    b_query,
    w_key,
    w_value,
    b_value,
    w_out,
    b_out,
    gain_one,
    shift_one,
    w_up,
    b_up,
    w_down,
    b_down,
    gain_two,
    shift_two,
    lengths,
    global_raw,
    random_raw,
):
    own_rows = hidden_in.shape[0]
    tensor_index = lax.axis_index("tensor")
    local_width = w_query.shape[1]
    hidden_width = w_up.shape[1]
    f32 = jnp.float32
    bf16 = jnp.bfloat16
    hidden_start = tensor_index * hidden_width
    width_start = tensor_index * local_width
    b_up_used = lax.dynamic_slice_in_dim(b_up, hidden_start, hidden_width)
    biases = (b_query, b_value, b_out, gain_one, shift_one, b_up_used, b_down, gain_two, shift_two)
    key_table, key_valid = block_tables(lengths, global_raw, random_raw)
    weights_fwd = gather_layer((w_query, w_key, w_value, w_out, w_up, w_down))
    layer_out = layer_forward(hidden_in, weights_fwd, biases, key_table, key_valid)[0]
    held = lax.optimization_barrier(
        (hidden_in, (w_query, w_key, w_value, w_out, w_up, w_down), layer_out)
    )
    weights_back = gather_layer(held[1])
    query_back, key_back, value_back, out_back, up_back, down_back = weights_back
    replay = layer_forward(held[0], weights_back, biases, key_table, key_valid)
    full_in = replay[1]
    queries_blk, keys_blk, values_blk, log_total = replay[2]
    mixed_low = replay[3]
    scaled_one, inv_one = replay[4]
    ffn_rows = replay[5]
    up_pre = replay[6]
    activated = replay[7]
    scaled_two, inv_two = replay[8]
    group_rows = full_in.shape[0]
    row_ids = tensor_index * own_rows + jnp.arange(own_rows, dtype=jnp.int32)
    seq_ids = row_ids // LMAX
    keep_rows = row_ids % LMAX < jnp.take(lengths, seq_ids)
    upstream = jnp.where(keep_rows[:, None], grad_out.astype(f32), 0.0)
    grad_summed, grad_gain_two, grad_shift_two = norm_backward(
        upstream, scaled_two, inv_two, gain_two
    )
    grad_summed_low = grad_summed.astype(bf16)
    grad_b_down = jnp.sum(grad_summed_low.astype(f32), axis=0)
    unused, gelu_pull = jax.vjp(partial(jax.nn.gelu, approximate=True), up_pre)
    full_grad = lax.all_gather(grad_summed_low, "tensor", axis=0, tiled=True)
    grad_w_down = jnp.einsum("rf,rd->fd", activated, full_grad, preferred_element_type=f32)
    grad_act = jnp.einsum("rd,fd->rf", full_grad, down_back, preferred_element_type=f32)
    grad_up_low = gelu_pull(grad_act)[0].astype(bf16)
    grad_b_up = jnp.sum(grad_up_low.astype(f32), axis=0)
    grad_w_up = jnp.einsum("rd,rf->df", ffn_rows, grad_up_low, preferred_element_type=f32)
    grad_normed = lax.psum_scatter(
        jnp.einsum("rf,df->rd", grad_up_low, up_back, preferred_element_type=f32),
        "tensor",
        scatter_dimension=0,
        tiled=True,
    ) + grad_summed_low.astype(f32)
    ffn_pair = (grad_w_up, grad_w_down)
    full_b_up = lax.dynamic_update_slice(jnp.zeros((FF,), f32), grad_b_up, (hidden_start,))
    ffn_grads = (
        sent_and_summed(ffn_pair[0].astype(jnp.bfloat16), "dp", 0),
        sent_and_summed(ffn_pair[1].astype(jnp.bfloat16), "dp", 1),
    )
    grad_after, grad_gain_one, grad_shift_one = norm_backward(
        grad_normed, scaled_one, inv_one, gain_one
    )
    grad_after_low = grad_after.astype(bf16)
    grad_b_out = jnp.sum(grad_after_low.astype(f32), axis=0)
    full_after = lax.all_gather(grad_after_low, "tensor", axis=0, tiled=True)
    grad_w_out = jnp.einsum("rh,rd->hd", mixed_low, full_after, preferred_element_type=f32)
    grad_mixed = jnp.einsum("rd,hd->rh", full_after, out_back, preferred_element_type=f32).astype(
        bf16
    )
    grad_query, grad_keys, grad_values = attend_backward(
        queries_blk, keys_blk, values_blk, key_table, key_valid, log_total, grad_mixed
    )
    grad_query_low = grad_query.reshape(group_rows, local_width).astype(bf16)
    grad_key_low = grad_keys.reshape(group_rows, local_width).astype(bf16)
    grad_value_low = grad_values.reshape(group_rows, local_width).astype(bf16)
    grad_b_query = jnp.sum(grad_query_low.astype(f32), axis=0)
    grad_b_value = jnp.sum(grad_value_low.astype(f32), axis=0)
    grad_w_query = jnp.einsum("rd,rh->dh", full_in, grad_query_low, preferred_element_type=f32)
    grad_w_key = jnp.einsum("rd,rh->dh", full_in, grad_key_low, preferred_element_type=f32)
    grad_w_value = jnp.einsum("rd,rh->dh", full_in, grad_value_low, preferred_element_type=f32)
    part_query = jnp.einsum("rh,dh->rd", grad_query_low, query_back, preferred_element_type=f32)
    part_key = jnp.einsum("rh,dh->rd", grad_key_low, key_back, preferred_element_type=f32)
    part_value = jnp.einsum("rh,dh->rd", grad_value_low, value_back, preferred_element_type=f32)
    grad_in = lax.psum_scatter(
        (part_query + part_key + part_value).astype(jnp.bfloat16),
        "tensor",
        scatter_dimension=0,
        tiled=True,
    ).astype(jnp.float32) + grad_after_low.astype(f32)
    attn_grads = (
        lax.psum_scatter(grad_w_query, "dp", scatter_dimension=0, tiled=True),
        lax.psum_scatter(grad_w_key, "dp", scatter_dimension=0, tiled=True),
        lax.psum_scatter(grad_w_value, "dp", scatter_dimension=0, tiled=True),
        lax.psum_scatter(grad_w_out, "dp", scatter_dimension=1, tiled=True),
    )
    full_b_query = lax.dynamic_update_slice(jnp.zeros((D,), f32), grad_b_query, (width_start,))
    full_b_value = lax.dynamic_update_slice(jnp.zeros((D,), f32), grad_b_value, (width_start,))
    small_sums = lax.psum(
        (
            grad_gain_one,
            grad_shift_one,
            grad_b_out,
            grad_gain_two,
            grad_shift_two,
            grad_b_down,
            full_b_query,
            full_b_value,
            full_b_up,
        ),
        ("dp", "tensor"),
    )
    bias_query = lax.dynamic_slice_in_dim(small_sums[6], width_start, local_width)
    bias_value = lax.dynamic_slice_in_dim(small_sums[7], width_start, local_width)
    bias_up = lax.dynamic_slice_in_dim(small_sums[8], hidden_start, hidden_width)
    return (
        layer_out.astype(bf16),
        grad_in,
        attn_grads[0],
        bias_query,
        attn_grads[1],
        attn_grads[2],
        bias_value,
        attn_grads[3],
        small_sums[2],
        small_sums[0],
        small_sums[1],
        ffn_grads[0],
        bias_up,
        ffn_grads[1],
        small_sums[5],
        small_sums[3],
        small_sums[4],
    )


def solution(mesh):
    in_specs = (
        P(("dp", "tensor"), None),
        P(("dp", "tensor"), None),
        P("dp", "tensor"),
        P("tensor"),
        P("dp", "tensor"),
        P("dp", "tensor"),
        P("tensor"),
        P("tensor", "dp"),
        P(),
        P(),
        P(),
        P("dp", "tensor"),
        P(),
        P("tensor", "dp"),
        P(),
        P(),
        P(),
        P("dp"),
        P("dp", None),
        P("dp", None, None),
    )
    out_specs = (
        P(("dp", "tensor"), None),
        P(("dp", "tensor"), None),
        P("dp", "tensor"),
        P("tensor"),
        P("dp", "tensor"),
        P("dp", "tensor"),
        P("tensor"),
        P("tensor", "dp"),
        P(),
        P(),
        P(),
        P("dp", "tensor"),
        P("tensor"),
        P("tensor", "dp"),
        P(),
        P(),
        P(),
    )
    return jax.shard_map(
        per_device, mesh=mesh, in_specs=in_specs, out_specs=out_specs, check_vma=False
    )
```

profile of v0, /device:TPU:0, one launch (start us, length us, event | category | flops | bytes accessed | tf_op | source)
XLA Modules:
  0.0 1858.8 jit_solution(4992220759504508902)
XLA Ops:
  13.4 33.2 %all_gather.55 = bf16[768,192]{1,0:T(8,128)(2,1)S(1)} all-gather(bf16[96,192]{1,0:T(8,128)(2,1)} %param.31), channel_id=1, replica_groups=mesh['dp'=8,'tensor'=4] {'dp'}, dimensions={0}, use_global_device_ids=true | all-gather | bytes 331776 | tf_op jit(solution)/shard_map/all_gather | solution.py:166
  46.5 33.3 %all_gather.57 = bf16[768,192]{1,0:T(8,128)(2,1)} all-gather(bf16[96,192]{1,0:T(8,128)(2,1)} %param.30), channel_id=1, replica_groups=mesh['dp'=8,'tensor'=4] {'dp'}, dimensions={0}, use_global_device_ids=true | all-gather | bytes 331776 | tf_op jit(solution)/shard_map/all_gather | solution.py:165
  79.9 33.5 %all_gather.56 = bf16[768,192]{1,0:T(8,128)(2,1)} all-gather(bf16[96,192]{1,0:T(8,128)(2,1)} %param.28), channel_id=1, replica_groups=mesh['dp'=8,'tensor'=4] {'dp'}, dimensions={0}, use_global_device_ids=true | all-gather | bytes 331776 | tf_op jit(solution)/shard_map/all_gather | solution.py:164
  113.3 31.0 %all_gather.58 = bf16[192,768]{0,1:T(8,128)(2,1)S(1)} all-gather(bf16[192,96]{0,1:T(8,128)(2,1)S(1)} %copy.119), channel_id=1, replica_groups=mesh['dp'=8,'tensor'=4] {'dp'}, dimensions={1}, use_global_device_ids=true | all-gather | bytes 331776 | tf_op jit(solution)/shard_map/all_gather | solution.py:167
  170.8 107.2 %while.36 = (s32[]{:T(128)}, bf16[4,8,64,3,64]{2,4,3,1,0:T(8,128)(2,1)}, s32[4,8,8]{2,1,0:T(8,128)S(1)}, bf16[32,64,3,64]{3,2,1,0:T(4,128)(2,1)S(1)}, pred[4,8,5...) while((s32[]{:T(128)}, ...), condition=%wide.region_3.4_spmd, body=%wide.region_0.3_spmd.sunk | while | flops 207619776 | bytes 26442080 | solution.py:98
  171.1 7.9 gather_fusion
  224.6 7.9 gather_fusion
  251.3 7.9 gather_fusion
  286.7 58.2 %reduce-scatter.13.cloned.1.call-done = f32[512,768]{1,0:T(8,128)} async-done(((f32[2048,768]{1,0:T(8,128)}), f32[512,768]{1,0:T(8,128)}) %reduce-scatter.13.cloned.1.call-update) | async-done | bytes 1572880 | tf_op jit(solution)/shard_map/reduce_scatter | solution.py:194
  349.7 22.7 %all-gather.17.cloned.1.call-done = bf16[768,768]{0,1:T(8,128)(2,1)} async-done(((bf16[768,96]{0,1:T(8,128)(2,1)}), bf16[768,768]{0,1:T(8,128)(2,1)}) %all-gather.17.cloned.1.call-update) | async-done | bytes 1179664 | tf_op jit(solution)/shard_map/all_gather | solution.py:169
  372.4 29.0 %all-gather.13.cloned.1.call-done = bf16[2048,768]{1,0:T(8,128)(2,1)} async-done(((bf16[512,768]{1,0:T(8,128)(2,1)}), bf16[2048,768]{1,0:T(8,128)(2,1)}) %all-gather.13.cloned.1.call-update) | async-done | bytes 3145744 | tf_op jit(solution)/shard_map/all_gather | solution.py:204
  401.4 11.3 fusion.79
  412.8 58.3 %reduce-scatter.15.cloned.1.call-done = f32[512,768]{1,0:T(8,128)} async-done(((f32[2048,768]{1,0:T(8,128)}), f32[512,768]{1,0:T(8,128)}) %reduce-scatter.15.cloned.1.call-update) | async-done | bytes 1572880 | tf_op jit(solution)/shard_map/reduce_scatter | solution.py:207
  475.0 31.4 %all_gather.64 = bf16[768,192]{1,0:T(8,128)(2,1)S(1)} all-gather(bf16[96,192]{1,0:T(8,128)(2,1)S(1)} %copy-done.23), channel_id=1, replica_groups=mesh['dp'=8,'tensor'=4] {'dp'}, dimensions={0}, use_global_device_ids=true | all-gather | bytes 331776 | tf_op jit(solution)/shard_map/all_gather | solution.py:165
  506.3 33.2 %all_gather.63 = bf16[768,192]{1,0:T(8,128)(2,1)} all-gather(bf16[96,192]{1,0:T(8,128)(2,1)S(1)} %copy-done.24), channel_id=1, replica_groups=mesh['dp'=8,'tensor'=4] {'dp'}, dimensions={0}, use_global_device_ids=true | all-gather | bytes 331776 | tf_op jit(solution)/shard_map/all_gather | solution.py:164
  539.6 33.3 %all_gather.65 = bf16[768,192]{1,0:T(8,128)(2,1)} all-gather(bf16[96,192]{1,0:T(8,128)(2,1)S(1)} %copy-done.25), channel_id=1, replica_groups=mesh['dp'=8,'tensor'=4] {'dp'}, dimensions={0}, use_global_device_ids=true | all-gather | bytes 331776 | tf_op jit(solution)/shard_map/all_gather | solution.py:166
  572.8 31.0 %all_gather.66 = bf16[192,768]{0,1:T(8,128)(2,1)S(1)} all-gather(bf16[192,96]{0,1:T(8,128)(2,1)S(1)} %copy.125), channel_id=1, replica_groups=mesh['dp'=8,'tensor'=4] {'dp'}, dimensions={1}, use_global_device_ids=true | all-gather | bytes 331776 | tf_op jit(solution)/shard_map/all_gather | solution.py:167
  637.1 104.6 %while.37 = (s32[]{:T(128)}, bf16[4,8,64,3,64]{2,4,3,1,0:T(8,128)(2,1)}, f32[4,8,3,64]{3,2,1,0:T(4,128)S(1)}, s32[4,8,8]{2,1,0:T(8,128)S(1)}, bf16[32,64,3,64]{3...) while((s32[]{:T(128)}, ...), condition=%wide.region_13.14_spmd, body=%wide.region_10.13_spmd.sunk | while | flops 210763456 | bytes 37987204 | solution.py:98
  650.0 7.9 gather_fusion.3
  752.6 57.4 %reduce-scatter.17.cloned.1.call-done = f32[512,768]{1,0:T(8,128)} async-done(((f32[2048,768]{1,0:T(8,128)}), f32[512,768]{1,0:T(8,128)}) %reduce-scatter.17.cloned.1.call-update) | async-done | bytes 1572880 | tf_op jit(solution)/shard_map/reduce_scatter | solution.py:194
  815.2 38.9 %all-gather.23.cloned.1.call-done = bf16[768,768]{1,0:T(8,128)(2,1)} async-done(((bf16[96,768]{1,0:T(8,128)(2,1)}), bf16[768,768]{1,0:T(8,128)(2,1)}) %all-gather.23.cloned.1.call-update) | async-done | bytes 1179664 | tf_op jit(solution)/shard_map/all_gather | solution.py:168
  854.0 28.4 %all-gather.21.cloned.1.call-done = bf16[2048,768]{1,0:T(8,128)(2,1)} async-done(((bf16[512,768]{1,0:T(8,128)(2,1)}), bf16[2048,768]{1,0:T(8,128)(2,1)}) %all-gather.21.cloned.1.call-update) | async-done | bytes 3145744 | tf_op jit(solution)/shard_map/all_gather | solution.py:204
  889.9 36.4 %all-gather.25.cloned.1.call-done = bf16[768,768]{0,1:T(8,128)(2,1)} async-done(((bf16[768,96]{0,1:T(8,128)(2,1)}), bf16[768,768]{0,1:T(8,128)(2,1)}) %all-gather.25.cloned.1.call-update) | async-done | bytes 1179664 | tf_op jit(solution)/shard_map/all_gather | solution.py:169
  926.3 9.8 fusion.94
  936.2 56.9 %reduce-scatter.19.cloned.1.call-done = f32[512,768]{1,0:T(8,128)} async-done(((f32[2048,768]{1,0:T(8,128)}), f32[512,768]{1,0:T(8,128)}) %reduce-scatter.19.cloned.1.call-update) | async-done | bytes 1572880 | tf_op jit(solution)/shard_map/reduce_scatter | solution.py:207
  998.8 28.6 %all-gather.27.cloned.1.call-done = bf16[2048,768]{1,0:T(8,128)(2,1)} async-done(((bf16[512,768]{1,0:T(8,128)(2,1)}), bf16[2048,768]{1,0:T(8,128)(2,1)}) %all-gather.27.cloned.1.call-update) | async-done | bytes 3145744 | tf_op jit(solution)/shard_map/all_gather | solution.py:288
  1027.5 9.9 convert_reduce_fusion
  1043.6 58.5 %reduce-scatter.21.cloned.1.call-done = f32[512,768]{1,0:T(8,128)} async-done(((f32[2048,768]{1,0:T(8,128)}), f32[512,768]{1,0:T(8,128)}) %reduce-scatter.21.cloned.1.call-update) | async-done | bytes 1572880 | tf_op jit(solution)/shard_map/reduce_scatter | solution.py:294
  1107.9 28.4 %all-gather.29.cloned.1.call-done = bf16[2048,768]{1,0:T(8,128)(2,1)} async-done(((bf16[512,768]{1,0:T(8,128)(2,1)}), bf16[2048,768]{1,0:T(8,128)(2,1)}) %all-gather.29.cloned.1.call-update) | async-done | bytes 3145744 | tf_op jit(solution)/shard_map/all_gather | solution.py:311
  1152.0 421.7 %while.38 = (s32[]{:T(128)}, f32[32,64,3,64]{3,1,2,0:T(8,128)}, f32[32,64,3,64]{3,1,2,0:T(8,128)}, bf16[4,8,64,3,64]{2,4,3,1,0:T(8,128)(2,1)}, s32[4,8,8]{2,1,0:...) while((s32[]{:T(128)}, f32[32,64,3,64]{3,1,2,0:T(8,128)}, ...), condition=%wide.region_29.30_spmd, body=%wide.region_25.29_spmd.sunk | while | flops 512851840 | bytes 134925552 | solution.py:148
  1152.3 8.0 gather_fusion.4
  1203.4 16.2 scatter_fusion
  1238.3 16.2 scatter_fusion.1
  1257.8 7.9 gather_fusion.4
  1308.8 16.1 scatter_fusion
  1343.6 16.1 scatter_fusion.1
  1363.0 7.9 gather_fusion.4
  1414.0 16.1 scatter_fusion
  1448.8 16.2 scatter_fusion.1
  1468.3 7.9 gather_fusion.4
  1519.3 16.1 scatter_fusion
  1554.1 16.0 scatter_fusion.1
  1607.4 8.1 convolution_convert_fusion.3
  1631.0 18.4 all-to-all-done.1
  1664.3 23.9 %all-to-all-done = bf16[8,96,768]{2,1,0:T(8,128)(2,1)} async-done(((bf16[8,96,768]{2,1,0:T(8,128)(2,1)}), bf16[8,96,768]{2,1,0:T(8,128)(2,1)}, u32[]{:S(2)}, u32[]{:S(2)}) %all-to-all-start) | async-done | bytes 1179680 | tf_op jit(solution)/shard_map/all_to_all | solution.py:31
  1691.4 38.5 %all-reduce = (f32[768]{0:T(1024)S(1)}, f32[768]{0:T(1024)S(1)}, f32[768]{0:T(1024)}, f32[768]{0:T(1024)}, f32[768]{0:T(1024)}, /*index=5*/f32[3072]{0:T(1024)S(1)}, f32[768]{0:T(1024)}, f32[768]{0:T(1024)}, f32[768]{0:T(1024)}) all-reduce(f32[768]{0:T(1024)S(1)} %dynamic_update_slice.23, ...), channel_id=1, replica_groups=mesh['dp'=8,'tensor'=4] {'dp','tensor'}, use_global_device_ids=true, to_apply=%region_33.34 | all-reduce | flops 9216 | bytes 73728 | tf_op jit(solution)/shard_map/psum | solution.py:344
  1735.9 49.3 %reduce-scatter.27.cloned.1.call-done = f32[96,192]{1,0:T(8,128)} async-done(((f32[768,192]{1,0:T(8,128)}), f32[96,192]{1,0:T(8,128)}) %reduce-scatter.27.cloned.1.call-update) | async-done | bytes 73744 | tf_op jit(solution)/shard_map/reduce_scatter | solution.py:338
  1785.2 65.9 %reduce-scatter.25.cloned.1.call-done = f32[96,192]{1,0:T(8,128)} async-done(((f32[768,192]{1,0:T(8,128)}), f32[96,192]{1,0:T(8,128)}) %reduce-scatter.25.cloned.1.call-update) | async-done | bytes 73744 | tf_op jit(solution)/shard_map/reduce_scatter | solution.py:337
  (460 shorter events, 651.3 us)
Async XLA Ops:
  8.0 136.3 %copy-start.44 = (f32[192]{0:T(256)S(1)}, f32[192]{0:T(256)}, u32[]{:S(2)}) copy-start(f32[192]{0:T(256)} %param.32) | copy-start | bytes 2308
  8.0 136.3 %all-gather.11.cloned.1.call-start = ((), (), s32[]{:S(2)}) async-start(), calls=%async_computation.12 | async-start | bytes 3932160 | tf_op jit(solution)/shard_map/all_gather | solution.py:181
  8.8 336.1 %reduce-scatter.13.cloned.1.call-start = ((), (), s32[]{:S(2)}) async-start(), calls=%async_computation.13 | async-start | bytes 7864320 | tf_op jit(solution)/shard_map/reduce_scatter | solution.py:194
  156.5 7.0 copy-start.43
  285.4 59.4 %copy-start.7 = (bf16[512,768]{1,0:T(8,128)(2,1)S(1)}, bf16[512,768]{1,0:T(8,128)(2,1)}, u32[]{:S(2)}) copy-start(bf16[512,768]{1,0:T(8,128)(2,1)} %param.26) | copy-start | bytes 2359300
  285.4 59.4 %copy-start.28 = (f32[768]{0:T(1024)S(1)}, f32[768]{0:T(1024)}, u32[]{:S(2)}) copy-start(f32[768]{0:T(1024)} %param.34) | copy-start | bytes 9220
  285.4 61.7 %copy-start.27 = (f32[768]{0:T(1024)S(1)}, f32[768]{0:T(1024)}, u32[]{:S(2)}) copy-start(f32[768]{0:T(1024)} %param.35) | copy-start | bytes 9220
  285.4 61.7 %copy-start.29 = (f32[768]{0:T(1024)S(1)}, f32[768]{0:T(1024)}, u32[]{:S(2)}) copy-start(f32[768]{0:T(1024)} %param.36) | copy-start | bytes 9220
  285.4 64.3 %all-gather.15.cloned.1.call-start = ((), (), s32[]{:S(2)}) async-start(), calls=%async_computation.15 | async-start | bytes 1327104 | tf_op jit(solution)/shard_map/all_gather | solution.py:168
  286.0 86.4 %all-gather.17.cloned.1.call-start = ((), (), s32[]{:S(2)}) async-start(), calls=%async_computation.16 | async-start | bytes 1327104 | tf_op jit(solution)/shard_map/all_gather | solution.py:169
  286.6 114.8 %all-gather.13.cloned.1.call-start = ((), (), s32[]{:S(2)}) async-start(), calls=%async_computation.14 | async-start | bytes 3932160 | tf_op jit(solution)/shard_map/all_gather | solution.py:204
  348.5 122.6 %reduce-scatter.15.cloned.1.call-start = ((), (), s32[]{:S(2)}) async-start(), calls=%async_computation.17 | async-start | bytes 7864320 | tf_op jit(solution)/shard_map/reduce_scatter | solution.py:207
  349.7 677.8 %copy-start.39 = (f32[768]{0:T(1024)}, f32[768]{0:T(1024)S(1)}, u32[]{:S(2)}) copy-start(f32[768]{0:T(1024)S(1)} %dynamic_slice.49) | copy-start | bytes 9220
  412.7 58.4 %copy-start.37 = (f32[768]{0:T(1024)S(1)}, f32[768]{0:T(1024)}, u32[]{:S(2)}) copy-start(f32[768]{0:T(1024)} %param.40) | copy-start | bytes 9220
  412.7 60.8 %copy-start.30 = (f32[768]{0:T(1024)S(1)}, f32[768]{0:T(1024)}, u32[]{:S(2)}) copy-start(f32[768]{0:T(1024)} %param.41) | copy-start | bytes 9220
  412.8 60.8 %copy-start.38 = (f32[768]{0:T(1024)S(1)}, f32[768]{0:T(1024)}, u32[]{:S(2)}) copy-start(f32[768]{0:T(1024)} %param.42) | copy-start | bytes 9220
  412.8 191.0 %all-gather.19.cloned.1.call-start = ((), (), s32[]{:S(2)}) async-start(), calls=%async_computation.18 | async-start | bytes 3932160 | tf_op jit(solution)/shard_map/all_gather | solution.py:181
  473.2 33.1 %copy-start.24 = (bf16[96,192]{1,0:T(8,128)(2,1)S(1)}, bf16[96,192]{1,0:T(8,128)(2,1)}, u32[]{:S(2)}) copy-start(bf16[96,192]{1,0:T(8,128)(2,1)} %param.28) | copy-start | bytes 110596
  473.2 66.3 %copy-start.25 = (bf16[96,192]{1,0:T(8,128)(2,1)S(1)}, bf16[96,192]{1,0:T(8,128)(2,1)}, u32[]{:S(2)}) copy-start(bf16[96,192]{1,0:T(8,128)(2,1)} %param.31) | copy-start | bytes 110596
  474.8 335.3 %reduce-scatter.17.cloned.1.call-start = ((), (), s32[]{:S(2)}) async-start(), calls=%async_computation.19 | async-start | bytes 7864320 | tf_op jit(solution)/shard_map/reduce_scatter | solution.py:194
  506.3 100.5 %copy-start.15 = (bf16[768,192]{1,0:T(8,128)(2,1)}, bf16[768,192]{1,0:T(8,128)(2,1)S(1)}, u32[]{:S(2)}) copy-start(bf16[768,192]{1,0:T(8,128)(2,1)S(1)} %all_gather.64) | copy-start | bytes 884740
  616.9 6.8 copy-start.21
  751.8 58.2 %copy-start.8 = (bf16[512,768]{1,0:T(8,128)(2,1)S(1)}, bf16[512,768]{1,0:T(8,128)(2,1)}, u32[]{:S(2)}) copy-start(bf16[512,768]{1,0:T(8,128)(2,1)} %param.26) | copy-start | bytes 2359300
  751.8 102.2 %all-gather.23.cloned.1.call-start = ((), (), s32[]{:S(2)}) async-start(), calls=%async_computation.21 | async-start | bytes 1327104 | tf_op jit(solution)/shard_map/all_gather | solution.py:168
  752.6 129.9 %all-gather.21.cloned.1.call-start = ((), (), s32[]{:S(2)}) async-start(), calls=%async_computation.20 | async-start | bytes 3932160 | tf_op jit(solution)/shard_map/all_gather | solution.py:204
  814.1 112.2 %all-gather.25.cloned.1.call-start = ((), (), s32[]{:S(2)}) async-start(), calls=%async_computation.22 | async-start | bytes 1327104 | tf_op jit(solution)/shard_map/all_gather | solution.py:169
  814.7 178.4 %reduce-scatter.19.cloned.1.call-start = ((), (), s32[]{:S(2)}) async-start(), calls=%async_computation.23 | async-start | bytes 7864320 | tf_op jit(solution)/shard_map/reduce_scatter | solution.py:207
  936.1 91.4 %all-gather.27.cloned.1.call-start = ((), (), s32[]{:S(2)}) async-start(), calls=%async_computation.24 | async-start | bytes 3932160 | tf_op jit(solution)/shard_map/all_gather | solution.py:288
  936.2 59.7 %copy-start.18 = (bf16[512,768]{1,0:T(8,128)(2,1)S(1)}, bf16[512,768]{1,0:T(8,128)(2,1)}, u32[]{:S(2)}) copy-start(bf16[512,768]{1,0:T(8,128)(2,1)} %param.27) | copy-start | bytes 2359300
  998.8 103.3 %reduce-scatter.21.cloned.1.call-start = ((), (), s32[]{:S(2)}) async-start(), calls=%async_computation.25 | async-start | bytes 7864320 | tf_op jit(solution)/shard_map/reduce_scatter | solution.py:294
  1027.5 11.6 copy-start.42
  1043.5 58.5 %copy-start.11 = (bf16[512,768]{1,0:T(8,128)(2,1)S(1)}, bf16[512,768]{1,0:T(8,128)(2,1)}, u32[]{:S(2)}) copy-start(bf16[512,768]{1,0:T(8,128)(2,1)} %multiply_convert_fusion.3) | copy-start | bytes 2359300
  1043.6 92.7 %all-gather.29.cloned.1.call-start = ((), (), s32[]{:S(2)}) async-start(), calls=%async_computation.26 | async-start | bytes 3932160 | tf_op jit(solution)/shard_map/all_gather | solution.py:311
  1107.8 624.0 %reduce-scatter.31.cloned.1.call-start = ((), (), s32[]{:S(2)}) async-start(), calls=%async_computation.31 | async-start | bytes 884736
  1140.7 592.7 %reduce-scatter.23.cloned.1.call-start = ((), (), s32[]{:S(2)}) async-start(), calls=%async_computation.27 | async-start | bytes 3932160 | tf_op jit(solution)/shard_map/reduce_scatter | solution.py:330
  1586.1 6.9 copy-start.10
  1615.5 33.9 %all-to-all-start.1 = ((bf16[8,768,96]{1,2,0:T(8,128)(2,1)}), bf16[8,768,96]{1,2,0:T(8,128)(2,1)}, u32[]{:S(2)}, u32[]{:S(2)}) async-start(bf16[8,768,96]{1,2,0:T(8,128)(2,1)} %bitcast.255), calls=%async_computation.10 | async-start | bytes 2359296 | tf_op jit(solution)/shard_map/all_to_all | solution.py:31
  1620.4 115.5 %reduce-scatter.29.cloned.1.call-start = ((), (), s32[]{:S(2)}) async-start(), calls=%async_computation.30 | async-start | bytes 884736 | tf_op jit(solution)/shard_map/reduce_scatter | solution.py:339
  1649.4 38.8 %all-to-all-start = ((bf16[8,96,768]{2,1,0:T(8,128)(2,1)}), bf16[8,96,768]{2,1,0:T(8,128)(2,1)}, u32[]{:S(2)}, u32[]{:S(2)}) async-start(bf16[8,96,768]{2,1,0:T(8,128)(2,1)} %bitcast.254), calls=%async_computation.9 | async-start | bytes 2359296 | tf_op jit(solution)/shard_map/all_to_all | solution.py:31
  1653.7 131.5 %reduce-scatter.27.cloned.1.call-start = ((), (), s32[]{:S(2)}) async-start(), calls=%async_computation.29 | async-start | bytes 884736 | tf_op jit(solution)/shard_map/reduce_scatter | solution.py:338
  1657.7 193.4 %reduce-scatter.25.cloned.1.call-start = ((), (), s32[]{:S(2)}) async-start(), calls=%async_computation.28 | async-start | bytes 884736 | tf_op jit(solution)/shard_map/reduce_scatter | solution.py:337
  1661.7 29.6 %copy-start.31 = (f32[768]{0:T(1024)S(1)}, f32[768]{0:T(1024)}, u32[]{:S(2)}) copy-start(f32[768]{0:T(1024)} %get-tuple-element.256) | copy-start | bytes 9220
  1661.7 29.6 %copy-start.32 = (f32[768]{0:T(1024)S(1)}, f32[768]{0:T(1024)}, u32[]{:S(2)}) copy-start(f32[768]{0:T(1024)} %get-tuple-element.261) | copy-start | bytes 9220
  1661.7 29.6 %copy-start.33 = (f32[768]{0:T(1024)S(1)}, f32[768]{0:T(1024)}, u32[]{:S(2)}) copy-start(f32[768]{0:T(1024)} %get-tuple-element.328) | copy-start | bytes 9220
  1661.7 29.6 %copy-start.34 = (f32[768]{0:T(1024)S(1)}, f32[768]{0:T(1024)}, u32[]{:S(2)}) copy-start(f32[768]{0:T(1024)} %get-tuple-element.254) | copy-start | bytes 9220
  1661.7 29.6 %copy-start.35 = (f32[768]{0:T(1024)S(1)}, f32[768]{0:T(1024)}, u32[]{:S(2)}) copy-start(f32[768]{0:T(1024)} %get-tuple-element.259) | copy-start | bytes 9220
  1661.7 29.6 %copy-start.36 = (f32[768]{0:T(1024)S(1)}, f32[768]{0:T(1024)}, u32[]{:S(2)}) copy-start(f32[768]{0:T(1024)} %get-tuple-element.262) | copy-start | bytes 9220
  1661.8 71.7 %copy-start.12 = (bf16[512,768]{1,0:T(8,128)(2,1)S(1)}, bf16[512,768]{1,0:T(8,128)(2,1)}, u32[]{:S(2)}) copy-start(bf16[512,768]{1,0:T(8,128)(2,1)} %get-tuple-element.329) | copy-start | bytes 2359300
  (32 other events, 81.0 us)
Sparse Core Ops, SparseCore 0:
  10.4 31.2 all-gather.10
  285.5 59.2 reduce-scatter.12
  474.9 28.5 all-gather.18
  936.2 56.8 reduce-scatter.18
  998.9 28.5 all-gather.26
  1043.7 58.3 reduce-scatter.20
Sparse Core Ops, SparseCore 1:
  288.1 42.4 all-gather.14
  332.6 39.8 all-gather.16
  374.5 26.8 all-gather.12
  412.8 58.2 reduce-scatter.14
  751.9 58.1 reduce-scatter.16
  812.5 41.5 all-gather.22
  855.6 26.8 all-gather.20
  884.7 41.5 all-gather.24
  1107.9 28.3 all-gather.28
  1140.8 62.5 reduce-scatter.30
  1606.8 36.9 reduce-scatter.22
  1648.1 71.6 reduce-scatter.28
  1723.5 61.6 reduce-scatter.26
  1789.4 61.5 reduce-scatter.24
where the time goes:
time: 1870 us; the launch traced here: 1860 us
  waiting for transfers between devices  662 us (35%)
  local copies, waits for them, and re-layouts  435 us (23%)
  blocking collectives  298 us (16%)
  matrix products  253 us (14%)
  other arithmetic  181 us (10%)
    reduce_scatter x2, waiting for transfers between devices, layer_forward(): lax.psum_scatter(jnp.dot(mixed_low, out_all, preferred_element_type=f32),...  116 us
    reduce_scatter x2, waiting for transfers between devices, layer_forward(): lax.psum_scatter(jnp.dot(activated, down_all, preferred_element_type=f32)...  115 us
    gather x12, local copies, waits for them, and re-layouts, one_group(): v_part = value_rows[table_part].reshape(group_size, -1, local_heads, HD)  88.5 us
    gather x12, local copies, waits for them, and re-layouts, one_group(): k_part = key_rows[table_part].reshape(group_size, -1, local_heads, HD)  82.1 us
    all_gather x2, blocking collectives, gather_layer(): lax.all_gather(shards[0], 'dp', axis=0, tiled=True)  66.7 us
    all_gather x2, blocking collectives, gather_layer(): lax.all_gather(shards[2], 'dp', axis=0, tiled=True)  66.4 us
    reduce_scatter x1, waiting for transfers between devices, per_device(): lax.psum_scatter(grad_w_query, 'dp', scatter_dimension=0, tiled=True)  65.9 us
    all_gather x2, blocking collectives, gather_layer(): lax.all_gather(shards[1], 'dp', axis=0, tiled=True)  64.7 us
  transfers between devices with their start and end apart: 22, of which 16 were waited for; matrix products, arithmetic and copies ran while one was open for 28% of the time, Pallas kernels for 0%

commit v1 on v0

v1 whole, which is shorter than its diff:
```python
from functools import partial

import jax
import jax.numpy as jnp
from jax import lax
from jax.experimental import pallas as pl
from jax.experimental.pallas import tpu as pltpu
from jax.sharding import PartitionSpec as P

D = 768
HD = 64
FF = 3072
BLK = 64
GLOB = 2
RAND = 3
LMAX = 2048
NB = 32
KEYS = (3 + GLOB + RAND) * BLK
PAD = 256
LANES = 128

masked_score = -1e30
EPSILON = 1e-12
f32 = jnp.float32
bf16 = jnp.bfloat16


def swap(array, bit):
    size = lax.axis_size("tensor")
    return lax.ppermute(array, "tensor", [(t, t ^ bit) for t in range(size)])


def dp_swap(array, bit):
    size = lax.axis_size("dp")
    return lax.ppermute(array, "dp", [(t, t ^ bit) for t in range(size)])


def ring_order(size):
    return list(range(0, size, 2)) + list(range(size - 1, 0, -2))


def ring_member(steps):
    size = lax.axis_size("dp")
    me = lax.axis_index("dp")
    place = jnp.where(me % 2 == 0, me // 2, size - 1 - me // 2)
    place = (place + steps + size) % size
    return jnp.where(place < size // 2, 2 * place, 2 * (size - 1 - place) + 1)


def ring_send(array, step):
    size = lax.axis_size("dp")
    order = ring_order(size)
    return lax.ppermute(
        array, "dp", [(order[i], order[(i + step) % size]) for i in range(size)]
    )


def gather_rows(shard):
    size = lax.axis_size("dp")
    if size != 8:
        return lax.all_gather(shard, "dp", axis=0, tiled=True)
    rows, width = shard.shape
    whole = jnp.zeros((size, rows, width), shard.dtype)

    def put(whole, piece, steps):
        return lax.dynamic_update_slice(whole, piece[None], (ring_member(steps), 0, 0))

    whole = put(whole, shard, 0)
    ahead, behind = shard, shard
    for step in range(1, size // 2 + 1):
        ahead = ring_send(ahead, 1)
        if step < size // 2:
            behind = ring_send(behind, -1)
        whole = put(whole, ahead, -step)
        if step < size // 2:
            whole = put(whole, behind, step)
    return whole.reshape(size * rows, width)


def scatter_sum(partial_sums):
    size = lax.axis_size("dp")
    if size != 8:
        return lax.psum_scatter(partial_sums, "dp", scatter_dimension=0, tiled=True).astype(f32)
    width = partial_sums.shape[1]
    blocks = partial_sums.reshape(size, -1, width)

    def part(steps):
        return lax.dynamic_index_in_dim(blocks, ring_member(steps), 0, keepdims=False)

    half = size // 2
    ahead = ring_send(part(half), 1)
    behind = ring_send(part(1 - half), -1)
    for left in range(half - 1, 0, -1):
        ahead = ring_send((ahead.astype(f32) + part(left).astype(f32)).astype(bf16), 1)
        if left > 1:
            behind = ring_send(
                (behind.astype(f32) + part(1 - left).astype(f32)).astype(bf16), -1
            )
    return ahead.astype(f32) + behind.astype(f32) + part(0).astype(f32)


def sum_over(vector, dp_only=False):
    if not dp_only:
        bit = 1
        while bit < lax.axis_size("tensor"):
            vector = vector + swap(vector, bit)
            bit *= 2
    bit = 1
    while bit < lax.axis_size("dp"):
        vector = vector + dp_swap(vector, bit)
        bit *= 2
    return vector


def layer_norm(values, gain_vec, shift_vec):
    centred = values - jnp.mean(values, axis=-1, keepdims=True)
    inv_std = lax.rsqrt(jnp.mean(centred * centred, axis=-1, keepdims=True) + EPSILON)
    scaled = centred * inv_std
    return (scaled * gain_vec + shift_vec, scaled, inv_std)


def norm_backward(upstream, scaled, inv_std, gain_vec):
    weighted = upstream * gain_vec
    inner_sum = jnp.mean(weighted * scaled, axis=-1, keepdims=True)
    grad_values = inv_std * (
        weighted - jnp.mean(weighted, axis=-1, keepdims=True) - scaled * inner_sum
    )
    return (grad_values, jnp.sum(upstream * scaled, axis=0), jnp.sum(upstream, axis=0))


def block_tables(lengths, global_raw, random_raw, own_blocks):
    seq_count = lengths.shape[0]
    me = lax.axis_index("tensor")
    live_count = (lengths + BLK - 1) // BLK
    block_ids = jnp.arange(NB, dtype=jnp.int32)
    left_block = jnp.maximum(block_ids - 1, 0)
    right_block = jnp.minimum(block_ids + 1, NB - 1)
    near_ids = jnp.broadcast_to(
        jnp.stack([left_block, block_ids, right_block], axis=1)[None], (seq_count, NB, 3)
    )
    global_ids = jnp.broadcast_to(
        (global_raw % live_count[:, None])[:, None, :], (seq_count, NB, GLOB)
    )
    random_ids = random_raw % live_count[:, None, None]
    key_table = jnp.concatenate([near_ids, global_ids, random_ids], axis=2)
    near_ok = jnp.stack([block_ids >= 1, block_ids >= 0, block_ids + 1 < NB], axis=1)
    block_ok = jnp.concatenate([near_ok, jnp.ones((NB, GLOB + RAND), dtype=jnp.bool_)], axis=1)
    position = key_table[..., None] * BLK + jnp.arange(BLK, dtype=jnp.int32)
    key_valid = block_ok[None, :, :, None] & (position < lengths[:, None, None, None])
    bias = jnp.where(key_valid, 0.0, masked_score).astype(f32).reshape(seq_count * NB, KEYS)
    offsets = jnp.arange(seq_count, dtype=jnp.int32)[:, None, None] * NB
    table = (key_table + offsets).reshape(seq_count * NB, -1)
    table = ((table // own_blocks) ^ me) * own_blocks + table % own_blocks
    pieces = seq_count * NB // own_blocks
    order = jnp.arange(pieces, dtype=jnp.int32) ^ me
    table = jnp.take(table.reshape(pieces, own_blocks, -1), order, axis=0)
    bias = jnp.take(bias.reshape(pieces, own_blocks, KEYS), order, axis=0)
    return table.reshape(pieces * own_blocks, -1), bias.reshape(pieces * own_blocks, KEYS)


def head_masks(heads, scale, dtype):
    lane = lax.broadcasted_iota(jnp.int32, (1, PAD), 1)
    return [
        jnp.where((lane >= h * HD) & (lane < (h + 1) * HD), scale, 0.0).astype(dtype)
        for h in range(heads)
    ]


def stacked_heads(rows, masks):
    return jnp.concatenate([rows * mask for mask in masks], axis=0)


def unstacked_heads(stacked, masks):
    rows = stacked.shape[0] // len(masks)
    total = stacked[:rows] * masks[0]
    for h in range(1, len(masks)):
        total = total + stacked[h * rows : (h + 1) * rows] * masks[h]
    return total


def key_blocks(ref, table, block, column):
    return jnp.concatenate(
        [
            ref[pl.ds(pl.multiple_of(table[block, j] * BLK, BLK), BLK), column : column + PAD]
            for j in range(KEYS // BLK)
        ],
        axis=0,
    )


def contract(a, b, dims):
    return lax.dot_general(a, b, ((dims[:1], dims[1:]), ((), ())), preferred_element_type=f32)


def attend_kernel(heads, chosen, pieces, own_blocks, table, *refs):
    parts = refs[:pieces]
    bias = refs[pieces]
    outs = refs[pieces + 1 : pieces + 1 + len(chosen)]
    totals = refs[pieces + 1 + len(chosen) : pieces + 1 + 2 * len(chosen)]
    rows, sems = refs[pieces + 1 + 2 * len(chosen) :]
    own_rows = own_blocks * BLK
    copies = [
        pltpu.make_async_copy(
            parts[s], rows.at[pl.ds(s * own_rows, own_rows)], sems.at[s]
        )
        for s in range(pieces)
    ]
    for copy in copies:
        copy.start()
    for copy in copies:
        copy.wait()
    query_masks = head_masks(heads, HD**-0.5, bf16)
    out_masks = head_masks(heads, 1.0, f32)
    lane = lax.broadcasted_iota(jnp.int32, (BLK, LANES), 1)

    def step(i, carry):
        for at, s in enumerate(chosen):
            block = s * own_blocks + i
            start = pl.multiple_of(i * BLK, BLK)
            queries = stacked_heads(
                rows[pl.ds(pl.multiple_of(block * BLK, BLK), BLK), 0:PAD], query_masks
            )
            keys = key_blocks(rows, table, block, PAD)
            values = key_blocks(rows, table, block, 2 * PAD)
            scores = contract(queries, keys, (1, 1)) + bias[pl.ds(block, 1), :]
            top = jnp.max(scores, axis=-1, keepdims=True)
            weights = jnp.exp(scores - top)
            total = jnp.sum(weights, axis=-1, keepdims=True)
            mixed = contract(weights.astype(bf16), values, (1, 0)) / total
            outs[at][pl.ds(start, BLK), :] = unstacked_heads(mixed, out_masks).astype(bf16)
            log_total = top + jnp.log(total)
            kept = jnp.zeros((BLK, LANES), f32)
            for h in range(heads):
                kept = jnp.where(lane == h, log_total[h * BLK : (h + 1) * BLK], kept)
            totals[at][pl.ds(start, BLK), :] = kept
        return carry

    lax.fori_loop(0, own_blocks, step, 0)


def attend_forward(parts, table, bias, heads, chosen):
    own_rows = parts[0].shape[0]
    pieces = len(parts)
    own_blocks = own_rows // BLK
    n = len(chosen)
    vmem = pl.BlockSpec(memory_space=pltpu.VMEM)
    work = n * own_rows * KEYS * heads
    results = pl.pallas_call(
        partial(attend_kernel, heads, chosen, pieces, own_blocks),
        out_shape=[jax.ShapeDtypeStruct((own_rows, PAD), bf16)] * n
        + [jax.ShapeDtypeStruct((own_rows, LANES), f32)] * n,
        in_specs=[pl.BlockSpec(memory_space=pltpu.SMEM)]
        + [pl.BlockSpec(memory_space=pl.ANY)] * pieces
        + [vmem],
        out_specs=[vmem] * (2 * n),
        scratch_shapes=[
            pltpu.VMEM((pieces * own_rows, 3 * PAD), bf16),
            pltpu.SemaphoreType.DMA((pieces,)),
        ],
        cost_estimate=pl.CostEstimate(
            flops=12 * work * HD, bytes_accessed=4 << 20, transcendentals=work
        ),
        name="attend_forward",
    )(table, *parts, bias)
    return results[:n], results[n:]


def attend_back_kernel(heads, pieces, own_blocks, table, *refs):
    parts = refs[:pieces]
    ups = refs[pieces : 2 * pieces]
    totals = refs[2 * pieces : 3 * pieces]
    bias = refs[3 * pieces]
    outs = refs[3 * pieces + 1 : 4 * pieces + 1]
    rows, up_rows, key_sum, value_sum, sems = refs[4 * pieces + 1 :]
    own_rows = own_blocks * BLK
    copies = [
        pltpu.make_async_copy(
            parts[s], rows.at[pl.ds(s * own_rows, own_rows)], sems.at[s]
        )
        for s in range(pieces)
    ] + [
        pltpu.make_async_copy(
            ups[s], up_rows.at[pl.ds(s * own_rows, own_rows)], sems.at[pieces + s]
        )
        for s in range(pieces)
    ]
    for copy in copies:
        copy.start()
    key_sum[...] = jnp.zeros_like(key_sum)
    value_sum[...] = jnp.zeros_like(value_sum)
    for copy in copies:
        copy.wait()
    query_masks = head_masks(heads, HD**-0.5, bf16)
    up_masks = head_masks(heads, 1.0, bf16)
    out_masks = head_masks(heads, HD**-0.5, f32)
    for s in range(pieces):

        def step(i, carry, s=s):
            block = s * own_blocks + i
            start = pl.multiple_of(i * BLK, BLK)
            at = pl.ds(pl.multiple_of(block * BLK, BLK), BLK)
            queries = stacked_heads(rows[at, 0:PAD], query_masks)
            upstream = stacked_heads(up_rows[at, :], up_masks)
            keys = key_blocks(rows, table, block, PAD)
            values = key_blocks(rows, table, block, 2 * PAD)
            kept = totals[s][pl.ds(start, BLK), :]
            log_total = jnp.concatenate([kept[:, h : h + 1] for h in range(heads)], axis=0)
            scores = contract(queries, keys, (1, 1)) + bias[pl.ds(block, 1), :]
            weights = jnp.exp(scores - log_total)
            grad_weights = contract(upstream, values, (1, 1))
            inner = jnp.sum(weights * grad_weights, axis=-1, keepdims=True)
            grad_scores = (weights * (grad_weights - inner)).astype(bf16)
            grad_query = contract(grad_scores, keys, (1, 0))
            outs[s][pl.ds(start, BLK), 0:PAD] = unstacked_heads(grad_query, out_masks).astype(bf16)
            key_part = contract(grad_scores, queries, (0, 0))
            value_part = contract(weights.astype(bf16), upstream, (0, 0))
            for j in range(KEYS // BLK):
                there = pl.ds(pl.multiple_of(table[block, j] * BLK, BLK), BLK)
                key_sum[there, :] += key_part[j * BLK : (j + 1) * BLK]
                value_sum[there, :] += value_part[j * BLK : (j + 1) * BLK]
            return carry

        lax.fori_loop(0, own_blocks, step, 0)
    for s in range(pieces):
        span = pl.ds(s * own_rows, own_rows)
        outs[s][:, PAD : 2 * PAD] = key_sum[span, :].astype(bf16)
        outs[s][:, 2 * PAD : 3 * PAD] = value_sum[span, :].astype(bf16)


def attend_backward(parts, ups, totals, table, bias, heads):
    own_rows = parts[0].shape[0]
    pieces = len(parts)
    own_blocks = own_rows // BLK
    vmem = pl.BlockSpec(memory_space=pltpu.VMEM)
    work = pieces * own_rows * KEYS * heads
    return pl.pallas_call(
        partial(attend_back_kernel, heads, pieces, own_blocks),
        out_shape=[jax.ShapeDtypeStruct((own_rows, 3 * PAD), bf16)] * pieces,
        in_specs=[pl.BlockSpec(memory_space=pltpu.SMEM)]
        + [pl.BlockSpec(memory_space=pl.ANY)] * (2 * pieces)
        + [vmem] * (pieces + 1),
        out_specs=[vmem] * pieces,
        scratch_shapes=[
            pltpu.VMEM((pieces * own_rows, 3 * PAD), bf16),
            pltpu.VMEM((pieces * own_rows, PAD), bf16),
            pltpu.VMEM((pieces * own_rows, PAD), f32),
            pltpu.VMEM((pieces * own_rows, PAD), f32),
            pltpu.SemaphoreType.DMA((2 * pieces,)),
        ],
        cost_estimate=pl.CostEstimate(
            flops=30 * work * HD, bytes_accessed=12 << 20, transcendentals=work
        ),
        name="attend_backward",
    )(table, *parts, *ups, *totals, bias)


def padded(array):
    return jnp.pad(array, ((0, 0), (0, PAD - array.shape[1])))


def dot(a, b, dims=(1, 0)):
    return contract(a, b, dims)


def per_device(
    hidden_in,
    grad_out,
    w_query,
    b_query,
    w_key,
    w_value,
    b_value,
    w_out,
    b_out,
    gain_one,
    shift_one,
    w_up,
    b_up,
    w_down,
    b_down,
    gain_two,
    shift_two,
    lengths,
    global_raw,
    random_raw,
):
    own_rows = hidden_in.shape[0]
    me = lax.axis_index("tensor")
    width = w_query.shape[1]
    heads = width // HD
    hidden = w_up.shape[1]

    table, bias = block_tables(lengths, global_raw, random_raw, own_rows // BLK)

    x2 = swap(hidden_in, 2)
    x1 = swap(hidden_in, 1)
    x3 = swap(x2, 1)
    x_parts = [hidden_in, x1, x2, x3]

    qkv_w = gather_rows(jnp.concatenate([padded(w_query), padded(w_key), padded(w_value)], axis=1))
    out_t = padded(w_out.T)
    down_t = w_down.T
    up_far, out_far, down_far = swap(w_up, 2), swap(out_t, 2), swap(down_t, 2)
    up_out = gather_rows(jnp.concatenate([w_up, up_far, out_t, out_far], axis=1))
    up_w = up_out[:, : 2 * hidden]
    out_near = up_out[:, 2 * hidden :]
    down_w = gather_rows(jnp.concatenate([down_t, down_far], axis=1))
    out_other = swap(out_near, 1)
    out_ws = [
        out_near[:, :PAD],
        out_other[:, :PAD],
        out_near[:, PAD:],
        out_other[:, PAD:],
    ]
    b_up_parts = b_up.reshape(-1, hidden)
    b_up_used = jnp.concatenate([jnp.take(b_up_parts, me, axis=0), jnp.take(b_up_parts, me ^ 2, axis=0)])

    qkv_b = jnp.concatenate(
        [jnp.pad(b_query, (0, PAD - width)), jnp.zeros((PAD,), f32), jnp.pad(b_value, (0, PAD - width))]
    )
    qkv = [(dot(x, qkv_w) + qkv_b).astype(bf16) for x in x_parts]

    (o2, o3), (t2, t3) = attend_forward(qkv, table, bias, heads, (2, 3))
    r2 = swap(o2, 2)
    r3 = swap(o3, 3)
    (o0, o1), (t0, t1) = attend_forward(qkv, table, bias, heads, (0, 1))
    r1 = swap(o1, 1)
    mixed = [o0, r1, r2, r3]

    after = hidden_in.astype(f32) + b_out
    for o, w in zip(mixed, out_ws):
        after = after + dot(o, w, (1, 1))
    normed, scaled_one, inv_one = layer_norm(after, gain_one, shift_one)
    normed_low = normed.astype(bf16)
    rows_low = jnp.concatenate([normed_low, swap(normed_low, 1)], axis=0)
    up_pre = dot(rows_low, up_w) + b_up_used
    activated, gelu_pull = jax.vjp(partial(jax.nn.gelu, approximate=True), up_pre)
    activated = activated.astype(bf16)
    ffn = dot(activated, down_w, (1, 1))
    summed = normed + b_down + ffn[:own_rows] + swap(ffn[own_rows:], 1)
    layer_out, scaled_two, inv_two = layer_norm(summed, gain_two, shift_two)

    row_ids = me * own_rows + jnp.arange(own_rows, dtype=jnp.int32)
    keep_rows = row_ids % LMAX < jnp.take(lengths, row_ids // LMAX)
    upstream = jnp.where(keep_rows[:, None], grad_out.astype(f32), 0.0)
    grad_summed, grad_gain_two, grad_shift_two = norm_backward(
        upstream, scaled_two, inv_two, gain_two
    )
    grad_low = grad_summed.astype(bf16)
    grad_b_down = jnp.sum(grad_low.astype(f32), axis=0)
    grads_low = jnp.concatenate([grad_low, swap(grad_low, 1)], axis=0)
    down_sums = dot(grads_low, activated, (0, 0)).astype(bf16)
    grad_up = gelu_pull(dot(grads_low, down_w))[0].astype(bf16)
    grad_b_up = jnp.sum(grad_up.astype(f32), axis=0)
    back = dot(grad_up, up_w, (1, 1))
    up_sums = dot(rows_low, grad_up, (0, 0)).astype(bf16)
    grad_normed = grad_low.astype(f32) + back[:own_rows] + swap(back[own_rows:], 1)
    grad_after, grad_gain_one, grad_shift_one = norm_backward(
        grad_normed, scaled_one, inv_one, gain_one
    )
    after_low = grad_after.astype(bf16)
    grad_b_out = jnp.sum(after_low.astype(f32), axis=0)

    grad_mixed = [dot(after_low, w).astype(bf16) for w in out_ws]
    ups = [grad_mixed[0]] + [swap(grad_mixed[s], s) for s in range(1, 4)]
    out_sums = [dot(after_low, o, (0, 0)).astype(bf16) for o in mixed]
    out_pair = jnp.concatenate([out_sums[0], out_sums[2]], axis=1).astype(f32) + swap(
        jnp.concatenate([out_sums[1], out_sums[3]], axis=1), 1
    ).astype(f32)

    down_part = scatter_sum(down_sums)
    up_part = scatter_sum(jnp.concatenate([up_sums, out_pair.astype(bf16)], axis=1))

    grads = attend_backward(qkv, ups, [t0, t1, t2, t3], table, bias, heads)
    parts = [dot(g, qkv_w, (1, 1)) for g in grads]
    far = parts[2] + swap(parts[3].astype(bf16), 1).astype(f32)
    far = swap(far.astype(bf16), 2)
    near = parts[0] + swap(parts[1].astype(bf16), 1).astype(f32)
    grad_in = after_low.astype(f32) + near + far.astype(f32)

    qkv_sums = dot(x_parts[0], grads[0], (0, 0))
    for s in range(1, 4):
        qkv_sums = qkv_sums + dot(x_parts[s], grads[s], (0, 0))
    qkv_part = scatter_sum(qkv_sums.astype(bf16))

    def far_sum(part, cut):
        return part[:, :cut] + swap(part[:, cut:].astype(bf16), 2).astype(f32)

    grad_w_down = far_sum(down_part, hidden).T
    grad_w_up = far_sum(up_part[:, : 2 * hidden], hidden)
    grad_w_out = far_sum(up_part[:, 2 * hidden :], PAD)[:, :width].T

    up_slots = jnp.zeros((FF // hidden, hidden), f32)
    up_slots = lax.dynamic_update_slice(up_slots, grad_b_up[None, :hidden], (me, 0))
    up_slots = lax.dynamic_update_slice(up_slots, grad_b_up[None, hidden:], (me ^ 2, 0))
    rows = [grad_gain_two, grad_shift_two, grad_b_down, grad_gain_one, grad_shift_one, grad_b_out]
    small = sum_over(jnp.concatenate([jnp.stack(rows).reshape(-1), up_slots.reshape(-1)]))
    small_rows = small[: 6 * D].reshape(6, D)
    bias_up = jnp.take(small[6 * D :].reshape(-1, hidden), me, axis=0)
    row_sums = sum(jnp.sum(g.astype(f32), axis=0) for g in grads)
    bias_pair = sum_over(jnp.concatenate([row_sums[:PAD], row_sums[2 * PAD :]]), dp_only=True)

    return (
        layer_out.astype(bf16),
        grad_in,
        qkv_part[:, :width],
        bias_pair[:width],
        qkv_part[:, PAD : PAD + width],
        qkv_part[:, 2 * PAD : 2 * PAD + width],
        bias_pair[PAD : PAD + width],
        grad_w_out,
        small_rows[5],
        small_rows[3],
        small_rows[4],
        grad_w_up,
        bias_up,
        grad_w_down,
        small_rows[2],
        small_rows[0],
        small_rows[1],
    )


def solution(mesh):
    in_specs = (
        P(("dp", "tensor"), None),
        P(("dp", "tensor"), None),
        P("dp", "tensor"),
        P("tensor"),
        P("dp", "tensor"),
        P("dp", "tensor"),
        P("tensor"),
        P("tensor", "dp"),
        P(),
        P(),
        P(),
        P("dp", "tensor"),
        P(),
        P("tensor", "dp"),
        P(),
        P(),
        P(),
        P("dp"),
        P("dp", None),
        P("dp", None, None),
    )
    out_specs = (
        P(("dp", "tensor"), None),
        P(("dp", "tensor"), None),
        P("dp", "tensor"),
        P("tensor"),
        P("dp", "tensor"),
        P("dp", "tensor"),
        P("tensor"),
        P("tensor", "dp"),
        P(),
        P(),
        P(),
        P("dp", "tensor"),
        P("tensor"),
        P("tensor", "dp"),
        P(),
        P(),
        P(),
    )
    return jax.shard_map(
        per_device, mesh=mesh, in_specs=in_specs, out_specs=out_specs, check_vma=False
    )
```

time: 1870 us -> 375 us (0.20)
  waiting for transfers between devices: 662 us -> 122 us
  local copies, waits for them, and re-layouts: 435 us -> 35.3 us
  blocking collectives: 298 us -> 0 us
  matrix products: 253 us -> 68 us
  other arithmetic: 181 us -> 23.8 us
  starting transfers between devices: 10.8 us -> 69.2 us
  Pallas kernels: 0 us -> 47.1 us
    reduce_scatter x9 -> x0, waiting for transfers between devices: 404 us -> none  [the longest x2 116 us: layer_forward(): lax.psum_scatter(jnp.dot(mixed_low, out_all, preferred_element_type=f32),...]
    all_gather x8 -> x0, blocking collectives: 260 us -> none  [the longest x2 66.7 us: gather_layer(): lax.all_gather(shards[0], 'dp', axis=0, tiled=True)]
    all_gather x10 -> x0, waiting for transfers between devices: 212 us -> none  [the longest x2 59.1 us: gather_layer(): lax.all_gather(shards[5], 'dp', axis=1, tiled=True)]
    dot_general x58 -> x30, matrix products: 248 us -> 68 us  [contract(): lax.dot_general(a, b, ((dims[:1], dims[1:]), ((), ())), preferred_element...]
    gather x24 -> x2, local copies, waits for them, and re-layouts: 171 us -> 1.1 us  [the longest x1 0.55 us: block_tables(): bias = jnp.take(bias.reshape(pieces, own_blocks, KEYS), order, axis=0)]
    reshape x29 -> x3, local copies, waits for them, and re-layouts: 142 us -> 0.03 us  [the longest x1 0.01 us: per_device(): b_up_parts = b_up.reshape(-1, hidden)]
    scatter-add x8 -> x0, other arithmetic: 129 us -> none  [the longest x4 64.6 us: one_group(): grad_keys.at[flat_ids].add(key_part.reshape(-1, BLK, local_heads, HD))]
    ppermute x0 -> x74, waiting for transfers between devices: none -> 122 us  [the longest x42 83.6 us: ring_send(): lax.ppermute(array, 'dp', [(order[i], order[(i + step) % size]) for i in...]
  transfers between devices with their start and end apart: 22 -> 74, of which waited for: 16 -> 34; matrix products, arithmetic and copies ran while one was open for 28% -> 23% of each run, Pallas kernels for 0% -> 13%
where the time goes in v1:
time: 375 us; the launch traced here: 368 us
  waiting for transfers between devices  122 us (33%)
  starting transfers between devices  69.2 us (18%)
  matrix products  68 us (18%)
  Pallas kernels  47.1 us (13%)
  local copies, waits for them, and re-layouts  35.3 us (9%)
  other arithmetic  23.8 us (6%)
    ppermute x42, waiting for transfers between devices, ring_send(): lax.ppermute(array, 'dp', [(order[i], order[(i + step) % size]) for i in...  83.6 us
    dot_general x30, matrix products, contract(): lax.dot_general(a, b, ((dims[:1], dims[1:]), ((), ())), preferred_element...  68 us
    ppermute x42, starting transfers between devices, ring_send(): lax.ppermute(array, 'dp', [(order[i], order[(i + step) % size]) for i in...  47.2 us
    ppermute x26, waiting for transfers between devices, swap(): return lax.ppermute(array, 'tensor', [(t, t ^ bit) for t in range(size)])  35.4 us
    pallas_call x1, Pallas kernels, attend_backward(): pl.pallas_call(partial(attend_back_kernel, heads, pieces, own_blocks), ou...  29.3 us
    pallas_call x2, Pallas kernels, attend_forward(): pl.pallas_call(partial(attend_kernel, heads, chosen, pieces, own_blocks),...  17.8 us
    ppermute x26, starting transfers between devices, swap(): return lax.ppermute(array, 'tensor', [(t, t ^ bit) for t in range(size)])  12.1 us
    dynamic_update_slice x21, local copies, waits for them, and re-layouts, put(): lax.dynamic_update_slice(whole, piece[None], (ring_member(steps), 0, 0))  11.5 us
  transfers between devices with their start and end apart: 74, of which 34 were waited for; matrix products, arithmetic and copies ran while one was open for 23% of the time, Pallas kernels for 13%

profile of v1, /device:TPU:0, one launch (start us, length us, event | category | flops | bytes accessed | tf_op | source)
XLA Modules:
  0.0 368.4 jit_solution(4202773801710002352)
XLA Ops:
  2.2 3.0 collective-permute-start
  20.1 10.1 %collective-permute-done.11 = bf16[96,256]{1,0:T(8,128)(2,1)S(1)} collective-permute-done((bf16[96,256]{1,0:T(8,128)(2,1)S(1)}, bf16[96,256]{1,0:T(8,128)(2,1)S(1)}, u32[]{:S(2)}, u32[]{:S(2)}) %collective-permute-start.11) | collective-permute-done | bytes 49184 | tf_op jit(solution)/shard_map/ppermute | solution.py:30
  37.2 5.7 %collective-permute-done.2 = bf16[96,768]{1,0:T(8,128)(2,1)S(1)} collective-permute-done((bf16[96,768]{1,0:T(8,128)(2,1)}, bf16[96,768]{1,0:T(8,128)(2,1)S(1)}, u32[]{:S(2)}, u32[]{:S(2)}) %collective-permute-start.2) | collective-permute-done | bytes 147488 | tf_op jit(solution)/shard_map/ppermute | solution.py:53
  44.6 3.4 collective-permute-done.3
  52.1 6.9 %collective-permute-done.4 = bf16[96,768]{1,0:T(8,128)(2,1)S(1)} collective-permute-done((bf16[96,768]{1,0:T(8,128)(2,1)S(1)}, bf16[96,768]{1,0:T(8,128)(2,1)S(1)}, u32[]{:S(2)}, u32[]{:S(2)}) %collective-permute-start.4) | collective-permute-done | bytes 147488 | tf_op jit(solution)/shard_map/ppermute | solution.py:53
  60.8 5.0 %collective-permute-done.5 = bf16[96,768]{1,0:T(8,128)(2,1)S(1)} collective-permute-done((bf16[96,768]{1,0:T(8,128)(2,1)S(1)}, bf16[96,768]{1,0:T(8,128)(2,1)S(1)}, u32[]{:S(2)}, u32[]{:S(2)}) %collective-permute-start.5) | collective-permute-done | bytes 147488 | tf_op jit(solution)/shard_map/ppermute | solution.py:53
  70.3 4.6 %collective-permute-done.13 = bf16[96,2048]{1,0:T(8,128)(2,1)S(1)} collective-permute-done((bf16[96,2048]{1,0:T(8,128)(2,1)S(1)}, bf16[96,2048]{1,0:T(8,128)(2,1)S(1)}, u32[]{:S(2)}, u32[]{:S(2)}) %collective-permute-start.13) | collective-permute-done | bytes 393248 | tf_op jit(solution)/shard_map/ppermute | solution.py:53
  76.7 5.0 %collective-permute-done.6 = bf16[96,768]{1,0:T(8,128)(2,1)S(1)} collective-permute-done((bf16[96,768]{1,0:T(8,128)(2,1)S(1)}, bf16[96,768]{1,0:T(8,128)(2,1)S(1)}, u32[]{:S(2)}, u32[]{:S(2)}) %collective-permute-start.6) | collective-permute-done | bytes 147488 | tf_op jit(solution)/shard_map/ppermute | solution.py:53
  90.0 2.9 fusion.20.refs_2_
  98.5 8.0 %collective-permute-done.16 = bf16[96,2048]{1,0:T(8,128)(2,1)S(1)} collective-permute-done((bf16[96,2048]{1,0:T(8,128)(2,1)S(1)}, bf16[96,2048]{1,0:T(8,128)(2,1)S(1)}, u32[]{:S(2)}, u32[]{:S(2)}) %collective-permute-start.16) | collective-permute-done | bytes 393248 | tf_op jit(solution)/shard_map/ppermute | solution.py:53
  110.9 8.9 %attend_forward.3 = (bf16[512,256]{1,0:T(8,128)(2,1)}, bf16[512,256]{1,0:T(8,128)(2,1)}, f32[512,128]{1,0:T(8,128)}, f32[512,128]{1,0:T(8,128)}) custom-call(s32[32,8]{1,0:T(8,128)} %bitcast_select_fusion.1.table, bf16[512,768]{1,0:T(8,128)(2,1)} %fusion.18.refs_0_, bf16[512,768]{1,0:T(8,128)(2,1)} %fusion.19.refs_1_, bf16[512,768]{1,0:T(8,128)(2,1)} %fusion.20.refs_2_, ...), custom_call_target="tpu_custom_call" | custom-call | flops 1207959552 | bytes 4194304 | tf_op jit(solution)/shard_map/attend_forward/pallas_call | solution.py:248
  125.4 8.9 %attend_forward.2 = (bf16[512,256]{1,0:T(8,128)(2,1)}, bf16[512,256]{1,0:T(8,128)(2,1)}, f32[512,128]{1,0:T(8,128)}, f32[512,128]{1,0:T(8,128)}) custom-call(s32[32,8]{1,0:T(8,128)} %bitcast_select_fusion.1.table, bf16[512,768]{1,0:T(8,128)(2,1)} %fusion.18.refs_0_, bf16[512,768]{1,0:T(8,128)(2,1)} %fusion.19.refs_1_, bf16[512,768]{1,0:T(8,128)(2,1)} %fusion.20.refs_2_, ...), custom_call_target="tpu_custom_call" | custom-call | flops 1207959552 | bytes 4194304 | tf_op jit(solution)/shard_map/attend_forward/pallas_call | solution.py:248
  138.7 4.2 %collective-permute-done.22 = bf16[512,256]{1,0:T(8,128)(2,1)S(1)} collective-permute-done((bf16[512,256]{1,0:T(8,128)(2,1)S(1)}, bf16[512,256]{1,0:T(8,128)(2,1)S(1)}, u32[]{:S(2)}, u32[]{:S(2)}) %collective-permute-start.22) | collective-permute-done | bytes 262176 | tf_op jit(solution)/shard_map/ppermute | solution.py:30
  150.0 6.5 %multiply_convert_fusion = (bf16[1024,1536]{1,0:T(8,128)(2,1)S(1)}, f32[1024,1536]{1,0:T(8,128)}) fusion(f32[1536]{0:T(1024)S(1)} %pad_maximum_fusion.12, bf16[768,2048]{1,0:T(8,128)(2,1)S(1)} %bitcast.216, bf16[512,768]{1,0:T(8,128)(2,1)S(1)} %collective-permute-done.23, bf16[512,768]{1,0:T(8,128)(2,1)S(1)} %fusion.17), kind=kOutput, calls=%fused_computation.12 | convolution fusion | flops 2434793472 | bytes 13377536 | tf_op jit(solution)/shard_map/dot_general | solution.py:192
  156.5 5.4 %fusion.92 = f32[1024,768]{1,0:T(8,128)S(1)} fusion(bf16[1024,1536]{1,0:T(8,128)(2,1)S(1)} %get-tuple-element.176, bf16[768,1536]{1,0:T(8,128)(2,1)} %bitcast.46), kind=kOutput, calls=%fused_computation.257 | convolution fusion | flops 2415919104 | bytes 8650752 | tf_op jit(solution)/shard_map/dot_general | solution.py:192
  164.4 3.4 collective-permute-done.32
  167.8 2.5 fusion.84
  174.3 2.1 collective-permute-done.33
  176.4 4.8 %convolution_convert_fusion = bf16[768,1536]{1,0:T(8,128)(2,1)S(1)} fusion(bf16[1024,1536]{1,0:T(8,128)(2,1)} %copy-done.52, bf16[512,768]{1,0:T(8,128)(2,1)} %collective-permute-done.33, bf16[512,768]{1,0:T(8,128)(2,1)S(1)} %get-tuple-element.134), kind=kOutput, calls=%fused_computation.13 | convolution fusion | flops 2420244480 | bytes 7077888 | tf_op jit(solution)/shard_map/dot_general | solution.py:192
  187.1 6.2 %collective-permute-done.66 = bf16[96,1536]{1,0:T(8,128)(2,1)S(1)} collective-permute-done((bf16[96,1536]{1,0:T(8,128)(2,1)}, bf16[96,1536]{1,0:T(8,128)(2,1)S(1)}, u32[]{:S(2)}, u32[]{:S(2)}) %collective-permute-start.66) | collective-permute-done | bytes 294944 | tf_op jit(solution)/shard_map/ppermute | solution.py:53
  196.0 9.4 %convert_reduce_fusion = (f32[1536]{0:T(1024)S(1)}, bf16[1024,1536]{1,0:T(8,128)(2,1)S(1)}) fusion(f32[1024,1536]{1,0:T(8,128)} %get-tuple-element.177, f32[1536]{0:T(1024)S(1)} %pad_maximum_fusion.12, bf16[768,1536]{1,0:T(8,128)(2,1)} %bitcast.46, bf16[512,768]{1,0:T(8,128)(2,1)} %collective-permute-done.33, bf16[512,768]{1,0:T(8,128)(2,1)S(1)} %get-tuple-element.134), kind=kOutput, calls=%fused_computation.11 | convolution fusion | flops 2455239168 | bytes 13381632 | tf_op jit(solution)/shard_map/dot_general | solution.py:192
  207.7 2.6 fusion.7
  217.4 3.9 %convolution_convert_fusion.1 = bf16[768,1536]{1,0:T(8,128)(2,1)} fusion(bf16[1024,1536]{1,0:T(8,128)(2,1)S(1)} %get-tuple-element.179, bf16[512,768]{1,0:T(8,128)(2,1)S(1)} %copy-done.50, bf16[512,768]{1,0:T(8,128)(2,1)S(1)} %copy-done.21), kind=kOutput, calls=%fused_computation.14 | convolution fusion | flops 2420244480 | bytes 7077888 | tf_op jit(solution)/shard_map/dot_general | solution.py:192
  226.0 3.7 %collective-permute-done.73 = bf16[96,768]{1,0:T(8,128)(2,1)S(1)} collective-permute-done((bf16[96,768]{1,0:T(8,128)(2,1)S(1)}, bf16[96,768]{1,0:T(8,128)(2,1)S(1)}, u32[]{:S(2)}, u32[]{:S(2)}) %collective-permute-start.73) | collective-permute-done | bytes 147488 | tf_op jit(solution)/shard_map/ppermute | solution.py:30
  231.4 2.8 multiply_reduce_fusion
  235.6 2.1 convolution_convert_fusion.9
  237.8 2.1 convolution_convert_fusion.11.refs_4_
  242.7 2.5 collective-permute-done.61
  245.8 2.1 convolution_convert_fusion.8
  250.5 2.1 convolution_convert_fusion.10
  253.1 2.0 collective-permute-start.64
  255.1 2.1 convolution_convert_fusion.6
  261.9 29.3 %attend_backward.1 = (bf16[512,768]{1,0:T(8,128)(2,1)}, bf16[512,768]{1,0:T(8,128)(2,1)}, bf16[512,768]{1,0:T(8,128)(2,1)}, bf16[512,768]{1,0:T(8,128)(2,1)}) custom-call(s32[32,8]{1,0:T(8,128)} %bitcast_select_fusion.1.table, bf16[512,768]{1,0:T(8,128)(2,1)} %fusion.18.refs_0_, bf16[512,768]{1,0:T(8,128)(2,1)} %fusion.19.refs_1_, ...), custom_call_target="tpu_custom_call" | custom-call | flops 6039797760 | bytes 12582912 | tf_op jit(solution)/shard_map/attend_backward/pallas_call | solution.py:336
  292.5 2.1 fusion.93
  298.4 2.1 fusion.95
  306.3 2.4 collective-permute-start.50
  314.6 7.0 %collective-permute-done.52 = bf16[96,2048]{1,0:T(8,128)(2,1)S(1)} collective-permute-done((bf16[96,2048]{1,0:T(8,128)(2,1)S(1)}, bf16[96,2048]{1,0:T(8,128)(2,1)S(1)}, u32[]{:S(2)}, u32[]{:S(2)}) %collective-permute-start.52) | collective-permute-done | bytes 393248 | tf_op jit(solution)/shard_map/ppermute | solution.py:53
  322.8 1.9 collective-permute-done.42
  326.9 6.9 %collective-permute-done.53 = bf16[96,2048]{1,0:T(8,128)(2,1)S(1)} collective-permute-done((bf16[96,2048]{1,0:T(8,128)(2,1)S(1)}, bf16[96,2048]{1,0:T(8,128)(2,1)S(1)}, u32[]{:S(2)}, u32[]{:S(2)}) %collective-permute-start.53) | collective-permute-done | bytes 393248 | tf_op jit(solution)/shard_map/ppermute | solution.py:53
  334.6 2.3 collective-permute-done.43
  337.1 2.0 collective-permute-start.44
  340.0 6.1 %collective-permute-done.54 = bf16[96,2048]{1,0:T(8,128)(2,1)S(1)} collective-permute-done((bf16[96,2048]{1,0:T(8,128)(2,1)S(1)}, bf16[96,2048]{1,0:T(8,128)(2,1)S(1)}, u32[]{:S(2)}, u32[]{:S(2)}) %collective-permute-start.54) | collective-permute-done | bytes 393248 | tf_op jit(solution)/shard_map/ppermute | solution.py:53
  346.8 2.5 collective-permute-done.44
  350.1 4.2 %collective-permute-done.55 = bf16[96,2048]{1,0:T(8,128)(2,1)S(1)} collective-permute-done((bf16[96,2048]{1,0:T(8,128)(2,1)S(1)}, bf16[96,2048]{1,0:T(8,128)(2,1)S(1)}, u32[]{:S(2)}, u32[]{:S(2)}) %collective-permute-start.55) | collective-permute-done | bytes 393248 | tf_op jit(solution)/shard_map/ppermute | solution.py:53
  354.2 2.8 collective-permute-done.58
  357.3 2.9 collective-permute-done.40
  360.2 2.1 fusion.12
  363.2 4.3 %collective-permute-done.65 = bf16[96,768]{1,0:T(8,128)(2,1)S(1)} collective-permute-done((bf16[96,768]{1,0:T(8,128)(2,1)S(1)}, bf16[96,768]{1,0:T(8,128)(2,1)S(1)}, u32[]{:S(2)}, u32[]{:S(2)}) %collective-permute-start.65) | collective-permute-done | bytes 147488 | tf_op jit(solution)/shard_map/ppermute | solution.py:30
  (401 shorter events, 139.2 us)
Async XLA Ops:
  2.2 31.8 %collective-permute-start = (bf16[96,768]{1,0:T(8,128)(2,1)}, bf16[96,768]{1,0:T(8,128)(2,1)}, u32[]{:S(2)}, u32[]{:S(2)}) collective-permute-start(bf16[96,768]{1,0:T(8,128)(2,1)} %fusion.55), channel_id=1, source_target_pairs={{0,8},{8,16},{16,24},{24,28},{28,20},{20,12},{12,4},{4,0},{1,9},{9... | collective-permute-start | bytes 442376 | tf_op jit(solution)/shard_map/ppermute | solution.py:53
  5.3 30.1 %collective-permute-start.1 = (bf16[96,768]{1,0:T(8,128)(2,1)}, bf16[96,768]{1,0:T(8,128)(2,1)S(1)}, u32[]{:S(2)}, u32[]{:S(2)}) collective-permute-start(bf16[96,768]{1,0:T(8,128)(2,1)} %fusion.55), channel_id=1, source_target_pairs={{0,4},{8,0},{16,8},{24,16},{28,24},{20,28},{12,20},{4,12},{1,5},{9... | collective-permute-start | bytes 442376 | tf_op jit(solution)/shard_map/ppermute | solution.py:53
  5.3 12.2 %collective-permute-start.24 = (bf16[96,768]{1,0:T(8,128)(2,1)}, bf16[96,768]{1,0:T(8,128)(2,1)S(1)}, u32[]{:S(2)}, u32[]{:S(2)}) collective-permute-start(bf16[96,768]{1,0:T(8,128)(2,1)} %bitcast.236), channel_id=1, source_target_pairs={{0,2},{1,3},{2,0},{3,1},{4,6},{5,7},{6,4},{7,5},{8,10},{9,11},{10,... | collective-permute-start | bytes 442376 | tf_op jit(solution)/shard_map/ppermute | solution.py:30
  7.2 82.5 %collective-permute-start.8 = (bf16[512,768]{1,0:T(8,128)(2,1)}, bf16[512,768]{1,0:T(8,128)(2,1)}, u32[]{:S(2)}, u32[]{:S(2)}) collective-permute-start(bf16[512,768]{1,0:T(8,128)(2,1)} %param.22), channel_id=1, source_target_pairs={{0,2},{1,3},{2,0},{3,1},{4,6},{5,7},{6,4},{7,5},{8,10},{9,11},{10,... | collective-permute-start | bytes 2359304 | tf_op jit(solution)/shard_map/ppermute | solution.py:30
  8.3 21.9 %collective-permute-start.11 = (bf16[96,256]{1,0:T(8,128)(2,1)S(1)}, bf16[96,256]{1,0:T(8,128)(2,1)S(1)}, u32[]{:S(2)}, u32[]{:S(2)}) collective-permute-start(bf16[96,256]{1,0:T(8,128)(2,1)S(1)} %pad.25), channel_id=1, source_target_pairs={{0,2},{1,3},{2,0},{3,1},{4,6},{5,7},{6,4},{7,5},{8,10},{9,11},{10,... | collective-permute-start | bytes 147464 | tf_op jit(solution)/shard_map/ppermute | solution.py:30
  17.5 14.5 %collective-permute-start.10 = (bf16[96,768]{1,0:T(8,128)(2,1)S(1)}, bf16[96,768]{1,0:T(8,128)(2,1)S(1)}, u32[]{:S(2)}, u32[]{:S(2)}) collective-permute-start(bf16[96,768]{1,0:T(8,128)(2,1)S(1)} %copy-done.25), channel_id=1, source_target_pairs={{0,2},{1,3},{2,0},{3,1},{4,6},{5,7},{6,4},{7,5},{8,10},{9,11},{10,... | collective-permute-start | bytes 442376 | tf_op jit(solution)/shard_map/ppermute | solution.py:30
  30.2 62.7 %collective-permute-start.7 = (bf16[512,768]{1,0:T(8,128)(2,1)S(1)}, bf16[512,768]{1,0:T(8,128)(2,1)S(1)}, u32[]{:S(2)}, u32[]{:S(2)}) collective-permute-start(bf16[512,768]{1,0:T(8,128)(2,1)S(1)} %copy-done.10), channel_id=1, source_target_pairs={{0,1},{1,0},{2,3},{3,2},{4,5},{5,4},{6,7},{7,6},{8,9},{9,8},{10,11... | collective-permute-start | bytes 2359304 | tf_op jit(solution)/shard_map/ppermute | solution.py:30
  31.9 17.8 %collective-permute-start.25 = (bf16[96,1536]{1,0:T(8,128)(2,1)S(1)}, bf16[96,1536]{1,0:T(8,128)(2,1)S(1)}, u32[]{:S(2)}, u32[]{:S(2)}) collective-permute-start(bf16[96,1536]{1,0:T(8,128)(2,1)S(1)} %pad_maximum_fusion.11), channel_id=1, source_target_pairs={{0,8},{8,16},{16,24},{24,28},{28,20},{20,12},{12,4},{4,0},{1,9},{9... | collective-permute-start | bytes 884744 | tf_op jit(solution)/shard_map/ppermute | solution.py:53
  34.1 33.4 %collective-permute-start.26 = (bf16[96,1536]{1,0:T(8,128)(2,1)S(1)}, bf16[96,1536]{1,0:T(8,128)(2,1)S(1)}, u32[]{:S(2)}, u32[]{:S(2)}) collective-permute-start(bf16[96,1536]{1,0:T(8,128)(2,1)S(1)} %pad_maximum_fusion.11), channel_id=1, source_target_pairs={{0,4},{8,0},{16,8},{24,16},{28,24},{20,28},{12,20},{4,12},{1,5},{9... | collective-permute-start | bytes 884744 | tf_op jit(solution)/shard_map/ppermute | solution.py:53
  48.0 20.6 %collective-permute-start.12 = (bf16[96,2048]{1,0:T(8,128)(2,1)S(1)}, bf16[96,2048]{1,0:T(8,128)(2,1)S(1)}, u32[]{:S(2)}, u32[]{:S(2)}) collective-permute-start(bf16[96,2048]{1,0:T(8,128)(2,1)S(1)} %pad_maximum_fusion.10), channel_id=1, source_target_pairs={{0,8},{8,16},{16,24},{24,28},{28,20},{20,12},{12,4},{4,0},{1,9},{9... | collective-permute-start | bytes 1179656 | tf_op jit(solution)/shard_map/ppermute | solution.py:53
  49.8 9.3 %collective-permute-start.4 = (bf16[96,768]{1,0:T(8,128)(2,1)S(1)}, bf16[96,768]{1,0:T(8,128)(2,1)S(1)}, u32[]{:S(2)}, u32[]{:S(2)}) collective-permute-start(bf16[96,768]{1,0:T(8,128)(2,1)S(1)} %collective-permute-done.2), channel_id=1, source_target_pairs={{0,8},{8,16},{16,24},{24,28},{28,20},{20,12},{12,4},{4,0},{1,9},{9... | collective-permute-start | bytes 442376 | tf_op jit(solution)/shard_map/ppermute | solution.py:53
  65.7 9.2 %collective-permute-start.13 = (bf16[96,2048]{1,0:T(8,128)(2,1)S(1)}, bf16[96,2048]{1,0:T(8,128)(2,1)S(1)}, u32[]{:S(2)}, u32[]{:S(2)}) collective-permute-start(bf16[96,2048]{1,0:T(8,128)(2,1)S(1)} %pad_maximum_fusion.10), channel_id=1, source_target_pairs={{0,4},{8,0},{16,8},{24,16},{28,24},{20,28},{12,20},{4,12},{1,5},{9... | collective-permute-start | bytes 1179656 | tf_op jit(solution)/shard_map/ppermute | solution.py:53
  67.5 17.8 %collective-permute-start.27 = (bf16[96,1536]{1,0:T(8,128)(2,1)S(1)}, bf16[96,1536]{1,0:T(8,128)(2,1)S(1)}, u32[]{:S(2)}, u32[]{:S(2)}) collective-permute-start(bf16[96,1536]{1,0:T(8,128)(2,1)S(1)} %collective-permute-done.25), channel_id=1, source_target_pairs={{0,8},{8,16},{16,24},{24,28},{28,20},{20,12},{12,4},{4,0},{1,9},{9... | collective-permute-start | bytes 884744 | tf_op jit(solution)/shard_map/ppermute | solution.py:53
  68.6 17.7 %collective-permute-start.28 = (bf16[96,1536]{1,0:T(8,128)(2,1)S(1)}, bf16[96,1536]{1,0:T(8,128)(2,1)}, u32[]{:S(2)}, u32[]{:S(2)}) collective-permute-start(bf16[96,1536]{1,0:T(8,128)(2,1)S(1)} %collective-permute-done.26), channel_id=1, source_target_pairs={{0,4},{8,0},{16,8},{24,16},{28,24},{20,28},{12,20},{4,12},{1,5},{9... | collective-permute-start | bytes 884744 | tf_op jit(solution)/shard_map/ppermute | solution.py:53
  81.7 12.9 %collective-permute-start.14 = (bf16[96,2048]{1,0:T(8,128)(2,1)S(1)}, bf16[96,2048]{1,0:T(8,128)(2,1)S(1)}, u32[]{:S(2)}, u32[]{:S(2)}) collective-permute-start(bf16[96,2048]{1,0:T(8,128)(2,1)S(1)} %collective-permute-done.12), channel_id=1, source_target_pairs={{0,8},{8,16},{16,24},{24,28},{28,20},{20,12},{12,4},{4,0},{1,9},{9... | collective-permute-start | bytes 1179656 | tf_op jit(solution)/shard_map/ppermute | solution.py:53
  85.2 11.1 %collective-permute-start.15 = (bf16[96,2048]{1,0:T(8,128)(2,1)S(1)}, bf16[96,2048]{1,0:T(8,128)(2,1)S(1)}, u32[]{:S(2)}, u32[]{:S(2)}) collective-permute-start(bf16[96,2048]{1,0:T(8,128)(2,1)S(1)} %collective-permute-done.13), channel_id=1, source_target_pairs={{0,4},{8,0},{16,8},{24,16},{28,24},{20,28},{12,20},{4,12},{1,5},{9... | collective-permute-start | bytes 1179656 | tf_op jit(solution)/shard_map/ppermute | solution.py:53
  86.3 10.5 %collective-permute-start.29 = (bf16[96,1536]{1,0:T(8,128)(2,1)S(1)}, bf16[96,1536]{1,0:T(8,128)(2,1)}, u32[]{:S(2)}, u32[]{:S(2)}) collective-permute-start(bf16[96,1536]{1,0:T(8,128)(2,1)S(1)} %collective-permute-done.27), channel_id=1, source_target_pairs={{0,8},{8,16},{16,24},{24,28},{28,20},{20,12},{12,4},{4,0},{1,9},{9... | collective-permute-start | bytes 884744 | tf_op jit(solution)/shard_map/ppermute | solution.py:53
  89.7 56.8 %collective-permute-start.30 = (bf16[96,1536]{1,0:T(8,128)(2,1)}, bf16[96,1536]{1,0:T(8,128)(2,1)}, u32[]{:S(2)}, u32[]{:S(2)}) collective-permute-start(bf16[96,1536]{1,0:T(8,128)(2,1)} %collective-permute-done.28), channel_id=1, source_target_pairs={{0,4},{8,0},{16,8},{24,16},{28,24},{20,28},{12,20},{4,12},{1,5},{9... | collective-permute-start | bytes 884744 | tf_op jit(solution)/shard_map/ppermute | solution.py:53
  92.9 15.4 %collective-permute-start.9 = (bf16[512,768]{1,0:T(8,128)(2,1)}, bf16[512,768]{1,0:T(8,128)(2,1)S(1)}, u32[]{:S(2)}, u32[]{:S(2)}) collective-permute-start(bf16[512,768]{1,0:T(8,128)(2,1)} %collective-permute-done.8), channel_id=1, source_target_pairs={{0,1},{1,0},{2,3},{3,2},{4,5},{5,4},{6,7},{7,6},{8,9},{9,8},{10,11... | collective-permute-start | bytes 2359304 | tf_op jit(solution)/shard_map/ppermute | solution.py:30
  94.6 11.9 %collective-permute-start.16 = (bf16[96,2048]{1,0:T(8,128)(2,1)S(1)}, bf16[96,2048]{1,0:T(8,128)(2,1)S(1)}, u32[]{:S(2)}, u32[]{:S(2)}) collective-permute-start(bf16[96,2048]{1,0:T(8,128)(2,1)S(1)} %collective-permute-done.14), channel_id=1, source_target_pairs={{0,8},{8,16},{16,24},{24,28},{28,20},{20,12},{12,4},{4,0},{1,9},{9... | collective-permute-start | bytes 1179656 | tf_op jit(solution)/shard_map/ppermute | solution.py:53
  96.3 11.9 %collective-permute-start.17 = (bf16[96,2048]{1,0:T(8,128)(2,1)S(1)}, bf16[96,2048]{1,0:T(8,128)(2,1)S(1)}, u32[]{:S(2)}, u32[]{:S(2)}) collective-permute-start(bf16[96,2048]{1,0:T(8,128)(2,1)S(1)} %collective-permute-done.15), channel_id=1, source_target_pairs={{0,4},{8,0},{16,8},{24,16},{28,24},{20,28},{12,20},{4,12},{1,5},{9... | collective-permute-start | bytes 1179656 | tf_op jit(solution)/shard_map/ppermute | solution.py:53
  96.8 51.5 %collective-permute-start.31 = (bf16[96,1536]{1,0:T(8,128)(2,1)}, bf16[96,1536]{1,0:T(8,128)(2,1)}, u32[]{:S(2)}, u32[]{:S(2)}) collective-permute-start(bf16[96,1536]{1,0:T(8,128)(2,1)} %collective-permute-done.29), channel_id=1, source_target_pairs={{0,8},{8,16},{16,24},{24,28},{28,20},{20,12},{12,4},{4,0},{1,9},{9... | collective-permute-start | bytes 884744 | tf_op jit(solution)/shard_map/ppermute | solution.py:53
  106.5 14.9 %collective-permute-start.18 = (bf16[96,2048]{1,0:T(8,128)(2,1)S(1)}, bf16[96,2048]{1,0:T(8,128)(2,1)}, u32[]{:S(2)}, u32[]{:S(2)}) collective-permute-start(bf16[96,2048]{1,0:T(8,128)(2,1)S(1)} %collective-permute-done.16), channel_id=1, source_target_pairs={{0,8},{8,16},{16,24},{24,28},{28,20},{20,12},{12,4},{4,0},{1,9},{9... | collective-permute-start | bytes 1179656 | tf_op jit(solution)/shard_map/ppermute | solution.py:53
  119.8 14.9 %collective-permute-start.21 = (bf16[512,256]{1,0:T(8,128)(2,1)}, bf16[512,256]{1,0:T(8,128)(2,1)}, u32[]{:S(2)}, u32[]{:S(2)}) collective-permute-start(bf16[512,256]{1,0:T(8,128)(2,1)} %get-tuple-element.32), channel_id=1, source_target_pairs={{0,2},{1,3},{2,0},{3,1},{4,6},{5,7},{6,4},{7,5},{8,10},{9,11},{10,... | collective-permute-start | bytes 786440 | tf_op jit(solution)/shard_map/ppermute | solution.py:30
  123.5 13.6 %collective-permute-start.20 = (bf16[768,512]{1,0:T(8,128)(2,1)}, bf16[768,512]{1,0:T(8,128)(2,1)}, u32[]{:S(2)}, u32[]{:S(2)}) collective-permute-start(bf16[768,512]{1,0:T(8,128)(2,1)} %slice.179), channel_id=1, source_target_pairs={{0,1},{1,0},{2,3},{3,2},{4,5},{5,4},{6,7},{7,6},{8,9},{9,8},{10,11... | collective-permute-start | bytes 2359304 | tf_op jit(solution)/shard_map/ppermute | solution.py:30
  134.7 8.3 %collective-permute-start.22 = (bf16[512,256]{1,0:T(8,128)(2,1)S(1)}, bf16[512,256]{1,0:T(8,128)(2,1)S(1)}, u32[]{:S(2)}, u32[]{:S(2)}) collective-permute-start(bf16[512,256]{1,0:T(8,128)(2,1)S(1)} %copy-done.51), channel_id=1, source_target_pairs={{0,3},{1,2},{2,1},{3,0},{4,7},{5,6},{6,5},{7,4},{8,11},{9,10},{10,... | collective-permute-start | bytes 786440 | tf_op jit(solution)/shard_map/ppermute | solution.py:30
  183.5 9.8 %collective-permute-start.66 = (bf16[96,1536]{1,0:T(8,128)(2,1)}, bf16[96,1536]{1,0:T(8,128)(2,1)S(1)}, u32[]{:S(2)}, u32[]{:S(2)}) collective-permute-start(bf16[96,1536]{1,0:T(8,128)(2,1)} %get-tuple-element.150), channel_id=1, source_target_pairs={{0,8},{8,16},{16,24},{24,28},{28,20},{20,12},{12,4},{4,0},{1,9},{9... | collective-permute-start | bytes 884744 | tf_op jit(solution)/shard_map/ppermute | solution.py:53
  186.6 18.8 %collective-permute-start.70 = (bf16[96,1536]{1,0:T(8,128)(2,1)}, bf16[96,1536]{1,0:T(8,128)(2,1)S(1)}, u32[]{:S(2)}, u32[]{:S(2)}) collective-permute-start(bf16[96,1536]{1,0:T(8,128)(2,1)} %get-tuple-element.151), channel_id=1, source_target_pairs={{0,4},{8,0},{16,8},{24,16},{28,24},{20,28},{12,20},{4,12},{1,5},{9... | collective-permute-start | bytes 884744 | tf_op jit(solution)/shard_map/ppermute | solution.py:53
  194.4 11.1 %collective-permute-start.67 = (bf16[96,1536]{1,0:T(8,128)(2,1)S(1)}, bf16[96,1536]{1,0:T(8,128)(2,1)S(1)}, u32[]{:S(2)}, u32[]{:S(2)}) collective-permute-start(bf16[96,1536]{1,0:T(8,128)(2,1)S(1)} %fusion.32), channel_id=1, source_target_pairs={{0,8},{8,16},{16,24},{24,28},{28,20},{20,12},{12,4},{4,0},{1,9},{9... | collective-permute-start | bytes 884744 | tf_op jit(solution)/shard_map/ppermute | solution.py:53
  212.4 19.0 %collective-permute-start.34 = (f32[512,768]{1,0:T(8,128)}, f32[512,768]{1,0:T(8,128)}, u32[]{:S(2)}, u32[]{:S(2)}) collective-permute-start(f32[512,768]{1,0:T(8,128)} %slice.187), channel_id=1, source_target_pairs={{0,1},{1,0},{2,3},{3,2},{4,5},{5,4},{6,7},{7,6},{8,9},{9,8},{10,11... | collective-permute-start | bytes 4718600 | tf_op jit(solution)/shard_map/ppermute | solution.py:30
  242.6 66.1 %collective-permute-start.51 = (bf16[768,512]{1,0:T(8,128)(2,1)S(1)}, bf16[768,512]{1,0:T(8,128)(2,1)S(1)}, u32[]{:S(2)}, u32[]{:S(2)}) collective-permute-start(bf16[768,512]{1,0:T(8,128)(2,1)S(1)} %pad_maximum_fusion.9), channel_id=1, source_target_pairs={{0,1},{1,0},{2,3},{3,2},{4,5},{5,4},{6,7},{7,6},{8,9},{9,8},{10,11... | collective-permute-start | bytes 2359304 | tf_op jit(solution)/shard_map/ppermute | solution.py:30
  247.9 14.0 %collective-permute-start.37 = (bf16[512,256]{1,0:T(8,128)(2,1)}, bf16[512,256]{1,0:T(8,128)(2,1)}, u32[]{:S(2)}, u32[]{:S(2)}) collective-permute-start(bf16[512,256]{1,0:T(8,128)(2,1)} %convolution_convert_fusion.8), channel_id=1, source_target_pairs={{0,3},{1,2},{2,1},{3,0},{4,7},{5,6},{6,5},{7,4},{8,11},{9,10},{10,... | collective-permute-start | bytes 786440 | tf_op jit(solution)/shard_map/ppermute | solution.py:30
  247.9 14.0 %collective-permute-start.36 = (bf16[512,256]{1,0:T(8,128)(2,1)}, bf16[512,256]{1,0:T(8,128)(2,1)}, u32[]{:S(2)}, u32[]{:S(2)}) collective-permute-start(bf16[512,256]{1,0:T(8,128)(2,1)} %convolution_convert_fusion.9), channel_id=1, source_target_pairs={{0,2},{1,3},{2,0},{3,1},{4,6},{5,7},{6,4},{7,5},{8,10},{9,11},{10,... | collective-permute-start | bytes 786440 | tf_op jit(solution)/shard_map/ppermute | solution.py:30
  252.6 9.3 %collective-permute-start.35 = (bf16[512,256]{1,0:T(8,128)(2,1)}, bf16[512,256]{1,0:T(8,128)(2,1)}, u32[]{:S(2)}, u32[]{:S(2)}) collective-permute-start(bf16[512,256]{1,0:T(8,128)(2,1)} %convolution_convert_fusion.10), channel_id=1, source_target_pairs={{0,1},{1,0},{2,3},{3,2},{4,5},{5,4},{6,7},{7,6},{8,9},{9,8},{10,11... | collective-permute-start | bytes 786440 | tf_op jit(solution)/shard_map/ppermute | solution.py:30
  309.5 12.1 %collective-permute-start.52 = (bf16[96,2048]{1,0:T(8,128)(2,1)S(1)}, bf16[96,2048]{1,0:T(8,128)(2,1)S(1)}, u32[]{:S(2)}, u32[]{:S(2)}) collective-permute-start(bf16[96,2048]{1,0:T(8,128)(2,1)S(1)} %get-tuple-element.144), channel_id=1, source_target_pairs={{0,8},{8,16},{16,24},{24,28},{28,20},{20,12},{12,4},{4,0},{1,9},{9... | collective-permute-start | bytes 1179656 | tf_op jit(solution)/shard_map/ppermute | solution.py:53
  310.8 12.0 %collective-permute-start.45 = (bf16[96,768]{1,0:T(8,128)(2,1)S(1)}, bf16[96,768]{1,0:T(8,128)(2,1)S(1)}, u32[]{:S(2)}, u32[]{:S(2)}) collective-permute-start(bf16[96,768]{1,0:T(8,128)(2,1)S(1)} %get-tuple-element.158), channel_id=1, source_target_pairs={{0,4},{8,0},{16,8},{24,16},{28,24},{20,28},{12,20},{4,12},{1,5},{9... | collective-permute-start | bytes 442376 | tf_op jit(solution)/shard_map/ppermute | solution.py:53
  312.4 44.9 %collective-permute-start.38 = (bf16[512,768]{1,0:T(8,128)(2,1)S(1)}, bf16[512,768]{1,0:T(8,128)(2,1)S(1)}, u32[]{:S(2)}, u32[]{:S(2)}) collective-permute-start(bf16[512,768]{1,0:T(8,128)(2,1)S(1)} %convolution_convert_fusion.3), channel_id=1, source_target_pairs={{0,1},{1,0},{2,3},{3,2},{4,5},{5,4},{6,7},{7,6},{8,9},{9,8},{10,11... | collective-permute-start | bytes 2359304 | tf_op jit(solution)/shard_map/ppermute | solution.py:30
  312.5 12.2 %collective-permute-start.42 = (bf16[96,768]{1,0:T(8,128)(2,1)S(1)}, bf16[96,768]{1,0:T(8,128)(2,1)S(1)}, u32[]{:S(2)}, u32[]{:S(2)}) collective-permute-start(bf16[96,768]{1,0:T(8,128)(2,1)S(1)} %fusion.49), channel_id=1, source_target_pairs={{0,8},{8,16},{16,24},{24,28},{28,20},{20,12},{12,4},{4,0},{1,9},{9... | collective-permute-start | bytes 442376 | tf_op jit(solution)/shard_map/ppermute | solution.py:53
  313.0 12.3 %collective-permute-start.56 = (bf16[96,2048]{1,0:T(8,128)(2,1)S(1)}, bf16[96,2048]{1,0:T(8,128)(2,1)S(1)}, u32[]{:S(2)}, u32[]{:S(2)}) collective-permute-start(bf16[96,2048]{1,0:T(8,128)(2,1)S(1)} %get-tuple-element.145), channel_id=1, source_target_pairs={{0,4},{8,0},{16,8},{24,16},{28,24},{20,28},{12,20},{4,12},{1,5},{9... | collective-permute-start | bytes 1179656 | tf_op jit(solution)/shard_map/ppermute | solution.py:53
  321.7 12.1 %collective-permute-start.53 = (bf16[96,2048]{1,0:T(8,128)(2,1)S(1)}, bf16[96,2048]{1,0:T(8,128)(2,1)S(1)}, u32[]{:S(2)}, u32[]{:S(2)}) collective-permute-start(bf16[96,2048]{1,0:T(8,128)(2,1)S(1)} %fusion.27), channel_id=1, source_target_pairs={{0,8},{8,16},{16,24},{24,28},{28,20},{20,12},{12,4},{4,0},{1,9},{9... | collective-permute-start | bytes 1179656 | tf_op jit(solution)/shard_map/ppermute | solution.py:53
  322.8 16.3 %collective-permute-start.39 = (bf16[512,768]{1,0:T(8,128)(2,1)S(1)}, bf16[512,768]{1,0:T(8,128)(2,1)S(1)}, u32[]{:S(2)}, u32[]{:S(2)}) collective-permute-start(bf16[512,768]{1,0:T(8,128)(2,1)S(1)} %convolution_convert_fusion.2), channel_id=1, source_target_pairs={{0,1},{1,0},{2,3},{3,2},{4,5},{5,4},{6,7},{7,6},{8,9},{9,8},{10,11... | collective-permute-start | bytes 2359304 | tf_op jit(solution)/shard_map/ppermute | solution.py:30
  324.8 12.1 %collective-permute-start.43 = (bf16[96,768]{1,0:T(8,128)(2,1)S(1)}, bf16[96,768]{1,0:T(8,128)(2,1)S(1)}, u32[]{:S(2)}, u32[]{:S(2)}) collective-permute-start(bf16[96,768]{1,0:T(8,128)(2,1)S(1)} %get-tuple-element.155), channel_id=1, source_target_pairs={{0,8},{8,16},{16,24},{24,28},{28,20},{20,12},{12,4},{4,0},{1,9},{9... | collective-permute-start | bytes 442376 | tf_op jit(solution)/shard_map/ppermute | solution.py:53
  325.4 11.6 %collective-permute-start.46 = (bf16[96,768]{1,0:T(8,128)(2,1)S(1)}, bf16[96,768]{1,0:T(8,128)(2,1)S(1)}, u32[]{:S(2)}, u32[]{:S(2)}) collective-permute-start(bf16[96,768]{1,0:T(8,128)(2,1)S(1)} %get-tuple-element.156), channel_id=1, source_target_pairs={{0,4},{8,0},{16,8},{24,16},{28,24},{20,28},{12,20},{4,12},{1,5},{9... | collective-permute-start | bytes 442376 | tf_op jit(solution)/shard_map/ppermute | solution.py:53
  334.1 12.0 %collective-permute-start.54 = (bf16[96,2048]{1,0:T(8,128)(2,1)S(1)}, bf16[96,2048]{1,0:T(8,128)(2,1)S(1)}, u32[]{:S(2)}, u32[]{:S(2)}) collective-permute-start(bf16[96,2048]{1,0:T(8,128)(2,1)S(1)} %get-tuple-element.142), channel_id=1, source_target_pairs={{0,8},{8,16},{16,24},{24,28},{28,20},{20,12},{12,4},{4,0},{1,9},{9... | collective-permute-start | bytes 1179656 | tf_op jit(solution)/shard_map/ppermute | solution.py:53
  337.0 9.2 %collective-permute-start.57 = (bf16[96,2048]{1,0:T(8,128)(2,1)S(1)}, bf16[96,2048]{1,0:T(8,128)(2,1)S(1)}, u32[]{:S(2)}, u32[]{:S(2)}) collective-permute-start(bf16[96,2048]{1,0:T(8,128)(2,1)S(1)} %get-tuple-element.143), channel_id=1, source_target_pairs={{0,4},{8,0},{16,8},{24,16},{28,24},{20,28},{12,20},{4,12},{1,5},{9... | collective-permute-start | bytes 1179656 | tf_op jit(solution)/shard_map/ppermute | solution.py:53
  337.1 12.2 %collective-permute-start.44 = (bf16[96,768]{1,0:T(8,128)(2,1)S(1)}, bf16[96,768]{1,0:T(8,128)(2,1)S(1)}, u32[]{:S(2)}, u32[]{:S(2)}) collective-permute-start(bf16[96,768]{1,0:T(8,128)(2,1)S(1)} %get-tuple-element.153), channel_id=1, source_target_pairs={{0,8},{8,16},{16,24},{24,28},{28,20},{20,12},{12,4},{4,0},{1,9},{9... | collective-permute-start | bytes 442376 | tf_op jit(solution)/shard_map/ppermute | solution.py:53
  339.1 10.2 %collective-permute-start.47 = (bf16[96,768]{1,0:T(8,128)(2,1)S(1)}, bf16[96,768]{1,0:T(8,128)(2,1)S(1)}, u32[]{:S(2)}, u32[]{:S(2)}) collective-permute-start(bf16[96,768]{1,0:T(8,128)(2,1)S(1)} %get-tuple-element.154), channel_id=1, source_target_pairs={{0,4},{8,0},{16,8},{24,16},{28,24},{20,28},{12,20},{4,12},{1,5},{9... | collective-permute-start | bytes 442376 | tf_op jit(solution)/shard_map/ppermute | solution.py:53
  346.1 14.1 %collective-permute-start.40 = (bf16[512,768]{1,0:T(8,128)(2,1)S(1)}, bf16[512,768]{1,0:T(8,128)(2,1)S(1)}, u32[]{:S(2)}, u32[]{:S(2)}) collective-permute-start(bf16[512,768]{1,0:T(8,128)(2,1)S(1)} %add_convert_fusion.2), channel_id=1, source_target_pairs={{0,2},{1,3},{2,0},{3,1},{4,6},{5,7},{6,4},{7,5},{8,10},{9,11},{10,... | collective-permute-start | bytes 2359304 | tf_op jit(solution)/shard_map/ppermute | solution.py:30
  (79 other events, 464.4 us)

commit v2 on v1

v2 whole, which is shorter than its diff:
```python
from functools import partial

import jax
import jax.numpy as jnp
from jax import lax
from jax.experimental import pallas as pl
from jax.experimental.pallas import tpu as pltpu
from jax.sharding import PartitionSpec as P

D = 768
HD = 64
FF = 3072
BLK = 64
GLOB = 2
RAND = 3
LMAX = 2048
NB = 32
KEYS = (3 + GLOB + RAND) * BLK
PAD = 256
LANES = 128
SUM_ROW = 10

masked_score = -1e30
EPSILON = 1e-12
f32 = jnp.float32
bf16 = jnp.bfloat16


def swap(array, bit):
    size = lax.axis_size("tensor")
    return lax.ppermute(array, "tensor", [(t, t ^ bit) for t in range(size)])


def dp_swap(array, bit):
    size = lax.axis_size("dp")
    return lax.ppermute(array, "dp", [(t, t ^ bit) for t in range(size)])


def ring_order(size):
    return list(range(0, size, 2)) + list(range(size - 1, 0, -2))


def ring_member(steps):
    size = lax.axis_size("dp")
    me = lax.axis_index("dp")
    place = jnp.where(me % 2 == 0, me // 2, size - 1 - me // 2)
    place = (place + steps + size) % size
    return jnp.where(place < size // 2, 2 * place, 2 * (size - 1 - place) + 1)


def ring_send(array, step):
    size = lax.axis_size("dp")
    order = ring_order(size)
    return lax.ppermute(
        array, "dp", [(order[i], order[(i + step) % size]) for i in range(size)]
    )


RING_STEPS = (0, -1, 1, -2, 2, -3, 3, -4)


def ring_pieces(shard, gate=None):
    pieces = [shard]
    ahead, behind = shard, shard
    for step in range(1, 5):
        if gate is not None:
            ahead, behind = gate(step, ahead, behind)
        ahead = ring_send(ahead, 1)
        pieces.append(ahead)
        if step < 4:
            behind = ring_send(behind, -1)
            pieces.append(behind)
    return pieces


def dp_scatter_sum(sums):
    size = lax.axis_size("dp")
    if size != 8:
        return lax.psum_scatter(sums, "dp", scatter_dimension=0, tiled=True).astype(f32)
    blocks = lax.all_to_all(sums.reshape(size, -1, sums.shape[1]), "dp", 0, 0, tiled=True)
    return jnp.sum(blocks.astype(f32), axis=0)


def sum_over(vector, dp_only=False):
    if not dp_only:
        bit = 1
        while bit < lax.axis_size("tensor"):
            vector = vector + swap(vector, bit)
            bit *= 2
    bit = 1
    while bit < lax.axis_size("dp"):
        vector = vector + dp_swap(vector, bit)
        bit *= 2
    return vector


def block_tables(lengths, global_raw, random_raw, own_blocks, pieces):
    count = own_blocks * pieces
    per_block = KEYS // BLK

    def kernel(length_ref, global_ref, random_ref, table, bias):
        me = lax.axis_index("tensor")
        lane = lax.broadcasted_iota(jnp.int32, (1, KEYS), 1)
        slot = lane // BLK
        within = lane % BLK

        def step(i, carry):
            block = ((i // own_blocks) ^ me) * own_blocks + i % own_blocks
            seq = block // NB
            block = block % NB
            length = length_ref[seq]
            live = (length + BLK - 1) // BLK
            ids = [jnp.maximum(block - 1, 0), block, jnp.minimum(block + 1, NB - 1)]
            ids += [lax.rem(global_ref[seq, j], live) for j in range(GLOB)]
            ids += [lax.rem(random_ref[seq, block, r], live) for r in range(RAND)]
            spread_ids = jnp.zeros((1, KEYS), jnp.int32)
            for j in range(per_block):
                spread_ids = jnp.where(slot == j, ids[j], spread_ids)
                there = ids[j] + seq * NB
                table[i, j] = ((there // own_blocks) ^ me) * own_blocks + there % own_blocks
            position = spread_ids * BLK + within
            lost = (position >= length) | ((slot == 0) & (block == 0))
            lost = lost | ((slot == 2) & (block == NB - 1))
            bias[pl.ds(i, 1), :] = jnp.where(lost, masked_score, 0.0).astype(f32)
            return carry

        lax.fori_loop(0, count, step, 0)

    smem = pl.BlockSpec(memory_space=pltpu.SMEM)
    return pl.pallas_call(
        kernel,
        out_shape=[
            jax.ShapeDtypeStruct((count, per_block), jnp.int32),
            jax.ShapeDtypeStruct((count, KEYS), f32),
        ],
        in_specs=[smem] * 3,
        out_specs=[smem, pl.BlockSpec(memory_space=pltpu.VMEM)],
        cost_estimate=cost(count * KEYS * 16, count * KEYS * 4),
        name="block_tables",
    )(lengths, global_raw, random_raw)


def head_masks(heads, scale, dtype):
    lane = lax.broadcasted_iota(jnp.int32, (1, PAD), 1)
    return [
        jnp.where((lane >= h * HD) & (lane < (h + 1) * HD), scale, 0.0).astype(dtype)
        for h in range(heads)
    ]


def stacked_heads(rows, masks):
    return jnp.concatenate([rows * mask for mask in masks], axis=0)


def unstacked_heads(stacked, masks):
    rows = stacked.shape[0] // len(masks)
    total = stacked[:rows] * masks[0]
    for h in range(1, len(masks)):
        total = total + stacked[h * rows : (h + 1) * rows] * masks[h]
    return total


def key_blocks(ref, table, block, column):
    return jnp.concatenate(
        [
            ref[pl.ds(pl.multiple_of(table[block, j] * BLK, BLK), BLK), column : column + PAD]
            for j in range(KEYS // BLK)
        ],
        axis=0,
    )


def contract(a, b, dims):
    return lax.dot_general(a, b, ((dims[:1], dims[1:]), ((), ())), preferred_element_type=f32)


def attend_kernel(heads, chosen, pieces, own_blocks, table, *refs):
    parts = refs[:pieces]
    bias = refs[pieces]
    outs = refs[pieces + 1 : pieces + 1 + len(chosen)]
    totals = refs[pieces + 1 + len(chosen) : pieces + 1 + 2 * len(chosen)]
    rows, sems = refs[pieces + 1 + 2 * len(chosen) :]
    own_rows = own_blocks * BLK
    copies = [
        pltpu.make_async_copy(
            parts[s], rows.at[pl.ds(s * own_rows, own_rows)], sems.at[s]
        )
        for s in range(pieces)
    ]
    for copy in copies:
        copy.start()
    for copy in copies:
        copy.wait()
    query_masks = head_masks(heads, HD**-0.5, bf16)
    out_masks = head_masks(heads, 1.0, f32)
    lane = lax.broadcasted_iota(jnp.int32, (BLK, LANES), 1)

    def step(i, carry):
        for at, s in enumerate(chosen):
            block = s * own_blocks + i
            start = pl.multiple_of(i * BLK, BLK)
            queries = stacked_heads(
                rows[pl.ds(pl.multiple_of(block * BLK, BLK), BLK), 0:PAD], query_masks
            )
            keys = key_blocks(rows, table, block, PAD)
            values = key_blocks(rows, table, block, 2 * PAD)
            scores = contract(queries, keys, (1, 1)) + bias[pl.ds(block, 1), :]
            top = jnp.max(scores, axis=-1, keepdims=True)
            weights = jnp.exp(scores - top)
            total = jnp.sum(weights, axis=-1, keepdims=True)
            mixed = contract(weights.astype(bf16), values, (1, 0)) / total
            outs[at][pl.ds(start, BLK), :] = unstacked_heads(mixed, out_masks).astype(bf16)
            log_total = top + jnp.log(total)
            kept = jnp.zeros((BLK, LANES), f32)
            for h in range(heads):
                kept = jnp.where(lane == h, log_total[h * BLK : (h + 1) * BLK], kept)
            totals[at][pl.ds(start, BLK), :] = kept
        return carry

    lax.fori_loop(0, own_blocks, step, 0)


def attend_forward(parts, table, bias, heads, chosen):
    own_rows = parts[0].shape[0]
    pieces = len(parts)
    own_blocks = own_rows // BLK
    n = len(chosen)
    vmem = pl.BlockSpec(memory_space=pltpu.VMEM)
    work = n * own_rows * KEYS * heads
    results = pl.pallas_call(
        partial(attend_kernel, heads, chosen, pieces, own_blocks),
        out_shape=[jax.ShapeDtypeStruct((own_rows, PAD), bf16)] * n
        + [jax.ShapeDtypeStruct((own_rows, LANES), f32)] * n,
        in_specs=[pl.BlockSpec(memory_space=pltpu.SMEM)]
        + [pl.BlockSpec(memory_space=pl.ANY)] * pieces
        + [vmem],
        out_specs=[vmem] * (2 * n),
        scratch_shapes=[
            pltpu.VMEM((pieces * own_rows, 3 * PAD), bf16),
            pltpu.SemaphoreType.DMA((pieces,)),
        ],
        cost_estimate=cost(12 * work * HD, 4 << 20, work),
        name="attend_forward",
    )(table, *parts, bias)
    return results[:n], results[n:]


def attend_back_kernel(heads, chosen, pieces, own_blocks, waited, carried, table, *refs):
    refs = list(refs)

    def take(count):
        taken = refs[:count]
        del refs[:count]
        return taken

    parts = take(pieces)
    ups = take(len(chosen))
    totals = take(len(chosen))
    (bias,) = take(1)
    take(waited)
    if carried:
        key_before, value_before = take(2)
        query_before = take(pieces - len(chosen))
        (small,) = take(1)
        outs = take(pieces)
        (tail,) = take(1)
        key_sum, value_sum, key_kept, value_kept, row_sums = take(5)
    else:
        outs = take(len(chosen))
        key_sum, value_sum = take(2)
    rows, up_rows, sems = refs
    own_rows = own_blocks * BLK
    copies = [
        pltpu.make_async_copy(parts[s], rows.at[pl.ds(s * own_rows, own_rows)], sems.at[s])
        for s in range(pieces)
    ] + [
        pltpu.make_async_copy(ups[at], up_rows.at[at], sems.at[pieces + at])
        for at in range(len(chosen))
    ]
    late = []
    if carried:
        late = [
            pltpu.make_async_copy(key_before, key_kept, sems.at[pieces + len(chosen)]),
            pltpu.make_async_copy(value_before, value_kept, sems.at[pieces + len(chosen) + 1]),
        ]
    for copy in copies + late:
        copy.start()
    key_sum[...] = jnp.zeros_like(key_sum)
    value_sum[...] = jnp.zeros_like(value_sum)
    for copy in copies:
        copy.wait()
    query_masks = head_masks(heads, HD**-0.5, bf16)
    up_masks = head_masks(heads, 1.0, bf16)
    out_masks = head_masks(heads, HD**-0.5, f32)

    def step(i, carry):
        for at, s in enumerate(chosen):
            block = s * own_blocks + i
            start = pl.multiple_of(i * BLK, BLK)
            here = pl.ds(pl.multiple_of(block * BLK, BLK), BLK)
            queries = stacked_heads(rows[here, 0:PAD], query_masks)
            upstream = stacked_heads(up_rows[at, pl.ds(start, BLK), :], up_masks)
            keys = key_blocks(rows, table, block, PAD)
            values = key_blocks(rows, table, block, 2 * PAD)
            kept = totals[at][pl.ds(start, BLK), :]
            log_total = jnp.concatenate([kept[:, h : h + 1] for h in range(heads)], axis=0)
            scores = contract(queries, keys, (1, 1)) + bias[pl.ds(block, 1), :]
            weights = jnp.exp(scores - log_total)
            grad_weights = contract(upstream, values, (1, 1))
            inner = jnp.sum(weights * grad_weights, axis=-1, keepdims=True)
            grad_scores = (weights * (grad_weights - inner)).astype(bf16)
            grad_query = contract(grad_scores, keys, (1, 0))
            to = outs[s] if carried else outs[at]
            to[pl.ds(start, BLK), 0:PAD] = unstacked_heads(grad_query, out_masks).astype(bf16)
            key_part = contract(grad_scores, queries, (0, 0))
            value_part = contract(weights.astype(bf16), upstream, (0, 0))
            for j in range(KEYS // BLK):
                there = pl.ds(pl.multiple_of(table[block, j] * BLK, BLK), BLK)
                key_sum[there, :] += key_part[j * BLK : (j + 1) * BLK]
                value_sum[there, :] += value_part[j * BLK : (j + 1) * BLK]
        return carry

    lax.fori_loop(0, own_blocks, step, 0)
    if not carried:
        return
    for copy in late:
        copy.wait()
    before = [s for s in range(pieces) if s not in chosen]
    for at, s in enumerate(before):
        outs[s][:, 0:PAD] = query_before[at][...]
    row_sums[...] = jnp.zeros_like(row_sums)
    for s in range(pieces):

        def finish(i, carry, s=s):
            at = pl.ds(pl.multiple_of(i * BLK, BLK), BLK)
            span = pl.ds(pl.multiple_of(s * own_rows + i * BLK, BLK), BLK)
            outs[s][at, PAD : 2 * PAD] = (key_sum[span, :] + key_kept[span, :]).astype(bf16)
            outs[s][at, 2 * PAD : 3 * PAD] = (value_sum[span, :] + value_kept[span, :]).astype(bf16)
            whole = outs[s][at, :].astype(f32)
            row_sums[...] += jnp.sum(whole.reshape(BLK // 8, 8, 3 * PAD), axis=0)
            return carry

        lax.fori_loop(0, own_blocks, finish, 0)
    slot = lax.broadcasted_iota(jnp.int32, small.shape, 0)
    whole = jnp.sum(row_sums[...], axis=0, keepdims=True)
    tail[...] = jnp.where(slot == SUM_ROW, whole, small[...]).astype(bf16)


def attend_backward(parts, ups, totals, table, bias, heads, chosen, waited=(), before=None):
    own_rows = parts[0].shape[0]
    pieces = len(parts)
    n = len(chosen)
    own_blocks = own_rows // BLK
    vmem = pl.BlockSpec(memory_space=pltpu.VMEM)
    anyspace = pl.BlockSpec(memory_space=pl.ANY)
    work = n * own_rows * KEYS * heads
    sum_shape = (pieces * own_rows, PAD)
    if before is None:
        outs = [((own_rows, PAD), bf16)] * n + [(sum_shape, f32)] * 2
        extra, extra_specs, scratch = [], [], []
    else:
        outs = [((own_rows, 3 * PAD), bf16)] * pieces + [((16, 3 * PAD), bf16)]
        extra = list(before)
        extra_specs = [anyspace] * 2 + [vmem] * (len(before) - 2)
        scratch = [pltpu.VMEM(sum_shape, f32)] * 4 + [pltpu.VMEM((8, 3 * PAD), f32)]
    return pl.pallas_call(
        partial(
            attend_back_kernel, heads, chosen, pieces, own_blocks, len(waited), before is not None
        ),
        out_shape=[jax.ShapeDtypeStruct(*out) for out in outs],
        in_specs=[pl.BlockSpec(memory_space=pltpu.SMEM)]
        + [anyspace] * (pieces + n)
        + [vmem] * (n + 1)
        + [anyspace] * len(waited)
        + extra_specs,
        out_specs=[vmem] * len(outs),
        scratch_shapes=scratch
        + [
            pltpu.VMEM((pieces * own_rows, 3 * PAD), bf16),
            pltpu.VMEM((n, own_rows, PAD), bf16),
            pltpu.SemaphoreType.DMA((pieces + n + 2,)),
        ],
        cost_estimate=cost(30 * work * HD, 12 << 20, work),
        name="attend_backward",
    )(table, *parts, *ups, *totals, bias, *waited, *extra)


VMEM_SPEC = pl.BlockSpec(memory_space=pltpu.VMEM)
ANY_SPEC = pl.BlockSpec(memory_space=pl.ANY)
SMEM_SPEC = pl.BlockSpec(memory_space=pltpu.SMEM)
COST_CUT = 64
GELU_A = 0.7978845608028654
GELU_B = 0.044715


def cost(flops, size, transcendentals=0):
    return pl.CostEstimate(
        flops=flops // COST_CUT, bytes_accessed=size // COST_CUT, transcendentals=transcendentals // COST_CUT
    )


def struct(shape, dtype):
    return jax.ShapeDtypeStruct(shape, dtype)


def row_stats(values):
    centred = values - jnp.mean(values, axis=-1, keepdims=True)
    inv_std = lax.rsqrt(jnp.mean(centred * centred, axis=-1, keepdims=True) + EPSILON)
    return centred * inv_std, inv_std


def norm_backward(upstream, scaled, inv_std, gain):
    weighted = upstream * gain
    inner = jnp.mean(weighted * scaled, axis=-1, keepdims=True)
    return inv_std * (weighted - jnp.mean(weighted, axis=-1, keepdims=True) - scaled * inner)


def column_sum(array):
    return jnp.sum(array.reshape(array.shape[0] // 8, 8, array.shape[1]), axis=0)


def rows_kernel(teams, sources, length, *refs):
    refs = list(refs)

    def take(count):
        taken = refs[:count]
        del refs[:count]
        return taken

    mixed = take(teams)
    x_in, g_in = take(2)
    weights = take(sources)
    vectors, b_up = take(2)
    b_out, g1, c1, b_down, g2, c2 = [vectors.at[k : k + 1, :] for k in range(6)]
    layer_out, low_out, grad_out, act_near, act_far, up_near, up_far = take(7)
    back_out = take(teams)
    after_out, after_turned, small = take(3)
    (
        o_buf,
        x_buf,
        g_buf,
        out_w,
        up_w,
        down_w,
        scaled_buf,
        inv_buf,
        wide_buf,
        low_buf,
        act_buf,
        slope_buf,
        last_buf,
        turned_buf,
        sums,
        up_sums,
        in_sems,
        w_sems,
        out_sems,
    ) = refs
    rows = x_in.shape[0]
    hidden = up_w.shape[2]
    tile, cut = 64, 256
    me = lax.axis_index("tensor")
    ring = sources > 1

    first = []
    for s in range(teams):
        first.append(pltpu.make_async_copy(mixed[s], o_buf.at[s], in_sems.at[s]))
    first.append(pltpu.make_async_copy(x_in, x_buf, in_sems.at[teams]))
    upstream_copy = pltpu.make_async_copy(g_in, g_buf, in_sems.at[teams + 1])
    fetched = ([], [], [])

    def fetch(kind, source, to):
        sem = w_sems.at[kind, len(fetched[kind])]
        fetched[kind].append(pltpu.make_async_copy(source, to, sem))

    wholes = (out_w, up_w, down_w)
    if ring:
        part = weights[0].shape[0]
        spans = ((2 * hidden, PAD), (0, hidden), (2 * hidden + 2 * PAD, hidden))
        for at, piece in enumerate(weights):
            row = pl.multiple_of(ring_member(RING_STEPS[at % 8]) * part, 16)
            for kind, (start, size) in enumerate(spans):
                for pair in range(2):
                    fetch(
                        kind,
                        piece.at[:, pl.ds(start + pair * size, size)],
                        wholes[kind].at[2 * pair + at // 8, pl.ds(row, part), :],
                    )
    else:
        spans = ((hidden, PAD), (0, hidden), (hidden + PAD, hidden))
        for kind, (start, size) in enumerate(spans):
            for s in range(teams):
                fetch(kind, weights[0].at[me ^ s, :, pl.ds(start, size)], wholes[kind].at[s])
    for copy in first + fetched[0] + fetched[1] + fetched[2] + [upstream_copy]:
        copy.start()
    sums[...] = jnp.zeros_like(sums)
    up_sums[...] = jnp.zeros_like(up_sums)
    leaving = []

    def leave(ref, to):
        copy = pltpu.make_async_copy(ref, to, out_sems.at[len(leaving)])
        copy.start()
        leaving.append(copy)

    def leave_turned(k, source, to):
        for n in range(D // LANES):
            span = slice(n * LANES, (n + 1) * LANES)
            turned_buf[k, span, :] = source[:, span].T
        bits, far, part, _ = to.shape
        here = lax.axis_index("dp")
        for b in range(bits):
            for z in range(far):
                row = (here ^ (2 * z + b)) * part if ring else 0
                leave(turned_buf.at[k, pl.ds(pl.multiple_of(row, 16), part), :], to.at[b, z])

    def tiles(body):
        def step(i, carry):
            body(i, pl.ds(pl.multiple_of(i * tile, tile), tile))
            return carry

        lax.fori_loop(0, rows // tile, step, 0)

    for copy in first + fetched[0]:
        copy.wait()
    for n in range(D // cut):
        cols = slice(n * cut, (n + 1) * cut)
        total = contract(o_buf[0], out_w[0, cols, :], (1, 1))
        for s in range(1, teams):
            total = total + contract(o_buf[s], out_w[s, cols, :], (1, 1))
        wide_buf[:, cols] = total

    def first_norm(i, at):
        after = x_buf[at, :].astype(f32) + wide_buf[at, :] + b_out[...]
        scaled, inv_std = row_stats(after)
        scaled_buf[at, :] = scaled
        inv_buf[at, :] = jnp.broadcast_to(inv_std, (tile, LANES))
        low_buf[at, :] = (scaled * g1[...] + c1[...]).astype(bf16)

    tiles(first_norm)
    leave_turned(0, low_buf, low_out)
    for copy in fetched[1]:
        copy.wait()

    def up_step(s, carry):
        bias = b_up[pl.ds(s ^ me, 1), :]
        for c in range(hidden // cut):
            cols = slice(c * cut, (c + 1) * cut)
            u = contract(low_buf[...], up_w[s, :, cols], (1, 0)) + bias[:, cols]
            square = u * u
            t = jnp.tanh(u * (GELU_A + GELU_A * GELU_B * square))
            half = 0.5 + 0.5 * t
            act_buf[s, :, cols] = (u * half).astype(bf16)
            slope_buf[s, :, cols] = (
                half + (0.5 * u) * (1.0 - t * t) * (GELU_A + 3.0 * GELU_A * GELU_B * square)
            ).astype(bf16)
        return carry

    lax.fori_loop(0, teams, up_step, 0)
    for s in range(teams):
        leave(act_buf.at[s], (act_far if s % 2 else act_near).at[s // 2])
    for copy in fetched[2]:
        copy.wait()
    upstream_copy.wait()
    for n in range(D // cut):
        cols = slice(n * cut, (n + 1) * cut)
        total = contract(act_buf[0], down_w[0, cols, :], (1, 1))
        for s in range(1, teams):
            total = total + contract(act_buf[s], down_w[s, cols, :], (1, 1))
        wide_buf[:, cols] = total
    start = me * rows
    seq = start // LMAX
    live = length[seq] - (start - seq * LMAX)

    def second_norm(i, at):
        z = (scaled_buf[at, :] * g1[...] + c1[...]) + wide_buf[at, :] + b_down[...]
        scaled, inv_std = row_stats(z)
        x_buf[at, :] = (scaled * g2[...] + c2[...]).astype(bf16)
        row = lax.broadcasted_iota(jnp.int32, (tile, D), 0) + i * tile
        upstream = jnp.where(row < live, g_buf[at, :].astype(f32), 0.0)
        grad = norm_backward(upstream, scaled, inv_std, g2[...]).astype(bf16)
        g_buf[at, :] = grad
        sums[0:8, :] += column_sum(upstream * scaled)
        sums[8:16, :] += column_sum(upstream)
        sums[16:24, :] += column_sum(grad.astype(f32))

    tiles(second_norm)
    leave(x_buf, layer_out)
    leave_turned(1, g_buf, grad_out)

    def down_back(s, carry):
        for c in range(hidden // cut):
            cols = slice(c * cut, (c + 1) * cut)
            g = contract(g_buf[...], down_w[s, :, cols], (1, 0))
            g = (g * slope_buf[s, :, cols].astype(f32)).astype(bf16)
            slope_buf[s, :, cols] = g
            up_sums[pl.ds(pl.multiple_of(s * 8, 8), 8), cols] = column_sum(g.astype(f32))
        return carry

    lax.fori_loop(0, teams, down_back, 0)
    for s in range(teams):
        leave(slope_buf.at[s], (up_far if s % 2 else up_near).at[s // 2])
    for n in range(D // cut):
        cols = slice(n * cut, (n + 1) * cut)
        total = contract(slope_buf[0], up_w[0, cols, :], (1, 1))
        for s in range(1, teams):
            total = total + contract(slope_buf[s], up_w[s, cols, :], (1, 1))
        wide_buf[:, cols] = total

    def first_back(i, at):
        upstream = g_buf[at, :].astype(f32) + wide_buf[at, :]
        scaled = scaled_buf[at, :]
        grad = norm_backward(upstream, scaled, inv_buf[at, :][:, :1], g1[...]).astype(bf16)
        last_buf[at, :] = grad
        sums[24:32, :] += column_sum(upstream * scaled)
        sums[32:40, :] += column_sum(upstream)
        sums[40:48, :] += column_sum(grad.astype(f32))

    tiles(first_back)
    leave(last_buf, after_out)
    leave_turned(2, last_buf, after_turned)
    for s in (2, 3, 1, 0):
        o_buf[s] = contract(last_buf[...], out_w[s], (1, 0)).astype(bf16)
        leave(o_buf.at[s], back_out[s])
    small[...] = jnp.zeros_like(small)
    for k in range(6):
        small[k : k + 1, :] = jnp.sum(sums[8 * k : 8 * k + 8, :], axis=0, keepdims=True)
    for s in range(teams):
        small[pl.ds(6 + (s ^ me), 1), :] = jnp.sum(
            up_sums[8 * s : 8 * s + 8, :], axis=0, keepdims=True
        )
    for copy in leaving:
        copy.wait()


def layer_rows(mixed, hidden_in, grad_out, weights, vectors, lengths):
    teams = len(mixed)
    rows = hidden_in.shape[0]
    rows_of, b_up = vectors
    hidden = b_up.shape[1]
    half = teams // 2
    low = struct((rows, D), bf16)
    pair = struct((half, rows, hidden), bf16)
    ring = len(weights) > 1
    turned = struct((2, 4, D // 8, rows) if ring else (1, 1, D, rows), bf16)
    return pl.pallas_call(
        partial(rows_kernel, teams, len(weights)),
        out_shape=[low, turned, turned, pair, pair, pair, pair]
        + [struct((rows, PAD), bf16)] * teams
        + [low, turned, struct((16, D), f32)],
        in_specs=[SMEM_SPEC] + [ANY_SPEC] * (teams + 2 + len(weights)) + [VMEM_SPEC] * 2,
        out_specs=[ANY_SPEC] * (9 + teams) + [VMEM_SPEC],
        scratch_shapes=[
            pltpu.VMEM((teams, rows, PAD), bf16),
            pltpu.VMEM((rows, D), bf16),
            pltpu.VMEM((rows, D), bf16),
            pltpu.VMEM((teams, D, PAD), bf16),
            pltpu.VMEM((teams, D, hidden), bf16),
            pltpu.VMEM((teams, D, hidden), bf16),
            pltpu.VMEM((rows, D), f32),
            pltpu.VMEM((rows, LANES), f32),
            pltpu.VMEM((rows, D), f32),
            pltpu.VMEM((rows, D), bf16),
            pltpu.VMEM((teams, rows, hidden), bf16),
            pltpu.VMEM((teams, rows, hidden), bf16),
            pltpu.VMEM((rows, D), bf16),
            pltpu.VMEM((3, D, rows), bf16),
            pltpu.VMEM((48, D), f32),
            pltpu.VMEM((8 * teams, hidden), f32),
            pltpu.SemaphoreType.DMA((teams + 2,)),
            pltpu.SemaphoreType.DMA((3, 32)),
            pltpu.SemaphoreType.DMA((2 + 3 * teams + 24,)),
        ],
        cost_estimate=cost(8 * rows * D * (teams * hidden) + 4 * rows * D * teams * PAD, 24 << 20),
        compiler_params=pltpu.CompilerParams(vmem_limit_bytes=60 << 20),
        name="layer_rows",
    )(
        lengths,
        *mixed,
        hidden_in,
        grad_out,
        *weights,
        rows_of,
        b_up,
    )


def row_dot(groups, cut_by=None, waited=(), tail=None):
    sets = len(groups[0][0])
    bits, far, part, rows = groups[0][0][0].shape
    count = groups[0][1][0].shape[0]
    cut = 256
    lows = [0]
    for _, rights in groups:
        lows.append(lows[-1] + rights[0].shape[2] // cut)
    high = bits * far * part
    below = 0 if tail is None else tail.shape[0]
    cuts = 1 if cut_by is None else 2

    def kernel(*refs):
        refs = list(refs)
        ins = [[refs.pop(0) for _ in range(sets)] for _ in groups]
        others = [[refs.pop(0) for _ in range(sets)] for _ in groups]
        if below:
            tail_ref = refs.pop(0)
        outs = refs[len(waited) :]
        j = pl.program_id(0)
        for g in range(len(groups)):

            @pl.when((j >= lows[g]) & (j < lows[g + 1]))
            def _(g=g):
                for i in range(count):
                    total = contract(ins[g][0][...].reshape(high, rows), others[g][0][i], (1, 0))
                    for k in range(1, sets):
                        total = total + contract(
                            ins[g][k][...].reshape(high, rows), others[g][k][i], (1, 0)
                        )
                    total = total.astype(bf16).reshape(bits, far, part, cut)
                    for b in range(bits):
                        if cut_by == "bits":
                            to = outs[b].at[i, 0]
                        elif cut_by == "rights":
                            to = outs[i].at[0, b]
                        else:
                            to = outs[0].at[i, b]
                        if below:
                            to[:, :part, :] = total[b]
                            to[:, part:, :] = jnp.broadcast_to(
                                tail_ref[...][None], (far, below, cut)
                            )
                        else:
                            to[...] = total[b]

    def column(g):
        return lambda j: (0, 0, jnp.clip(j - lows[g], 0, lows[g + 1] - lows[g] - 1))

    specs, arrays = [], []
    for lefts, _ in groups:
        specs += [pl.BlockSpec((bits, far, part, rows), lambda j: (0, 0, 0, 0))] * sets
        arrays += list(lefts)
    for g, (_, rights) in enumerate(groups):
        specs += [pl.BlockSpec((count, rows, cut), column(g))] * sets
        arrays += list(rights)
    if below:
        specs.append(pl.BlockSpec((below, cut), lambda j: (0, j)))
        arrays.append(tail)
    width = lows[-1] * cut
    lead = (count // 2 if cut_by == "rights" else count, bits // 2 if cut_by == "bits" else bits)
    return pl.pallas_call(
        kernel,
        grid=(lows[-1],),
        out_shape=[struct((*lead, far, part + below, width), bf16)] * cuts,
        in_specs=specs + [ANY_SPEC] * len(waited),
        out_specs=[
            pl.BlockSpec((*lead, far, part + below, cut), lambda j: (0, 0, 0, 0, j))
        ]
        * cuts,
        cost_estimate=cost(2 * sets * rows * high * count * width, 8 << 20),
        name="row_dot",
    )(*arrays, *waited)


def plus(a, b, waited=(), cuts=1, dtype=bf16):
    lead = a.shape[0] // cuts

    def kernel(a_ref, b_ref, *refs):
        for k in range(cuts):
            span = slice(k * lead, (k + 1) * lead)
            refs[len(waited) + k][...] = (
                a_ref[span].astype(f32) + b_ref[span].astype(f32)
            ).astype(dtype)

    return pl.pallas_call(
        kernel,
        out_shape=[struct((lead, *a.shape[1:]), dtype)] * cuts,
        in_specs=[VMEM_SPEC] * 2 + [ANY_SPEC] * len(waited),
        out_specs=[VMEM_SPEC] * cuts,
        cost_estimate=cost(a.size, 6 * a.size),
        name="plus",
    )(a, b, *waited)


def joined_sums(pairs, waited=()):
    rows = pairs[0][0].shape[1]
    widths = [a.shape[2] for a, _ in pairs]
    count = 2 * len(pairs)

    def kernel(*refs):
        outs = refs[count + len(waited) :]
        for z in range(4):
            at = 0
            for k, width in enumerate(widths):
                outs[z][:, at : at + width] = (
                    refs[2 * k][z].astype(f32) + refs[2 * k + 1][z].astype(f32)
                ).astype(bf16)
                at += width

    return pl.pallas_call(
        kernel,
        out_shape=[struct((rows, sum(widths)), bf16)] * 4,
        in_specs=[VMEM_SPEC] * count + [ANY_SPEC] * len(waited),
        out_specs=[VMEM_SPEC] * 4,
        cost_estimate=cost(rows * sum(widths) * 4, rows * sum(widths) * 24),
        name="joined_sums",
    )(*[array for pair in pairs for array in pair], *waited)


def held(array, waited):
    def kernel(a_ref, *refs):
        refs[-1][...] = a_ref[...]

    return pl.pallas_call(
        kernel,
        out_shape=struct(array.shape, array.dtype),
        in_specs=[VMEM_SPEC] + [ANY_SPEC] * len(waited),
        out_specs=VMEM_SPEC,
        cost_estimate=cost(array.size, 8 * array.size),
        name="held",
    )(array, *waited)


def spread(grads, weight, added=None, after=None, waited=()):
    rows = grads[0].shape[0]

    def kernel(first, second, w, *refs):
        if added is None:
            out = refs[-1]
            out[0] = contract(first[...], w[...], (1, 1)).astype(bf16)
            out[1] = contract(second[...], w[...], (1, 1)).astype(bf16)
            return
        plus_ref, after_ref = refs[:2]
        away, here = refs[-2:]
        away[...] = (contract(first[...], w[...], (1, 1)) + plus_ref[0].astype(f32)).astype(bf16)
        here[...] = contract(second[...], w[...], (1, 1)) + (
            plus_ref[1].astype(f32) + after_ref[...].astype(f32)
        )

    if added is None:
        outs, more = struct((2, rows, D), bf16), []
    else:
        outs, more = [struct((rows, D), bf16), struct((rows, D), f32)], [added, after]
    return pl.pallas_call(
        kernel,
        out_shape=outs,
        in_specs=[VMEM_SPEC] * (3 + len(more)) + [ANY_SPEC] * len(waited),
        out_specs=VMEM_SPEC if added is None else [VMEM_SPEC] * 2,
        cost_estimate=cost(4 * rows * D * weight.shape[1], 5 << 20),
        name="spread",
    )(*grads, weight, *more, *waited)


def pack_weights(w_query, w_key, w_value, w_up, w_out, w_down):
    rows, width = w_query.shape
    hidden = w_up.shape[1]

    def kernel(q, k, v, up, out, down, qkv, own):
        for at, ref in enumerate((q, k, v)):
            qkv[:, at * PAD : (at + 1) * PAD] = jnp.zeros((rows, PAD), bf16)
            qkv[:, at * PAD : at * PAD + width] = ref[...]
        own[:, :hidden] = up[...]
        own[:, hidden : hidden + PAD] = jnp.zeros((rows, PAD), bf16)
        own[:, hidden : hidden + width] = out[...].T
        own[:, hidden + PAD :] = down[...].T

    return pl.pallas_call(
        kernel,
        out_shape=[
            struct((rows, 3 * PAD), bf16),
            struct((rows, 2 * hidden + PAD), bf16),
        ],
        in_specs=[VMEM_SPEC] * 6,
        out_specs=[VMEM_SPEC] * 2,
        cost_estimate=cost(rows * hidden, 4 << 20),
        name="pack_weights",
    )(w_query, w_key, w_value, w_up, w_out, w_down)


def pair_weights(own, beyond, hidden):
    rows, width = own.shape
    starts = (0, hidden, hidden + PAD, width)

    def kernel(a, b, out):
        for at, end in zip(starts, starts[1:]):
            out[:, 2 * at : at + end] = a[:, at:end]
            out[:, at + end : 2 * end] = b[:, at:end]

    return pl.pallas_call(
        kernel,
        out_shape=struct((rows, 2 * width), bf16),
        in_specs=[VMEM_SPEC] * 2,
        out_specs=VMEM_SPEC,
        cost_estimate=cost(rows * width, 4 * rows * width),
        name="pair_weights",
    )(own, beyond)


def project_in(xs, weights, bias):
    rows = xs[0].shape[0]
    pieces = len(xs)
    sources = len(weights)
    ordered = sources > 1
    bits, far = (2, 4) if ordered else (1, 1)
    part = D // (bits * far)
    wide = weights[0].shape[1]

    def kernel(*refs):
        refs = list(refs)
        ins = [refs.pop(0) for _ in range(pieces)]
        shards = [refs.pop(0) for _ in range(sources)]
        b = refs.pop(0)
        outs = [refs.pop(0) for _ in range(pieces)]
        turned_outs = [refs.pop(0) for _ in range(pieces)]
        whole_out, x_buf, w, out_buf, turned, sems, w_sems, out_sems = refs
        here = lax.axis_index("dp") if ordered else 0
        copies = [
            pltpu.make_async_copy(ins[s], x_buf.at[s], sems.at[s]) for s in range(pieces)
        ]
        fetched = []
        for at in range(sources):
            row = ring_member(RING_STEPS[at]) * part if ordered else 0
            fetched.append(
                pltpu.make_async_copy(
                    shards[at],
                    w.at[pl.ds(pl.multiple_of(row, 16), shards[at].shape[0]), :],
                    w_sems.at[at],
                )
            )
        for copy in fetched + copies:
            copy.start()
        for copy in fetched:
            copy.wait()
        leaving = []

        def leave(ref, to):
            copy = pltpu.make_async_copy(ref, to, out_sems.at[len(leaving)])
            copy.start()
            leaving.append(copy)

        leave(w, whole_out)
        for s in range(pieces):
            copies[s].wait()
            for c in range(0, wide, PAD):
                cols = slice(c, c + PAD)
                out_buf[s, :, cols] = (
                    contract(x_buf[s], w[:, cols], (1, 0)) + b[:, cols]
                ).astype(bf16)
            leave(out_buf.at[s], outs[s])
            for n in range(D // LANES):
                span = slice(n * LANES, (n + 1) * LANES)
                turned[s, span, :] = x_buf[s, :, span].T
            for k in range(bits):
                for z in range(far):
                    row = (here ^ (2 * z + k)) * part if ordered else 0
                    leave(
                        turned.at[s, pl.ds(pl.multiple_of(row, 16), part), :],
                        turned_outs[s].at[k, z],
                    )
        for copy in leaving:
            copy.wait()

    results = pl.pallas_call(
        kernel,
        out_shape=[struct((rows, wide), bf16)] * pieces
        + [struct((bits, far, part, rows), bf16)] * pieces
        + [struct((D, wide), bf16)],
        in_specs=[ANY_SPEC] * (pieces + sources) + [VMEM_SPEC],
        out_specs=[ANY_SPEC] * (2 * pieces + 1),
        scratch_shapes=[
            pltpu.VMEM((pieces, rows, D), bf16),
            pltpu.VMEM((D, wide), bf16),
            pltpu.VMEM((pieces, rows, wide), bf16),
            pltpu.VMEM((pieces, D, rows), bf16),
            pltpu.SemaphoreType.DMA((pieces,)),
            pltpu.SemaphoreType.DMA((sources,)),
            pltpu.SemaphoreType.DMA((1 + pieces * (1 + bits * far),)),
        ],
        cost_estimate=cost(2 * pieces * rows * D * wide, 12 << 20),
        name="project_in",
    )(*xs, *weights, bias)
    return results[:pieces], results[pieces : 2 * pieces], results[2 * pieces]


def padded(array):
    return jnp.pad(array, ((0, 0), (0, PAD - array.shape[1])))


def dot(a, b, dims=(1, 0)):
    return contract(a, b, dims)


def per_device(
    hidden_in,
    grad_out,
    w_query,
    b_query,
    w_key,
    w_value,
    b_value,
    w_out,
    b_out,
    gain_one,
    shift_one,
    w_up,
    b_up,
    w_down,
    b_down,
    gain_two,
    shift_two,
    lengths,
    global_raw,
    random_raw,
):
    own_rows = hidden_in.shape[0]
    me = lax.axis_index("tensor")
    teams = lax.axis_size("tensor")
    members = lax.axis_size("dp")
    width = w_query.shape[1]
    heads = width // HD
    hidden = w_up.shape[1]

    table, bias = block_tables(lengths, global_raw, random_raw, own_rows // BLK, teams)

    x2 = swap(hidden_in, 2)
    x1 = swap(hidden_in, 1)
    x3 = swap(x2, 1)
    x_parts = [hidden_in, x1, x2, x3]

    qkv_b = jnp.concatenate(
        [jnp.pad(b_query, (0, PAD - width)), jnp.zeros((PAD,), f32), jnp.pad(b_value, (0, PAD - width))]
    )
    halved = members == 8
    if halved:
        qkv_shard, own = pack_weights(w_query, w_key, w_value, w_up, w_out, w_down)
        shard = pair_weights(own, swap(own, 2), hidden)
        qkv_pieces = ring_pieces(qkv_shard)
    else:
        qkv_shard = jnp.concatenate([padded(w_query), padded(w_key), padded(w_value)], axis=1)
        qkv_pieces = [lax.all_gather(qkv_shard, "dp", axis=0, tiled=True)]
        shard = jnp.concatenate([w_up, padded(w_out.T), w_down.T], axis=1)
        weights = lax.all_gather(shard, ("dp", "tensor"), axis=0, tiled=False)
        weights = jnp.swapaxes(weights.reshape(members, teams, *shard.shape), 0, 1)
        weights = [weights.reshape(teams, D, shard.shape[1])]

    qkv, x_turned, qkv_w = project_in(x_parts, qkv_pieces, qkv_b[None])
    (o2, o3), (t2, t3) = attend_forward(qkv, table, bias, heads, (2, 3))
    r2 = swap(o2, 2)
    r3 = swap(o3, 3)
    (o0, o1), (t0, t1) = attend_forward(qkv, table, bias, heads, (0, 1))
    r1 = swap(o1, 1)
    if halved:

        def gate(step, ahead, behind):
            waited = {3: qkv[0], 4: o2}.get(step)
            if waited is None:
                return ahead, behind
            ahead = held(ahead, (waited,))
            if step < 4:
                behind = held(behind, (waited,))
            return ahead, behind

        weights = ring_pieces(shard, gate)
        weights = weights + [swap(piece, 1) for piece in weights]

    results = layer_rows(
        [o0, r1, r2, r3],
        hidden_in,
        grad_out,
        weights,
        (
            jnp.stack([b_out, gain_one, shift_one, b_down, gain_two, shift_two]),
            b_up.reshape(teams, hidden),
        ),
        lengths,
    )
    layer_out, low, grad_low, act_near, act_far, up_near, up_far = results[:7]
    backs = results[7 : 7 + teams]
    after_low, after_turned, small = results[7 + teams :]
    ups = [backs[0]] + [swap(backs[s], s) for s in range(1, teams)]
    small = small + swap(small, 1)
    small = small + swap(small, 2)

    down_group = ([grad_low, swap(grad_low, 1)], [act_near, swap(act_far, 1)])
    up_group = ([low, swap(low, 1)], [up_near, swap(up_far, 1)])
    out_group = (
        [after_turned, swap(after_turned, 1)],
        [jnp.stack([o0, r2]), jnp.stack([o1, swap(r3, 1)])],
    )
    if halved:
        up_kept, up_gone = row_dot([up_group, out_group], "bits")
        up_away = dp_swap(up_gone, 1)
        down_kept, down_gone = row_dot([down_group], "rights", (up_gone, ups[2], ups[3], small))
        down_away = swap(down_gone, 2)
        waited = (down_gone,)
    else:
        down_sums = row_dot([down_group])[0].reshape(2, D, -1)
        up_sums = row_dot([up_group, out_group])[0].reshape(2, D, -1)
        waited = ()

    totals = [t0, t1, t2, t3]
    before = attend_backward(qkv, ups[:2], totals[:2], table, bias, heads, (0, 1), waited)
    if halved:
        down_here, down_next = plus(down_kept[0], down_away[0], (before[0],), 2)
        down_away = dp_swap(down_next, 1)
        up_here, up_next = plus(up_kept, up_away, (before[0],), 2)
        up_away = swap(up_next, 2)
        waited = (down_next, up_next)
    results = attend_backward(
        qkv,
        ups[2:],
        totals[2:],
        table,
        bias,
        heads,
        (2, 3),
        waited,
        (before[2], before[3], before[0], before[1], small),
    )
    grads, tail = results[:4], results[4]
    waited = ()
    if halved:
        sums = joined_sums(
            [(down_here[0], down_away[0]), (up_here[0, 0], up_away[0, 0])], (grads[0],)
        )
        waited = (sums[0],)
    parts = spread([grads[3], grads[1]], qkv_w, waited=waited)
    spread_away = swap(parts, 1)
    qkv_group = (x_turned, [g[None] for g in grads])
    if halved:
        kept, gone = row_dot([qkv_group], "bits", (parts,), tail)
        away = dp_swap(gone, 1)
        beyond, here = spread([grads[2], grads[0]], qkv_w, spread_away, after_low, (kept,))
        total = sums[0].astype(f32)
        for z in range(1, 4):
            total = total + dp_swap(sums[z], 2 * z).astype(f32)
        down_part, up_part = total[:, :hidden], total[:, hidden:]
        blocks = joined_sums([(kept[0, 0], away[0, 0])], (beyond,))
        beyond = swap(beyond, 2)
        qkv_part = blocks[0].astype(f32)
        for z in range(1, 4):
            qkv_part = qkv_part + dp_swap(blocks[z], 2 * z).astype(f32)
        qkv_part, small = qkv_part[:-16], qkv_part[-16:]
    else:
        blocks = row_dot([qkv_group])[0].reshape(D, -1)
        qkv_part = dp_scatter_sum(blocks)
        small = lax.psum(tail.astype(f32), "dp")
        beyond, here = spread([grads[2], grads[0]], qkv_w, spread_away, after_low)
        beyond = swap(beyond, 2)
        down_part = dp_scatter_sum(down_sums[0] + swap(down_sums[1], 2))
        up_part = dp_scatter_sum(up_sums[0] + swap(up_sums[1], 2))
    grad_in = here + beyond.astype(f32)

    bias_row = small[SUM_ROW]
    return (
        layer_out,
        grad_in,
        qkv_part[:, :width],
        bias_row[:width],
        qkv_part[:, PAD : PAD + width],
        qkv_part[:, 2 * PAD : 2 * PAD + width],
        bias_row[2 * PAD : 2 * PAD + width],
        up_part[:, hidden : hidden + width].T,
        small[5],
        small[3],
        small[4],
        up_part[:, :hidden],
        jnp.take(small[6 : 6 + teams], me, axis=0),
        down_part.T,
        small[2],
        small[0],
        small[1],
    )


def solution(mesh):
    in_specs = (
        P(("dp", "tensor"), None),
        P(("dp", "tensor"), None),
        P("dp", "tensor"),
        P("tensor"),
        P("dp", "tensor"),
        P("dp", "tensor"),
        P("tensor"),
        P("tensor", "dp"),
        P(),
        P(),
        P(),
        P("dp", "tensor"),
        P(),
        P("tensor", "dp"),
        P(),
        P(),
        P(),
        P("dp"),
        P("dp", None),
        P("dp", None, None),
    )
    out_specs = (
        P(("dp", "tensor"), None),
        P(("dp", "tensor"), None),
        P("dp", "tensor"),
        P("tensor"),
        P("dp", "tensor"),
        P("dp", "tensor"),
        P("tensor"),
        P("tensor", "dp"),
        P(),
        P(),
        P(),
        P("dp", "tensor"),
        P("tensor"),
        P("tensor", "dp"),
        P(),
        P(),
        P(),
    )
    return jax.shard_map(
        per_device, mesh=mesh, in_specs=in_specs, out_specs=out_specs, check_vma=False
    )
```

time: 375 us -> 349 us (0.931); the launches traced: 368 us -> 348 us
  Pallas kernels: 47.1 us -> 147 us
  matrix products: 68 us -> 0 us
  starting transfers between devices: 69.2 us -> 50.6 us
  other arithmetic: 23.8 us -> 7.61 us
  local copies, waits for them, and re-layouts: 35.3 us -> 23.7 us
  waiting for transfers between devices: 122 us -> 117 us
    pallas_call x1 -> x19, Pallas kernels: 29.3 us -> 130 us  [the longest x2 32.9 us: attend_backward(): pl.pallas_call(partial(attend_back_kernel, heads, chosen, pieces, own_blo...]
    dot_general x30 -> x0, matrix products: 68 us -> none  [contract(): lax.dot_general(a, b, ((dims[:1], dims[1:]), ((), ())), preferred_element...]
    ppermute x42 -> x14, waiting for transfers between devices: 83.6 us -> 30.2 us  [ring_send(): lax.ppermute(array, 'dp', [(order[i], order[(i + step) % size]) for i in...]
    ppermute x42 -> x14, starting transfers between devices: 47.2 us -> 18.4 us  [ring_send(): lax.ppermute(array, 'dp', [(order[i], order[(i + step) % size]) for i in...]
    ppermute x6 -> x9, waiting for transfers between devices: 2.79 us -> 27 us  [dp_swap(): return lax.ppermute(array, 'dp', [(t, t ^ bit) for t in range(size)])]
    ppermute x26 -> x30, waiting for transfers between devices: 35.4 us -> 59.4 us  [swap(): return lax.ppermute(array, 'tensor', [(t, t ^ bit) for t in range(size)])]
    dynamic_update_slice x23 -> x0, local copies, waits for them, and re-layouts: 11.7 us -> none  [the longest x21 11.5 us: put(): lax.dynamic_update_slice(whole, piece[None], (ring_member(steps), 0, 0))]
    reduce_sum x11 -> x0, other arithmetic: 10.7 us -> none  [the longest x2 3.66 us: norm_backward(): jnp.sum(upstream * scaled, axis=0)]
  transfers between devices with their start and end apart: 74 -> 53, of which waited for: 34 -> 25; matrix products, arithmetic and copies ran while one was open for 23% -> 3% of each run, Pallas kernels for 13% -> 30%
where the time goes in v2:
time: 349 us; the launch traced here: 348 us
  Pallas kernels  147 us (42%)
  waiting for transfers between devices  117 us (34%)
  starting transfers between devices  50.6 us (14%)
  local copies, waits for them, and re-layouts  23.7 us (7%)
  other arithmetic  7.61 us (2%)
    ppermute x30, waiting for transfers between devices, swap(): return lax.ppermute(array, 'tensor', [(t, t ^ bit) for t in range(size)])  59.4 us
    pallas_call x2, Pallas kernels, attend_backward(): pl.pallas_call(partial(attend_back_kernel, heads, chosen, pieces, own_blo...  32.9 us
    pallas_call x1, Pallas kernels, layer_rows(): pl.pallas_call(partial(rows_kernel, teams, len(weights)), out_shape=[low,...  32.4 us
    ppermute x14, waiting for transfers between devices, ring_send(): lax.ppermute(array, 'dp', [(order[i], order[(i + step) % size]) for i in...  30.2 us
    ppermute x9, waiting for transfers between devices, dp_swap(): return lax.ppermute(array, 'dp', [(t, t ^ bit) for t in range(size)])  27 us
    pallas_call x3, Pallas kernels, row_dot(): pl.pallas_call(kernel, grid=(lows[-1],), out_shape=[struct((*lead, far, p...  20.9 us
    unnamed x109, local copies, waits for them, and re-layouts  19.7 us
    ppermute x14, starting transfers between devices, ring_send(): lax.ppermute(array, 'dp', [(order[i], order[(i + step) % size]) for i in...  18.4 us
  transfers between devices with their start and end apart: 53, of which 25 were waited for; matrix products, arithmetic and copies ran while one was open for 3% of the time, Pallas kernels for 30%

profile of v2, /device:TPU:0, one launch (start us, length us, event | category | flops | bytes accessed | tf_op | source)
XLA Modules:
  0.0 347.7 jit_solution(1811673756182107569)
XLA Ops:
  0.7 1.8 copy.38.down
  2.5 1.9 pack_weights.1
  4.4 2.9 collective-permute-start.13
  7.4 9.1 %collective-permute-done.13.b = bf16[96,1792]{1,0:T(8,128)(2,1)S(1)} collective-permute-done((bf16[96,1792]{1,0:T(8,128)(2,1)}, bf16[96,1792]{1,0:T(8,128)(2,1)S(1)}, u32[]{:S(2)}, u32[]{:S(2)}) %collective-permute-start.13) | collective-permute-done | bytes 344096 | tf_op jit(solution)/shard_map/ppermute | solution.py:31
  17.2 2.0 pair_weights.1.refs_6_
  19.2 2.1 collective-permute-start.14
  23.4 9.1 %collective-permute-done.1.refs_2_ = bf16[512,768]{1,0:T(8,128)(2,1)S(1)} collective-permute-done((bf16[512,768]{1,0:T(8,128)(2,1)}, bf16[512,768]{1,0:T(8,128)(2,1)S(1)}, u32[]{:S(2)}, u32[]{:S(2)}) %collective-permute-start.1) | collective-permute-done | bytes 786464 | tf_op jit(solution)/shard_map/ppermute | solution.py:31
  32.5 5.8 %collective-permute-done.3.refs_5_ = bf16[96,768]{1,0:T(8,128)(2,1)S(1)} collective-permute-done((bf16[96,768]{1,0:T(8,128)(2,1)}, bf16[96,768]{1,0:T(8,128)(2,1)S(1)}, u32[]{:S(2)}, u32[]{:S(2)}) %collective-permute-start.3) | collective-permute-done | bytes 147488 | tf_op jit(solution)/shard_map/ppermute | solution.py:54
  38.3 1.8 collective-permute-start.5
  40.4 1.8 collective-permute-start.16
  42.2 2.9 collective-permute-done.5.refs_7_
  46.9 10.4 %collective-permute-done.6.refs_8_ = bf16[96,768]{1,0:T(8,128)(2,1)S(1)} collective-permute-done((bf16[96,768]{1,0:T(8,128)(2,1)S(1)}, bf16[96,768]{1,0:T(8,128)(2,1)S(1)}, u32[]{:S(2)}, u32[]{:S(2)}) %collective-permute-start.6) | collective-permute-done | bytes 147488 | tf_op jit(solution)/shard_map/ppermute | solution.py:54
  58.9 3.6 %collective-permute-done.7.refs_9_ = bf16[96,768]{1,0:T(8,128)(2,1)S(1)} collective-permute-done((bf16[96,768]{1,0:T(8,128)(2,1)S(1)}, bf16[96,768]{1,0:T(8,128)(2,1)S(1)}, u32[]{:S(2)}, u32[]{:S(2)}) %collective-permute-start.7) | collective-permute-done | bytes 147488 | tf_op jit(solution)/shard_map/ppermute | solution.py:54
  63.5 5.0 %collective-permute-done.8.refs_10_ = bf16[96,768]{1,0:T(8,128)(2,1)S(1)} collective-permute-done((bf16[96,768]{1,0:T(8,128)(2,1)S(1)}, bf16[96,768]{1,0:T(8,128)(2,1)S(1)}, u32[]{:S(2)}, u32[]{:S(2)}) %collective-permute-start.8) | collective-permute-done | bytes 147488 | tf_op jit(solution)/shard_map/ppermute | solution.py:54
  71.3 2.5 collective-permute-done.9.refs_11_
  75.3 8.4 %project_in.1 = (bf16[512,768]{1,0:T(8,128)(2,1)}, bf16[512,768]{1,0:T(8,128)(2,1)}, bf16[512,768]{1,0:T(8,128)(2,1)}, bf16[512,768]{1,0:T(8,128)(2,1)}, bf16[2,...) custom-call(bf16[512,768]{1,0:T(8,128)(2,1)} %refs_4_.1, ...), custom_call_target="tpu_custom_call" | custom-call | flops 37748736 | bytes 196608 | tf_op jit(solution)/shard_map/project_in/pallas_call | solution.py:960
  84.6 2.0 held.3
  90.0 4.8 %block_tables.1 = (s32[32,8]{1,0:T(8,128)}, f32[32,512]{1,0:T(8,128)}) custom-call(s32[1]{0:T(128)S(6)} %copy.40.length_ref.length, s32[1,2]{1,0:T(1,128)} %global_ref.1, s32[1,32,3]{2,1,0:T(8,128)} %copy.37.random_ref), custom_call_target="tpu_custom_call" | custom-call | flops 4096 | bytes 1024 | tf_op jit(solution)/shard_map/block_tables/pallas_call | solution.py:130
  94.8 8.8 %attend_forward.3 = (bf16[512,256]{1,0:T(8,128)(2,1)}, bf16[512,256]{1,0:T(8,128)(2,1)}, f32[512,128]{1,0:T(8,128)}, f32[512,128]{1,0:T(8,128)}) custom-call(s32[32,8]{1,0:T(8,128)} %get-tuple-element.81.table, bf16[512,768]{1,0:T(8,128)(2,1)} %get-tuple-element.83.refs_0_, bf16[512,768]{1,0:T(8,128)(2,1)} %get-tuple-element.84.refs_1_, ...), custom_call_target="tpu_custom_call" | custom-call | flops 18874368 | bytes 65536 | tf_op jit(solution)/shard_map/attend_forward/pallas_call | solution.py:230
  104.5 2.0 held.4
  107.8 2.0 held.5
  109.9 1.8 collective-permute-start.20
  111.7 8.8 %attend_forward.2 = (bf16[512,256]{1,0:T(8,128)(2,1)}, bf16[512,256]{1,0:T(8,128)(2,1)}, f32[512,128]{1,0:T(8,128)}, f32[512,128]{1,0:T(8,128)}) custom-call(s32[32,8]{1,0:T(8,128)} %get-tuple-element.81.table, bf16[512,768]{1,0:T(8,128)(2,1)} %get-tuple-element.83.refs_0_, bf16[512,768]{1,0:T(8,128)(2,1)} %get-tuple-element.84.refs_1_, ...), custom_call_target="tpu_custom_call" | custom-call | flops 18874368 | bytes 65536 | tf_op jit(solution)/shard_map/attend_forward/pallas_call | solution.py:230
  122.7 7.2 %collective-permute-done.11.refs_2_ = bf16[512,256]{1,0:T(8,128)(2,1)S(1)} collective-permute-done((bf16[512,256]{1,0:T(8,128)(2,1)}, bf16[512,256]{1,0:T(8,128)(2,1)S(1)}, u32[]{:S(2)}, u32[]{:S(2)}) %collective-permute-start.11) | collective-permute-done | bytes 262176 | tf_op jit(solution)/shard_map/ppermute | solution.py:31
  130.0 3.7 %collective-permute-done.12.refs_3_ = bf16[512,256]{1,0:T(8,128)(2,1)S(1)} collective-permute-done((bf16[512,256]{1,0:T(8,128)(2,1)}, bf16[512,256]{1,0:T(8,128)(2,1)S(1)}, u32[]{:S(2)}, u32[]{:S(2)}) %collective-permute-start.12) | collective-permute-done | bytes 262176 | tf_op jit(solution)/shard_map/ppermute | solution.py:31
  139.5 32.4 %layer_rows.1 = (bf16[512,768]{1,0:T(8,128)(2,1)}, bf16[2,4,96,512]{3,2,1,0:T(8,128)(2,1)}, bf16[2,4,96,512]{3,2,1,0:T(8,128)(2,1)}, bf16[2,512,768]{2,1,0:T(8,1...) custom-call(s32[1]{0:T(128)S(6)} %copy.40.length_ref.length, ...), custom_call_target="tpu_custom_call" | custom-call | flops 176160768 | bytes 393216 | tf_op jit(solution)/shard_map/layer_rows/pallas_call | solution.py:645
  173.4 7.1 %collective-permute-done.36 = bf16[512,256]{1,0:T(8,128)(2,1)S(1)} collective-permute-done((bf16[512,256]{1,0:T(8,128)(2,1)}, bf16[512,256]{1,0:T(8,128)(2,1)S(1)}, u32[]{:S(2)}, u32[]{:S(2)}) %collective-permute-start.36) | collective-permute-done | bytes 262176 | tf_op jit(solution)/shard_map/ppermute | solution.py:31
  180.9 1.8 pad_maximum_fusion.refs_6_
  186.0 8.1 %row_dot.3 = (bf16[2,1,4,96,1024]{4,3,2,1,0:T(8,128)(2,1)}, bf16[2,1,4,96,1024]{4,3,2,1,0:T(8,128)(2,1)}) custom-call(bf16[2,4,96,512]{3,2,1,0:T(8,128)(2,1)} %get-tuple-element.101.refs_0_, bf16[2,4,96,512]{3,2,1,0:T(8,128)(2,1)} %copy-done.20, bf16[2,4,96,512]{3,2,1,0:T(8,128)(2,1)} %get-tuple-element.102.refs_2_, bf16[2,4,96,512]{3,2,1,0:T(8,128)(2,1)} %copy-done.21, ...), custom_call_target="tpu_custom_call" | custom-call | flops 50331648 | bytes 131072 | tf_op jit(solution)/shard_map/row_dot/pallas_call | solution.py:748
  197.9 2.1 collective-permute-done.38
  200.9 5.9 %collective-permute-done.29.refs_5_.refs_4_ = bf16[512,256]{1,0:T(8,128)(2,1)S(1)} collective-permute-done((bf16[512,256]{1,0:T(8,128)(2,1)}, bf16[512,256]{1,0:T(8,128)(2,1)S(1)}, u32[]{:S(2)}, u32[]{:S(2)}) %collective-permute-start.29) | collective-permute-done | bytes 262176 | tf_op jit(solution)/shard_map/ppermute | solution.py:31
  206.8 3.2 collective-permute-done.30.refs_6_.refs_5_
  211.9 6.1 %row_dot.4 = (bf16[1,2,4,96,768]{4,3,2,1,0:T(8,128)(2,1)}, bf16[1,2,4,96,768]{4,3,2,1,0:T(8,128)(2,1)}) custom-call(bf16[2,4,96,512]{3,2,1,0:T(8,128)(2,1)} %get-tuple-element.98.refs_0_, bf16[2,4,96,512]{3,2,1,0:T(8,128)(2,1)} %collective-permute-done.31.refs_1_, bf16[2,512,768]{2,1,0:T(8,128)(2,1)} %get-tuple-element.99.refs_2_, ...), custom_call_target="tpu_custom_call" | custom-call | flops 37748736 | bytes 131072 | tf_op jit(solution)/shard_map/row_dot/pallas_call | solution.py:748
  222.2 16.0 %attend_backward.2 = (bf16[512,256]{1,0:T(8,128)(2,1)}, bf16[512,256]{1,0:T(8,128)(2,1)}, f32[2048,256]{1,0:T(8,128)}, f32[2048,256]{1,0:T(8,128)}) custom-call(s32[32,8]{1,0:T(8,128)} %get-tuple-element.81.table, bf16[512,768]{1,0:T(8,128)(2,1)} %get-tuple-element.83.refs_0_, bf16[512,768]{1,0:T(8,128)(2,1)} %get-tuple-element.84.refs_1_, ...), custom_call_target="tpu_custom_call" | custom-call | flops 47185920 | bytes 196608 | tf_op jit(solution)/shard_map/attend_backward/pallas_call | solution.py:366
  239.3 3.2 plus.3
  243.4 3.3 collective-permute-done.39
  247.7 2.8 plus.2
  252.0 16.9 %attend_backward.3 = (bf16[512,768]{1,0:T(8,128)(2,1)}, bf16[512,768]{1,0:T(8,128)(2,1)}, bf16[512,768]{1,0:T(8,128)(2,1)}, bf16[512,768]{1,0:T(8,128)(2,1)}, bf16[16,768]{1,0:T(8,128)(2,1)}) custom-call(s32[32,8]{1,0:T(8,128)} %get-tuple-element.81.table, bf16[512,768]{1,0:T(8,128)(2,1)} %get-tuple-element.83.refs_0_, ...), custom_call_target="tpu_custom_call" | custom-call | flops 47185920 | bytes 196608 | tf_op jit(solution)/shard_map/attend_backward/pallas_call | solution.py:366
  270.1 2.9 joined_sums.2
  273.0 4.3 %spread.2.refs_9_ = bf16[2,512,768]{2,1,0:T(8,128)(2,1)} custom-call(bf16[512,768]{1,0:T(8,128)(2,1)} %get-tuple-element.123.first, bf16[512,768]{1,0:T(8,128)(2,1)} %get-tuple-element.124.second, bf16[768,768]{1,0:T(8,128)(2,1)} %get-tuple-element.122.w, bf16[96,1792]{1,0:T(8,128)(2,1)} %get-tuple-element.127.refs_0_), custom_call_target="tpu_custom_call" | custom-call | flops 18874368 | bytes 81920 | tf_op jit(solution)/shard_map/spread/pallas_call | solution.py:841
  282.2 6.6 %row_dot.5 = (bf16[1,1,4,112,768]{4,3,2,1,0:T(8,128)(2,1)}, bf16[1,1,4,112,768]{4,3,2,1,0:T(8,128)(2,1)}) custom-call(bf16[2,4,96,512]{3,2,1,0:T(8,128)(2,1)} %get-tuple-element.129.refs_0_, bf16[2,4,96,512]{3,2,1,0:T(8,128)(2,1)} %get-tuple-element.130.refs_1_, bf16[2,4,96,512]{3,2,1,0:T(8,128)(2,1)} %get-tuple-element.131.refs_2_, ...), custom_call_target="tpu_custom_call" | custom-call | flops 37748736 | bytes 131072 | tf_op jit(solution)/shard_map/row_dot/pallas_call | solution.py:748
  289.3 5.5 %collective-permute-done.50 = bf16[96,1792]{1,0:T(8,128)(2,1)S(1)} collective-permute-done((bf16[96,1792]{1,0:T(8,128)(2,1)}, bf16[96,1792]{1,0:T(8,128)(2,1)S(1)}, u32[]{:S(2)}, u32[]{:S(2)}) %collective-permute-start.50) | collective-permute-done | bytes 344096 | tf_op jit(solution)/shard_map/ppermute | solution.py:36
  294.8 11.4 %collective-permute-done.51 = bf16[96,1792]{1,0:T(8,128)(2,1)S(1)} collective-permute-done((bf16[96,1792]{1,0:T(8,128)(2,1)}, bf16[96,1792]{1,0:T(8,128)(2,1)S(1)}, u32[]{:S(2)}, u32[]{:S(2)}) %collective-permute-start.51) | collective-permute-done | bytes 344096 | tf_op jit(solution)/shard_map/ppermute | solution.py:36
  310.2 5.1 %spread.3 = (bf16[512,768]{1,0:T(8,128)(2,1)}, f32[512,768]{1,0:T(8,128)}) custom-call(bf16[512,768]{1,0:T(8,128)(2,1)} %get-tuple-element.120.first, bf16[512,768]{1,0:T(8,128)(2,1)} %get-tuple-element.121.refs_4_.second, bf16[768,768]{1,0:T(8,128)(2,1)} %get-tuple-element.122.w, bf16[2,512,768]{2,1,0:T(8,128)(2,1)} %copy-done.10, ...), custom_call_target="tpu_custom_call" | custom-call | flops 18874368 | bytes 81920 | tf_op jit(solution)/shard_map/spread/pallas_call | solution.py:841
  316.1 2.3 joined_sums.3
  318.5 6.1 %collective-permute-start.47 = (bf16[112,768]{1,0:T(8,128)(2,1)}, bf16[112,768]{1,0:T(8,128)(2,1)S(1)}, u32[]{:S(2)}, u32[]{:S(2)}) collective-permute-start(bf16[112,768]{1,0:T(8,128)(2,1)} %get-tuple-element.139), channel_id=1, source_target_pairs={{0,8},{4,12},{8,0},{12,4},{16,24},{20,28},{24,16},{28,20},{1,9},{5... | collective-permute-start | bytes 516104 | tf_op jit(solution)/shard_map/ppermute | solution.py:36
  330.3 9.6 %collective-permute-done.48 = bf16[112,768]{1,0:T(8,128)(2,1)S(1)} collective-permute-done((bf16[112,768]{1,0:T(8,128)(2,1)}, bf16[112,768]{1,0:T(8,128)(2,1)S(1)}, u32[]{:S(2)}, u32[]{:S(2)}) %collective-permute-start.48) | collective-permute-done | bytes 172064 | tf_op jit(solution)/shard_map/ppermute | solution.py:36
  342.8 3.6 %collective-permute-done.45 = bf16[512,768]{1,0:T(8,128)(2,1)S(1)} collective-permute-done((bf16[512,768]{1,0:T(8,128)(2,1)S(1)}, bf16[512,768]{1,0:T(8,128)(2,1)S(1)}, u32[]{:S(2)}, u32[]{:S(2)}) %collective-permute-start.45) | collective-permute-done | bytes 786464 | tf_op jit(solution)/shard_map/ppermute | solution.py:31
  (212 shorter events, 67.2 us)
Async XLA Ops:
  4.4 12.0 %collective-permute-start.13 = (bf16[96,1792]{1,0:T(8,128)(2,1)}, bf16[96,1792]{1,0:T(8,128)(2,1)S(1)}, u32[]{:S(2)}, u32[]{:S(2)}) collective-permute-start(bf16[96,1792]{1,0:T(8,128)(2,1)} %get-tuple-element.92.a), channel_id=1, source_target_pairs={{0,2},{1,3},{2,0},{3,1},{4,6},{5,7},{6,4},{7,5},{8,10},{9,11},{10,... | collective-permute-start | bytes 1032200 | tf_op jit(solution)/shard_map/ppermute | solution.py:31
  7.4 25.1 %collective-permute-start.1 = (bf16[512,768]{1,0:T(8,128)(2,1)}, bf16[512,768]{1,0:T(8,128)(2,1)S(1)}, u32[]{:S(2)}, u32[]{:S(2)}) collective-permute-start(bf16[512,768]{1,0:T(8,128)(2,1)} %refs_4_.1), channel_id=1, source_target_pairs={{0,2},{1,3},{2,0},{3,1},{4,6},{5,7},{6,4},{7,5},{8,10},{9,11},{10,... | collective-permute-start | bytes 2359304 | tf_op jit(solution)/shard_map/ppermute | solution.py:31
  19.2 21.2 %collective-permute-start.14 = (bf16[96,3584]{1,0:T(8,128)(2,1)}, bf16[96,3584]{1,0:T(8,128)(2,1)}, u32[]{:S(2)}, u32[]{:S(2)}) collective-permute-start(bf16[96,3584]{1,0:T(8,128)(2,1)} %pair_weights.1.refs_6_), channel_id=1, source_target_pairs={{0,8},{8,16},{16,24},{24,28},{28,20},{20,12},{12,4},{4,0},{1,9},{9... | collective-permute-start | bytes 2064392 | tf_op jit(solution)/shard_map/ppermute | solution.py:54
  21.3 17.0 %collective-permute-start.3 = (bf16[96,768]{1,0:T(8,128)(2,1)}, bf16[96,768]{1,0:T(8,128)(2,1)S(1)}, u32[]{:S(2)}, u32[]{:S(2)}) collective-permute-start(bf16[96,768]{1,0:T(8,128)(2,1)} %get-tuple-element.82.refs_4_), channel_id=1, source_target_pairs={{0,8},{8,16},{16,24},{24,28},{28,20},{20,12},{12,4},{4,0},{1,9},{9... | collective-permute-start | bytes 442376 | tf_op jit(solution)/shard_map/ppermute | solution.py:54
  22.9 17.3 %collective-permute-start.4 = (bf16[96,768]{1,0:T(8,128)(2,1)}, bf16[96,768]{1,0:T(8,128)(2,1)S(1)}, u32[]{:S(2)}, u32[]{:S(2)}) collective-permute-start(bf16[96,768]{1,0:T(8,128)(2,1)} %get-tuple-element.82.refs_4_), channel_id=1, source_target_pairs={{0,4},{8,0},{16,8},{24,16},{28,24},{20,28},{12,20},{4,12},{1,5},{9... | collective-permute-start | bytes 442376 | tf_op jit(solution)/shard_map/ppermute | solution.py:54
  23.4 50.4 %collective-permute-start = (bf16[512,768]{1,0:T(8,128)(2,1)S(1)}, bf16[512,768]{1,0:T(8,128)(2,1)S(1)}, u32[]{:S(2)}, u32[]{:S(2)}) collective-permute-start(bf16[512,768]{1,0:T(8,128)(2,1)S(1)} %copy-done), channel_id=1, source_target_pairs={{0,1},{1,0},{2,3},{3,2},{4,5},{5,4},{6,7},{7,6},{8,9},{9,8},{10,11... | collective-permute-start | bytes 2359304 | tf_op jit(solution)/shard_map/ppermute | solution.py:31
  32.5 42.8 %collective-permute-start.2 = (bf16[512,768]{1,0:T(8,128)(2,1)S(1)}, bf16[512,768]{1,0:T(8,128)(2,1)}, u32[]{:S(2)}, u32[]{:S(2)}) collective-permute-start(bf16[512,768]{1,0:T(8,128)(2,1)S(1)} %collective-permute-done.1.refs_2_), channel_id=1, source_target_pairs={{0,1},{1,0},{2,3},{3,2},{4,5},{5,4},{6,7},{7,6},{8,9},{9,8},{10,11... | collective-permute-start | bytes 2359304 | tf_op jit(solution)/shard_map/ppermute | solution.py:31
  38.3 6.8 %collective-permute-start.5 = (bf16[96,768]{1,0:T(8,128)(2,1)S(1)}, bf16[96,768]{1,0:T(8,128)(2,1)S(1)}, u32[]{:S(2)}, u32[]{:S(2)}) collective-permute-start(bf16[96,768]{1,0:T(8,128)(2,1)S(1)} %collective-permute-done.3.refs_5_), channel_id=1, source_target_pairs={{0,8},{8,16},{16,24},{24,28},{28,20},{20,12},{12,4},{4,0},{1,9},{9... | collective-permute-start | bytes 442376 | tf_op jit(solution)/shard_map/ppermute | solution.py:54
  40.2 30.6 %collective-permute-start.15 = (bf16[96,3584]{1,0:T(8,128)(2,1)}, bf16[96,3584]{1,0:T(8,128)(2,1)}, u32[]{:S(2)}, u32[]{:S(2)}) collective-permute-start(bf16[96,3584]{1,0:T(8,128)(2,1)} %pair_weights.1.refs_6_), channel_id=1, source_target_pairs={{0,4},{8,0},{16,8},{24,16},{28,24},{20,28},{12,20},{4,12},{1,5},{9... | collective-permute-start | bytes 2064392 | tf_op jit(solution)/shard_map/ppermute | solution.py:54
  40.4 43.3 %collective-permute-start.16 = (bf16[96,3584]{1,0:T(8,128)(2,1)}, bf16[96,3584]{1,0:T(8,128)(2,1)S(1)}, u32[]{:S(2)}, u32[]{:S(2)}) collective-permute-start(bf16[96,3584]{1,0:T(8,128)(2,1)} %collective-permute-done.14.refs_7_), channel_id=1, source_target_pairs={{0,8},{8,16},{16,24},{24,28},{28,20},{20,12},{12,4},{4,0},{1,9},{9... | collective-permute-start | bytes 2064392 | tf_op jit(solution)/shard_map/ppermute | solution.py:54
  45.1 12.2 %collective-permute-start.6 = (bf16[96,768]{1,0:T(8,128)(2,1)S(1)}, bf16[96,768]{1,0:T(8,128)(2,1)S(1)}, u32[]{:S(2)}, u32[]{:S(2)}) collective-permute-start(bf16[96,768]{1,0:T(8,128)(2,1)S(1)} %collective-permute-done.4.refs_6_), channel_id=1, source_target_pairs={{0,4},{8,0},{16,8},{24,16},{28,24},{20,28},{12,20},{4,12},{1,5},{9... | collective-permute-start | bytes 442376 | tf_op jit(solution)/shard_map/ppermute | solution.py:54
  57.3 5.1 %collective-permute-start.7 = (bf16[96,768]{1,0:T(8,128)(2,1)S(1)}, bf16[96,768]{1,0:T(8,128)(2,1)S(1)}, u32[]{:S(2)}, u32[]{:S(2)}) collective-permute-start(bf16[96,768]{1,0:T(8,128)(2,1)S(1)} %collective-permute-done.5.refs_7_), channel_id=1, source_target_pairs={{0,8},{8,16},{16,24},{24,28},{28,20},{20,12},{12,4},{4,0},{1,9},{9... | collective-permute-start | bytes 442376 | tf_op jit(solution)/shard_map/ppermute | solution.py:54
  62.4 6.1 %collective-permute-start.8 = (bf16[96,768]{1,0:T(8,128)(2,1)S(1)}, bf16[96,768]{1,0:T(8,128)(2,1)S(1)}, u32[]{:S(2)}, u32[]{:S(2)}) collective-permute-start(bf16[96,768]{1,0:T(8,128)(2,1)S(1)} %collective-permute-done.6.refs_8_), channel_id=1, source_target_pairs={{0,4},{8,0},{16,8},{24,16},{28,24},{20,28},{12,20},{4,12},{1,5},{9... | collective-permute-start | bytes 442376 | tf_op jit(solution)/shard_map/ppermute | solution.py:54
  68.6 5.1 %collective-permute-start.9 = (bf16[96,768]{1,0:T(8,128)(2,1)S(1)}, bf16[96,768]{1,0:T(8,128)(2,1)S(1)}, u32[]{:S(2)}, u32[]{:S(2)}) collective-permute-start(bf16[96,768]{1,0:T(8,128)(2,1)S(1)} %collective-permute-done.7.refs_9_), channel_id=1, source_target_pairs={{0,8},{8,16},{16,24},{24,28},{28,20},{20,12},{12,4},{4,0},{1,9},{9... | collective-permute-start | bytes 442376 | tf_op jit(solution)/shard_map/ppermute | solution.py:54
  70.8 32.8 %collective-permute-start.17 = (bf16[96,3584]{1,0:T(8,128)(2,1)}, bf16[96,3584]{1,0:T(8,128)(2,1)S(1)}, u32[]{:S(2)}, u32[]{:S(2)}) collective-permute-start(bf16[96,3584]{1,0:T(8,128)(2,1)} %collective-permute-done.15.refs_8_), channel_id=1, source_target_pairs={{0,4},{8,0},{16,8},{24,16},{28,24},{20,28},{12,20},{4,12},{1,5},{9... | collective-permute-start | bytes 2064392 | tf_op jit(solution)/shard_map/ppermute | solution.py:54
  86.6 20.4 %collective-permute-start.18 = (bf16[96,3584]{1,0:T(8,128)(2,1)}, bf16[96,3584]{1,0:T(8,128)(2,1)S(1)}, u32[]{:S(2)}, u32[]{:S(2)}) collective-permute-start(bf16[96,3584]{1,0:T(8,128)(2,1)} %held.3), channel_id=1, source_target_pairs={{0,8},{8,16},{16,24},{24,28},{28,20},{20,12},{12,4},{4,0},{1,9},{9... | collective-permute-start | bytes 2064392 | tf_op jit(solution)/shard_map/ppermute | solution.py:54
  88.1 32.4 %collective-permute-start.21 = (bf16[96,3584]{1,0:T(8,128)(2,1)S(1)}, bf16[96,3584]{1,0:T(8,128)(2,1)}, u32[]{:S(2)}, u32[]{:S(2)}) collective-permute-start(bf16[96,3584]{1,0:T(8,128)(2,1)S(1)} %copy-done.3), channel_id=1, source_target_pairs={{0,1},{1,0},{2,3},{3,2},{4,5},{5,4},{6,7},{7,6},{8,9},{9,8},{10,11... | collective-permute-start | bytes 2064392 | tf_op jit(solution)/shard_map/ppermute | solution.py:31
  88.1 33.9 %collective-permute-start.22 = (bf16[96,3584]{1,0:T(8,128)(2,1)}, bf16[96,3584]{1,0:T(8,128)(2,1)}, u32[]{:S(2)}, u32[]{:S(2)}) collective-permute-start(bf16[96,3584]{1,0:T(8,128)(2,1)} %collective-permute-done.14.refs_7_), channel_id=1, source_target_pairs={{0,1},{1,0},{2,3},{3,2},{4,5},{5,4},{6,7},{7,6},{8,9},{9,8},{10,11... | collective-permute-start | bytes 2064392 | tf_op jit(solution)/shard_map/ppermute | solution.py:31
  88.7 33.4 %collective-permute-start.23 = (bf16[96,3584]{1,0:T(8,128)(2,1)}, bf16[96,3584]{1,0:T(8,128)(2,1)}, u32[]{:S(2)}, u32[]{:S(2)}) collective-permute-start(bf16[96,3584]{1,0:T(8,128)(2,1)} %collective-permute-done.15.refs_8_), channel_id=1, source_target_pairs={{0,1},{1,0},{2,3},{3,2},{4,5},{5,4},{6,7},{7,6},{8,9},{9,8},{10,11... | collective-permute-start | bytes 2064392 | tf_op jit(solution)/shard_map/ppermute | solution.py:31
  106.5 28.6 %collective-permute-start.19 = (bf16[96,3584]{1,0:T(8,128)(2,1)}, bf16[96,3584]{1,0:T(8,128)(2,1)}, u32[]{:S(2)}, u32[]{:S(2)}) collective-permute-start(bf16[96,3584]{1,0:T(8,128)(2,1)} %held.4), channel_id=1, source_target_pairs={{0,4},{8,0},{16,8},{24,16},{28,24},{20,28},{12,20},{4,12},{1,5},{9... | collective-permute-start | bytes 2064392 | tf_op jit(solution)/shard_map/ppermute | solution.py:54
  109.9 25.3 %collective-permute-start.20 = (bf16[96,3584]{1,0:T(8,128)(2,1)}, bf16[96,3584]{1,0:T(8,128)(2,1)}, u32[]{:S(2)}, u32[]{:S(2)}) collective-permute-start(bf16[96,3584]{1,0:T(8,128)(2,1)} %held.5), channel_id=1, source_target_pairs={{0,8},{8,16},{16,24},{24,28},{28,20},{20,12},{12,4},{4,0},{1,9},{9... | collective-permute-start | bytes 2064392 | tf_op jit(solution)/shard_map/ppermute | solution.py:54
  120.5 9.5 %collective-permute-start.11 = (bf16[512,256]{1,0:T(8,128)(2,1)}, bf16[512,256]{1,0:T(8,128)(2,1)S(1)}, u32[]{:S(2)}, u32[]{:S(2)}) collective-permute-start(bf16[512,256]{1,0:T(8,128)(2,1)} %get-tuple-element.90.refs_0_), channel_id=1, source_target_pairs={{0,2},{1,3},{2,0},{3,1},{4,6},{5,7},{6,4},{7,5},{8,10},{9,11},{10,... | collective-permute-start | bytes 786440 | tf_op jit(solution)/shard_map/ppermute | solution.py:31
  122.1 11.6 %collective-permute-start.12 = (bf16[512,256]{1,0:T(8,128)(2,1)}, bf16[512,256]{1,0:T(8,128)(2,1)S(1)}, u32[]{:S(2)}, u32[]{:S(2)}) collective-permute-start(bf16[512,256]{1,0:T(8,128)(2,1)} %get-tuple-element.91), channel_id=1, source_target_pairs={{0,3},{1,2},{2,1},{3,0},{4,7},{5,6},{6,5},{7,4},{8,11},{9,10},{10,... | collective-permute-start | bytes 786440 | tf_op jit(solution)/shard_map/ppermute | solution.py:31
  122.1 12.3 %collective-permute-start.10 = (bf16[512,256]{1,0:T(8,128)(2,1)}, bf16[512,256]{1,0:T(8,128)(2,1)S(1)}, u32[]{:S(2)}, u32[]{:S(2)}) collective-permute-start(bf16[512,256]{1,0:T(8,128)(2,1)} %get-tuple-element.89), channel_id=1, source_target_pairs={{0,1},{1,0},{2,3},{3,2},{4,5},{5,4},{6,7},{7,6},{8,9},{9,8},{10,11... | collective-permute-start | bytes 786440 | tf_op jit(solution)/shard_map/ppermute | solution.py:31
  130.0 7.0 %collective-permute-start.24 = (bf16[96,3584]{1,0:T(8,128)(2,1)S(1)}, bf16[96,3584]{1,0:T(8,128)(2,1)S(1)}, u32[]{:S(2)}, u32[]{:S(2)}) collective-permute-start(bf16[96,3584]{1,0:T(8,128)(2,1)S(1)} %copy-done.5), channel_id=1, source_target_pairs={{0,1},{1,0},{2,3},{3,2},{4,5},{5,4},{6,7},{7,6},{8,9},{9,8},{10,11... | collective-permute-start | bytes 2064392 | tf_op jit(solution)/shard_map/ppermute | solution.py:31
  135.2 4.3 %collective-permute-start.28 = (bf16[96,3584]{1,0:T(8,128)(2,1)}, bf16[96,3584]{1,0:T(8,128)(2,1)}, u32[]{:S(2)}, u32[]{:S(2)}) collective-permute-start(bf16[96,3584]{1,0:T(8,128)(2,1)} %collective-permute-done.20.refs_13_), channel_id=1, source_target_pairs={{0,1},{1,0},{2,3},{3,2},{4,5},{5,4},{6,7},{7,6},{8,9},{9,8},{10,11... | collective-permute-start | bytes 2064392 | tf_op jit(solution)/shard_map/ppermute | solution.py:31
  171.9 11.7 %collective-permute-start.35 = (bf16[2,512,768]{2,1,0:T(8,128)(2,1)}, bf16[2,512,768]{2,1,0:T(8,128)(2,1)S(1)}, u32[]{:S(2)}, u32[]{:S(2)}) collective-permute-start(bf16[2,512,768]{2,1,0:T(8,128)(2,1)} %get-tuple-element.104), channel_id=1, source_target_pairs={{0,1},{1,0},{2,3},{3,2},{4,5},{5,4},{6,7},{7,6},{8,9},{9,8},{10,11... | collective-permute-start | bytes 4718600 | tf_op jit(solution)/shard_map/ppermute | solution.py:31
  172.4 37.6 %collective-permute-start.32 = (bf16[2,512,768]{2,1,0:T(8,128)(2,1)}, bf16[2,512,768]{2,1,0:T(8,128)(2,1)S(1)}, u32[]{:S(2)}, u32[]{:S(2)}) collective-permute-start(bf16[2,512,768]{2,1,0:T(8,128)(2,1)} %get-tuple-element.100), channel_id=1, source_target_pairs={{0,1},{1,0},{2,3},{3,2},{4,5},{5,4},{6,7},{7,6},{8,9},{9,8},{10,11... | collective-permute-start | bytes 4718600 | tf_op jit(solution)/shard_map/ppermute | solution.py:31
  172.5 11.1 %collective-permute-start.33 = (bf16[2,4,96,512]{3,2,1,0:T(8,128)(2,1)}, bf16[2,4,96,512]{3,2,1,0:T(8,128)(2,1)S(1)}, u32[]{:S(2)}, u32[]{:S(2)}) collective-permute-start(bf16[2,4,96,512]{3,2,1,0:T(8,128)(2,1)} %get-tuple-element.101.refs_0_), channel_id=1, source_target_pairs={{0,1},{1,0},{2,3},{3,2},{4,5},{5,4},{6,7},{7,6},{8,9},{9,8},{10,11... | collective-permute-start | bytes 2359304 | tf_op jit(solution)/shard_map/ppermute | solution.py:31
  172.9 10.7 %collective-permute-start.34 = (bf16[2,4,96,512]{3,2,1,0:T(8,128)(2,1)}, bf16[2,4,96,512]{3,2,1,0:T(8,128)(2,1)S(1)}, u32[]{:S(2)}, u32[]{:S(2)}) collective-permute-start(bf16[2,4,96,512]{3,2,1,0:T(8,128)(2,1)} %get-tuple-element.102.refs_2_), channel_id=1, source_target_pairs={{0,1},{1,0},{2,3},{3,2},{4,5},{5,4},{6,7},{7,6},{8,9},{9,8},{10,11... | collective-permute-start | bytes 2359304 | tf_op jit(solution)/shard_map/ppermute | solution.py:31
  173.0 7.5 %collective-permute-start.36 = (bf16[512,256]{1,0:T(8,128)(2,1)}, bf16[512,256]{1,0:T(8,128)(2,1)S(1)}, u32[]{:S(2)}, u32[]{:S(2)}) collective-permute-start(bf16[512,256]{1,0:T(8,128)(2,1)} %copy-done.31), channel_id=1, source_target_pairs={{0,1},{1,0},{2,3},{3,2},{4,5},{5,4},{6,7},{7,6},{8,9},{9,8},{10,11... | collective-permute-start | bytes 786440 | tf_op jit(solution)/shard_map/ppermute | solution.py:31
  180.5 29.5 %collective-permute-start.31 = (bf16[2,4,96,512]{3,2,1,0:T(8,128)(2,1)}, bf16[2,4,96,512]{3,2,1,0:T(8,128)(2,1)}, u32[]{:S(2)}, u32[]{:S(2)}) collective-permute-start(bf16[2,4,96,512]{3,2,1,0:T(8,128)(2,1)} %get-tuple-element.98.refs_0_), channel_id=1, source_target_pairs={{0,1},{1,0},{2,3},{3,2},{4,5},{5,4},{6,7},{7,6},{8,9},{9,8},{10,11... | collective-permute-start | bytes 2359304 | tf_op jit(solution)/shard_map/ppermute | solution.py:31
  194.1 44.1 %collective-permute-start.41 = (bf16[2,1,4,96,1024]{4,3,2,1,0:T(8,128)(2,1)}, bf16[2,1,4,96,1024]{4,3,2,1,0:T(8,128)(2,1)S(1)}, u32[]{:S(2)}, u32[]{:S(2)}) collective-permute-start(bf16[2,1,4,96,1024]{4,3,2,1,0:T(8,128)(2,1)} %get-tuple-element.105.refs_4_), channel_id=1, source_target_pairs={{0,4},{4,0},{8,12},{12,8},{16,20},{20,16},{24,28},{28,24},{1,5},{5... | collective-permute-start | bytes 4718600 | tf_op jit(solution)/shard_map/ppermute | solution.py:36
  195.8 4.1 %collective-permute-start.38 = (f32[16,768]{1,0:T(8,128)S(1)}, f32[16,768]{1,0:T(8,128)S(1)}, u32[]{:S(2)}, u32[]{:S(2)}) collective-permute-start(f32[16,768]{1,0:T(8,128)S(1)} %add.35), channel_id=1, source_target_pairs={{0,2},{1,3},{2,0},{3,1},{4,6},{5,7},{6,4},{7,5},{8,10},{9,11},{10,... | collective-permute-start | bytes 147464 | tf_op jit(solution)/shard_map/ppermute | solution.py:31
  197.4 9.4 %collective-permute-start.29 = (bf16[512,256]{1,0:T(8,128)(2,1)}, bf16[512,256]{1,0:T(8,128)(2,1)S(1)}, u32[]{:S(2)}, u32[]{:S(2)}) collective-permute-start(bf16[512,256]{1,0:T(8,128)(2,1)} %get-tuple-element.94), channel_id=1, source_target_pairs={{0,2},{1,3},{2,0},{3,1},{4,6},{5,7},{6,4},{7,5},{8,10},{9,11},{10,... | collective-permute-start | bytes 786440 | tf_op jit(solution)/shard_map/ppermute | solution.py:31
  199.9 10.1 %collective-permute-start.30 = (bf16[512,256]{1,0:T(8,128)(2,1)}, bf16[512,256]{1,0:T(8,128)(2,1)S(1)}, u32[]{:S(2)}, u32[]{:S(2)}) collective-permute-start(bf16[512,256]{1,0:T(8,128)(2,1)} %get-tuple-element.95), channel_id=1, source_target_pairs={{0,3},{1,2},{2,1},{3,0},{4,7},{5,6},{6,5},{7,4},{8,11},{9,10},{10,... | collective-permute-start | bytes 786440 | tf_op jit(solution)/shard_map/ppermute | solution.py:31
  218.0 28.7 %collective-permute-start.39 = (bf16[1,2,4,96,768]{4,3,2,1,0:T(8,128)(2,1)}, bf16[1,2,4,96,768]{4,3,2,1,0:T(8,128)(2,1)S(1)}, u32[]{:S(2)}, u32[]{:S(2)}) collective-permute-start(bf16[1,2,4,96,768]{4,3,2,1,0:T(8,128)(2,1)} %get-tuple-element.108.refs_9_), channel_id=1, source_target_pairs={{0,2},{1,3},{2,0},{3,1},{4,6},{5,7},{6,4},{7,5},{8,10},{9,11},{10,... | collective-permute-start | bytes 3538952 | tf_op jit(solution)/shard_map/ppermute | solution.py:31
  242.5 26.5 %collective-permute-start.43 = (bf16[1,1,4,96,1024]{4,3,2,1,0:T(8,128)(2,1)}, bf16[1,1,4,96,1024]{4,3,2,1,0:T(8,128)(2,1)S(1)}, u32[]{:S(2)}, u32[]{:S(2)}) collective-permute-start(bf16[1,1,4,96,1024]{4,3,2,1,0:T(8,128)(2,1)} %get-tuple-element.116.refs_10_), channel_id=1, source_target_pairs={{0,2},{1,3},{2,0},{3,1},{4,6},{5,7},{6,4},{7,5},{8,10},{9,11},{10,... | collective-permute-start | bytes 2359304 | tf_op jit(solution)/shard_map/ppermute | solution.py:31
  250.5 18.5 %collective-permute-start.42 = (bf16[1,4,96,768]{3,2,1,0:T(8,128)(2,1)}, bf16[1,4,96,768]{3,2,1,0:T(8,128)(2,1)S(1)}, u32[]{:S(2)}, u32[]{:S(2)}) collective-permute-start(bf16[1,4,96,768]{3,2,1,0:T(8,128)(2,1)} %get-tuple-element.114.refs_9_), channel_id=1, source_target_pairs={{0,4},{4,0},{8,12},{12,8},{16,20},{20,16},{24,28},{28,24},{1,5},{5... | collective-permute-start | bytes 1769480 | tf_op jit(solution)/shard_map/ppermute | solution.py:36
  277.3 31.8 %collective-permute-start.44 = (bf16[2,512,768]{2,1,0:T(8,128)(2,1)}, bf16[2,512,768]{2,1,0:T(8,128)(2,1)S(1)}, u32[]{:S(2)}, u32[]{:S(2)}) collective-permute-start(bf16[2,512,768]{2,1,0:T(8,128)(2,1)} %spread.2.refs_9_), channel_id=1, source_target_pairs={{0,1},{1,0},{2,3},{3,2},{4,5},{5,4},{6,7},{7,6},{8,9},{9,8},{10,11... | collective-permute-start | bytes 4718600 | tf_op jit(solution)/shard_map/ppermute | solution.py:31
  277.8 17.0 %collective-permute-start.50 = (bf16[96,1792]{1,0:T(8,128)(2,1)}, bf16[96,1792]{1,0:T(8,128)(2,1)S(1)}, u32[]{:S(2)}, u32[]{:S(2)}) collective-permute-start(bf16[96,1792]{1,0:T(8,128)(2,1)} %get-tuple-element.142), channel_id=1, source_target_pairs={{0,8},{4,12},{8,0},{12,4},{16,24},{20,28},{24,16},{28,20},{1,9},{5... | collective-permute-start | bytes 1032200 | tf_op jit(solution)/shard_map/ppermute | solution.py:36
  279.4 26.8 %collective-permute-start.51 = (bf16[96,1792]{1,0:T(8,128)(2,1)}, bf16[96,1792]{1,0:T(8,128)(2,1)S(1)}, u32[]{:S(2)}, u32[]{:S(2)}) collective-permute-start(bf16[96,1792]{1,0:T(8,128)(2,1)} %get-tuple-element.143), channel_id=1, source_target_pairs={{0,16},{4,20},{8,24},{12,28},{16,0},{20,4},{24,8},{28,12},{1,17},{... | collective-permute-start | bytes 1032200 | tf_op jit(solution)/shard_map/ppermute | solution.py:36
  281.2 25.8 %collective-permute-start.52 = (bf16[96,1792]{1,0:T(8,128)(2,1)}, bf16[96,1792]{1,0:T(8,128)(2,1)}, u32[]{:S(2)}, u32[]{:S(2)}) collective-permute-start(bf16[96,1792]{1,0:T(8,128)(2,1)} %get-tuple-element.144), channel_id=1, source_target_pairs={{0,24},{4,28},{8,16},{12,20},{16,8},{20,12},{24,0},{28,4},{1,25},{... | collective-permute-start | bytes 1032200 | tf_op jit(solution)/shard_map/ppermute | solution.py:36
  288.8 26.5 %collective-permute-start.46 = (bf16[1,1,4,112,768]{4,3,2,1,0:T(8,128)(2,1)}, bf16[1,1,4,112,768]{4,3,2,1,0:T(8,128)(2,1)S(1)}, u32[]{:S(2)}, u32[]{:S(2)}) collective-permute-start(bf16[1,1,4,112,768]{4,3,2,1,0:T(8,128)(2,1)} %get-tuple-element.137), channel_id=1, source_target_pairs={{0,4},{4,0},{8,12},{12,8},{16,20},{20,16},{24,28},{28,24},{1,5},{5... | collective-permute-start | bytes 2064392 | tf_op jit(solution)/shard_map/ppermute | solution.py:36
  318.5 11.8 %collective-permute-start.47 = (bf16[112,768]{1,0:T(8,128)(2,1)}, bf16[112,768]{1,0:T(8,128)(2,1)S(1)}, u32[]{:S(2)}, u32[]{:S(2)}) collective-permute-start(bf16[112,768]{1,0:T(8,128)(2,1)} %get-tuple-element.139), channel_id=1, source_target_pairs={{0,8},{4,12},{8,0},{12,4},{16,24},{20,28},{24,16},{28,20},{1,9},{5... | collective-permute-start | bytes 516104 | tf_op jit(solution)/shard_map/ppermute | solution.py:36
  324.5 15.3 %collective-permute-start.48 = (bf16[112,768]{1,0:T(8,128)(2,1)}, bf16[112,768]{1,0:T(8,128)(2,1)S(1)}, u32[]{:S(2)}, u32[]{:S(2)}) collective-permute-start(bf16[112,768]{1,0:T(8,128)(2,1)} %get-tuple-element.140), channel_id=1, source_target_pairs={{0,16},{4,20},{8,24},{12,28},{16,0},{20,4},{24,8},{28,12},{1,17},{... | collective-permute-start | bytes 516104 | tf_op jit(solution)/shard_map/ppermute | solution.py:36
  325.8 14.0 %collective-permute-start.49 = (bf16[112,768]{1,0:T(8,128)(2,1)}, bf16[112,768]{1,0:T(8,128)(2,1)S(1)}, u32[]{:S(2)}, u32[]{:S(2)}) collective-permute-start(bf16[112,768]{1,0:T(8,128)(2,1)} %get-tuple-element.141), channel_id=1, source_target_pairs={{0,24},{4,28},{8,16},{12,20},{16,8},{20,12},{24,0},{28,4},{1,25},{... | collective-permute-start | bytes 516104 | tf_op jit(solution)/shard_map/ppermute | solution.py:36
  328.0 18.3 %collective-permute-start.45 = (bf16[512,768]{1,0:T(8,128)(2,1)S(1)}, bf16[512,768]{1,0:T(8,128)(2,1)S(1)}, u32[]{:S(2)}, u32[]{:S(2)}) collective-permute-start(bf16[512,768]{1,0:T(8,128)(2,1)S(1)} %copy-done.22), channel_id=1, source_target_pairs={{0,2},{1,3},{2,0},{3,1},{4,6},{5,7},{6,4},{7,5},{8,10},{9,11},{10,... | collective-permute-start | bytes 2359304 | tf_op jit(solution)/shard_map/ppermute | solution.py:31
  (58 other events, 815.9 us)

commit v3 on v2

--- a/solution.py
+++ b/solution.py
@@ -19,6 +19,7 @@
 PAD = 256
 LANES = 128
 SUM_ROW = 10
+GATE = 6
 
 masked_score = -1e30
 EPSILON = 1e-12
@@ -59,18 +60,21 @@
 RING_STEPS = (0, -1, 1, -2, 2, -3, 3, -4)
 
 
-def ring_pieces(shard, gate=None):
+def ring_pieces(shard):
     pieces = [shard]
     ahead, behind = shard, shard
     for step in range(1, 5):
-        if gate is not None:
-            ahead, behind = gate(step, ahead, behind)
         ahead = ring_send(ahead, 1)
         pieces.append(ahead)
         if step < 4:
             behind = ring_send(behind, -1)
             pieces.append(behind)
     return pieces
+
+
+def far_exchange(blocks):
+    groups = [[2 * f + n for f in range(4)] for n in range(2)]
+    return lax.all_to_all(blocks, "dp", 0, 0, axis_index_groups=groups, tiled=True)
 
 
 def dp_scatter_sum(sums):
@@ -96,45 +100,50 @@
 
 def block_tables(lengths, global_raw, random_raw, own_blocks, pieces):
     count = own_blocks * pieces
-    per_block = KEYS // BLK
 
     def kernel(length_ref, global_ref, random_ref, table, bias):
         me = lax.axis_index("tensor")
         lane = lax.broadcasted_iota(jnp.int32, (1, KEYS), 1)
         slot = lane // BLK
         within = lane % BLK
-
-        def step(i, carry):
-            block = ((i // own_blocks) ^ me) * own_blocks + i % own_blocks
-            seq = block // NB
-            block = block % NB
+        wide = lax.broadcasted_iota(jnp.int32, (own_blocks, LANES), 1)
+        row = lax.broadcasted_iota(jnp.int32, (own_blocks, 1), 0)
+        for s in range(pieces):
+            first = (s ^ me) * own_blocks
+            seq = first // NB
+            start = first - seq * NB
             length = length_ref[seq]
             live = (length + BLK - 1) // BLK
+            raw = random_ref[seq, pl.ds(pl.multiple_of(start, 8), own_blocks), :]
+            rest = raw - live * jnp.floor(raw.astype(f32) / live.astype(f32)).astype(jnp.int32)
+            rest = jnp.where(rest < 0, rest + live, rest)
+            rest = jnp.where(rest >= live, rest - live, rest)
+            block = row + start
             ids = [jnp.maximum(block - 1, 0), block, jnp.minimum(block + 1, NB - 1)]
-            ids += [lax.rem(global_ref[seq, j], live) for j in range(GLOB)]
-            ids += [lax.rem(random_ref[seq, block, r], live) for r in range(RAND)]
-            spread_ids = jnp.zeros((1, KEYS), jnp.int32)
-            for j in range(per_block):
-                spread_ids = jnp.where(slot == j, ids[j], spread_ids)
-                there = ids[j] + seq * NB
-                table[i, j] = ((there // own_blocks) ^ me) * own_blocks + there % own_blocks
-            position = spread_ids * BLK + within
-            lost = (position >= length) | ((slot == 0) & (block == 0))
-            lost = lost | ((slot == 2) & (block == NB - 1))
-            bias[pl.ds(i, 1), :] = jnp.where(lost, masked_score, 0.0).astype(f32)
-            return carry
-
-        lax.fori_loop(0, count, step, 0)
+            ids += [jnp.full((own_blocks, 1), lax.rem(global_ref[seq, j], live)) for j in range(GLOB)]
+            ids += [rest[:, r : r + 1] for r in range(RAND)]
+            spread_ids = jnp.zeros((own_blocks, KEYS), jnp.int32)
+            packed = jnp.zeros((own_blocks, LANES), jnp.int32)
+            for j, own in enumerate(ids):
+                spread_ids = jnp.where(slot == j, own, spread_ids)
+                there = own + seq * NB
+                there = ((there // own_blocks) ^ me) * own_blocks + there % own_blocks
+                packed = jnp.where(wide == j, there, packed)
+            table[s * own_blocks : (s + 1) * own_blocks, :] = packed
+            lost = (spread_ids * BLK + within) >= length
+            lost = lost | ((slot == 0) & (block == 0)) | ((slot == 2) & (block == NB - 1))
+            bias[s * own_blocks : (s + 1) * own_blocks, :] = jnp.where(lost, masked_score, 0.0).astype(f32)
 
     smem = pl.BlockSpec(memory_space=pltpu.SMEM)
+    vmem = pl.BlockSpec(memory_space=pltpu.VMEM)
     return pl.pallas_call(
         kernel,
         out_shape=[
-            jax.ShapeDtypeStruct((count, per_block), jnp.int32),
+            jax.ShapeDtypeStruct((count, LANES), jnp.int32),
             jax.ShapeDtypeStruct((count, KEYS), f32),
         ],
-        in_specs=[smem] * 3,
-        out_specs=[smem, pl.BlockSpec(memory_space=pltpu.VMEM)],
+        in_specs=[smem, smem, vmem],
+        out_specs=[vmem, vmem],
         cost_estimate=cost(count * KEYS * 16, count * KEYS * 4),
         name="block_tables",
     )(lengths, global_raw, random_raw)
@@ -177,9 +186,9 @@
 def attend_kernel(heads, chosen, pieces, own_blocks, table, *refs):
     parts = refs[:pieces]
     bias = refs[pieces]
-    outs = refs[pieces + 1 : pieces + 1 + len(chosen)]
-    totals = refs[pieces + 1 + len(chosen) : pieces + 1 + 2 * len(chosen)]
-    rows, sems = refs[pieces + 1 + 2 * len(chosen) :]
+    out = refs[pieces + 1]
+    totals = refs[pieces + 2 : pieces + 2 + len(chosen)]
+    rows, sems = refs[pieces + 2 + len(chosen) :]
     own_rows = own_blocks * BLK
     copies = [
         pltpu.make_async_copy(
@@ -209,7 +218,7 @@
             weights = jnp.exp(scores - top)
             total = jnp.sum(weights, axis=-1, keepdims=True)
             mixed = contract(weights.astype(bf16), values, (1, 0)) / total
-            outs[at][pl.ds(start, BLK), :] = unstacked_heads(mixed, out_masks).astype(bf16)
+            out[at, pl.ds(start, BLK), :] = unstacked_heads(mixed, out_masks).astype(bf16)
             log_total = top + jnp.log(total)
             kept = jnp.zeros((BLK, LANES), f32)
             for h in range(heads):
@@ -229,20 +238,20 @@
     work = n * own_rows * KEYS * heads
     results = pl.pallas_call(
         partial(attend_kernel, heads, chosen, pieces, own_blocks),
-        out_shape=[jax.ShapeDtypeStruct((own_rows, PAD), bf16)] * n
+        out_shape=[jax.ShapeDtypeStruct((n, own_rows, PAD), bf16)]
         + [jax.ShapeDtypeStruct((own_rows, LANES), f32)] * n,
         in_specs=[pl.BlockSpec(memory_space=pltpu.SMEM)]
         + [pl.BlockSpec(memory_space=pl.ANY)] * pieces
         + [vmem],
-        out_specs=[vmem] * (2 * n),
+        out_specs=[vmem] * (1 + n),
         scratch_shapes=[
             pltpu.VMEM((pieces * own_rows, 3 * PAD), bf16),
             pltpu.SemaphoreType.DMA((pieces,)),
         ],
-        cost_estimate=cost(12 * work * HD, 4 << 20, work),
+        cost_estimate=cost(48 * work * HD, 16 << 20, 4 * work, 1),
         name="attend_forward",
     )(table, *parts, bias)
-    return results[:n], results[n:]
+    return results[0], results[1:]
 
 
 def attend_back_kernel(heads, chosen, pieces, own_blocks, waited, carried, table, *refs):
@@ -266,8 +275,11 @@
         (tail,) = take(1)
         key_sum, value_sum, key_kept, value_kept, row_sums = take(5)
     else:
+        (small,) = take(1)
         outs = take(len(chosen))
         key_sum, value_sum = take(2)
+        (small_out,) = take(1)
+        small_out[...] = small[...]
     rows, up_rows, sems = refs
     own_rows = own_blocks * BLK
     copies = [
@@ -293,8 +305,12 @@
     up_masks = head_masks(heads, 1.0, bf16)
     out_masks = head_masks(heads, HD**-0.5, f32)
 
-    def step(i, carry):
-        for at, s in enumerate(chosen):
+    side = 2 if len(chosen) == 1 else 1
+
+    def step(step_at, carry):
+        for at, s in enumerate(chosen * side):
+            i = step_at * side + at // len(chosen)
+            at = at % len(chosen)
             block = s * own_blocks + i
             start = pl.multiple_of(i * BLK, BLK)
             here = pl.ds(pl.multiple_of(block * BLK, BLK), BLK)
@@ -320,7 +336,7 @@
                 value_sum[there, :] += value_part[j * BLK : (j + 1) * BLK]
         return carry
 
-    lax.fori_loop(0, own_blocks, step, 0)
+    lax.fori_loop(0, own_blocks // side, step, 0)
     if not carried:
         return
     for copy in late:
@@ -346,7 +362,7 @@
     tail[...] = jnp.where(slot == SUM_ROW, whole, small[...]).astype(bf16)
 
 
-def attend_backward(parts, ups, totals, table, bias, heads, chosen, waited=(), before=None):
+def attend_backward(parts, ups, totals, table, bias, heads, chosen, small, waited=(), before=None):
     own_rows = parts[0].shape[0]
     pieces = len(parts)
     n = len(chosen)
@@ -356,12 +372,12 @@
     work = n * own_rows * KEYS * heads
     sum_shape = (pieces * own_rows, PAD)
     if before is None:
-        outs = [((own_rows, PAD), bf16)] * n + [(sum_shape, f32)] * 2
-        extra, extra_specs, scratch = [], [], []
+        outs = [((own_rows, PAD), bf16)] * n + [(sum_shape, f32)] * 2 + [((16, 3 * PAD), f32)]
+        extra, extra_specs, scratch = [small], [vmem], []
     else:
         outs = [((own_rows, 3 * PAD), bf16)] * pieces + [((16, 3 * PAD), bf16)]
-        extra = list(before)
-        extra_specs = [anyspace] * 2 + [vmem] * (len(before) - 2)
+        extra = [*before, small]
+        extra_specs = [anyspace] * 2 + [vmem] * (len(before) - 1)
         scratch = [pltpu.VMEM(sum_shape, f32)] * 4 + [pltpu.VMEM((8, 3 * PAD), f32)]
     return pl.pallas_call(
         partial(
@@ -393,9 +409,10 @@
 GELU_B = 0.044715
 
 
-def cost(flops, size, transcendentals=0):
+def cost(flops, size, transcendentals=0, cut=None):
+    cut = cut or COST_CUT
     return pl.CostEstimate(
-        flops=flops // COST_CUT, bytes_accessed=size // COST_CUT, transcendentals=transcendentals // COST_CUT
+        flops=flops // cut, bytes_accessed=size // cut, transcendentals=transcendentals // cut
     )
 
 
@@ -419,7 +436,8 @@
     return jnp.sum(array.reshape(array.shape[0] // 8, 8, array.shape[1]), axis=0)
 
 
-def rows_kernel(teams, sources, length, *refs):
+def rows_kernel(places, sources, length, *refs):
+    teams = len(places)
     refs = list(refs)
 
     def take(count):
@@ -432,9 +450,9 @@
     weights = take(sources)
     vectors, b_up = take(2)
     b_out, g1, c1, b_down, g2, c2 = [vectors.at[k : k + 1, :] for k in range(6)]
-    layer_out, low_out, grad_out, act_near, act_far, up_near, up_far = take(7)
+    layer_out, near_out, far_out, turned_out = take(4)
     back_out = take(teams)
-    after_out, after_turned, small = take(3)
+    after_out, small = take(2)
     (
         o_buf,
         x_buf,
@@ -464,7 +482,8 @@
 
     first = []
     for s in range(teams):
-        first.append(pltpu.make_async_copy(mixed[s], o_buf.at[s], in_sems.at[s]))
+        source = mixed[s] if places[s] is None else mixed[s].at[places[s]]
+        first.append(pltpu.make_async_copy(source, o_buf.at[s], in_sems.at[s]))
     first.append(pltpu.make_async_copy(x_in, x_buf, in_sems.at[teams]))
     upstream_copy = pltpu.make_async_copy(g_in, g_buf, in_sems.at[teams + 1])
     fetched = ([], [], [])
@@ -537,7 +556,7 @@
         low_buf[at, :] = (scaled * g1[...] + c1[...]).astype(bf16)
 
     tiles(first_norm)
-    leave_turned(0, low_buf, low_out)
+    leave_turned(0, low_buf, turned_out.at[0])
     for copy in fetched[1]:
         copy.wait()
 
@@ -557,7 +576,7 @@
 
     lax.fori_loop(0, teams, up_step, 0)
     for s in range(teams):
-        leave(act_buf.at[s], (act_far if s % 2 else act_near).at[s // 2])
+        leave(act_buf.at[s], (far_out if s % 2 else near_out).at[s // 2])
     for copy in fetched[2]:
         copy.wait()
     upstream_copy.wait()
@@ -585,7 +604,7 @@
 
     tiles(second_norm)
     leave(x_buf, layer_out)
-    leave_turned(1, g_buf, grad_out)
+    leave_turned(1, g_buf, turned_out.at[1])
 
     def down_back(s, carry):
         for c in range(hidden // cut):
@@ -598,7 +617,7 @@
 
     lax.fori_loop(0, teams, down_back, 0)
     for s in range(teams):
-        leave(slope_buf.at[s], (up_far if s % 2 else up_near).at[s // 2])
+        leave(slope_buf.at[s], (far_out if s % 2 else near_out).at[2 + s // 2])
     for n in range(D // cut):
         cols = slice(n * cut, (n + 1) * cut)
         total = contract(slope_buf[0], up_w[0, cols, :], (1, 1))
@@ -617,7 +636,7 @@
 
     tiles(first_back)
     leave(last_buf, after_out)
-    leave_turned(2, last_buf, after_turned)
+    leave_turned(2, last_buf, turned_out.at[2])
     for s in (2, 3, 1, 0):
         o_buf[s] = contract(last_buf[...], out_w[s], (1, 0)).astype(bf16)
         leave(o_buf.at[s], back_out[s])
@@ -639,16 +658,18 @@
     hidden = b_up.shape[1]
     half = teams // 2
     low = struct((rows, D), bf16)
-    pair = struct((half, rows, hidden), bf16)
+    pair = struct((2 * half, rows, hidden), bf16)
     ring = len(weights) > 1
-    turned = struct((2, 4, D // 8, rows) if ring else (1, 1, D, rows), bf16)
+    turned = struct((3, 2, 4, D // 8, rows) if ring else (3, 1, 1, D, rows), bf16)
     return pl.pallas_call(
-        partial(rows_kernel, teams, len(weights)),
-        out_shape=[low, turned, turned, pair, pair, pair, pair]
+        partial(rows_kernel, [at for _, at in mixed], len(weights)),
+        out_shape=[low, pair, pair, turned]
         + [struct((rows, PAD), bf16)] * teams
-        + [low, turned, struct((16, D), f32)],
-        in_specs=[SMEM_SPEC] + [ANY_SPEC] * (teams + 2 + len(weights)) + [VMEM_SPEC] * 2,
-        out_specs=[ANY_SPEC] * (9 + teams) + [VMEM_SPEC],
+        + [low, struct((16, D), f32)],
+        in_specs=[SMEM_SPEC]
+        + [ANY_SPEC] * (teams + 2 + len(weights))
+        + [VMEM_SPEC] * 2,
+        out_specs=[ANY_SPEC] * (5 + teams) + [VMEM_SPEC],
         scratch_shapes=[
             pltpu.VMEM((teams, rows, PAD), bf16),
             pltpu.VMEM((rows, D), bf16),
@@ -675,7 +696,7 @@
         name="layer_rows",
     )(
         lengths,
-        *mixed,
+        *[array for array, _ in mixed],
         hidden_in,
         grad_out,
         *weights,
@@ -684,22 +705,21 @@
     )
 
 
-def row_dot(groups, cut_by=None, waited=(), tail=None):
+def row_dot(groups, count, cut_by=None, waited=(), tail=None):
     sets = len(groups[0][0])
-    bits, far, part, rows = groups[0][0][0].shape
-    count = groups[0][1][0].shape[0]
+    bits, far, part, rows = groups[0][0][0][0].shape[1:]
     cut = 256
     lows = [0]
     for _, rights in groups:
-        lows.append(lows[-1] + rights[0].shape[2] // cut)
+        lows.append(lows[-1] + rights[0][0][0].shape[2] // cut)
     high = bits * far * part
     below = 0 if tail is None else tail.shape[0]
-    cuts = 1 if cut_by is None else 2
+    cuts = 2 if cut_by in ("bits", "rights") else 1
 
     def kernel(*refs):
         refs = list(refs)
         ins = [[refs.pop(0) for _ in range(sets)] for _ in groups]
-        others = [[refs.pop(0) for _ in range(sets)] for _ in groups]
+        others = [[[refs.pop(0) for _ in range(count)] for _ in range(sets)] for _ in groups]
         if below:
             tail_ref = refs.pop(0)
         outs = refs[len(waited) :]
@@ -709,12 +729,17 @@
             @pl.when((j >= lows[g]) & (j < lows[g + 1]))
             def _(g=g):
                 for i in range(count):
-                    total = contract(ins[g][0][...].reshape(high, rows), others[g][0][i], (1, 0))
+                    total = contract(ins[g][0][...].reshape(high, rows), others[g][0][i][...], (1, 0))
                     for k in range(1, sets):
                         total = total + contract(
-                            ins[g][k][...].reshape(high, rows), others[g][k][i], (1, 0)
+                            ins[g][k][...].reshape(high, rows), others[g][k][i][...], (1, 0)
                         )
                     total = total.astype(bf16).reshape(bits, far, part, cut)
+                    if cut_by == "far":
+                        mine = lax.axis_index("dp") // 2
+                        for z in range(far):
+                            outs[0][z ^ mine, i] = total[:, z]
+                        continue
                     for b in range(bits):
                         if cut_by == "bits":
                             to = outs[b].at[i, 0]
@@ -730,16 +755,21 @@
                         else:
                             to[...] = total[b]
 
-    def column(g):
-        return lambda j: (0, 0, jnp.clip(j - lows[g], 0, lows[g + 1] - lows[g] - 1))
+    def column(g, at):
+        return lambda j: (at, 0, jnp.clip(j - lows[g], 0, lows[g + 1] - lows[g] - 1))
 
     specs, arrays = [], []
     for lefts, _ in groups:
-        specs += [pl.BlockSpec((bits, far, part, rows), lambda j: (0, 0, 0, 0))] * sets
-        arrays += list(lefts)
+        for array, at in lefts:
+            specs.append(
+                pl.BlockSpec((None, bits, far, part, rows), lambda j, at=at: (at, 0, 0, 0, 0))
+            )
+            arrays.append(array)
     for g, (_, rights) in enumerate(groups):
-        specs += [pl.BlockSpec((count, rows, cut), column(g))] * sets
-        arrays += list(rights)
+        for pairs in rights:
+            for array, at in pairs:
+                specs.append(pl.BlockSpec((None, rows, cut), column(g, at)))
+                arrays.append(array)
     if below:
         specs.append(pl.BlockSpec((below, cut), lambda j: (0, j)))
         arrays.append(tail)
@@ -748,10 +778,16 @@
     return pl.pallas_call(
         kernel,
         grid=(lows[-1],),
-        out_shape=[struct((*lead, far, part + below, width), bf16)] * cuts,
+        out_shape=[
+            struct((far, *lead, part, width) if cut_by == "far" else (*lead, far, part + below, width), bf16)
+        ]
+        * cuts,
         in_specs=specs + [ANY_SPEC] * len(waited),
         out_specs=[
-            pl.BlockSpec((*lead, far, part + below, cut), lambda j: (0, 0, 0, 0, j))
+            pl.BlockSpec(
+                (far, *lead, part, cut) if cut_by == "far" else (*lead, far, part + below, cut),
+                lambda j: (0, 0, 0, 0, j),
+            )
         ]
         * cuts,
         cost_estimate=cost(2 * sets * rows * high * count * width, 8 << 20),
@@ -779,43 +815,52 @@
     )(a, b, *waited)
 
 
+def fold(blocks, waited=()):
+    def kernel(ref, *refs):
+        for k in range(2):
+            total = ref[0, k].astype(f32)
+            for z in range(1, 4):
+                total = total + ref[z, k].astype(f32)
+            refs[len(waited) + k][...] = total.astype(bf16)
+
+    return pl.pallas_call(
+        kernel,
+        out_shape=[struct(blocks.shape[2:], bf16)] * 2,
+        in_specs=[VMEM_SPEC] + [ANY_SPEC] * len(waited),
+        out_specs=[VMEM_SPEC] * 2,
+        cost_estimate=cost(blocks.size, 3 * blocks.size),
+        name="fold",
+    )(blocks, *waited)
+
+
 def joined_sums(pairs, waited=()):
-    rows = pairs[0][0].shape[1]
+    heights = [a.shape[1] for a, _ in pairs]
+    rows = max(heights)
     widths = [a.shape[2] for a, _ in pairs]
     count = 2 * len(pairs)
 
     def kernel(*refs):
-        outs = refs[count + len(waited) :]
+        out = refs[-1]
+        mine = lax.axis_index("dp") // 2
         for z in range(4):
             at = 0
+            to = out.at[z ^ mine]
             for k, width in enumerate(widths):
-                outs[z][:, at : at + width] = (
+                if heights[k] < rows:
+                    to[heights[k] :, at : at + width] = jnp.zeros((rows - heights[k], width), bf16)
+                to[: heights[k], at : at + width] = (
                     refs[2 * k][z].astype(f32) + refs[2 * k + 1][z].astype(f32)
                 ).astype(bf16)
                 at += width
 
     return pl.pallas_call(
         kernel,
-        out_shape=[struct((rows, sum(widths)), bf16)] * 4,
+        out_shape=struct((4, rows, sum(widths)), bf16),
         in_specs=[VMEM_SPEC] * count + [ANY_SPEC] * len(waited),
-        out_specs=[VMEM_SPEC] * 4,
+        out_specs=VMEM_SPEC,
         cost_estimate=cost(rows * sum(widths) * 4, rows * sum(widths) * 24),
         name="joined_sums",
     )(*[array for pair in pairs for array in pair], *waited)
-
-
-def held(array, waited):
-    def kernel(a_ref, *refs):
-        refs[-1][...] = a_ref[...]
-
-    return pl.pallas_call(
-        kernel,
-        out_shape=struct(array.shape, array.dtype),
-        in_specs=[VMEM_SPEC] + [ANY_SPEC] * len(waited),
-        out_specs=VMEM_SPEC,
-        cost_estimate=cost(array.size, 8 * array.size),
-        name="held",
-    )(array, *waited)
 
 
 def spread(grads, weight, added=None, after=None, waited=()):
@@ -848,14 +893,29 @@
     )(*grads, weight, *more, *waited)
 
 
-def pack_weights(w_query, w_key, w_value, w_up, w_out, w_down):
+def pack_queries(w_query, w_key, w_value):
     rows, width = w_query.shape
-    hidden = w_up.shape[1]
-
-    def kernel(q, k, v, up, out, down, qkv, own):
+
+    def kernel(q, k, v, qkv):
+        qkv[...] = jnp.zeros_like(qkv)
         for at, ref in enumerate((q, k, v)):
-            qkv[:, at * PAD : (at + 1) * PAD] = jnp.zeros((rows, PAD), bf16)
             qkv[:, at * PAD : at * PAD + width] = ref[...]
+
+    return pl.pallas_call(
+        kernel,
+        out_shape=struct((rows, 3 * PAD), bf16),
+        in_specs=[VMEM_SPEC] * 3,
+        out_specs=VMEM_SPEC,
+        cost_estimate=cost(rows * PAD, rows * PAD * 8),
+        name="pack_queries",
+    )(w_query, w_key, w_value)
+
+
+def pack_weights(w_up, w_out, w_down):
+    rows, hidden = w_up.shape
+    width = w_out.shape[0]
+
+    def kernel(up, out, down, own):
         own[:, :hidden] = up[...]
         own[:, hidden : hidden + PAD] = jnp.zeros((rows, PAD), bf16)
         own[:, hidden : hidden + width] = out[...].T
@@ -863,22 +923,20 @@
 
     return pl.pallas_call(
         kernel,
-        out_shape=[
-            struct((rows, 3 * PAD), bf16),
-            struct((rows, 2 * hidden + PAD), bf16),
-        ],
-        in_specs=[VMEM_SPEC] * 6,
-        out_specs=[VMEM_SPEC] * 2,
-        cost_estimate=cost(rows * hidden, 4 << 20),
+        out_shape=struct((rows, 2 * hidden + PAD), bf16),
+        in_specs=[VMEM_SPEC] * 3,
+        out_specs=VMEM_SPEC,
+        cost_estimate=cost(rows * hidden, 2 << 20),
         name="pack_weights",
-    )(w_query, w_key, w_value, w_up, w_out, w_down)
-
-
-def pair_weights(own, beyond, hidden):
+    )(w_up, w_out, w_down)
+
+
+def pair_weights(own, beyond, hidden, waited):
     rows, width = own.shape
     starts = (0, hidden, hidden + PAD, width)
 
-    def kernel(a, b, out):
+    def kernel(a, b, *refs):
+        out = refs[-1]
         for at, end in zip(starts, starts[1:]):
             out[:, 2 * at : at + end] = a[:, at:end]
             out[:, at + end : 2 * end] = b[:, at:end]
@@ -886,11 +944,11 @@
     return pl.pallas_call(
         kernel,
         out_shape=struct((rows, 2 * width), bf16),
-        in_specs=[VMEM_SPEC] * 2,
+        in_specs=[VMEM_SPEC] * 2 + [ANY_SPEC] * len(waited),
         out_specs=VMEM_SPEC,
         cost_estimate=cost(rows * width, 4 * rows * width),
         name="pair_weights",
-    )(own, beyond)
+    )(own, beyond, *waited)
 
 
 def project_in(xs, weights, bias):
@@ -973,7 +1031,7 @@
             pltpu.SemaphoreType.DMA((sources,)),
             pltpu.SemaphoreType.DMA((1 + pieces * (1 + bits * far),)),
         ],
-        cost_estimate=cost(2 * pieces * rows * D * wide, 12 << 20),
+        cost_estimate=cost(4 * pieces * rows * D * wide, 24 << 20, 0, 1),
         name="project_in",
     )(*xs, *weights, bias)
     return results[:pieces], results[pieces : 2 * pieces], results[2 * pieces]
@@ -1029,9 +1087,9 @@
     )
     halved = members == 8
     if halved:
-        qkv_shard, own = pack_weights(w_query, w_key, w_value, w_up, w_out, w_down)
-        shard = pair_weights(own, swap(own, 2), hidden)
-        qkv_pieces = ring_pieces(qkv_shard)
+        qkv_pieces = ring_pieces(pack_queries(w_query, w_key, w_value))
+        own = pack_weights(w_up, w_out, w_down)
+        shard = pair_weights(own, swap(own, 2), hidden, qkv_pieces[GATE:])
     else:
         qkv_shard = jnp.concatenate([padded(w_query), padded(w_key), padded(w_value)], axis=1)
         qkv_pieces = [lax.all_gather(qkv_shard, "dp", axis=0, tiled=True)]
@@ -1041,27 +1099,18 @@
         weights = [weights.reshape(teams, D, shard.shape[1])]
 
     qkv, x_turned, qkv_w = project_in(x_parts, qkv_pieces, qkv_b[None])
-    (o2, o3), (t2, t3) = attend_forward(qkv, table, bias, heads, (2, 3))
-    r2 = swap(o2, 2)
-    r3 = swap(o3, 3)
-    (o0, o1), (t0, t1) = attend_forward(qkv, table, bias, heads, (0, 1))
-    r1 = swap(o1, 1)
+    far_mixed, (t2, t3) = attend_forward(qkv, table, bias, heads, (2, 3))
+    far_mixed = swap(far_mixed, 2)
+    near_mixed, (t0, t1) = attend_forward(qkv, table, bias, heads, (0, 1))
+    r1 = swap(near_mixed[1], 1)
+    r3 = swap(far_mixed[1], 1)
     if halved:
 
-        def gate(step, ahead, behind):
-            waited = {3: qkv[0], 4: o2}.get(step)
-            if waited is None:
-                return ahead, behind
-            ahead = held(ahead, (waited,))
-            if step < 4:
-                behind = held(behind, (waited,))
-            return ahead, behind
-
-        weights = ring_pieces(shard, gate)
+        weights = ring_pieces(shard)
         weights = weights + [swap(piece, 1) for piece in weights]
 
     results = layer_rows(
-        [o0, r1, r2, r3],
+        [(near_mixed, 0), (r1, None), (far_mixed, 0), (r3, None)],
         hidden_in,
         grad_out,
         weights,
@@ -1071,82 +1120,86 @@
         ),
         lengths,
     )
-    layer_out, low, grad_low, act_near, act_far, up_near, up_far = results[:7]
-    backs = results[7 : 7 + teams]
-    after_low, after_turned, small = results[7 + teams :]
+    layer_out, near_rows, far_rows, turned = results[:4]
+    backs = results[4 : 4 + teams]
+    after_low, small = results[4 + teams :]
     ups = [backs[0]] + [swap(backs[s], s) for s in range(1, teams)]
+    totals = [t0, t1, t2, t3]
+    before = attend_backward(qkv, ups[:1], totals[:1], table, bias, heads, (0,), small)
+    small = before[3]
     small = small + swap(small, 1)
     small = small + swap(small, 2)
 
-    down_group = ([grad_low, swap(grad_low, 1)], [act_near, swap(act_far, 1)])
-    up_group = ([low, swap(low, 1)], [up_near, swap(up_far, 1)])
+    next_rows, next_turned = swap(far_rows, 1), swap(turned, 1)
+    down_group = (
+        [(turned, 1), (next_turned, 1)],
+        [[(near_rows, 0), (near_rows, 1)], [(next_rows, 0), (next_rows, 1)]],
+    )
+    up_group = (
+        [(turned, 0), (next_turned, 0)],
+        [[(near_rows, 2), (near_rows, 3)], [(next_rows, 2), (next_rows, 3)]],
+    )
     out_group = (
-        [after_turned, swap(after_turned, 1)],
-        [jnp.stack([o0, r2]), jnp.stack([o1, swap(r3, 1)])],
+        [(turned, 2), (next_turned, 2)],
+        [[(near_mixed, 0), (far_mixed, 0)], [(near_mixed, 1), (far_mixed, 1)]],
     )
     if halved:
-        up_kept, up_gone = row_dot([up_group, out_group], "bits")
+        (down_gone,) = row_dot([down_group], 2, "far", (before[0], *ups[1:]))
+        down_blocks = far_exchange(down_gone)
+        up_kept, up_gone = row_dot([up_group, out_group], 2, "bits", (down_gone,))
         up_away = dp_swap(up_gone, 1)
-        down_kept, down_gone = row_dot([down_group], "rights", (up_gone, ups[2], ups[3], small))
-        down_away = swap(down_gone, 2)
-        waited = (down_gone,)
+        waited = (up_gone,)
     else:
-        down_sums = row_dot([down_group])[0].reshape(2, D, -1)
-        up_sums = row_dot([up_group, out_group])[0].reshape(2, D, -1)
+        down_sums = row_dot([down_group], 2)[0].reshape(2, D, -1)
+        up_sums = row_dot([up_group, out_group], 2)[0].reshape(2, D, -1)
         waited = ()
-
-    totals = [t0, t1, t2, t3]
-    before = attend_backward(qkv, ups[:2], totals[:2], table, bias, heads, (0, 1), waited)
-    if halved:
-        down_here, down_next = plus(down_kept[0], down_away[0], (before[0],), 2)
-        down_away = dp_swap(down_next, 1)
-        up_here, up_next = plus(up_kept, up_away, (before[0],), 2)
-        up_away = swap(up_next, 2)
-        waited = (down_next, up_next)
     results = attend_backward(
         qkv,
-        ups[2:],
-        totals[2:],
+        ups[1:],
+        totals[1:],
         table,
         bias,
         heads,
-        (2, 3),
+        (1, 2, 3),
+        small,
         waited,
-        (before[2], before[3], before[0], before[1], small),
+        (before[1], before[2], before[0]),
     )
     grads, tail = results[:4], results[4]
     waited = ()
     if halved:
-        sums = joined_sums(
-            [(down_here[0], down_away[0]), (up_here[0, 0], up_away[0, 0])], (grads[0],)
-        )
-        waited = (sums[0],)
+        up_here, up_next = plus(up_kept, up_away, (grads[0],), 2)
+        up_away = swap(up_next, 2)
+        waited = (up_next,)
     parts = spread([grads[3], grads[1]], qkv_w, waited=waited)
     spread_away = swap(parts, 1)
-    qkv_group = (x_turned, [g[None] for g in grads])
+    qkv_group = ([(x[None], 0) for x in x_turned], [[(g[None], 0)] for g in grads])
     if halved:
-        kept, gone = row_dot([qkv_group], "bits", (parts,), tail)
+        kept, gone = row_dot([qkv_group], 1, "bits", (parts,), tail)
         away = dp_swap(gone, 1)
-        beyond, here = spread([grads[2], grads[0]], qkv_w, spread_away, after_low, (kept,))
-        total = sums[0].astype(f32)
-        for z in range(1, 4):
-            total = total + dp_swap(sums[z], 2 * z).astype(f32)
-        down_part, up_part = total[:, :hidden], total[:, hidden:]
-        blocks = joined_sums([(kept[0, 0], away[0, 0])], (beyond,))
-        beyond = swap(beyond, 2)
-        qkv_part = blocks[0].astype(f32)
-        for z in range(1, 4):
-            qkv_part = qkv_part + dp_swap(blocks[z], 2 * z).astype(f32)
+        beyond, here = spread([grads[2], grads[0]], qkv_w, spread_away, after_low, (gone,))
+        beyond_away = swap(beyond, 2)
+        down_here, down_next = fold(down_blocks, (beyond,))
+        down_away = swap(down_next, 2)
+        blocks = joined_sums(
+            [(kept[0, 0], away[0, 0]), (up_here[0, 0], up_away[0, 0])], (down_next,)
+        )
+        total = far_exchange(blocks)
+        down_here, down_next = plus(down_here, down_away, (blocks,), 2)
+        down_away = dp_swap(down_next, 1)
+        down_part = down_here[0].astype(f32) + down_away[0].astype(f32)
+        total = jnp.sum(total.astype(f32), axis=0)
+        qkv_part, up_part = total[:, : 3 * PAD], total[:-16, 3 * PAD :]
         qkv_part, small = qkv_part[:-16], qkv_part[-16:]
     else:
-        blocks = row_dot([qkv_group])[0].reshape(D, -1)
+        blocks = row_dot([qkv_group], 1)[0].reshape(D, -1)
         qkv_part = dp_scatter_sum(blocks)
         small = lax.psum(tail.astype(f32), "dp")
         beyond, here = spread([grads[2], grads[0]], qkv_w, spread_away, after_low)
-        beyond = swap(beyond, 2)
+        beyond_away = swap(beyond, 2)
         down_part = dp_scatter_sum(down_sums[0] + swap(down_sums[1], 2))
         up_part = dp_scatter_sum(up_sums[0] + swap(up_sums[1], 2))
-    grad_in = here + beyond.astype(f32)
+    grad_in = here + beyond_away.astype(f32)
 
     bias_row = small[SUM_ROW]
     return (

time: 349 us -> 295 us (0.85)
  waiting for transfers between devices: 117 us -> 93.6 us
  starting transfers between devices: 50.6 us -> 40.4 us
  local copies, waits for them, and re-layouts: 23.7 us -> 14.2 us
  Pallas kernels: 147 us -> 139 us
    ppermute x30 -> x26, waiting for transfers between devices: 59.4 us -> 37.6 us  [swap(): return lax.ppermute(array, 'tensor', [(t, t ^ bit) for t in range(size)])]
    ppermute x9 -> x3, starting transfers between devices: 15.6 us -> 2.04 us  [dp_swap(): return lax.ppermute(array, 'dp', [(t, t ^ bit) for t in range(size)])]
    unnamed x109 -> x77, local copies, waits for them, and re-layouts: 19.7 us -> 9.35 us
    all_to_all x0 -> x2, starting transfers between devices: none -> 9.77 us  [far_exchange(): lax.all_to_all(blocks, 'dp', 0, 0, axis_index_groups=groups, tiled=True)]
    ppermute x9 -> x3, waiting for transfers between devices: 27 us -> 18.6 us  [dp_swap(): return lax.ppermute(array, 'dp', [(t, t ^ bit) for t in range(size)])]
    pallas_call x11 -> x9, Pallas kernels: 71.2 us -> 64.6 us  [the longest x1 32.6 us: layer_rows(): pl.pallas_call(partial(rows_kernel, [at for _, at in mixed], len(weights)...]
    all_to_all x0 -> x2, waiting for transfers between devices: none -> 4.14 us  [far_exchange(): lax.all_to_all(blocks, 'dp', 0, 0, axis_index_groups=groups, tiled=True)]
    ppermute x30 -> x26, starting transfers between devices: 16.6 us -> 13.5 us  [swap(): return lax.ppermute(array, 'tensor', [(t, t ^ bit) for t in range(size)])]
  transfers between devices with their start and end apart: 53 -> 45, of which waited for: 25 -> 18; matrix products, arithmetic and copies ran while one was open for 3% -> 3% of each run, Pallas kernels for 30% -> 33%
where the time goes in v3:
time: 295 us; the launch traced here: 294 us
  Pallas kernels  139 us (47%)
  waiting for transfers between devices  93.6 us (32%)
  starting transfers between devices  40.4 us (14%)
  local copies, waits for them, and re-layouts  14.2 us (5%)
  other arithmetic  4.72 us (2%)
    ppermute x26, waiting for transfers between devices, swap(): return lax.ppermute(array, 'tensor', [(t, t ^ bit) for t in range(size)])  37.6 us
    ppermute x14, waiting for transfers between devices, ring_send(): lax.ppermute(array, 'dp', [(order[i], order[(i + step) % size]) for i in...  33.2 us
    pallas_call x1, Pallas kernels, layer_rows(): pl.pallas_call(partial(rows_kernel, [at for _, at in mixed], len(weights)...  32.6 us
    pallas_call x2, Pallas kernels, attend_backward(): pl.pallas_call(partial(attend_back_kernel, heads, chosen, pieces, own_blo...  32.3 us
    pallas_call x3, Pallas kernels, row_dot(): pl.pallas_call(kernel, grid=(lows[-1],), out_shape=[struct((far, *lead, p...  21.1 us
    ppermute x3, waiting for transfers between devices, dp_swap(): return lax.ppermute(array, 'dp', [(t, t ^ bit) for t in range(size)])  18.6 us
    pallas_call x2, Pallas kernels, attend_forward(): pl.pallas_call(partial(attend_kernel, heads, chosen, pieces, own_blocks),...  17.5 us
    ppermute x14, starting transfers between devices, ring_send(): lax.ppermute(array, 'dp', [(order[i], order[(i + step) % size]) for i in...  15.2 us
  transfers between devices with their start and end apart: 45, of which 18 were waited for; matrix products, arithmetic and copies ran while one was open for 3% of the time, Pallas kernels for 33%

profile of v3, /device:TPU:0, one launch (start us, length us, event | category | flops | bytes accessed | tf_op | source)
XLA Modules:
  0.0 293.8 jit_solution(1074820120508858736)
XLA Ops:
  0.7 3.0 %collective-permute-start.1 = (bf16[512,768]{1,0:T(8,128)(2,1)}, bf16[512,768]{1,0:T(8,128)(2,1)}, u32[]{:S(2)}, u32[]{:S(2)}) collective-permute-start(bf16[512,768]{1,0:T(8,128)(2,1)} %refs_4_.1), channel_id=1, source_target_pairs={{0,2},{1,3},{2,0},{3,1},{4,6},{5,7},{6,4},{7,5},{8,10},{9,11},{10,... | collective-permute-start | bytes 2359304 | tf_op jit(solution)/shard_map/ppermute | solution.py:32
  3.7 1.5 pack_queries.1.refs_4_
  5.2 1.6 collective-permute-start.3
  7.3 3.5 %collective-permute-done.3.refs_5_ = bf16[96,768]{1,0:T(8,128)(2,1)S(1)} collective-permute-done((bf16[96,768]{1,0:T(8,128)(2,1)}, bf16[96,768]{1,0:T(8,128)(2,1)S(1)}, u32[]{:S(2)}, u32[]{:S(2)}) %collective-permute-start.3) | collective-permute-done | bytes 147488 | tf_op jit(solution)/shard_map/ppermute | solution.py:55
  10.8 1.6 collective-permute-start.5
  12.3 1.7 copy.38.down
  14.1 1.9 pack_weights.1.a
  16.7 1.8 collective-permute-start.7
  18.5 3.1 %collective-permute-done.6.refs_8_ = bf16[96,768]{1,0:T(8,128)(2,1)S(1)} collective-permute-done((bf16[96,768]{1,0:T(8,128)(2,1)S(1)}, bf16[96,768]{1,0:T(8,128)(2,1)S(1)}, u32[]{:S(2)}, u32[]{:S(2)}) %collective-permute-start.6) | collective-permute-done | bytes 147488 | tf_op jit(solution)/shard_map/ppermute | solution.py:55
  21.9 2.0 collective-permute-start.9
  23.8 5.0 %collective-permute-done.13.b = bf16[96,1792]{1,0:T(8,128)(2,1)S(1)} collective-permute-done((bf16[96,1792]{1,0:T(8,128)(2,1)}, bf16[96,1792]{1,0:T(8,128)(2,1)S(1)}, u32[]{:S(2)}, u32[]{:S(2)}) %collective-permute-start.13) | collective-permute-done | bytes 344096 | tf_op jit(solution)/shard_map/ppermute | solution.py:32
  30.3 2.0 pair_weights.1.refs_6_
  32.3 1.8 collective-permute-start.14
  34.8 14.3 %collective-permute-done.14.refs_7_ = bf16[96,3584]{1,0:T(8,128)(2,1)S(1)} collective-permute-done((bf16[96,3584]{1,0:T(8,128)(2,1)}, bf16[96,3584]{1,0:T(8,128)(2,1)S(1)}, u32[]{:S(2)}, u32[]{:S(2)}) %collective-permute-start.14) | collective-permute-done | bytes 688160 | tf_op jit(solution)/shard_map/ppermute | solution.py:55
  49.1 1.5 collective-permute-start.16
  52.0 1.5 block_tables.1
  55.1 8.3 %project_in.1 = (bf16[512,768]{1,0:T(8,128)(2,1)}, bf16[512,768]{1,0:T(8,128)(2,1)}, bf16[512,768]{1,0:T(8,128)(2,1)}, bf16[512,768]{1,0:T(8,128)(2,1)}, bf16[2,...) custom-call(bf16[512,768]{1,0:T(8,128)(2,1)} %refs_4_.1, ...), custom_call_target="tpu_custom_call" | custom-call | flops 4831838208 | bytes 25165824 | tf_op jit(solution)/shard_map/project_in/pallas_call | solution.py:1018
  66.0 8.8 %attend_forward.3 = (bf16[2,512,256]{2,1,0:T(8,128)(2,1)}, f32[512,128]{1,0:T(8,128)}, f32[512,128]{1,0:T(8,128)}) custom-call(s32[32,128]{1,0:T(8,128)} %get-tuple-element.65.table, bf16[512,768]{1,0:T(8,128)(2,1)} %get-tuple-element.66.refs_0_, bf16[512,768]{1,0:T(8,128)(2,1)} %get-tuple-element.67.refs_1_, bf16[512,768]{1,0:T(8,128)(2,1)} %get-tuple-element.68.refs_2_, ...), custom_call_target="tpu_custom_call" | custom-call | flops 4831838208 | bytes 16777216 | tf_op jit(solution)/shard_map/attend_forward/pallas_call | solution.py:239
  74.9 1.6 collective-permute-start.11
  76.4 8.8 %attend_forward.2 = (bf16[2,512,256]{2,1,0:T(8,128)(2,1)}, f32[512,128]{1,0:T(8,128)}, f32[512,128]{1,0:T(8,128)}) custom-call(s32[32,128]{1,0:T(8,128)} %get-tuple-element.65.table, bf16[512,768]{1,0:T(8,128)(2,1)} %get-tuple-element.66.refs_0_, bf16[512,768]{1,0:T(8,128)(2,1)} %get-tuple-element.67.refs_1_, bf16[512,768]{1,0:T(8,128)(2,1)} %get-tuple-element.68.refs_2_, ...), custom_call_target="tpu_custom_call" | custom-call | flops 4831838208 | bytes 16777216 | tf_op jit(solution)/shard_map/attend_forward/pallas_call | solution.py:239
  85.8 1.6 collective-permute-start.20
  88.5 1.5 collective-permute-done.10.refs_1_
  92.7 10.8 %collective-permute-done.19.refs_12_ = bf16[96,3584]{1,0:T(8,128)(2,1)} collective-permute-done((bf16[96,3584]{1,0:T(8,128)(2,1)}, bf16[96,3584]{1,0:T(8,128)(2,1)}, u32[]{:S(2)}, u32[]{:S(2)}) %collective-permute-start.19) | collective-permute-done | bytes 688160 | tf_op jit(solution)/shard_map/ppermute | solution.py:55
  107.0 32.6 %layer_rows.1 = (bf16[512,768]{1,0:T(8,128)(2,1)}, bf16[4,512,768]{2,1,0:T(8,128)(2,1)}, bf16[4,512,768]{2,1,0:T(8,128)(2,1)}, bf16[3,2,4,96,512]{4,3,2,1,0:T(8,...) custom-call(s32[1]{0:T(128)S(6)} %copy.40.length_ref.length, ...), custom_call_target="tpu_custom_call" | custom-call | flops 176160768 | bytes 393216 | tf_op jit(solution)/shard_map/layer_rows/pallas_call | solution.py:664
  142.0 10.4 %attend_backward.2 = (bf16[512,256]{1,0:T(8,128)(2,1)}, f32[2048,256]{1,0:T(8,128)}, f32[2048,256]{1,0:T(8,128)}, f32[16,768]{1,0:T(8,128)}) custom-call(s32[32,128]{1,0:T(8,128)} %get-tuple-element.65.table, bf16[512,768]{1,0:T(8,128)(2,1)} %get-tuple-element.66.refs_0_, bf16[512,768]{1,0:T(8,128)(2,1)} %get-tuple-element.67.refs_1_, ...), custom_call_target="tpu_custom_call" | custom-call | flops 23592960 | bytes 196608 | tf_op jit(solution)/shard_map/attend_backward/pallas_call | solution.py:382
  152.4 1.7 collective-permute-done.31.refs_9_.refs_6_
  154.2 1.7 copy-done
  155.9 6.4 %row_dot.3.refs_12_ = bf16[4,2,2,96,768]{4,3,2,1,0:T(8,128)(2,1)} custom-call(bf16[3,2,4,96,512]{4,3,2,1,0:T(8,128)(2,1)} %get-tuple-element.80.refs_0_.refs_2_, bf16[3,2,4,96,512]{4,3,2,1,0:T(8,128)(2,1)} %collective-permute-done.32.refs_1_.refs_3_, bf16[4,512,768]{2,1,0:T(8,128)(2,1)} %get-tuple-element.81.refs_2_.refs_3_.refs_4_.refs_5_, ...), custom_call_target="tpu_custom_call" | custom-call | flops 37748736 | bytes 131072 | tf_op jit(solution)/shard_map/row_dot/pallas_call | solution.py:778
  162.2 4.8 %all-to-all-start = ((bf16[4,2,2,96,768]{4,3,2,1,0:T(8,128)(2,1)}), bf16[4,2,2,96,768]{4,3,2,1,0:T(8,128)(2,1)S(1)}, u32[]{:S(2)}, u32[]{:S(2)}) async-start(bf16[4,2,2,96,768]{4,3,2,1,0:T(8,128)(2,1)} %row_dot.3.refs_12_), calls=%async_computation | async-start | bytes 4718592 | tf_op jit(solution)/shard_map/all_to_all | solution.py:77
  167.1 8.2 %row_dot.4 = (bf16[2,1,4,96,1024]{4,3,2,1,0:T(8,128)(2,1)}, bf16[2,1,4,96,1024]{4,3,2,1,0:T(8,128)(2,1)}) custom-call(bf16[3,2,4,96,512]{4,3,2,1,0:T(8,128)(2,1)} %get-tuple-element.80.refs_0_.refs_2_, bf16[3,2,4,96,512]{4,3,2,1,0:T(8,128)(2,1)} %collective-permute-done.32.refs_1_.refs_3_, bf16[3,2,4,96,512]{4,3,2,1,0:T(8,128)(2,1)} %get-tuple-element.80.refs_0_.refs_2_, ...), custom_call_target="tpu_custom_call" | custom-call | flops 50331648 | bytes 131072 | tf_op jit(solution)/shard_map/row_dot/pallas_call | solution.py:778
  177.6 3.5 %collective-permute-done.35 = f32[16,768]{1,0:T(8,128)S(1)} collective-permute-done((f32[16,768]{1,0:T(8,128)S(1)}, f32[16,768]{1,0:T(8,128)S(1)}, u32[]{:S(2)}, u32[]{:S(2)}) %collective-permute-start.35) | collective-permute-done | bytes 49184 | tf_op jit(solution)/shard_map/ppermute | solution.py:32
  181.8 21.8 %attend_backward.3 = (bf16[512,768]{1,0:T(8,128)(2,1)}, bf16[512,768]{1,0:T(8,128)(2,1)}, bf16[512,768]{1,0:T(8,128)(2,1)}, bf16[512,768]{1,0:T(8,128)(2,1)}, bf16[16,768]{1,0:T(8,128)(2,1)}) custom-call(s32[32,128]{1,0:T(8,128)} %get-tuple-element.65.table, bf16[512,768]{1,0:T(8,128)(2,1)} %get-tuple-element.66.refs_0_, ...), custom_call_target="tpu_custom_call" | custom-call | flops 70778880 | bytes 196608 | tf_op jit(solution)/shard_map/attend_backward/pallas_call | solution.py:382
  203.6 8.4 %collective-permute-done.36.b_ref = bf16[2,1,4,96,1024]{4,3,2,1,0:T(8,128)(2,1)} collective-permute-done((bf16[2,1,4,96,1024]{4,3,2,1,0:T(8,128)(2,1)}, bf16[2,1,4,96,1024]{4,3,2,1,0:T(8,128)(2,1)}, u32[]{:S(2)}, u32[]{:S(2)}) %collective-permute-start.36) | collective-permute-done | bytes 1572896 | tf_op jit(solution)/shard_map/ppermute | solution.py:37
  212.0 3.3 %plus.2 = (bf16[1,1,4,96,1024]{4,3,2,1,0:T(8,128)(2,1)}, bf16[1,1,4,96,1024]{4,3,2,1,0:T(8,128)(2,1)}) custom-call(bf16[2,1,4,96,1024]{4,3,2,1,0:T(8,128)(2,1)} %get-tuple-element.96.a_ref, bf16[2,1,4,96,1024]{4,3,2,1,0:T(8,128)(2,1)} %collective-permute-done.36.b_ref, bf16[512,768]{1,0:T(8,128)(2,1)} %get-tuple-element.92.refs_0_.second), custom_call_target="tpu_custom_call" | custom-call | flops 12288 | bytes 73728 | tf_op jit(solution)/shard_map/plus/pallas_call | solution.py:808
  215.3 4.4 %spread.2.refs_9_ = bf16[2,512,768]{2,1,0:T(8,128)(2,1)} custom-call(bf16[512,768]{1,0:T(8,128)(2,1)} %get-tuple-element.94.first, bf16[512,768]{1,0:T(8,128)(2,1)} %get-tuple-element.95.second, bf16[768,768]{1,0:T(8,128)(2,1)} %get-tuple-element.93.w, bf16[1,1,4,96,1024]{4,3,2,1,0:T(8,128)(2,1)} %get-tuple-element.97.refs_0_), custom_call_target="tpu_custom_call" | custom-call | flops 18874368 | bytes 81920 | tf_op jit(solution)/shard_map/spread/pallas_call | solution.py:886
  220.2 6.6 %row_dot.5 = (bf16[1,1,4,112,768]{4,3,2,1,0:T(8,128)(2,1)}, bf16[1,1,4,112,768]{4,3,2,1,0:T(8,128)(2,1)}) custom-call(bf16[1,2,4,96,512]{4,3,2,1,0:T(8,128)(2,1)} %bitcast.28, bf16[1,2,4,96,512]{4,3,2,1,0:T(8,128)(2,1)} %bitcast.29, bf16[1,2,4,96,512]{4,3,2,1,0:T(8,128)(2,1)} %bitcast.30, bf16[1,2,4,96,512]{4,3,2,1,0:T(8,128)(2,1)} %bitcast.31, ...), custom_call_target="tpu_custom_call" | custom-call | flops 37748736 | bytes 131072 | tf_op jit(solution)/shard_map/row_dot/pallas_call | solution.py:778
  227.6 5.0 %spread.3 = (bf16[512,768]{1,0:T(8,128)(2,1)}, f32[512,768]{1,0:T(8,128)}) custom-call(bf16[512,768]{1,0:T(8,128)(2,1)} %get-tuple-element.91.first, bf16[512,768]{1,0:T(8,128)(2,1)} %get-tuple-element.92.refs_0_.second, bf16[768,768]{1,0:T(8,128)(2,1)} %get-tuple-element.93.w, bf16[2,512,768]{2,1,0:T(8,128)(2,1)} %collective-permute-done.37.refs_0_, ...), custom_call_target="tpu_custom_call" | custom-call | flops 18874368 | bytes 81920 | tf_op jit(solution)/shard_map/spread/pallas_call | solution.py:886
  232.6 1.4 copy-done.1
  234.0 2.7 fold.1
  236.6 8.1 %collective-permute-done.39 = bf16[1,1,4,112,768]{4,3,2,1,0:T(8,128)(2,1)} collective-permute-done((bf16[1,1,4,112,768]{4,3,2,1,0:T(8,128)(2,1)}, bf16[1,1,4,112,768]{4,3,2,1,0:T(8,128)(2,1)}, u32[]{:S(2)}, u32[]{:S(2)}) %collective-permute-start.39) | collective-permute-done | bytes 688160 | tf_op jit(solution)/shard_map/ppermute | solution.py:37
  244.7 3.3 %joined_sums.1.refs_0_ = bf16[4,112,1792]{2,1,0:T(8,128)(2,1)} custom-call(bf16[4,112,768]{2,1,0:T(8,128)(2,1)} %bitcast.33, bf16[4,112,768]{2,1,0:T(8,128)(2,1)} %bitcast.11.refs_1_, bf16[4,96,1024]{2,1,0:T(8,128)(2,1)} %bitcast.32, bf16[4,96,1024]{2,1,0:T(8,128)(2,1)} %bitcast.13.refs_3_, bf16[2,96,768]{2,1,0:T(8,128)(2,1)} %get-tuple-element.109.refs_4_), custom_call_target="tpu_custom_call" | custom-call | flops 12544 | bytes 75264 | tf_op jit(solution)/shard_map/joined_sums/pallas_call | solution.py:856
  248.0 4.9 %all-to-all-start.1 = ((bf16[4,112,1792]{2,1,0:T(8,128)(2,1)}), bf16[4,112,1792]{2,1,0:T(8,128)(2,1)S(1)}, u32[]{:S(2)}, u32[]{:S(2)}) async-start(bf16[4,112,1792]{2,1,0:T(8,128)(2,1)} %joined_sums.1.refs_0_), calls=%async_computation.1 | async-start | bytes 3211264 | tf_op jit(solution)/shard_map/all_to_all | solution.py:77
  253.0 1.5 collective-permute-start.38
  255.0 23.2 %collective-permute-done.41.b_ref = bf16[2,96,768]{2,1,0:T(8,128)(2,1)} collective-permute-done((bf16[2,96,768]{2,1,0:T(8,128)(2,1)S(1)}, bf16[2,96,768]{2,1,0:T(8,128)(2,1)}, u32[]{:S(2)}, u32[]{:S(2)}) %collective-permute-start.41) | collective-permute-done | bytes 294944 | tf_op jit(solution)/shard_map/ppermute | solution.py:32
  278.2 1.8 plus.3
  280.7 2.5 convert_add_fusion
  283.2 2.1 collective-permute-done.42
  286.1 4.1 %all-to-all-done.1 = bf16[4,112,1792]{2,1,0:T(8,128)(2,1)S(1)} async-done(((bf16[4,112,1792]{2,1,0:T(8,128)(2,1)}), bf16[4,112,1792]{2,1,0:T(8,128)(2,1)S(1)}, u32[]{:S(2)}, u32[]{:S(2)}) %all-to-all-start.1) | async-done | bytes 1605664 | tf_op jit(solution)/shard_map/all_to_all | solution.py:77
  (161 shorter events, 28.8 us)
Async XLA Ops:
  0.7 50.6 %copy-start.29 = (s32[1,32,3]{1,0,2:T(1,128)S(1)}, s32[1,32,3]{1,0,2:T(1,128)}, u32[]{:S(2)}) copy-start(s32[1,32,3]{1,0,2:T(1,128)} %param.39) | copy-start | bytes 1156
  0.7 52.8 %copy-start.30 = (f32[192]{0:T(256)S(1)}, f32[192]{0:T(256)}, u32[]{:S(2)}) copy-start(f32[192]{0:T(256)} %param.26) | copy-start | bytes 2308
  0.7 52.8 %copy-start.31 = (f32[192]{0:T(256)S(1)}, f32[192]{0:T(256)}, u32[]{:S(2)}) copy-start(f32[192]{0:T(256)} %param.23) | copy-start | bytes 2308
  0.7 33.4 %collective-permute-start.1 = (bf16[512,768]{1,0:T(8,128)(2,1)}, bf16[512,768]{1,0:T(8,128)(2,1)}, u32[]{:S(2)}, u32[]{:S(2)}) collective-permute-start(bf16[512,768]{1,0:T(8,128)(2,1)} %refs_4_.1), channel_id=1, source_target_pairs={{0,2},{1,3},{2,0},{3,1},{4,6},{5,7},{6,4},{7,5},{8,10},{9,11},{10,... | collective-permute-start | bytes 2359304 | tf_op jit(solution)/shard_map/ppermute | solution.py:32
  5.2 5.5 %collective-permute-start.3 = (bf16[96,768]{1,0:T(8,128)(2,1)}, bf16[96,768]{1,0:T(8,128)(2,1)S(1)}, u32[]{:S(2)}, u32[]{:S(2)}) collective-permute-start(bf16[96,768]{1,0:T(8,128)(2,1)} %pack_queries.1.refs_4_), channel_id=1, source_target_pairs={{0,8},{8,16},{16,24},{24,28},{28,20},{20,12},{12,4},{4,0},{1,9},{9... | collective-permute-start | bytes 442376 | tf_op jit(solution)/shard_map/ppermute | solution.py:55
  6.8 9.7 %collective-permute-start.4 = (bf16[96,768]{1,0:T(8,128)(2,1)}, bf16[96,768]{1,0:T(8,128)(2,1)S(1)}, u32[]{:S(2)}, u32[]{:S(2)}) collective-permute-start(bf16[96,768]{1,0:T(8,128)(2,1)} %pack_queries.1.refs_4_), channel_id=1, source_target_pairs={{0,4},{8,0},{16,8},{24,16},{28,24},{20,28},{12,20},{4,12},{1,5},{9... | collective-permute-start | bytes 442376 | tf_op jit(solution)/shard_map/ppermute | solution.py:55
  10.8 6.0 %collective-permute-start.5 = (bf16[96,768]{1,0:T(8,128)(2,1)S(1)}, bf16[96,768]{1,0:T(8,128)(2,1)S(1)}, u32[]{:S(2)}, u32[]{:S(2)}) collective-permute-start(bf16[96,768]{1,0:T(8,128)(2,1)S(1)} %collective-permute-done.3.refs_5_), channel_id=1, source_target_pairs={{0,8},{8,16},{16,24},{24,28},{28,20},{20,12},{12,4},{4,0},{1,9},{9... | collective-permute-start | bytes 442376 | tf_op jit(solution)/shard_map/ppermute | solution.py:55
  15.9 12.9 %collective-permute-start.13 = (bf16[96,1792]{1,0:T(8,128)(2,1)}, bf16[96,1792]{1,0:T(8,128)(2,1)S(1)}, u32[]{:S(2)}, u32[]{:S(2)}) collective-permute-start(bf16[96,1792]{1,0:T(8,128)(2,1)} %pack_weights.1.a), channel_id=1, source_target_pairs={{0,2},{1,3},{2,0},{3,1},{4,6},{5,7},{6,4},{7,5},{8,10},{9,11},{10,... | collective-permute-start | bytes 1032200 | tf_op jit(solution)/shard_map/ppermute | solution.py:32
  16.5 5.1 %collective-permute-start.6 = (bf16[96,768]{1,0:T(8,128)(2,1)S(1)}, bf16[96,768]{1,0:T(8,128)(2,1)S(1)}, u32[]{:S(2)}, u32[]{:S(2)}) collective-permute-start(bf16[96,768]{1,0:T(8,128)(2,1)S(1)} %collective-permute-done.4.refs_6_), channel_id=1, source_target_pairs={{0,4},{8,0},{16,8},{24,16},{28,24},{20,28},{12,20},{4,12},{1,5},{9... | collective-permute-start | bytes 442376 | tf_op jit(solution)/shard_map/ppermute | solution.py:55
  16.7 5.1 %collective-permute-start.7 = (bf16[96,768]{1,0:T(8,128)(2,1)S(1)}, bf16[96,768]{1,0:T(8,128)(2,1)S(1)}, u32[]{:S(2)}, u32[]{:S(2)}) collective-permute-start(bf16[96,768]{1,0:T(8,128)(2,1)S(1)} %collective-permute-done.5.refs_7_), channel_id=1, source_target_pairs={{0,8},{8,16},{16,24},{24,28},{28,20},{20,12},{12,4},{4,0},{1,9},{9... | collective-permute-start | bytes 442376 | tf_op jit(solution)/shard_map/ppermute | solution.py:55
  21.6 7.2 %collective-permute-start.8 = (bf16[96,768]{1,0:T(8,128)(2,1)S(1)}, bf16[96,768]{1,0:T(8,128)(2,1)S(1)}, u32[]{:S(2)}, u32[]{:S(2)}) collective-permute-start(bf16[96,768]{1,0:T(8,128)(2,1)S(1)} %collective-permute-done.6.refs_8_), channel_id=1, source_target_pairs={{0,4},{8,0},{16,8},{24,16},{28,24},{20,28},{12,20},{4,12},{1,5},{9... | collective-permute-start | bytes 442376 | tf_op jit(solution)/shard_map/ppermute | solution.py:55
  21.9 6.9 %collective-permute-start.9 = (bf16[96,768]{1,0:T(8,128)(2,1)S(1)}, bf16[96,768]{1,0:T(8,128)(2,1)S(1)}, u32[]{:S(2)}, u32[]{:S(2)}) collective-permute-start(bf16[96,768]{1,0:T(8,128)(2,1)S(1)} %collective-permute-done.7.refs_9_), channel_id=1, source_target_pairs={{0,8},{8,16},{16,24},{24,28},{28,20},{20,12},{12,4},{4,0},{1,9},{9... | collective-permute-start | bytes 442376 | tf_op jit(solution)/shard_map/ppermute | solution.py:55
  32.3 16.8 %collective-permute-start.14 = (bf16[96,3584]{1,0:T(8,128)(2,1)}, bf16[96,3584]{1,0:T(8,128)(2,1)S(1)}, u32[]{:S(2)}, u32[]{:S(2)}) collective-permute-start(bf16[96,3584]{1,0:T(8,128)(2,1)} %pair_weights.1.refs_6_), channel_id=1, source_target_pairs={{0,8},{8,16},{16,24},{24,28},{28,20},{20,12},{12,4},{4,0},{1,9},{9... | collective-permute-start | bytes 2064392 | tf_op jit(solution)/shard_map/ppermute | solution.py:55
  34.1 20.0 %collective-permute-start = (bf16[512,768]{1,0:T(8,128)(2,1)S(1)}, bf16[512,768]{1,0:T(8,128)(2,1)}, u32[]{:S(2)}, u32[]{:S(2)}) collective-permute-start(bf16[512,768]{1,0:T(8,128)(2,1)S(1)} %copy-done.5), channel_id=1, source_target_pairs={{0,1},{1,0},{2,3},{3,2},{4,5},{5,4},{6,7},{7,6},{8,9},{9,8},{10,11... | collective-permute-start | bytes 2359304 | tf_op jit(solution)/shard_map/ppermute | solution.py:32
  34.1 21.0 %collective-permute-start.2 = (bf16[512,768]{1,0:T(8,128)(2,1)}, bf16[512,768]{1,0:T(8,128)(2,1)}, u32[]{:S(2)}, u32[]{:S(2)}) collective-permute-start(bf16[512,768]{1,0:T(8,128)(2,1)} %collective-permute-done.1.refs_2_), channel_id=1, source_target_pairs={{0,1},{1,0},{2,3},{3,2},{4,5},{5,4},{6,7},{7,6},{8,9},{9,8},{10,11... | collective-permute-start | bytes 2359304 | tf_op jit(solution)/shard_map/ppermute | solution.py:32
  34.6 20.0 %collective-permute-start.15 = (bf16[96,3584]{1,0:T(8,128)(2,1)}, bf16[96,3584]{1,0:T(8,128)(2,1)S(1)}, u32[]{:S(2)}, u32[]{:S(2)}) collective-permute-start(bf16[96,3584]{1,0:T(8,128)(2,1)} %pair_weights.1.refs_6_), channel_id=1, source_target_pairs={{0,4},{8,0},{16,8},{24,16},{28,24},{20,28},{12,20},{4,12},{1,5},{9... | collective-permute-start | bytes 2064392 | tf_op jit(solution)/shard_map/ppermute | solution.py:55
  49.1 15.7 %collective-permute-start.16 = (bf16[96,3584]{1,0:T(8,128)(2,1)S(1)}, bf16[96,3584]{1,0:T(8,128)(2,1)S(1)}, u32[]{:S(2)}, u32[]{:S(2)}) collective-permute-start(bf16[96,3584]{1,0:T(8,128)(2,1)S(1)} %collective-permute-done.14.refs_7_), channel_id=1, source_target_pairs={{0,8},{8,16},{16,24},{24,28},{28,20},{20,12},{12,4},{4,0},{1,9},{9... | collective-permute-start | bytes 2064392 | tf_op jit(solution)/shard_map/ppermute | solution.py:55
  54.1 31.1 %collective-permute-start.21 = (bf16[96,3584]{1,0:T(8,128)(2,1)}, bf16[96,3584]{1,0:T(8,128)(2,1)}, u32[]{:S(2)}, u32[]{:S(2)}) collective-permute-start(bf16[96,3584]{1,0:T(8,128)(2,1)} %pair_weights.1.refs_6_), channel_id=1, source_target_pairs={{0,1},{1,0},{2,3},{3,2},{4,5},{5,4},{6,7},{7,6},{8,9},{9,8},{10,11... | collective-permute-start | bytes 2064392 | tf_op jit(solution)/shard_map/ppermute | solution.py:32
  54.1 36.0 %collective-permute-start.22 = (bf16[96,3584]{1,0:T(8,128)(2,1)S(1)}, bf16[96,3584]{1,0:T(8,128)(2,1)S(1)}, u32[]{:S(2)}, u32[]{:S(2)}) collective-permute-start(bf16[96,3584]{1,0:T(8,128)(2,1)S(1)} %collective-permute-done.14.refs_7_), channel_id=1, source_target_pairs={{0,1},{1,0},{2,3},{3,2},{4,5},{5,4},{6,7},{7,6},{8,9},{9,8},{10,11... | collective-permute-start | bytes 2064392 | tf_op jit(solution)/shard_map/ppermute | solution.py:32
  54.6 30.7 %collective-permute-start.17 = (bf16[96,3584]{1,0:T(8,128)(2,1)S(1)}, bf16[96,3584]{1,0:T(8,128)(2,1)}, u32[]{:S(2)}, u32[]{:S(2)}) collective-permute-start(bf16[96,3584]{1,0:T(8,128)(2,1)S(1)} %collective-permute-done.15.refs_8_), channel_id=1, source_target_pairs={{0,4},{8,0},{16,8},{24,16},{28,24},{20,28},{12,20},{4,12},{1,5},{9... | collective-permute-start | bytes 2064392 | tf_op jit(solution)/shard_map/ppermute | solution.py:55
  64.8 21.0 %collective-permute-start.18 = (bf16[96,3584]{1,0:T(8,128)(2,1)S(1)}, bf16[96,3584]{1,0:T(8,128)(2,1)}, u32[]{:S(2)}, u32[]{:S(2)}) collective-permute-start(bf16[96,3584]{1,0:T(8,128)(2,1)S(1)} %collective-permute-done.16.refs_9_), channel_id=1, source_target_pairs={{0,8},{8,16},{16,24},{24,28},{28,20},{20,12},{12,4},{4,0},{1,9},{9... | collective-permute-start | bytes 2064392 | tf_op jit(solution)/shard_map/ppermute | solution.py:55
  74.9 13.5 %collective-permute-start.11 = (bf16[2,512,256]{2,1,0:T(8,128)(2,1)}, bf16[2,512,256]{2,1,0:T(8,128)(2,1)S(1)}, u32[]{:S(2)}, u32[]{:S(2)}) collective-permute-start(bf16[2,512,256]{2,1,0:T(8,128)(2,1)} %get-tuple-element.72), channel_id=1, source_target_pairs={{0,2},{1,3},{2,0},{3,1},{4,6},{5,7},{6,4},{7,5},{8,10},{9,11},{10,... | collective-permute-start | bytes 1572872 | tf_op jit(solution)/shard_map/ppermute | solution.py:32
  85.2 5.3 %collective-permute-start.23 = (bf16[96,3584]{1,0:T(8,128)(2,1)S(1)}, bf16[96,3584]{1,0:T(8,128)(2,1)S(1)}, u32[]{:S(2)}, u32[]{:S(2)}) collective-permute-start(bf16[96,3584]{1,0:T(8,128)(2,1)S(1)} %collective-permute-done.15.refs_8_), channel_id=1, source_target_pairs={{0,1},{1,0},{2,3},{3,2},{4,5},{5,4},{6,7},{7,6},{8,9},{9,8},{10,11... | collective-permute-start | bytes 2064392 | tf_op jit(solution)/shard_map/ppermute | solution.py:32
  85.3 18.1 %collective-permute-start.19 = (bf16[96,3584]{1,0:T(8,128)(2,1)}, bf16[96,3584]{1,0:T(8,128)(2,1)}, u32[]{:S(2)}, u32[]{:S(2)}) collective-permute-start(bf16[96,3584]{1,0:T(8,128)(2,1)} %collective-permute-done.17.refs_10_), channel_id=1, source_target_pairs={{0,4},{8,0},{16,8},{24,16},{28,24},{20,28},{12,20},{4,12},{1,5},{9... | collective-permute-start | bytes 2064392 | tf_op jit(solution)/shard_map/ppermute | solution.py:55
  85.8 17.8 %collective-permute-start.20 = (bf16[96,3584]{1,0:T(8,128)(2,1)}, bf16[96,3584]{1,0:T(8,128)(2,1)}, u32[]{:S(2)}, u32[]{:S(2)}) collective-permute-start(bf16[96,3584]{1,0:T(8,128)(2,1)} %collective-permute-done.18.refs_11_), channel_id=1, source_target_pairs={{0,8},{8,16},{16,24},{24,28},{28,20},{20,12},{12,4},{4,0},{1,9},{9... | collective-permute-start | bytes 2064392 | tf_op jit(solution)/shard_map/ppermute | solution.py:55
  88.4 1.6 collective-permute-start.10
  90.0 1.6 collective-permute-start.12
  90.1 15.2 %collective-permute-start.24 = (bf16[96,3584]{1,0:T(8,128)(2,1)S(1)}, bf16[96,3584]{1,0:T(8,128)(2,1)S(1)}, u32[]{:S(2)}, u32[]{:S(2)}) collective-permute-start(bf16[96,3584]{1,0:T(8,128)(2,1)S(1)} %collective-permute-done.16.refs_9_), channel_id=1, source_target_pairs={{0,1},{1,0},{2,3},{3,2},{4,5},{5,4},{6,7},{7,6},{8,9},{9,8},{10,11... | collective-permute-start | bytes 2064392 | tf_op jit(solution)/shard_map/ppermute | solution.py:32
  91.5 13.9 %collective-permute-start.25 = (bf16[96,3584]{1,0:T(8,128)(2,1)}, bf16[96,3584]{1,0:T(8,128)(2,1)S(1)}, u32[]{:S(2)}, u32[]{:S(2)}) collective-permute-start(bf16[96,3584]{1,0:T(8,128)(2,1)} %collective-permute-done.17.refs_10_), channel_id=1, source_target_pairs={{0,1},{1,0},{2,3},{3,2},{4,5},{5,4},{6,7},{7,6},{8,9},{9,8},{10,11... | collective-permute-start | bytes 2064392 | tf_op jit(solution)/shard_map/ppermute | solution.py:32
  92.3 13.1 %collective-permute-start.26 = (bf16[96,3584]{1,0:T(8,128)(2,1)}, bf16[96,3584]{1,0:T(8,128)(2,1)}, u32[]{:S(2)}, u32[]{:S(2)}) collective-permute-start(bf16[96,3584]{1,0:T(8,128)(2,1)} %collective-permute-done.18.refs_11_), channel_id=1, source_target_pairs={{0,1},{1,0},{2,3},{3,2},{4,5},{5,4},{6,7},{7,6},{8,9},{9,8},{10,11... | collective-permute-start | bytes 2064392 | tf_op jit(solution)/shard_map/ppermute | solution.py:32
  103.5 2.5 collective-permute-start.27
  103.6 3.3 %collective-permute-start.28 = (bf16[96,3584]{1,0:T(8,128)(2,1)}, bf16[96,3584]{1,0:T(8,128)(2,1)}, u32[]{:S(2)}, u32[]{:S(2)}) collective-permute-start(bf16[96,3584]{1,0:T(8,128)(2,1)} %collective-permute-done.20.refs_13_), channel_id=1, source_target_pairs={{0,1},{1,0},{2,3},{3,2},{4,5},{5,4},{6,7},{7,6},{8,9},{9,8},{10,11... | collective-permute-start | bytes 2064392 | tf_op jit(solution)/shard_map/ppermute | solution.py:32
  139.5 14.7 %collective-permute-start.33 = (bf16[4,512,768]{2,1,0:T(8,128)(2,1)}, bf16[4,512,768]{2,1,0:T(8,128)(2,1)S(1)}, u32[]{:S(2)}, u32[]{:S(2)}) collective-permute-start(bf16[4,512,768]{2,1,0:T(8,128)(2,1)} %get-tuple-element.82), channel_id=1, source_target_pairs={{0,1},{1,0},{2,3},{3,2},{4,5},{5,4},{6,7},{7,6},{8,9},{9,8},{10,11... | collective-permute-start | bytes 9437192 | tf_op jit(solution)/shard_map/ppermute | solution.py:32
  139.7 14.5 %collective-permute-start.32 = (bf16[3,2,4,96,512]{4,3,2,1,0:T(8,128)(2,1)}, bf16[3,2,4,96,512]{4,3,2,1,0:T(8,128)(2,1)}, u32[]{:S(2)}, u32[]{:S(2)}) collective-permute-start(bf16[3,2,4,96,512]{4,3,2,1,0:T(8,128)(2,1)} %get-tuple-element.80.refs_0_.refs_2_), channel_id=1, source_target_pairs={{0,1},{1,0},{2,3},{3,2},{4,5},{5,4},{6,7},{7,6},{8,9},{9,8},{10,11... | collective-permute-start | bytes 7077896 | tf_op jit(solution)/shard_map/ppermute | solution.py:32
  140.1 12.3 %collective-permute-start.29 = (bf16[512,256]{1,0:T(8,128)(2,1)}, bf16[512,256]{1,0:T(8,128)(2,1)S(1)}, u32[]{:S(2)}, u32[]{:S(2)}) collective-permute-start(bf16[512,256]{1,0:T(8,128)(2,1)} %get-tuple-element.74), channel_id=1, source_target_pairs={{0,1},{1,0},{2,3},{3,2},{4,5},{5,4},{6,7},{7,6},{8,9},{9,8},{10,11... | collective-permute-start | bytes 786440 | tf_op jit(solution)/shard_map/ppermute | solution.py:32
  140.2 12.2 %collective-permute-start.30 = (bf16[512,256]{1,0:T(8,128)(2,1)}, bf16[512,256]{1,0:T(8,128)(2,1)}, u32[]{:S(2)}, u32[]{:S(2)}) collective-permute-start(bf16[512,256]{1,0:T(8,128)(2,1)} %get-tuple-element.75), channel_id=1, source_target_pairs={{0,2},{1,3},{2,0},{3,1},{4,6},{5,7},{6,4},{7,5},{8,10},{9,11},{10,... | collective-permute-start | bytes 786440 | tf_op jit(solution)/shard_map/ppermute | solution.py:32
  140.8 13.4 %collective-permute-start.31 = (bf16[512,256]{1,0:T(8,128)(2,1)}, bf16[512,256]{1,0:T(8,128)(2,1)}, u32[]{:S(2)}, u32[]{:S(2)}) collective-permute-start(bf16[512,256]{1,0:T(8,128)(2,1)} %get-tuple-element.76), channel_id=1, source_target_pairs={{0,3},{1,2},{2,1},{3,0},{4,7},{5,6},{6,5},{7,4},{8,11},{9,10},{10,... | collective-permute-start | bytes 786440 | tf_op jit(solution)/shard_map/ppermute | solution.py:32
  162.2 70.4 %all-to-all-start = ((bf16[4,2,2,96,768]{4,3,2,1,0:T(8,128)(2,1)}), bf16[4,2,2,96,768]{4,3,2,1,0:T(8,128)(2,1)S(1)}, u32[]{:S(2)}, u32[]{:S(2)}) async-start(bf16[4,2,2,96,768]{4,3,2,1,0:T(8,128)(2,1)} %row_dot.3.refs_12_), calls=%async_computation | async-start | bytes 4718592 | tf_op jit(solution)/shard_map/all_to_all | solution.py:77
  175.2 36.8 %collective-permute-start.36 = (bf16[2,1,4,96,1024]{4,3,2,1,0:T(8,128)(2,1)}, bf16[2,1,4,96,1024]{4,3,2,1,0:T(8,128)(2,1)}, u32[]{:S(2)}, u32[]{:S(2)}) collective-permute-start(bf16[2,1,4,96,1024]{4,3,2,1,0:T(8,128)(2,1)} %get-tuple-element.87.refs_11_), channel_id=1, source_target_pairs={{0,4},{4,0},{8,12},{12,8},{16,20},{20,16},{24,28},{28,24},{1,5},{5... | collective-permute-start | bytes 4718600 | tf_op jit(solution)/shard_map/ppermute | solution.py:37
  175.8 1.2 collective-permute-start.34
  177.0 4.1 %collective-permute-start.35 = (f32[16,768]{1,0:T(8,128)S(1)}, f32[16,768]{1,0:T(8,128)S(1)}, u32[]{:S(2)}, u32[]{:S(2)}) collective-permute-start(f32[16,768]{1,0:T(8,128)S(1)} %add.23), channel_id=1, source_target_pairs={{0,2},{1,3},{2,0},{3,1},{4,6},{5,7},{6,4},{7,5},{8,10},{9,11},{10,... | collective-permute-start | bytes 147464 | tf_op jit(solution)/shard_map/ppermute | solution.py:32
  219.7 7.9 %collective-permute-start.37 = (bf16[2,512,768]{2,1,0:T(8,128)(2,1)}, bf16[2,512,768]{2,1,0:T(8,128)(2,1)}, u32[]{:S(2)}, u32[]{:S(2)}) collective-permute-start(bf16[2,512,768]{2,1,0:T(8,128)(2,1)} %spread.2.refs_9_), channel_id=1, source_target_pairs={{0,1},{1,0},{2,3},{3,2},{4,5},{5,4},{6,7},{7,6},{8,9},{9,8},{10,11... | collective-permute-start | bytes 4718600 | tf_op jit(solution)/shard_map/ppermute | solution.py:32
  219.7 25.0 %collective-permute-start.40 = (bf16[1,1,4,96,1024]{4,3,2,1,0:T(8,128)(2,1)S(1)}, bf16[1,1,4,96,1024]{4,3,2,1,0:T(8,128)(2,1)}, u32[]{:S(2)}, u32[]{:S(2)}) collective-permute-start(bf16[1,1,4,96,1024]{4,3,2,1,0:T(8,128)(2,1)S(1)} %copy-done.6), channel_id=1, source_target_pairs={{0,2},{1,3},{2,0},{3,1},{4,6},{5,7},{6,4},{7,5},{8,10},{9,11},{10,... | collective-permute-start | bytes 2359304 | tf_op jit(solution)/shard_map/ppermute | solution.py:32
  226.8 17.9 %collective-permute-start.39 = (bf16[1,1,4,112,768]{4,3,2,1,0:T(8,128)(2,1)}, bf16[1,1,4,112,768]{4,3,2,1,0:T(8,128)(2,1)}, u32[]{:S(2)}, u32[]{:S(2)}) collective-permute-start(bf16[1,1,4,112,768]{4,3,2,1,0:T(8,128)(2,1)} %get-tuple-element.104.refs_2_), channel_id=1, source_target_pairs={{0,4},{4,0},{8,12},{12,8},{16,20},{20,16},{24,28},{28,24},{1,5},{5... | collective-permute-start | bytes 2064392 | tf_op jit(solution)/shard_map/ppermute | solution.py:37
  248.0 42.2 %all-to-all-start.1 = ((bf16[4,112,1792]{2,1,0:T(8,128)(2,1)}), bf16[4,112,1792]{2,1,0:T(8,128)(2,1)S(1)}, u32[]{:S(2)}, u32[]{:S(2)}) async-start(bf16[4,112,1792]{2,1,0:T(8,128)(2,1)} %joined_sums.1.refs_0_), calls=%async_computation.1 | async-start | bytes 3211264 | tf_op jit(solution)/shard_map/all_to_all | solution.py:77
  253.0 27.8 %collective-permute-start.38 = (bf16[512,768]{1,0:T(8,128)(2,1)}, bf16[512,768]{1,0:T(8,128)(2,1)}, u32[]{:S(2)}, u32[]{:S(2)}) collective-permute-start(bf16[512,768]{1,0:T(8,128)(2,1)} %get-tuple-element.106.refs_0_), channel_id=1, source_target_pairs={{0,2},{1,3},{2,0},{3,1},{4,6},{5,7},{6,4},{7,5},{8,10},{9,11},{10,... | collective-permute-start | bytes 2359304 | tf_op jit(solution)/shard_map/ppermute | solution.py:32
  254.4 23.7 %collective-permute-start.41 = (bf16[2,96,768]{2,1,0:T(8,128)(2,1)S(1)}, bf16[2,96,768]{2,1,0:T(8,128)(2,1)}, u32[]{:S(2)}, u32[]{:S(2)}) collective-permute-start(bf16[2,96,768]{2,1,0:T(8,128)(2,1)S(1)} %copy-done.15), channel_id=1, source_target_pairs={{0,2},{1,3},{2,0},{3,1},{4,6},{5,7},{6,4},{7,5},{8,10},{9,11},{10,... | collective-permute-start | bytes 884744 | tf_op jit(solution)/shard_map/ppermute | solution.py:32
  280.0 5.4 %collective-permute-start.42 = (bf16[1,96,768]{2,1,0:T(8,128)(2,1)}, bf16[1,96,768]{2,1,0:T(8,128)(2,1)S(1)}, u32[]{:S(2)}, u32[]{:S(2)}) collective-permute-start(bf16[1,96,768]{2,1,0:T(8,128)(2,1)} %get-tuple-element.112), channel_id=1, source_target_pairs={{0,4},{4,0},{8,12},{12,8},{16,20},{20,16},{24,28},{28,24},{1,5},{5... | collective-permute-start | bytes 442376 | tf_op jit(solution)/shard_map/ppermute | solution.py:37
  (34 other events, 455.5 us)

commit v4 on v3

--- a/solution.py
+++ b/solution.py
@@ -19,7 +19,9 @@
 PAD = 256
 LANES = 128
 SUM_ROW = 10
-GATE = 6
+SUM_ROWS = 16
+BELOW = SUM_ROWS * (D // PAD)
+GATE = 5
 
 masked_score = -1e30
 EPSILON = 1e-12
@@ -35,6 +37,12 @@
 def dp_swap(array, bit):
     size = lax.axis_size("dp")
     return lax.ppermute(array, "dp", [(t, t ^ bit) for t in range(size)])
+
+
+def swap_both(array):
+    size = lax.axis_size("dp") * 4
+    axes = ("dp", "tensor")
+    return lax.ppermute(array, axes, [(t, t ^ 6) for t in range(size)])
 
 
 def ring_order(size):
@@ -270,16 +278,13 @@
     if carried:
         key_before, value_before = take(2)
         query_before = take(pieces - len(chosen))
-        (small,) = take(1)
+        (small_ref,) = take(1)
         outs = take(pieces)
         (tail,) = take(1)
         key_sum, value_sum, key_kept, value_kept, row_sums = take(5)
     else:
-        (small,) = take(1)
         outs = take(len(chosen))
         key_sum, value_sum = take(2)
-        (small_out,) = take(1)
-        small_out[...] = small[...]
     rows, up_rows, sems = refs
     own_rows = own_blocks * BLK
     copies = [
@@ -357,12 +362,19 @@
             return carry
 
         lax.fori_loop(0, own_blocks, finish, 0)
-    slot = lax.broadcasted_iota(jnp.int32, small.shape, 0)
+    slot = lax.broadcasted_iota(jnp.int32, tail.shape, 0)
     whole = jnp.sum(row_sums[...], axis=0, keepdims=True)
-    tail[...] = jnp.where(slot == SUM_ROW, whole, small[...]).astype(bf16)
-
-
-def attend_backward(parts, ups, totals, table, bias, heads, chosen, small, waited=(), before=None):
+    small = small_ref[...]
+    for at in range(len(chosen)):
+        parts = [
+            up_rows[at, own_rows + k * SUM_ROWS : own_rows + (k + 1) * SUM_ROWS, :]
+            for k in range(BELOW // SUM_ROWS)
+        ]
+        small = small + jnp.concatenate(parts, axis=1).astype(f32)
+    tail[...] = jnp.where(slot == SUM_ROW, whole, small).astype(bf16)
+
+
+def attend_backward(parts, ups, totals, table, bias, heads, chosen, small=None, waited=(), before=None):
     own_rows = parts[0].shape[0]
     pieces = len(parts)
     n = len(chosen)
@@ -372,8 +384,8 @@
     work = n * own_rows * KEYS * heads
     sum_shape = (pieces * own_rows, PAD)
     if before is None:
-        outs = [((own_rows, PAD), bf16)] * n + [(sum_shape, f32)] * 2 + [((16, 3 * PAD), f32)]
-        extra, extra_specs, scratch = [small], [vmem], []
+        outs = [((own_rows, PAD), bf16)] * n + [(sum_shape, f32)] * 2
+        extra, extra_specs, scratch = [], [], []
     else:
         outs = [((own_rows, 3 * PAD), bf16)] * pieces + [((16, 3 * PAD), bf16)]
         extra = [*before, small]
@@ -393,7 +405,7 @@
         scratch_shapes=scratch
         + [
             pltpu.VMEM((pieces * own_rows, 3 * PAD), bf16),
-            pltpu.VMEM((n, own_rows, PAD), bf16),
+            pltpu.VMEM((n, own_rows + BELOW, PAD), bf16),
             pltpu.SemaphoreType.DMA((pieces + n + 2,)),
         ],
         cost_estimate=cost(30 * work * HD, 12 << 20, work),
@@ -483,7 +495,9 @@
     first = []
     for s in range(teams):
         source = mixed[s] if places[s] is None else mixed[s].at[places[s]]
-        first.append(pltpu.make_async_copy(source, o_buf.at[s], in_sems.at[s]))
+        first.append(
+            pltpu.make_async_copy(source, o_buf.at[s, pl.ds(0, x_in.shape[0]), :], in_sems.at[s])
+        )
     first.append(pltpu.make_async_copy(x_in, x_buf, in_sems.at[teams]))
     upstream_copy = pltpu.make_async_copy(g_in, g_buf, in_sems.at[teams + 1])
     fetched = ([], [], [])
@@ -543,9 +557,9 @@
         copy.wait()
     for n in range(D // cut):
         cols = slice(n * cut, (n + 1) * cut)
-        total = contract(o_buf[0], out_w[0, cols, :], (1, 1))
+        total = contract(o_buf[0, :rows, :], out_w[0, cols, :], (1, 1))
         for s in range(1, teams):
-            total = total + contract(o_buf[s], out_w[s, cols, :], (1, 1))
+            total = total + contract(o_buf[s, :rows, :], out_w[s, cols, :], (1, 1))
         wide_buf[:, cols] = total
 
     def first_norm(i, at):
@@ -637,9 +651,6 @@
     tiles(first_back)
     leave(last_buf, after_out)
     leave_turned(2, last_buf, turned_out.at[2])
-    for s in (2, 3, 1, 0):
-        o_buf[s] = contract(last_buf[...], out_w[s], (1, 0)).astype(bf16)
-        leave(o_buf.at[s], back_out[s])
     small[...] = jnp.zeros_like(small)
     for k in range(6):
         small[k : k + 1, :] = jnp.sum(sums[8 * k : 8 * k + 8, :], axis=0, keepdims=True)
@@ -647,6 +658,13 @@
         small[pl.ds(6 + (s ^ me), 1), :] = jnp.sum(
             up_sums[8 * s : 8 * s + 8, :], axis=0, keepdims=True
         )
+    for s in (2, 3, 1, 0):
+        o_buf[s, :rows, :] = contract(last_buf[...], out_w[s], (1, 0)).astype(bf16)
+        for k in range(D // PAD):
+            o_buf[s, rows + k * SUM_ROWS : rows + (k + 1) * SUM_ROWS, :] = small[
+                :, k * PAD : (k + 1) * PAD
+            ].astype(bf16)
+        leave(o_buf.at[s], back_out[s])
     for copy in leaving:
         copy.wait()
 
@@ -664,14 +682,14 @@
     return pl.pallas_call(
         partial(rows_kernel, [at for _, at in mixed], len(weights)),
         out_shape=[low, pair, pair, turned]
-        + [struct((rows, PAD), bf16)] * teams
+        + [struct((rows + BELOW, PAD), bf16)] * teams
         + [low, struct((16, D), f32)],
         in_specs=[SMEM_SPEC]
         + [ANY_SPEC] * (teams + 2 + len(weights))
         + [VMEM_SPEC] * 2,
         out_specs=[ANY_SPEC] * (5 + teams) + [VMEM_SPEC],
         scratch_shapes=[
-            pltpu.VMEM((teams, rows, PAD), bf16),
+            pltpu.VMEM((teams, rows + BELOW, PAD), bf16),
             pltpu.VMEM((rows, D), bf16),
             pltpu.VMEM((rows, D), bf16),
             pltpu.VMEM((teams, D, PAD), bf16),
@@ -714,7 +732,7 @@
         lows.append(lows[-1] + rights[0][0][0].shape[2] // cut)
     high = bits * far * part
     below = 0 if tail is None else tail.shape[0]
-    cuts = 2 if cut_by in ("bits", "rights") else 1
+    cuts = {"bits": 2, "quads": 4}.get(cut_by, 1)
 
     def kernel(*refs):
         refs = list(refs)
@@ -743,8 +761,8 @@
                     for b in range(bits):
                         if cut_by == "bits":
                             to = outs[b].at[i, 0]
-                        elif cut_by == "rights":
-                            to = outs[i].at[0, b]
+                        elif cut_by == "quads":
+                            to = outs[2 * b + i].at[0, 0]
                         else:
                             to = outs[0].at[i, b]
                         if below:
@@ -774,7 +792,7 @@
         specs.append(pl.BlockSpec((below, cut), lambda j: (0, j)))
         arrays.append(tail)
     width = lows[-1] * cut
-    lead = (count // 2 if cut_by == "rights" else count, bits // 2 if cut_by == "bits" else bits)
+    lead = (1 if cut_by == "quads" else count, 1 if cut_by in ("bits", "quads") else bits)
     return pl.pallas_call(
         kernel,
         grid=(lows[-1],),
@@ -815,6 +833,20 @@
     )(a, b, *waited)
 
 
+def held(array, waited):
+    def kernel(a_ref, *refs):
+        refs[-1][...] = a_ref[...]
+
+    return pl.pallas_call(
+        kernel,
+        out_shape=struct(array.shape, array.dtype),
+        in_specs=[VMEM_SPEC] + [ANY_SPEC] * len(waited),
+        out_specs=VMEM_SPEC,
+        cost_estimate=cost(array.size, 8 * array.size),
+        name="held",
+    )(array, *waited)
+
+
 def fold(blocks, waited=()):
     def kernel(ref, *refs):
         for k in range(2):
@@ -833,34 +865,29 @@
     )(blocks, *waited)
 
 
-def joined_sums(pairs, waited=()):
-    heights = [a.shape[1] for a, _ in pairs]
-    rows = max(heights)
-    widths = [a.shape[2] for a, _ in pairs]
-    count = 2 * len(pairs)
+def joined_sums(lists, waited=(), apart=False):
+    rows, width = lists[0].shape[1:]
+    count = len(lists)
 
     def kernel(*refs):
-        out = refs[-1]
         mine = lax.axis_index("dp") // 2
         for z in range(4):
-            at = 0
-            to = out.at[z ^ mine]
-            for k, width in enumerate(widths):
-                if heights[k] < rows:
-                    to[heights[k] :, at : at + width] = jnp.zeros((rows - heights[k], width), bf16)
-                to[: heights[k], at : at + width] = (
-                    refs[2 * k][z].astype(f32) + refs[2 * k + 1][z].astype(f32)
-                ).astype(bf16)
-                at += width
+            total = refs[0][z].astype(f32)
+            for k in range(1, count):
+                total = total + refs[k][z].astype(f32)
+            if apart:
+                refs[count + len(waited) + z][...] = total.astype(bf16)
+            else:
+                refs[-1][z ^ mine] = total.astype(bf16)
 
     return pl.pallas_call(
         kernel,
-        out_shape=struct((4, rows, sum(widths)), bf16),
+        out_shape=[struct((rows, width), bf16)] * 4 if apart else struct((4, rows, width), bf16),
         in_specs=[VMEM_SPEC] * count + [ANY_SPEC] * len(waited),
-        out_specs=VMEM_SPEC,
-        cost_estimate=cost(rows * sum(widths) * 4, rows * sum(widths) * 24),
+        out_specs=[VMEM_SPEC] * 4 if apart else VMEM_SPEC,
+        cost_estimate=cost(rows * width * 4 * count, rows * width * 8 * count),
         name="joined_sums",
-    )(*[array for pair in pairs for array in pair], *waited)
+    )(*lists, *waited)
 
 
 def spread(grads, weight, added=None, after=None, waited=()):
@@ -911,11 +938,11 @@
     )(w_query, w_key, w_value)
 
 
-def pack_weights(w_up, w_out, w_down):
+def pack_weights(w_up, w_out, w_down, waited):
     rows, hidden = w_up.shape
     width = w_out.shape[0]
 
-    def kernel(up, out, down, own):
+    def kernel(up, out, down, _, own):
         own[:, :hidden] = up[...]
         own[:, hidden : hidden + PAD] = jnp.zeros((rows, PAD), bf16)
         own[:, hidden : hidden + width] = out[...].T
@@ -924,11 +951,11 @@
     return pl.pallas_call(
         kernel,
         out_shape=struct((rows, 2 * hidden + PAD), bf16),
-        in_specs=[VMEM_SPEC] * 3,
+        in_specs=[VMEM_SPEC] * 3 + [ANY_SPEC],
         out_specs=VMEM_SPEC,
         cost_estimate=cost(rows * hidden, 2 << 20),
         name="pack_weights",
-    )(w_up, w_out, w_down)
+    )(w_up, w_out, w_down, waited)
 
 
 def pair_weights(own, beyond, hidden, waited):
@@ -1077,19 +1104,16 @@
 
     table, bias = block_tables(lengths, global_raw, random_raw, own_rows // BLK, teams)
 
-    x2 = swap(hidden_in, 2)
-    x1 = swap(hidden_in, 1)
-    x3 = swap(x2, 1)
-    x_parts = [hidden_in, x1, x2, x3]
-
     qkv_b = jnp.concatenate(
         [jnp.pad(b_query, (0, PAD - width)), jnp.zeros((PAD,), f32), jnp.pad(b_value, (0, PAD - width))]
     )
     halved = members == 8
     if halved:
-        qkv_pieces = ring_pieces(pack_queries(w_query, w_key, w_value))
-        own = pack_weights(w_up, w_out, w_down)
-        shard = pair_weights(own, swap(own, 2), hidden, qkv_pieces[GATE:])
+        queries = pack_queries(w_query, w_key, w_value)
+        own = pack_weights(w_up, w_out, w_down, queries)
+        qkv_pieces = ring_pieces(queries)
+        beyond_own = swap(own, 2)
+        shard = pair_weights(own, beyond_own, hidden, qkv_pieces[GATE:])
     else:
         qkv_shard = jnp.concatenate([padded(w_query), padded(w_key), padded(w_value)], axis=1)
         qkv_pieces = [lax.all_gather(qkv_shard, "dp", axis=0, tiled=True)]
@@ -1098,7 +1122,10 @@
         weights = jnp.swapaxes(weights.reshape(members, teams, *shard.shape), 0, 1)
         weights = [weights.reshape(teams, D, shard.shape[1])]
 
-    qkv, x_turned, qkv_w = project_in(x_parts, qkv_pieces, qkv_b[None])
+    x2 = swap(held(hidden_in, (beyond_own,)) if halved else hidden_in, 2)
+    x1 = swap(hidden_in, 1)
+    x3 = swap(x2, 1)
+    qkv, x_turned, qkv_w = project_in([hidden_in, x1, x2, x3], qkv_pieces, qkv_b[None])
     far_mixed, (t2, t3) = attend_forward(qkv, table, bias, heads, (2, 3))
     far_mixed = swap(far_mixed, 2)
     near_mixed, (t0, t1) = attend_forward(qkv, table, bias, heads, (0, 1))
@@ -1125,10 +1152,7 @@
     after_low, small = results[4 + teams :]
     ups = [backs[0]] + [swap(backs[s], s) for s in range(1, teams)]
     totals = [t0, t1, t2, t3]
-    before = attend_backward(qkv, ups[:1], totals[:1], table, bias, heads, (0,), small)
-    small = before[3]
-    small = small + swap(small, 1)
-    small = small + swap(small, 2)
+    before = attend_backward(qkv, ups[:1], totals[:1], table, bias, heads, (0,))
 
     next_rows, next_turned = swap(far_rows, 1), swap(turned, 1)
     down_group = (
@@ -1146,8 +1170,9 @@
     if halved:
         (down_gone,) = row_dot([down_group], 2, "far", (before[0], *ups[1:]))
         down_blocks = far_exchange(down_gone)
-        up_kept, up_gone = row_dot([up_group, out_group], 2, "bits", (down_gone,))
-        up_away = dp_swap(up_gone, 1)
+        up_quads = row_dot([up_group, out_group], 2, "quads", (down_gone,))
+        up_gone = up_quads[3]
+        up_away = [swap(up_quads[1], 2), dp_swap(up_quads[2], 1), swap_both(up_gone)]
         waited = (up_gone,)
     else:
         down_sums = row_dot([down_group], 2)[0].reshape(2, D, -1)
@@ -1166,35 +1191,31 @@
         (before[1], before[2], before[0]),
     )
     grads, tail = results[:4], results[4]
-    waited = ()
-    if halved:
-        up_here, up_next = plus(up_kept, up_away, (grads[0],), 2)
-        up_away = swap(up_next, 2)
-        waited = (up_next,)
-    parts = spread([grads[3], grads[1]], qkv_w, waited=waited)
-    spread_away = swap(parts, 1)
     qkv_group = ([(x[None], 0) for x in x_turned], [[(g[None], 0)] for g in grads])
     if halved:
-        kept, gone = row_dot([qkv_group], 1, "bits", (parts,), tail)
+        kept, gone = row_dot([qkv_group], 1, "bits", (), tail)
         away = dp_swap(gone, 1)
-        beyond, here = spread([grads[2], grads[0]], qkv_w, spread_away, after_low, (gone,))
+        parts = spread([grads[3], grads[1]], qkv_w, waited=(gone,))
+        spread_away = swap(parts, 1)
+        up_blocks = joined_sums([a[0, 0] for a in (up_quads[0], *up_away)], (parts,))
+        up_arrived = far_exchange(up_blocks)
+        beyond, here = spread([grads[2], grads[0]], qkv_w, spread_away, after_low, (up_blocks,))
         beyond_away = swap(beyond, 2)
         down_here, down_next = fold(down_blocks, (beyond,))
         down_away = swap(down_next, 2)
-        blocks = joined_sums(
-            [(kept[0, 0], away[0, 0]), (up_here[0, 0], up_away[0, 0])], (down_next,)
-        )
-        total = far_exchange(blocks)
+        blocks = joined_sums([kept[0, 0], away[0, 0]], (down_next,))
+        arrived = far_exchange(blocks)
+        qkv_part = jnp.sum(arrived.astype(f32), axis=0)
         down_here, down_next = plus(down_here, down_away, (blocks,), 2)
         down_away = dp_swap(down_next, 1)
         down_part = down_here[0].astype(f32) + down_away[0].astype(f32)
-        total = jnp.sum(total.astype(f32), axis=0)
-        qkv_part, up_part = total[:, : 3 * PAD], total[:-16, 3 * PAD :]
+        up_part = jnp.sum(up_arrived.astype(f32), axis=0)
         qkv_part, small = qkv_part[:-16], qkv_part[-16:]
     else:
         blocks = row_dot([qkv_group], 1)[0].reshape(D, -1)
         qkv_part = dp_scatter_sum(blocks)
         small = lax.psum(tail.astype(f32), "dp")
+        spread_away = swap(spread([grads[3], grads[1]], qkv_w), 1)
         beyond, here = spread([grads[2], grads[0]], qkv_w, spread_away, after_low)
         beyond_away = swap(beyond, 2)
         down_part = dp_scatter_sum(down_sums[0] + swap(down_sums[1], 2))

time: 295 us -> 263 us (0.89)
  waiting for transfers between devices: 93.6 us -> 58.5 us
  starting transfers between devices: 40.4 us -> 43.9 us
    ppermute x26 -> x24, waiting for transfers between devices: 37.6 us -> 17.3 us  [swap(): return lax.ppermute(array, 'tensor', [(t, t ^ bit) for t in range(size)])]
    ppermute x14, waiting for transfers between devices: 33.2 us -> 23.6 us  [ring_send(): lax.ppermute(array, 'dp', [(order[i], order[(i + step) % size]) for i in...]
    ppermute x3, waiting for transfers between devices: 18.6 us -> 9.49 us  [dp_swap(): return lax.ppermute(array, 'dp', [(t, t ^ bit) for t in range(size)])]
    pallas_call x1 -> x3, Pallas kernels: 3.3 us -> 7.52 us  [the longest x2 5.46 us: joined_sums(): pl.pallas_call(kernel, out_shape=[struct((rows, width), bf16)] * 4 if apa...]
    ppermute x26 -> x24, starting transfers between devices: 13.5 us -> 9.32 us  [swap(): return lax.ppermute(array, 'tensor', [(t, t ^ bit) for t in range(size)])]
    pallas_call x2 -> x1, Pallas kernels: 5.07 us -> 1.81 us  [plus(): pl.pallas_call(kernel, out_shape=[struct((lead, *a.shape[1:]), dtype)] *...]
    all_to_all x2 -> x3, waiting for transfers between devices: 4.14 us -> 7.19 us  [far_exchange(): lax.all_to_all(blocks, 'dp', 0, 0, axis_index_groups=groups, tiled=True)]
    all_to_all x2 -> x3, starting transfers between devices: 9.77 us -> 12.6 us  [far_exchange(): lax.all_to_all(blocks, 'dp', 0, 0, axis_index_groups=groups, tiled=True)]
  transfers between devices with their start and end apart: 45 -> 45, of which waited for: 18 -> 20; matrix products, arithmetic and copies ran while one was open for 3% -> 4% of each run, Pallas kernels for 33% -> 38%
where the time goes in v4:
time: 263 us; the launch traced here: 262 us
  Pallas kernels  140 us (53%)
  waiting for transfers between devices  58.5 us (22%)
  starting transfers between devices  43.9 us (17%)
  local copies, waits for them, and re-layouts  14 us (5%)
  other arithmetic  4.36 us (2%)
    pallas_call x1, Pallas kernels, layer_rows(): pl.pallas_call(partial(rows_kernel, [at for _, at in mixed], len(weights)...  32.3 us
    pallas_call x2, Pallas kernels, attend_backward(): pl.pallas_call(partial(attend_back_kernel, heads, chosen, pieces, own_blo...  32.2 us
    ppermute x14, waiting for transfers between devices, ring_send(): lax.ppermute(array, 'dp', [(order[i], order[(i + step) % size]) for i in...  23.6 us
    pallas_call x3, Pallas kernels, row_dot(): pl.pallas_call(kernel, grid=(lows[-1],), out_shape=[struct((far, *lead, p...  21 us
    pallas_call x2, Pallas kernels, attend_forward(): pl.pallas_call(partial(attend_kernel, heads, chosen, pieces, own_blocks),...  17.6 us
    ppermute x24, waiting for transfers between devices, swap(): return lax.ppermute(array, 'tensor', [(t, t ^ bit) for t in range(size)])  17.3 us
    ppermute x14, starting transfers between devices, ring_send(): lax.ppermute(array, 'dp', [(order[i], order[(i + step) % size]) for i in...  16.9 us
    all_to_all x3, starting transfers between devices, far_exchange(): lax.all_to_all(blocks, 'dp', 0, 0, axis_index_groups=groups, tiled=True)  12.6 us
  transfers between devices with their start and end apart: 45, of which 20 were waited for; matrix products, arithmetic and copies ran while one was open for 4% of the time, Pallas kernels for 38%

profile of v4, /device:TPU:0, one launch (start us, length us, event | category | flops | bytes accessed | tf_op | source)
XLA Modules:
  0.0 262.1 jit_solution(4943754086683166823)
XLA Ops:
  0.7 1.5 pack_queries.1._.refs_4_
  2.2 3.0 %collective-permute-start.4 = (bf16[96,768]{1,0:T(8,128)(2,1)}, bf16[96,768]{1,0:T(8,128)(2,1)S(1)}, u32[]{:S(2)}, u32[]{:S(2)}) collective-permute-start(bf16[96,768]{1,0:T(8,128)(2,1)} %pack_queries.1._.refs_4_), channel_id=1, source_target_pairs={{0,8},{8,16},{16,24},{24,28},{28,20},{20,12},{12,4},{4,0},{1,9},{9... | collective-permute-start | bytes 442376 | tf_op jit(solution)/shard_map/ppermute | solution.py:63
  5.2 1.7 copy.38.down
  6.9 1.9 pack_weights.1.a
  8.8 1.6 collective-permute-start.1
  10.8 1.6 collective-permute-start.6
  12.4 3.3 %collective-permute-done.5.refs_6_ = bf16[96,768]{1,0:T(8,128)(2,1)S(1)} collective-permute-done((bf16[96,768]{1,0:T(8,128)(2,1)}, bf16[96,768]{1,0:T(8,128)(2,1)S(1)}, u32[]{:S(2)}, u32[]{:S(2)}) %collective-permute-start.5) | collective-permute-done | bytes 147488 | tf_op jit(solution)/shard_map/ppermute | solution.py:63
  16.2 1.6 collective-permute-start.8
  19.4 2.1 held.1
  23.4 1.6 collective-permute-start.10
  25.0 3.1 %collective-permute-done.9.refs_10_.refs_1_ = bf16[96,768]{1,0:T(8,128)(2,1)S(1)} collective-permute-done((bf16[96,768]{1,0:T(8,128)(2,1)S(1)}, bf16[96,768]{1,0:T(8,128)(2,1)S(1)}, u32[]{:S(2)}, u32[]{:S(2)}) %collective-permute-start.9) | collective-permute-done | bytes 147488 | tf_op jit(solution)/shard_map/ppermute | solution.py:63
  29.4 2.0 pair_weights.1.refs_6_
  31.4 1.6 collective-permute-start.14
  32.9 6.9 %collective-permute-done.2.refs_2_ = bf16[512,768]{1,0:T(8,128)(2,1)} collective-permute-done((bf16[512,768]{1,0:T(8,128)(2,1)}, bf16[512,768]{1,0:T(8,128)(2,1)}, u32[]{:S(2)}, u32[]{:S(2)}) %collective-permute-start.2) | collective-permute-done | bytes 786464 | tf_op jit(solution)/shard_map/ppermute | solution.py:34
  40.4 6.8 %collective-permute-done.14.refs_7_ = bf16[96,3584]{1,0:T(8,128)(2,1)S(1)} collective-permute-done((bf16[96,3584]{1,0:T(8,128)(2,1)}, bf16[96,3584]{1,0:T(8,128)(2,1)S(1)}, u32[]{:S(2)}, u32[]{:S(2)}) %collective-permute-start.14) | collective-permute-done | bytes 688160 | tf_op jit(solution)/shard_map/ppermute | solution.py:63
  47.2 1.6 collective-permute-start.16
  50.1 1.5 block_tables.1
  52.7 5.2 %collective-permute-done.15.refs_8_ = bf16[96,3584]{1,0:T(8,128)(2,1)S(1)} collective-permute-done((bf16[96,3584]{1,0:T(8,128)(2,1)}, bf16[96,3584]{1,0:T(8,128)(2,1)S(1)}, u32[]{:S(2)}, u32[]{:S(2)}) %collective-permute-start.15) | collective-permute-done | bytes 688160 | tf_op jit(solution)/shard_map/ppermute | solution.py:63
  58.5 2.8 %collective-permute-done.16.refs_9_ = bf16[96,3584]{1,0:T(8,128)(2,1)S(1)} collective-permute-done((bf16[96,3584]{1,0:T(8,128)(2,1)S(1)}, bf16[96,3584]{1,0:T(8,128)(2,1)S(1)}, u32[]{:S(2)}, u32[]{:S(2)}) %collective-permute-start.16) | collective-permute-done | bytes 688160 | tf_op jit(solution)/shard_map/ppermute | solution.py:63
  61.3 1.6 collective-permute-start.18
  62.9 8.3 %project_in.1 = (bf16[512,768]{1,0:T(8,128)(2,1)}, bf16[512,768]{1,0:T(8,128)(2,1)}, bf16[512,768]{1,0:T(8,128)(2,1)}, bf16[512,768]{1,0:T(8,128)(2,1)}, bf16[2,...) custom-call(bf16[512,768]{1,0:T(8,128)(2,1)} %refs_4_.1, ...), custom_call_target="tpu_custom_call" | custom-call | flops 4831838208 | bytes 25165824 | tf_op jit(solution)/shard_map/project_in/pallas_call | solution.py:1045
  71.1 8.8 %attend_forward.3 = (bf16[2,512,256]{2,1,0:T(8,128)(2,1)}, f32[512,128]{1,0:T(8,128)}, f32[512,128]{1,0:T(8,128)}) custom-call(s32[32,128]{1,0:T(8,128)} %get-tuple-element.64.table, bf16[512,768]{1,0:T(8,128)(2,1)} %get-tuple-element.65.refs_0_, bf16[512,768]{1,0:T(8,128)(2,1)} %get-tuple-element.66.refs_1_, bf16[512,768]{1,0:T(8,128)(2,1)} %get-tuple-element.67.refs_2_, ...), custom_call_target="tpu_custom_call" | custom-call | flops 4831838208 | bytes 16777216 | tf_op jit(solution)/shard_map/attend_forward/pallas_call | solution.py:247
  80.7 1.6 collective-permute-start.20
  82.2 8.8 %attend_forward.2 = (bf16[2,512,256]{2,1,0:T(8,128)(2,1)}, f32[512,128]{1,0:T(8,128)}, f32[512,128]{1,0:T(8,128)}) custom-call(s32[32,128]{1,0:T(8,128)} %get-tuple-element.64.table, bf16[512,768]{1,0:T(8,128)(2,1)} %get-tuple-element.65.refs_0_, bf16[512,768]{1,0:T(8,128)(2,1)} %get-tuple-element.66.refs_1_, bf16[512,768]{1,0:T(8,128)(2,1)} %get-tuple-element.67.refs_2_, ...), custom_call_target="tpu_custom_call" | custom-call | flops 4831838208 | bytes 16777216 | tf_op jit(solution)/shard_map/attend_forward/pallas_call | solution.py:247
  94.5 1.8 collective-permute-done.19.refs_12_
  100.7 32.3 %layer_rows.1 = (bf16[512,768]{1,0:T(8,128)(2,1)}, bf16[4,512,768]{2,1,0:T(8,128)(2,1)}, bf16[4,512,768]{2,1,0:T(8,128)(2,1)}, bf16[3,2,4,96,512]{4,3,2,1,0:T(8,...) custom-call(s32[1]{0:T(128)S(6)} %copy.40.length_ref.length, ...), custom_call_target="tpu_custom_call" | custom-call | flops 176160768 | bytes 393216 | tf_op jit(solution)/shard_map/layer_rows/pallas_call | solution.py:682
  135.5 10.4 %attend_backward.2 = (bf16[512,256]{1,0:T(8,128)(2,1)}, f32[2048,256]{1,0:T(8,128)}, f32[2048,256]{1,0:T(8,128)}) custom-call(s32[32,128]{1,0:T(8,128)} %get-tuple-element.64.table, bf16[512,768]{1,0:T(8,128)(2,1)} %get-tuple-element.65.refs_0_, bf16[512,768]{1,0:T(8,128)(2,1)} %get-tuple-element.66.refs_1_, bf16[512,768]{1,0:T(8,128)(2,1)} %get-tuple-element.67.refs_2_, ...), custom_call_target="tpu_custom_call" | custom-call | flops 23592960 | bytes 196608 | tf_op jit(solution)/shard_map/attend_backward/pallas_call | solution.py:394
  145.9 2.9 %collective-permute-done.31.refs_9_.refs_6_ = bf16[560,256]{1,0:T(8,128)(2,1)} collective-permute-done((bf16[560,256]{1,0:T(8,128)(2,1)}, bf16[560,256]{1,0:T(8,128)(2,1)}, u32[]{:S(2)}, u32[]{:S(2)}) %collective-permute-start.31) | collective-permute-done | bytes 286752 | tf_op jit(solution)/shard_map/ppermute | solution.py:34
  148.8 1.7 copy-done
  150.4 6.3 %row_dot.3.refs_12_ = bf16[4,2,2,96,768]{4,3,2,1,0:T(8,128)(2,1)} custom-call(bf16[3,2,4,96,512]{4,3,2,1,0:T(8,128)(2,1)} %get-tuple-element.79.refs_0_.refs_2_, bf16[3,2,4,96,512]{4,3,2,1,0:T(8,128)(2,1)} %collective-permute-done.32.refs_1_.refs_3_, bf16[4,512,768]{2,1,0:T(8,128)(2,1)} %get-tuple-element.80.refs_2_.refs_3_.refs_4_.refs_5_, ...), custom_call_target="tpu_custom_call" | custom-call | flops 37748736 | bytes 131072 | tf_op jit(solution)/shard_map/row_dot/pallas_call | solution.py:796
  156.7 4.8 %all-to-all-start = ((bf16[4,2,2,96,768]{4,3,2,1,0:T(8,128)(2,1)}), bf16[4,2,2,96,768]{4,3,2,1,0:T(8,128)(2,1)S(1)}, u32[]{:S(2)}, u32[]{:S(2)}) async-start(bf16[4,2,2,96,768]{4,3,2,1,0:T(8,128)(2,1)} %row_dot.3.refs_12_), calls=%async_computation | async-start | bytes 4718592 | tf_op jit(solution)/shard_map/all_to_all | solution.py:85
  161.5 8.2 %row_dot.4 = (bf16[1,1,4,96,1024]{4,3,2,1,0:T(8,128)(2,1)}, bf16[1,1,4,96,1024]{4,3,2,1,0:T(8,128)(2,1)}, bf16[1,1,4,96,1024]{4,3,2,1,0:T(8,128)(2,1)}, bf16[1,1,4,96,1024]{4,3,2,1,0:T(8,128)(2,1)}) custom-call(bf16[3,2,4,96,512]{4,3,2,1,0:T(8,128)(2,1)} %get-tuple-element.79.refs_0_.refs_2_, ...), custom_call_target="tpu_custom_call" | custom-call | flops 50331648 | bytes 131072 | tf_op jit(solution)/shard_map/row_dot/pallas_call | solution.py:796
  171.2 2.0 collective-permute-start.37
  173.3 21.8 %attend_backward.3 = (bf16[512,768]{1,0:T(8,128)(2,1)}, bf16[512,768]{1,0:T(8,128)(2,1)}, bf16[512,768]{1,0:T(8,128)(2,1)}, bf16[512,768]{1,0:T(8,128)(2,1)}, bf16[16,768]{1,0:T(8,128)(2,1)}) custom-call(s32[32,128]{1,0:T(8,128)} %get-tuple-element.64.table, bf16[512,768]{1,0:T(8,128)(2,1)} %get-tuple-element.65.refs_0_, ...), custom_call_target="tpu_custom_call" | custom-call | flops 70778880 | bytes 196608 | tf_op jit(solution)/shard_map/attend_backward/pallas_call | solution.py:394
  195.1 6.6 %row_dot.5 = (bf16[1,1,4,112,768]{4,3,2,1,0:T(8,128)(2,1)}, bf16[1,1,4,112,768]{4,3,2,1,0:T(8,128)(2,1)}) custom-call(bf16[1,2,4,96,512]{4,3,2,1,0:T(8,128)(2,1)} %bitcast.30, bf16[1,2,4,96,512]{4,3,2,1,0:T(8,128)(2,1)} %bitcast.31, bf16[1,2,4,96,512]{4,3,2,1,0:T(8,128)(2,1)} %bitcast.32, bf16[1,2,4,96,512]{4,3,2,1,0:T(8,128)(2,1)} %bitcast.33, ...), custom_call_target="tpu_custom_call" | custom-call | flops 37748736 | bytes 131072 | tf_op jit(solution)/shard_map/row_dot/pallas_call | solution.py:796
  201.6 4.3 %spread.2.refs_4_ = bf16[2,512,768]{2,1,0:T(8,128)(2,1)} custom-call(bf16[512,768]{1,0:T(8,128)(2,1)} %get-tuple-element.92.first, bf16[512,768]{1,0:T(8,128)(2,1)} %get-tuple-element.93.second, bf16[768,768]{1,0:T(8,128)(2,1)} %get-tuple-element.91.w, bf16[1,1,4,112,768]{4,3,2,1,0:T(8,128)(2,1)} %get-tuple-element.99.refs_0_), custom_call_target="tpu_custom_call" | custom-call | flops 18874368 | bytes 81920 | tf_op jit(solution)/shard_map/spread/pallas_call | solution.py:913
  206.8 3.1 %joined_sums.2.refs_2_ = bf16[4,96,1024]{2,1,0:T(8,128)(2,1)} custom-call(bf16[4,96,1024]{2,1,0:T(8,128)(2,1)} %bitcast.34, bf16[4,96,1024]{2,1,0:T(8,128)(2,1)} %bitcast.35, bf16[4,96,1024]{2,1,0:T(8,128)(2,1)} %bitcast.12.refs_2_, bf16[4,96,1024]{2,1,0:T(8,128)(2,1)} %bitcast.13.refs_3_, bf16[2,512,768]{2,1,0:T(8,128)(2,1)} %spread.2.refs_4_), custom_call_target="tpu_custom_call" | custom-call | flops 24576 | bytes 49152 | tf_op jit(solution)/shard_map/joined_sums/pallas_call | solution.py:883
  209.9 6.0 %all-to-all-done.ref = bf16[4,2,2,96,768]{4,3,2,1,0:T(8,128)(2,1)S(1)} async-done(((bf16[4,2,2,96,768]{4,3,2,1,0:T(8,128)(2,1)}), bf16[4,2,2,96,768]{4,3,2,1,0:T(8,128)(2,1)S(1)}, u32[]{:S(2)}, u32[]{:S(2)}) %all-to-all-start) | async-done | bytes 2359328 | tf_op jit(solution)/shard_map/all_to_all | solution.py:85
  215.9 3.5 %all-to-all-start.2 = ((bf16[4,96,1024]{2,1,0:T(8,128)(2,1)}), bf16[4,96,1024]{2,1,0:T(8,128)(2,1)S(1)}, u32[]{:S(2)}, u32[]{:S(2)}) async-start(bf16[4,96,1024]{2,1,0:T(8,128)(2,1)} %joined_sums.2.refs_2_), calls=%async_computation.2 | async-start | bytes 1572864 | tf_op jit(solution)/shard_map/all_to_all | solution.py:85
  220.4 5.0 %spread.3 = (bf16[512,768]{1,0:T(8,128)(2,1)}, f32[512,768]{1,0:T(8,128)}) custom-call(bf16[512,768]{1,0:T(8,128)(2,1)} %get-tuple-element.89.first, bf16[512,768]{1,0:T(8,128)(2,1)} %get-tuple-element.90.second, bf16[768,768]{1,0:T(8,128)(2,1)} %get-tuple-element.91.w, bf16[2,512,768]{2,1,0:T(8,128)(2,1)} %collective-permute-done.34.refs_0_, ...), custom_call_target="tpu_custom_call" | custom-call | flops 18874368 | bytes 81920 | tf_op jit(solution)/shard_map/spread/pallas_call | solution.py:913
  225.9 2.7 %fold.1 = (bf16[2,96,768]{2,1,0:T(8,128)(2,1)}, bf16[2,96,768]{2,1,0:T(8,128)(2,1)}) custom-call(bf16[4,2,2,96,768]{4,3,2,1,0:T(8,128)(2,1)} %copy-done.1, bf16[512,768]{1,0:T(8,128)(2,1)} %get-tuple-element.105.refs_0_), custom_call_target="tpu_custom_call" | custom-call | flops 18432 | bytes 55296 | tf_op jit(solution)/shard_map/fold/pallas_call | solution.py:858
  228.6 7.8 %collective-permute-done.39 = bf16[1,1,4,112,768]{4,3,2,1,0:T(8,128)(2,1)} collective-permute-done((bf16[1,1,4,112,768]{4,3,2,1,0:T(8,128)(2,1)}, bf16[1,1,4,112,768]{4,3,2,1,0:T(8,128)(2,1)}, u32[]{:S(2)}, u32[]{:S(2)}) %collective-permute-start.39) | collective-permute-done | bytes 688160 | tf_op jit(solution)/shard_map/ppermute | solution.py:39
  236.4 2.4 joined_sums.3.refs_0_
  239.2 4.3 %all-to-all-start.1 = ((bf16[4,112,768]{2,1,0:T(8,128)(2,1)}), bf16[4,112,768]{2,1,0:T(8,128)(2,1)S(1)}, u32[]{:S(2)}, u32[]{:S(2)}) async-start(bf16[4,112,768]{2,1,0:T(8,128)(2,1)} %joined_sums.3.refs_0_), calls=%async_computation.1 | async-start | bytes 1376256 | tf_op jit(solution)/shard_map/all_to_all | solution.py:85
  245.9 4.8 %collective-permute-done.40.b_ref = bf16[2,96,768]{2,1,0:T(8,128)(2,1)S(1)} collective-permute-done((bf16[2,96,768]{2,1,0:T(8,128)(2,1)S(1)}, bf16[2,96,768]{2,1,0:T(8,128)(2,1)S(1)}, u32[]{:S(2)}, u32[]{:S(2)}) %collective-permute-start.40) | collective-permute-done | bytes 294944 | tf_op jit(solution)/shard_map/ppermute | solution.py:34
  251.4 1.8 plus.1
  254.1 2.7 %convert_add_fusion = f32[512,768]{1,0:T(8,128)} fusion(f32[512,768]{1,0:T(8,128)} %get-tuple-element.104, bf16[512,768]{1,0:T(8,128)(2,1)S(1)} %collective-permute-done.38), kind=kLoop, calls=%fused_computation.1 | loop fusion | flops 786432 | bytes 3932160 | tf_op jit(solution)/shard_map/add | solution.py:1223
  256.9 1.7 collective-permute-done.41
  (158 shorter events, 31.5 us)
Async XLA Ops:
  2.2 8.6 %collective-permute-start.4 = (bf16[96,768]{1,0:T(8,128)(2,1)}, bf16[96,768]{1,0:T(8,128)(2,1)S(1)}, u32[]{:S(2)}, u32[]{:S(2)}) collective-permute-start(bf16[96,768]{1,0:T(8,128)(2,1)} %pack_queries.1._.refs_4_), channel_id=1, source_target_pairs={{0,8},{8,16},{16,24},{24,28},{28,20},{20,12},{12,4},{4,0},{1,9},{9... | collective-permute-start | bytes 442376 | tf_op jit(solution)/shard_map/ppermute | solution.py:63
  8.8 42.8 %copy-start.29 = (f32[192]{0:T(256)S(1)}, f32[192]{0:T(256)}, u32[]{:S(2)}) copy-start(f32[192]{0:T(256)} %param.26) | copy-start | bytes 2308
  8.8 42.8 %copy-start.30 = (f32[192]{0:T(256)S(1)}, f32[192]{0:T(256)}, u32[]{:S(2)}) copy-start(f32[192]{0:T(256)} %param.23) | copy-start | bytes 2308
  8.8 9.8 %collective-permute-start.1 = (bf16[96,1792]{1,0:T(8,128)(2,1)}, bf16[96,1792]{1,0:T(8,128)(2,1)S(1)}, u32[]{:S(2)}, u32[]{:S(2)}) collective-permute-start(bf16[96,1792]{1,0:T(8,128)(2,1)} %pack_weights.1.a), channel_id=1, source_target_pairs={{0,2},{1,3},{2,0},{3,1},{4,6},{5,7},{6,4},{7,5},{8,10},{9,11},{10,... | collective-permute-start | bytes 1032200 | tf_op jit(solution)/shard_map/ppermute | solution.py:34
  10.4 5.4 %collective-permute-start.5 = (bf16[96,768]{1,0:T(8,128)(2,1)}, bf16[96,768]{1,0:T(8,128)(2,1)S(1)}, u32[]{:S(2)}, u32[]{:S(2)}) collective-permute-start(bf16[96,768]{1,0:T(8,128)(2,1)} %pack_queries.1._.refs_4_), channel_id=1, source_target_pairs={{0,4},{8,0},{16,8},{24,16},{28,24},{20,28},{12,20},{4,12},{1,5},{9... | collective-permute-start | bytes 442376 | tf_op jit(solution)/shard_map/ppermute | solution.py:63
  10.8 52.0 %copy-start.31 = (bf16[96,768]{1,0:T(8,128)(2,1)}, bf16[96,768]{1,0:T(8,128)(2,1)S(1)}, u32[]{:S(2)}) copy-start(bf16[96,768]{1,0:T(8,128)(2,1)S(1)} %collective-permute-done.4.refs_5_) | copy-start | bytes 442372
  10.8 5.4 %collective-permute-start.6 = (bf16[96,768]{1,0:T(8,128)(2,1)S(1)}, bf16[96,768]{1,0:T(8,128)(2,1)S(1)}, u32[]{:S(2)}, u32[]{:S(2)}) collective-permute-start(bf16[96,768]{1,0:T(8,128)(2,1)S(1)} %collective-permute-done.4.refs_5_), channel_id=1, source_target_pairs={{0,8},{8,16},{16,24},{24,28},{28,20},{20,12},{12,4},{4,0},{1,9},{9... | collective-permute-start | bytes 442376 | tf_op jit(solution)/shard_map/ppermute | solution.py:63
  15.7 7.2 %collective-permute-start.7 = (bf16[96,768]{1,0:T(8,128)(2,1)S(1)}, bf16[96,768]{1,0:T(8,128)(2,1)S(1)}, u32[]{:S(2)}, u32[]{:S(2)}) collective-permute-start(bf16[96,768]{1,0:T(8,128)(2,1)S(1)} %collective-permute-done.5.refs_6_), channel_id=1, source_target_pairs={{0,4},{8,0},{16,8},{24,16},{28,24},{20,28},{12,20},{4,12},{1,5},{9... | collective-permute-start | bytes 442376 | tf_op jit(solution)/shard_map/ppermute | solution.py:63
  16.2 7.2 %collective-permute-start.8 = (bf16[96,768]{1,0:T(8,128)(2,1)S(1)}, bf16[96,768]{1,0:T(8,128)(2,1)S(1)}, u32[]{:S(2)}, u32[]{:S(2)}) collective-permute-start(bf16[96,768]{1,0:T(8,128)(2,1)S(1)} %collective-permute-done.6.refs_7_), channel_id=1, source_target_pairs={{0,8},{8,16},{16,24},{24,28},{28,20},{20,12},{12,4},{4,0},{1,9},{9... | collective-permute-start | bytes 442376 | tf_op jit(solution)/shard_map/ppermute | solution.py:63
  21.4 18.4 %collective-permute-start.2 = (bf16[512,768]{1,0:T(8,128)(2,1)}, bf16[512,768]{1,0:T(8,128)(2,1)}, u32[]{:S(2)}, u32[]{:S(2)}) collective-permute-start(bf16[512,768]{1,0:T(8,128)(2,1)} %held.1), channel_id=1, source_target_pairs={{0,2},{1,3},{2,0},{3,1},{4,6},{5,7},{6,4},{7,5},{8,10},{9,11},{10,... | collective-permute-start | bytes 2359304 | tf_op jit(solution)/shard_map/ppermute | solution.py:34
  22.9 5.1 %collective-permute-start.9 = (bf16[96,768]{1,0:T(8,128)(2,1)S(1)}, bf16[96,768]{1,0:T(8,128)(2,1)S(1)}, u32[]{:S(2)}, u32[]{:S(2)}) collective-permute-start(bf16[96,768]{1,0:T(8,128)(2,1)S(1)} %collective-permute-done.7.refs_8_), channel_id=1, source_target_pairs={{0,4},{8,0},{16,8},{24,16},{28,24},{20,28},{12,20},{4,12},{1,5},{9... | collective-permute-start | bytes 442376 | tf_op jit(solution)/shard_map/ppermute | solution.py:63
  23.4 5.1 %collective-permute-start.10 = (bf16[96,768]{1,0:T(8,128)(2,1)S(1)}, bf16[96,768]{1,0:T(8,128)(2,1)S(1)}, u32[]{:S(2)}, u32[]{:S(2)}) collective-permute-start(bf16[96,768]{1,0:T(8,128)(2,1)S(1)} %collective-permute-done.8.refs_9_.refs_0_), channel_id=1, source_target_pairs={{0,8},{8,16},{16,24},{24,28},{28,20},{20,12},{12,4},{4,0},{1,9},{9... | collective-permute-start | bytes 442376 | tf_op jit(solution)/shard_map/ppermute | solution.py:63
  31.4 15.8 %collective-permute-start.14 = (bf16[96,3584]{1,0:T(8,128)(2,1)}, bf16[96,3584]{1,0:T(8,128)(2,1)S(1)}, u32[]{:S(2)}, u32[]{:S(2)}) collective-permute-start(bf16[96,3584]{1,0:T(8,128)(2,1)} %pair_weights.1.refs_6_), channel_id=1, source_target_pairs={{0,8},{8,16},{16,24},{24,28},{28,20},{20,12},{12,4},{4,0},{1,9},{9... | collective-permute-start | bytes 2064392 | tf_op jit(solution)/shard_map/ppermute | solution.py:63
  32.9 19.3 %collective-permute-start = (bf16[512,768]{1,0:T(8,128)(2,1)S(1)}, bf16[512,768]{1,0:T(8,128)(2,1)}, u32[]{:S(2)}, u32[]{:S(2)}) collective-permute-start(bf16[512,768]{1,0:T(8,128)(2,1)S(1)} %copy-done.3), channel_id=1, source_target_pairs={{0,1},{1,0},{2,3},{3,2},{4,5},{5,4},{6,7},{7,6},{8,9},{9,8},{10,11... | collective-permute-start | bytes 2359304 | tf_op jit(solution)/shard_map/ppermute | solution.py:34
  39.8 18.6 %collective-permute-start.3 = (bf16[512,768]{1,0:T(8,128)(2,1)}, bf16[512,768]{1,0:T(8,128)(2,1)}, u32[]{:S(2)}, u32[]{:S(2)}) collective-permute-start(bf16[512,768]{1,0:T(8,128)(2,1)} %collective-permute-done.2.refs_2_), channel_id=1, source_target_pairs={{0,1},{1,0},{2,3},{3,2},{4,5},{5,4},{6,7},{7,6},{8,9},{9,8},{10,11... | collective-permute-start | bytes 2359304 | tf_op jit(solution)/shard_map/ppermute | solution.py:34
  39.8 18.1 %collective-permute-start.15 = (bf16[96,3584]{1,0:T(8,128)(2,1)}, bf16[96,3584]{1,0:T(8,128)(2,1)S(1)}, u32[]{:S(2)}, u32[]{:S(2)}) collective-permute-start(bf16[96,3584]{1,0:T(8,128)(2,1)} %pair_weights.1.refs_6_), channel_id=1, source_target_pairs={{0,4},{8,0},{16,8},{24,16},{28,24},{20,28},{12,20},{4,12},{1,5},{9... | collective-permute-start | bytes 2064392 | tf_op jit(solution)/shard_map/ppermute | solution.py:63
  47.2 14.1 %collective-permute-start.16 = (bf16[96,3584]{1,0:T(8,128)(2,1)S(1)}, bf16[96,3584]{1,0:T(8,128)(2,1)S(1)}, u32[]{:S(2)}, u32[]{:S(2)}) collective-permute-start(bf16[96,3584]{1,0:T(8,128)(2,1)S(1)} %collective-permute-done.14.refs_7_), channel_id=1, source_target_pairs={{0,8},{8,16},{16,24},{24,28},{28,20},{20,12},{12,4},{4,0},{1,9},{9... | collective-permute-start | bytes 2064392 | tf_op jit(solution)/shard_map/ppermute | solution.py:63
  52.2 27.7 %collective-permute-start.21 = (bf16[96,3584]{1,0:T(8,128)(2,1)}, bf16[96,3584]{1,0:T(8,128)(2,1)}, u32[]{:S(2)}, u32[]{:S(2)}) collective-permute-start(bf16[96,3584]{1,0:T(8,128)(2,1)} %pair_weights.1.refs_6_), channel_id=1, source_target_pairs={{0,1},{1,0},{2,3},{3,2},{4,5},{5,4},{6,7},{7,6},{8,9},{9,8},{10,11... | collective-permute-start | bytes 2064392 | tf_op jit(solution)/shard_map/ppermute | solution.py:34
  52.2 39.8 %collective-permute-start.22 = (bf16[96,3584]{1,0:T(8,128)(2,1)S(1)}, bf16[96,3584]{1,0:T(8,128)(2,1)S(1)}, u32[]{:S(2)}, u32[]{:S(2)}) collective-permute-start(bf16[96,3584]{1,0:T(8,128)(2,1)S(1)} %collective-permute-done.14.refs_7_), channel_id=1, source_target_pairs={{0,1},{1,0},{2,3},{3,2},{4,5},{5,4},{6,7},{7,6},{8,9},{9,8},{10,11... | collective-permute-start | bytes 2064392 | tf_op jit(solution)/shard_map/ppermute | solution.py:34
  57.9 22.3 %collective-permute-start.17 = (bf16[96,3584]{1,0:T(8,128)(2,1)S(1)}, bf16[96,3584]{1,0:T(8,128)(2,1)}, u32[]{:S(2)}, u32[]{:S(2)}) collective-permute-start(bf16[96,3584]{1,0:T(8,128)(2,1)S(1)} %collective-permute-done.15.refs_8_), channel_id=1, source_target_pairs={{0,4},{8,0},{16,8},{24,16},{28,24},{20,28},{12,20},{4,12},{1,5},{9... | collective-permute-start | bytes 2064392 | tf_op jit(solution)/shard_map/ppermute | solution.py:63
  58.5 33.7 %collective-permute-start.23 = (bf16[96,3584]{1,0:T(8,128)(2,1)S(1)}, bf16[96,3584]{1,0:T(8,128)(2,1)}, u32[]{:S(2)}, u32[]{:S(2)}) collective-permute-start(bf16[96,3584]{1,0:T(8,128)(2,1)S(1)} %collective-permute-done.15.refs_8_), channel_id=1, source_target_pairs={{0,1},{1,0},{2,3},{3,2},{4,5},{5,4},{6,7},{7,6},{8,9},{9,8},{10,11... | collective-permute-start | bytes 2064392 | tf_op jit(solution)/shard_map/ppermute | solution.py:34
  61.3 19.4 %collective-permute-start.18 = (bf16[96,3584]{1,0:T(8,128)(2,1)S(1)}, bf16[96,3584]{1,0:T(8,128)(2,1)}, u32[]{:S(2)}, u32[]{:S(2)}) collective-permute-start(bf16[96,3584]{1,0:T(8,128)(2,1)S(1)} %collective-permute-done.16.refs_9_), channel_id=1, source_target_pairs={{0,8},{8,16},{16,24},{24,28},{28,20},{20,12},{12,4},{4,0},{1,9},{9... | collective-permute-start | bytes 2064392 | tf_op jit(solution)/shard_map/ppermute | solution.py:63
  80.0 13.8 %collective-permute-start.12 = (bf16[2,512,256]{2,1,0:T(8,128)(2,1)}, bf16[2,512,256]{2,1,0:T(8,128)(2,1)S(1)}, u32[]{:S(2)}, u32[]{:S(2)}) collective-permute-start(bf16[2,512,256]{2,1,0:T(8,128)(2,1)} %get-tuple-element.71), channel_id=1, source_target_pairs={{0,2},{1,3},{2,0},{3,1},{4,6},{5,7},{6,4},{7,5},{8,10},{9,11},{10,... | collective-permute-start | bytes 1572872 | tf_op jit(solution)/shard_map/ppermute | solution.py:34
  80.2 16.1 %collective-permute-start.19 = (bf16[96,3584]{1,0:T(8,128)(2,1)}, bf16[96,3584]{1,0:T(8,128)(2,1)}, u32[]{:S(2)}, u32[]{:S(2)}) collective-permute-start(bf16[96,3584]{1,0:T(8,128)(2,1)} %collective-permute-done.17.refs_10_), channel_id=1, source_target_pairs={{0,4},{8,0},{16,8},{24,16},{28,24},{20,28},{12,20},{4,12},{1,5},{9... | collective-permute-start | bytes 2064392 | tf_op jit(solution)/shard_map/ppermute | solution.py:63
  80.7 15.8 %collective-permute-start.20 = (bf16[96,3584]{1,0:T(8,128)(2,1)}, bf16[96,3584]{1,0:T(8,128)(2,1)}, u32[]{:S(2)}, u32[]{:S(2)}) collective-permute-start(bf16[96,3584]{1,0:T(8,128)(2,1)} %collective-permute-done.18.refs_11_), channel_id=1, source_target_pairs={{0,8},{8,16},{16,24},{24,28},{28,20},{20,12},{12,4},{4,0},{1,9},{9... | collective-permute-start | bytes 2064392 | tf_op jit(solution)/shard_map/ppermute | solution.py:63
  92.1 1.6 collective-permute-start.11
  92.2 5.3 %collective-permute-start.24 = (bf16[96,3584]{1,0:T(8,128)(2,1)S(1)}, bf16[96,3584]{1,0:T(8,128)(2,1)S(1)}, u32[]{:S(2)}, u32[]{:S(2)}) collective-permute-start(bf16[96,3584]{1,0:T(8,128)(2,1)S(1)} %collective-permute-done.16.refs_9_), channel_id=1, source_target_pairs={{0,1},{1,0},{2,3},{3,2},{4,5},{5,4},{6,7},{7,6},{8,9},{9,8},{10,11... | collective-permute-start | bytes 2064392 | tf_op jit(solution)/shard_map/ppermute | solution.py:34
  93.7 5.5 %collective-permute-start.25 = (bf16[96,3584]{1,0:T(8,128)(2,1)}, bf16[96,3584]{1,0:T(8,128)(2,1)S(1)}, u32[]{:S(2)}, u32[]{:S(2)}) collective-permute-start(bf16[96,3584]{1,0:T(8,128)(2,1)} %collective-permute-done.17.refs_10_), channel_id=1, source_target_pairs={{0,1},{1,0},{2,3},{3,2},{4,5},{5,4},{6,7},{7,6},{8,9},{9,8},{10,11... | collective-permute-start | bytes 2064392 | tf_op jit(solution)/shard_map/ppermute | solution.py:34
  94.4 5.6 %collective-permute-start.26 = (bf16[96,3584]{1,0:T(8,128)(2,1)}, bf16[96,3584]{1,0:T(8,128)(2,1)}, u32[]{:S(2)}, u32[]{:S(2)}) collective-permute-start(bf16[96,3584]{1,0:T(8,128)(2,1)} %collective-permute-done.18.refs_11_), channel_id=1, source_target_pairs={{0,1},{1,0},{2,3},{3,2},{4,5},{5,4},{6,7},{7,6},{8,9},{9,8},{10,11... | collective-permute-start | bytes 2064392 | tf_op jit(solution)/shard_map/ppermute | solution.py:34
  96.3 3.7 %collective-permute-start.27 = (bf16[96,3584]{1,0:T(8,128)(2,1)}, bf16[96,3584]{1,0:T(8,128)(2,1)}, u32[]{:S(2)}, u32[]{:S(2)}) collective-permute-start(bf16[96,3584]{1,0:T(8,128)(2,1)} %collective-permute-done.19.refs_12_), channel_id=1, source_target_pairs={{0,1},{1,0},{2,3},{3,2},{4,5},{5,4},{6,7},{7,6},{8,9},{9,8},{10,11... | collective-permute-start | bytes 2064392 | tf_op jit(solution)/shard_map/ppermute | solution.py:34
  96.5 3.5 %collective-permute-start.28 = (bf16[96,3584]{1,0:T(8,128)(2,1)}, bf16[96,3584]{1,0:T(8,128)(2,1)}, u32[]{:S(2)}, u32[]{:S(2)}) collective-permute-start(bf16[96,3584]{1,0:T(8,128)(2,1)} %collective-permute-done.20.refs_13_), channel_id=1, source_target_pairs={{0,1},{1,0},{2,3},{3,2},{4,5},{5,4},{6,7},{7,6},{8,9},{9,8},{10,11... | collective-permute-start | bytes 2064392 | tf_op jit(solution)/shard_map/ppermute | solution.py:34
  97.5 2.5 collective-permute-start.13
  133.0 15.7 %collective-permute-start.33 = (bf16[4,512,768]{2,1,0:T(8,128)(2,1)}, bf16[4,512,768]{2,1,0:T(8,128)(2,1)S(1)}, u32[]{:S(2)}, u32[]{:S(2)}) collective-permute-start(bf16[4,512,768]{2,1,0:T(8,128)(2,1)} %get-tuple-element.81), channel_id=1, source_target_pairs={{0,1},{1,0},{2,3},{3,2},{4,5},{5,4},{6,7},{7,6},{8,9},{9,8},{10,11... | collective-permute-start | bytes 9437192 | tf_op jit(solution)/shard_map/ppermute | solution.py:34
  133.2 15.5 %collective-permute-start.32 = (bf16[3,2,4,96,512]{4,3,2,1,0:T(8,128)(2,1)}, bf16[3,2,4,96,512]{4,3,2,1,0:T(8,128)(2,1)}, u32[]{:S(2)}, u32[]{:S(2)}) collective-permute-start(bf16[3,2,4,96,512]{4,3,2,1,0:T(8,128)(2,1)} %get-tuple-element.79.refs_0_.refs_2_), channel_id=1, source_target_pairs={{0,1},{1,0},{2,3},{3,2},{4,5},{5,4},{6,7},{7,6},{8,9},{9,8},{10,11... | collective-permute-start | bytes 7077896 | tf_op jit(solution)/shard_map/ppermute | solution.py:34
  133.6 12.2 %collective-permute-start.29 = (bf16[560,256]{1,0:T(8,128)(2,1)}, bf16[560,256]{1,0:T(8,128)(2,1)S(1)}, u32[]{:S(2)}, u32[]{:S(2)}) collective-permute-start(bf16[560,256]{1,0:T(8,128)(2,1)} %get-tuple-element.73), channel_id=1, source_target_pairs={{0,1},{1,0},{2,3},{3,2},{4,5},{5,4},{6,7},{7,6},{8,9},{9,8},{10,11... | collective-permute-start | bytes 860168 | tf_op jit(solution)/shard_map/ppermute | solution.py:34
  133.7 12.1 %collective-permute-start.30 = (bf16[560,256]{1,0:T(8,128)(2,1)}, bf16[560,256]{1,0:T(8,128)(2,1)}, u32[]{:S(2)}, u32[]{:S(2)}) collective-permute-start(bf16[560,256]{1,0:T(8,128)(2,1)} %get-tuple-element.74), channel_id=1, source_target_pairs={{0,2},{1,3},{2,0},{3,1},{4,6},{5,7},{6,4},{7,5},{8,10},{9,11},{10,... | collective-permute-start | bytes 860168 | tf_op jit(solution)/shard_map/ppermute | solution.py:34
  134.5 14.2 %collective-permute-start.31 = (bf16[560,256]{1,0:T(8,128)(2,1)}, bf16[560,256]{1,0:T(8,128)(2,1)}, u32[]{:S(2)}, u32[]{:S(2)}) collective-permute-start(bf16[560,256]{1,0:T(8,128)(2,1)} %get-tuple-element.75), channel_id=1, source_target_pairs={{0,3},{1,2},{2,1},{3,0},{4,7},{5,6},{6,5},{7,4},{8,11},{9,10},{10,... | collective-permute-start | bytes 860168 | tf_op jit(solution)/shard_map/ppermute | solution.py:34
  156.7 59.2 %all-to-all-start = ((bf16[4,2,2,96,768]{4,3,2,1,0:T(8,128)(2,1)}), bf16[4,2,2,96,768]{4,3,2,1,0:T(8,128)(2,1)S(1)}, u32[]{:S(2)}, u32[]{:S(2)}) async-start(bf16[4,2,2,96,768]{4,3,2,1,0:T(8,128)(2,1)} %row_dot.3.refs_12_), calls=%async_computation | async-start | bytes 4718592 | tf_op jit(solution)/shard_map/all_to_all | solution.py:85
  169.7 36.2 %collective-permute-start.35 = (bf16[1,1,4,96,1024]{4,3,2,1,0:T(8,128)(2,1)}, bf16[1,1,4,96,1024]{4,3,2,1,0:T(8,128)(2,1)S(1)}, u32[]{:S(2)}, u32[]{:S(2)}) collective-permute-start(bf16[1,1,4,96,1024]{4,3,2,1,0:T(8,128)(2,1)} %get-tuple-element.102), channel_id=1, source_target_pairs={{0,2},{1,3},{2,0},{3,1},{4,6},{5,7},{6,4},{7,5},{8,10},{9,11},{10,... | collective-permute-start | bytes 2359304 | tf_op jit(solution)/shard_map/ppermute | solution.py:34
  170.1 35.9 %collective-permute-start.36 = (bf16[1,1,4,96,1024]{4,3,2,1,0:T(8,128)(2,1)}, bf16[1,1,4,96,1024]{4,3,2,1,0:T(8,128)(2,1)}, u32[]{:S(2)}, u32[]{:S(2)}) collective-permute-start(bf16[1,1,4,96,1024]{4,3,2,1,0:T(8,128)(2,1)} %get-tuple-element.103), channel_id=1, source_target_pairs={{0,4},{4,0},{8,12},{12,8},{16,20},{20,16},{24,28},{28,24},{1,5},{5... | collective-permute-start | bytes 2359304 | tf_op jit(solution)/shard_map/ppermute | solution.py:39
  171.2 35.6 %collective-permute-start.37 = (bf16[1,1,4,96,1024]{4,3,2,1,0:T(8,128)(2,1)}, bf16[1,1,4,96,1024]{4,3,2,1,0:T(8,128)(2,1)}, u32[]{:S(2)}, u32[]{:S(2)}) collective-permute-start(bf16[1,1,4,96,1024]{4,3,2,1,0:T(8,128)(2,1)} %get-tuple-element.85.refs_11_), channel_id=1, source_target_pairs={{0,6},{1,7},{2,4},{3,5},{4,2},{5,3},{6,0},{7,1},{8,14},{9,15},{10,... | collective-permute-start | bytes 2359304 | tf_op jit(solution)/shard_map/ppermute | solution.py:45
  205.9 14.4 %collective-permute-start.34 = (bf16[2,512,768]{2,1,0:T(8,128)(2,1)}, bf16[2,512,768]{2,1,0:T(8,128)(2,1)}, u32[]{:S(2)}, u32[]{:S(2)}) collective-permute-start(bf16[2,512,768]{2,1,0:T(8,128)(2,1)} %spread.2.refs_4_), channel_id=1, source_target_pairs={{0,1},{1,0},{2,3},{3,2},{4,5},{5,4},{6,7},{7,6},{8,9},{9,8},{10,11... | collective-permute-start | bytes 4718600 | tf_op jit(solution)/shard_map/ppermute | solution.py:34
  215.9 23.3 %all-to-all-start.2 = ((bf16[4,96,1024]{2,1,0:T(8,128)(2,1)}), bf16[4,96,1024]{2,1,0:T(8,128)(2,1)S(1)}, u32[]{:S(2)}, u32[]{:S(2)}) async-start(bf16[4,96,1024]{2,1,0:T(8,128)(2,1)} %joined_sums.2.refs_2_), calls=%async_computation.2 | async-start | bytes 1572864 | tf_op jit(solution)/shard_map/all_to_all | solution.py:85
  219.4 17.0 %collective-permute-start.39 = (bf16[1,1,4,112,768]{4,3,2,1,0:T(8,128)(2,1)}, bf16[1,1,4,112,768]{4,3,2,1,0:T(8,128)(2,1)}, u32[]{:S(2)}, u32[]{:S(2)}) collective-permute-start(bf16[1,1,4,112,768]{4,3,2,1,0:T(8,128)(2,1)} %get-tuple-element.99.refs_0_), channel_id=1, source_target_pairs={{0,4},{4,0},{8,12},{12,8},{16,20},{20,16},{24,28},{28,24},{1,5},{5... | collective-permute-start | bytes 2064392 | tf_op jit(solution)/shard_map/ppermute | solution.py:39
  225.4 28.7 %collective-permute-start.38 = (bf16[512,768]{1,0:T(8,128)(2,1)}, bf16[512,768]{1,0:T(8,128)(2,1)S(1)}, u32[]{:S(2)}, u32[]{:S(2)}) collective-permute-start(bf16[512,768]{1,0:T(8,128)(2,1)} %get-tuple-element.105.refs_0_), channel_id=1, source_target_pairs={{0,2},{1,3},{2,0},{3,1},{4,6},{5,7},{6,4},{7,5},{8,10},{9,11},{10,... | collective-permute-start | bytes 2359304 | tf_op jit(solution)/shard_map/ppermute | solution.py:34
  239.2 20.9 %all-to-all-start.1 = ((bf16[4,112,768]{2,1,0:T(8,128)(2,1)}), bf16[4,112,768]{2,1,0:T(8,128)(2,1)S(1)}, u32[]{:S(2)}, u32[]{:S(2)}) async-start(bf16[4,112,768]{2,1,0:T(8,128)(2,1)} %joined_sums.3.refs_0_), calls=%async_computation.1 | async-start | bytes 1376256 | tf_op jit(solution)/shard_map/all_to_all | solution.py:85
  243.4 7.3 %collective-permute-start.40 = (bf16[2,96,768]{2,1,0:T(8,128)(2,1)S(1)}, bf16[2,96,768]{2,1,0:T(8,128)(2,1)S(1)}, u32[]{:S(2)}, u32[]{:S(2)}) collective-permute-start(bf16[2,96,768]{2,1,0:T(8,128)(2,1)S(1)} %copy-done.13), channel_id=1, source_target_pairs={{0,2},{1,3},{2,0},{3,1},{4,6},{5,7},{6,4},{7,5},{8,10},{9,11},{10,... | collective-permute-start | bytes 884744 | tf_op jit(solution)/shard_map/ppermute | solution.py:34
  253.2 5.4 %collective-permute-start.41 = (bf16[1,96,768]{2,1,0:T(8,128)(2,1)}, bf16[1,96,768]{2,1,0:T(8,128)(2,1)S(1)}, u32[]{:S(2)}, u32[]{:S(2)}) collective-permute-start(bf16[1,96,768]{2,1,0:T(8,128)(2,1)} %get-tuple-element.110), channel_id=1, source_target_pairs={{0,4},{4,0},{8,12},{12,8},{16,20},{20,16},{24,28},{28,24},{1,5},{5... | collective-permute-start | bytes 442376 | tf_op jit(solution)/shard_map/ppermute | solution.py:39
  (32 other events, 341.3 us)

commit v5 on v4

--- a/solution.py
+++ b/solution.py
@@ -19,6 +19,7 @@
 PAD = 256
 LANES = 128
 SUM_ROW = 10
+ORDER = (0, 1, 2, 3)
 SUM_ROWS = 16
 BELOW = SUM_ROWS * (D // PAD)
 GATE = 5
@@ -212,29 +213,59 @@
     out_masks = head_masks(heads, 1.0, f32)
     lane = lax.broadcasted_iota(jnp.int32, (BLK, LANES), 1)
 
-    def step(i, carry):
-        for at, s in enumerate(chosen):
-            block = s * own_blocks + i
-            start = pl.multiple_of(i * BLK, BLK)
-            queries = stacked_heads(
-                rows[pl.ds(pl.multiple_of(block * BLK, BLK), BLK), 0:PAD], query_masks
-            )
+    side = 2
+    count = len(chosen) * side
+
+    def step(step_at, carry):
+        blocks, held = [], [{} for _ in range(count)]
+        for at in range(count):
+            i = step_at * side + at // len(chosen)
+            piece = at % len(chosen)
+            blocks.append((piece, i, chosen[piece] * own_blocks + i))
+
+        def scored(at):
+            block = blocks[at][2]
+            here = pl.ds(pl.multiple_of(block * BLK, BLK), BLK)
+            queries = stacked_heads(rows[here, 0:PAD], query_masks)
             keys = key_blocks(rows, table, block, PAD)
+            held[at]["scores"] = contract(queries, keys, (1, 1))
+
+        def weighed(at):
+            has = held[at]
+            masked = bias[pl.ds(blocks[at][2], 1), :]
+            low, has["total"], has["log_total"] = [], [], []
+            for h in range(heads):
+                scores = has["scores"][h * BLK : (h + 1) * BLK] + masked
+                top = jnp.max(scores, axis=-1, keepdims=True)
+                weights = jnp.exp(scores - top)
+                total = jnp.sum(weights, axis=-1, keepdims=True)
+                low.append(weights.astype(bf16))
+                has["total"].append(total)
+                has["log_total"].append(top + jnp.log(total))
+            has["weights"] = jnp.concatenate(low, axis=0)
+
+        def mixed(at):
+            piece, i, block = blocks[at]
+            has = held[at]
             values = key_blocks(rows, table, block, 2 * PAD)
-            scores = contract(queries, keys, (1, 1)) + bias[pl.ds(block, 1), :]
-            top = jnp.max(scores, axis=-1, keepdims=True)
-            weights = jnp.exp(scores - top)
-            total = jnp.sum(weights, axis=-1, keepdims=True)
-            mixed = contract(weights.astype(bf16), values, (1, 0)) / total
-            out[at, pl.ds(start, BLK), :] = unstacked_heads(mixed, out_masks).astype(bf16)
-            log_total = top + jnp.log(total)
+            outs = contract(has["weights"], values, (1, 0))
+            start = pl.ds(pl.multiple_of(i * BLK, BLK), BLK)
             kept = jnp.zeros((BLK, LANES), f32)
+            total = jnp.zeros((BLK, PAD), f32)
             for h in range(heads):
-                kept = jnp.where(lane == h, log_total[h * BLK : (h + 1) * BLK], kept)
-            totals[at][pl.ds(start, BLK), :] = kept
+                total = total + outs[h * BLK : (h + 1) * BLK] * (out_masks[h] / has["total"][h])
+                kept = jnp.where(lane == h, has["log_total"][h], kept)
+            out[piece, start, :] = total.astype(bf16)
+            totals[piece][start, :] = kept
+
+        stages = (scored, weighed, mixed)
+        for turn in range(count + len(stages) - 1):
+            for k in range(len(stages)):
+                if 0 <= turn - k < count:
+                    stages[k](turn - k)
         return carry
 
-    lax.fori_loop(0, own_blocks, step, 0)
+    lax.fori_loop(0, own_blocks // side, step, 0)
 
 
 def attend_forward(parts, table, bias, heads, chosen):
@@ -312,33 +343,67 @@
 
     side = 2 if len(chosen) == 1 else 1
 
+    count = len(chosen) * side
+
     def step(step_at, carry):
-        for at, s in enumerate(chosen * side):
+        blocks, held = [], [{} for _ in range(count)]
+        for at in range(count):
             i = step_at * side + at // len(chosen)
-            at = at % len(chosen)
-            block = s * own_blocks + i
+            piece = at % len(chosen)
+            blocks.append((piece, i, chosen[piece] * own_blocks + i))
+
+        def scored(at):
+            piece, i, block = blocks[at]
             start = pl.multiple_of(i * BLK, BLK)
             here = pl.ds(pl.multiple_of(block * BLK, BLK), BLK)
-            queries = stacked_heads(rows[here, 0:PAD], query_masks)
-            upstream = stacked_heads(up_rows[at, pl.ds(start, BLK), :], up_masks)
-            keys = key_blocks(rows, table, block, PAD)
+            has = held[at]
+            has["queries"] = stacked_heads(rows[here, 0:PAD], query_masks)
+            has["upstream"] = stacked_heads(up_rows[piece, pl.ds(start, BLK), :], up_masks)
+            has["keys"] = key_blocks(rows, table, block, PAD)
             values = key_blocks(rows, table, block, 2 * PAD)
-            kept = totals[at][pl.ds(start, BLK), :]
-            log_total = jnp.concatenate([kept[:, h : h + 1] for h in range(heads)], axis=0)
-            scores = contract(queries, keys, (1, 1)) + bias[pl.ds(block, 1), :]
-            weights = jnp.exp(scores - log_total)
-            grad_weights = contract(upstream, values, (1, 1))
-            inner = jnp.sum(weights * grad_weights, axis=-1, keepdims=True)
-            grad_scores = (weights * (grad_weights - inner)).astype(bf16)
-            grad_query = contract(grad_scores, keys, (1, 0))
-            to = outs[s] if carried else outs[at]
-            to[pl.ds(start, BLK), 0:PAD] = unstacked_heads(grad_query, out_masks).astype(bf16)
-            key_part = contract(grad_scores, queries, (0, 0))
-            value_part = contract(weights.astype(bf16), upstream, (0, 0))
+            has["scores"] = contract(has["queries"], has["keys"], (1, 1))
+            has["grad_weights"] = contract(has["upstream"], values, (1, 1))
+
+        def weighed(at):
+            piece, i, block = blocks[at]
+            has = held[at]
+            kept = totals[piece][pl.ds(pl.multiple_of(i * BLK, BLK), BLK), :]
+            masked = bias[pl.ds(block, 1), :]
+            low, grad = [], []
+            for h in range(heads):
+                span = slice(h * BLK, (h + 1) * BLK)
+                weights = jnp.exp(has["scores"][span] + (masked - kept[:, h : h + 1]))
+                grad_weights = has["grad_weights"][span]
+                inner = jnp.sum(weights * grad_weights, axis=-1, keepdims=True)
+                low.append(weights.astype(bf16))
+                grad.append((weights * (grad_weights - inner)).astype(bf16))
+            has["weights"] = jnp.concatenate(low, axis=0)
+            has["grad_scores"] = jnp.concatenate(grad, axis=0)
+
+        def spread_back(at):
+            piece, i, block = blocks[at]
+            has = held[at]
+            to = outs[chosen[piece]] if carried else outs[piece]
+            grad_query = contract(has["grad_scores"], has["keys"], (1, 0))
+            to[pl.ds(pl.multiple_of(i * BLK, BLK), BLK), 0:PAD] = unstacked_heads(
+                grad_query, out_masks
+            ).astype(bf16)
+            has["key_part"] = contract(has["grad_scores"], has["queries"], (0, 0))
+            has["value_part"] = contract(has["weights"], has["upstream"], (0, 0))
+
+        def summed(at):
+            block, has = blocks[at][2], held[at]
             for j in range(KEYS // BLK):
                 there = pl.ds(pl.multiple_of(table[block, j] * BLK, BLK), BLK)
-                key_sum[there, :] += key_part[j * BLK : (j + 1) * BLK]
-                value_sum[there, :] += value_part[j * BLK : (j + 1) * BLK]
+                key_sum[there, :] += has["key_part"][j * BLK : (j + 1) * BLK]
+                value_sum[there, :] += has["value_part"][j * BLK : (j + 1) * BLK]
+
+        stages = (scored, weighed, spread_back, summed)
+        for turn in range(count + len(stages) - 1):
+            for k in ORDER:
+                at = turn - k
+                if 0 <= at < count:
+                    stages[k](at)
         return carry
 
     lax.fori_loop(0, own_blocks // side, step, 0)
@@ -579,12 +644,13 @@
         for c in range(hidden // cut):
             cols = slice(c * cut, (c + 1) * cut)
             u = contract(low_buf[...], up_w[s, :, cols], (1, 0)) + bias[:, cols]
-            square = u * u
-            t = jnp.tanh(u * (GELU_A + GELU_A * GELU_B * square))
+            cubic = (GELU_A * GELU_B) * (u * u)
+            t = jnp.tanh(u * (GELU_A + cubic))
             half = 0.5 + 0.5 * t
-            act_buf[s, :, cols] = (u * half).astype(bf16)
+            act = u * half
+            act_buf[s, :, cols] = act.astype(bf16)
             slope_buf[s, :, cols] = (
-                half + (0.5 * u) * (1.0 - t * t) * (GELU_A + 3.0 * GELU_A * GELU_B * square)
+                half + act * ((1.0 - t) * (GELU_A + 3.0 * cubic))
             ).astype(bf16)
         return carry
 

time: 263 us -> 261 us (level)
  Pallas kernels: 140 us -> 131 us
  waiting for transfers between devices: 58.5 us -> 65 us
    pallas_call x2, Pallas kernels: 32.2 us -> 27.6 us  [attend_backward(): pl.pallas_call(partial(attend_back_kernel, heads, chosen, pieces, own_blo...]
    ppermute x1, waiting for transfers between devices: 0.87 us -> 4.55 us  [swap_both(): return lax.ppermute(array, axes, [(t, t ^ 6) for t in range(size)])]
    pallas_call x2, Pallas kernels: 17.6 us -> 14.5 us  [attend_forward(): pl.pallas_call(partial(attend_kernel, heads, chosen, pieces, own_blocks),...]
  transfers between devices with their start and end apart: 45 -> 45, of which waited for: 20 -> 20; matrix products, arithmetic and copies ran while one was open for 4% -> 4% of each run, Pallas kernels for 38% -> 35%
where the time goes in v5:
time: 261 us; the launch traced here: 260 us
  Pallas kernels  131 us (50%)
  waiting for transfers between devices  65 us (25%)
  starting transfers between devices  43.6 us (17%)
  local copies, waits for them, and re-layouts  14 us (5%)
  other arithmetic  4.36 us (2%)
    pallas_call x1, Pallas kernels, layer_rows(): pl.pallas_call(partial(rows_kernel, [at for _, at in mixed], len(weights)...  31.9 us
    pallas_call x2, Pallas kernels, attend_backward(): pl.pallas_call(partial(attend_back_kernel, heads, chosen, pieces, own_blo...  27.6 us
    ppermute x14, waiting for transfers between devices, ring_send(): lax.ppermute(array, 'dp', [(order[i], order[(i + step) % size]) for i in...  25.2 us
    pallas_call x3, Pallas kernels, row_dot(): pl.pallas_call(kernel, grid=(lows[-1],), out_shape=[struct((far, *lead, p...  21 us
    ppermute x24, waiting for transfers between devices, swap(): return lax.ppermute(array, 'tensor', [(t, t ^ bit) for t in range(size)])  18.6 us
    ppermute x14, starting transfers between devices, ring_send(): lax.ppermute(array, 'dp', [(order[i], order[(i + step) % size]) for i in...  16.9 us
    pallas_call x2, Pallas kernels, attend_forward(): pl.pallas_call(partial(attend_kernel, heads, chosen, pieces, own_blocks),...  14.5 us
    all_to_all x3, starting transfers between devices, far_exchange(): lax.all_to_all(blocks, 'dp', 0, 0, axis_index_groups=groups, tiled=True)  12.6 us
  transfers between devices with their start and end apart: 45, of which 20 were waited for; matrix products, arithmetic and copies ran while one was open for 4% of the time, Pallas kernels for 35%

profile of v5, /device:TPU:0, one launch (start us, length us, event | category | flops | bytes accessed | tf_op | source)
XLA Modules:
  0.0 260.2 jit_solution(6853350612133090346)
XLA Ops:
  0.7 1.5 pack_queries.1._.refs_4_
  2.2 3.0 %collective-permute-start.4 = (bf16[96,768]{1,0:T(8,128)(2,1)}, bf16[96,768]{1,0:T(8,128)(2,1)S(1)}, u32[]{:S(2)}, u32[]{:S(2)}) collective-permute-start(bf16[96,768]{1,0:T(8,128)(2,1)} %pack_queries.1._.refs_4_), channel_id=1, source_target_pairs={{0,8},{8,16},{16,24},{24,28},{28,20},{20,12},{12,4},{4,0},{1,9},{9... | collective-permute-start | bytes 442376 | tf_op jit(solution)/shard_map/ppermute | solution.py:64
  5.2 1.7 copy.38.down
  6.9 1.9 pack_weights.1.a
  8.8 1.6 collective-permute-start.1
  10.8 1.6 collective-permute-start.6
  12.4 3.3 %collective-permute-done.5.refs_6_ = bf16[96,768]{1,0:T(8,128)(2,1)S(1)} collective-permute-done((bf16[96,768]{1,0:T(8,128)(2,1)}, bf16[96,768]{1,0:T(8,128)(2,1)S(1)}, u32[]{:S(2)}, u32[]{:S(2)}) %collective-permute-start.5) | collective-permute-done | bytes 147488 | tf_op jit(solution)/shard_map/ppermute | solution.py:64
  16.2 1.6 collective-permute-start.8
  19.4 2.1 held.1
  23.4 1.6 collective-permute-start.10
  25.0 3.1 %collective-permute-done.9.refs_10_.refs_1_ = bf16[96,768]{1,0:T(8,128)(2,1)S(1)} collective-permute-done((bf16[96,768]{1,0:T(8,128)(2,1)S(1)}, bf16[96,768]{1,0:T(8,128)(2,1)S(1)}, u32[]{:S(2)}, u32[]{:S(2)}) %collective-permute-start.9) | collective-permute-done | bytes 147488 | tf_op jit(solution)/shard_map/ppermute | solution.py:64
  29.4 2.0 pair_weights.1.refs_6_
  31.4 1.6 collective-permute-start.14
  32.9 6.9 %collective-permute-done.2.refs_2_ = bf16[512,768]{1,0:T(8,128)(2,1)} collective-permute-done((bf16[512,768]{1,0:T(8,128)(2,1)}, bf16[512,768]{1,0:T(8,128)(2,1)}, u32[]{:S(2)}, u32[]{:S(2)}) %collective-permute-start.2) | collective-permute-done | bytes 786464 | tf_op jit(solution)/shard_map/ppermute | solution.py:35
  40.4 6.8 %collective-permute-done.14.refs_7_ = bf16[96,3584]{1,0:T(8,128)(2,1)S(1)} collective-permute-done((bf16[96,3584]{1,0:T(8,128)(2,1)}, bf16[96,3584]{1,0:T(8,128)(2,1)S(1)}, u32[]{:S(2)}, u32[]{:S(2)}) %collective-permute-start.14) | collective-permute-done | bytes 688160 | tf_op jit(solution)/shard_map/ppermute | solution.py:64
  47.2 1.6 collective-permute-start.16
  52.7 5.2 %collective-permute-done.15.refs_8_ = bf16[96,3584]{1,0:T(8,128)(2,1)S(1)} collective-permute-done((bf16[96,3584]{1,0:T(8,128)(2,1)}, bf16[96,3584]{1,0:T(8,128)(2,1)S(1)}, u32[]{:S(2)}, u32[]{:S(2)}) %collective-permute-start.15) | collective-permute-done | bytes 688160 | tf_op jit(solution)/shard_map/ppermute | solution.py:64
  58.5 2.8 %collective-permute-done.16.refs_9_ = bf16[96,3584]{1,0:T(8,128)(2,1)S(1)} collective-permute-done((bf16[96,3584]{1,0:T(8,128)(2,1)S(1)}, bf16[96,3584]{1,0:T(8,128)(2,1)S(1)}, u32[]{:S(2)}, u32[]{:S(2)}) %collective-permute-start.16) | collective-permute-done | bytes 688160 | tf_op jit(solution)/shard_map/ppermute | solution.py:64
  61.3 1.6 collective-permute-start.18
  62.9 8.3 %project_in.1 = (bf16[512,768]{1,0:T(8,128)(2,1)}, bf16[512,768]{1,0:T(8,128)(2,1)}, bf16[512,768]{1,0:T(8,128)(2,1)}, bf16[512,768]{1,0:T(8,128)(2,1)}, bf16[2,...) custom-call(bf16[512,768]{1,0:T(8,128)(2,1)} %refs_4_.1, ...), custom_call_target="tpu_custom_call" | custom-call | flops 4831838208 | bytes 25165824 | tf_op jit(solution)/shard_map/project_in/pallas_call | solution.py:1111
  71.1 7.2 %attend_forward.3 = (bf16[2,512,256]{2,1,0:T(8,128)(2,1)}, f32[512,128]{1,0:T(8,128)}, f32[512,128]{1,0:T(8,128)}) custom-call(s32[32,128]{1,0:T(8,128)} %get-tuple-element.64.table, bf16[512,768]{1,0:T(8,128)(2,1)} %get-tuple-element.65.refs_0_, bf16[512,768]{1,0:T(8,128)(2,1)} %get-tuple-element.66.refs_1_, bf16[512,768]{1,0:T(8,128)(2,1)} %get-tuple-element.67.refs_2_, ...), custom_call_target="tpu_custom_call" | custom-call | flops 4831838208 | bytes 16777216 | tf_op jit(solution)/shard_map/attend_forward/pallas_call | solution.py:278
  79.1 1.6 collective-permute-start.20
  80.7 7.3 %attend_forward.2 = (bf16[2,512,256]{2,1,0:T(8,128)(2,1)}, f32[512,128]{1,0:T(8,128)}, f32[512,128]{1,0:T(8,128)}) custom-call(s32[32,128]{1,0:T(8,128)} %get-tuple-element.64.table, bf16[512,768]{1,0:T(8,128)(2,1)} %get-tuple-element.65.refs_0_, bf16[512,768]{1,0:T(8,128)(2,1)} %get-tuple-element.66.refs_1_, bf16[512,768]{1,0:T(8,128)(2,1)} %get-tuple-element.67.refs_2_, ...), custom_call_target="tpu_custom_call" | custom-call | flops 4831838208 | bytes 16777216 | tf_op jit(solution)/shard_map/attend_forward/pallas_call | solution.py:278
  91.4 3.3 %collective-permute-done.19.refs_12_ = bf16[96,3584]{1,0:T(8,128)(2,1)} collective-permute-done((bf16[96,3584]{1,0:T(8,128)(2,1)}, bf16[96,3584]{1,0:T(8,128)(2,1)}, u32[]{:S(2)}, u32[]{:S(2)}) %collective-permute-start.19) | collective-permute-done | bytes 688160 | tf_op jit(solution)/shard_map/ppermute | solution.py:64
  99.1 31.9 %layer_rows.1 = (bf16[512,768]{1,0:T(8,128)(2,1)}, bf16[4,512,768]{2,1,0:T(8,128)(2,1)}, bf16[4,512,768]{2,1,0:T(8,128)(2,1)}, bf16[3,2,4,96,512]{4,3,2,1,0:T(8,...) custom-call(s32[1]{0:T(128)S(6)} %copy.40.length_ref.length, ...), custom_call_target="tpu_custom_call" | custom-call | flops 176160768 | bytes 393216 | tf_op jit(solution)/shard_map/layer_rows/pallas_call | solution.py:748
  133.5 9.4 %attend_backward.2 = (bf16[512,256]{1,0:T(8,128)(2,1)}, f32[2048,256]{1,0:T(8,128)}, f32[2048,256]{1,0:T(8,128)}) custom-call(s32[32,128]{1,0:T(8,128)} %get-tuple-element.64.table, bf16[512,768]{1,0:T(8,128)(2,1)} %get-tuple-element.65.refs_0_, bf16[512,768]{1,0:T(8,128)(2,1)} %get-tuple-element.66.refs_1_, bf16[512,768]{1,0:T(8,128)(2,1)} %get-tuple-element.67.refs_2_, ...), custom_call_target="tpu_custom_call" | custom-call | flops 23592960 | bytes 196608 | tf_op jit(solution)/shard_map/attend_backward/pallas_call | solution.py:459
  143.0 3.8 %collective-permute-done.31.refs_9_.refs_6_ = bf16[560,256]{1,0:T(8,128)(2,1)} collective-permute-done((bf16[560,256]{1,0:T(8,128)(2,1)}, bf16[560,256]{1,0:T(8,128)(2,1)}, u32[]{:S(2)}, u32[]{:S(2)}) %collective-permute-start.31) | collective-permute-done | bytes 286752 | tf_op jit(solution)/shard_map/ppermute | solution.py:35
  146.8 1.7 copy-done
  148.4 6.3 %row_dot.3.refs_12_ = bf16[4,2,2,96,768]{4,3,2,1,0:T(8,128)(2,1)} custom-call(bf16[3,2,4,96,512]{4,3,2,1,0:T(8,128)(2,1)} %get-tuple-element.79.refs_0_.refs_2_, bf16[3,2,4,96,512]{4,3,2,1,0:T(8,128)(2,1)} %collective-permute-done.32.refs_1_.refs_3_, bf16[4,512,768]{2,1,0:T(8,128)(2,1)} %get-tuple-element.80.refs_2_.refs_3_.refs_4_.refs_5_, ...), custom_call_target="tpu_custom_call" | custom-call | flops 37748736 | bytes 131072 | tf_op jit(solution)/shard_map/row_dot/pallas_call | solution.py:862
  154.7 4.8 %all-to-all-start = ((bf16[4,2,2,96,768]{4,3,2,1,0:T(8,128)(2,1)}), bf16[4,2,2,96,768]{4,3,2,1,0:T(8,128)(2,1)S(1)}, u32[]{:S(2)}, u32[]{:S(2)}) async-start(bf16[4,2,2,96,768]{4,3,2,1,0:T(8,128)(2,1)} %row_dot.3.refs_12_), calls=%async_computation | async-start | bytes 4718592 | tf_op jit(solution)/shard_map/all_to_all | solution.py:86
  159.6 8.2 %row_dot.4 = (bf16[1,1,4,96,1024]{4,3,2,1,0:T(8,128)(2,1)}, bf16[1,1,4,96,1024]{4,3,2,1,0:T(8,128)(2,1)}, bf16[1,1,4,96,1024]{4,3,2,1,0:T(8,128)(2,1)}, bf16[1,1,4,96,1024]{4,3,2,1,0:T(8,128)(2,1)}) custom-call(bf16[3,2,4,96,512]{4,3,2,1,0:T(8,128)(2,1)} %get-tuple-element.79.refs_0_.refs_2_, ...), custom_call_target="tpu_custom_call" | custom-call | flops 50331648 | bytes 131072 | tf_op jit(solution)/shard_map/row_dot/pallas_call | solution.py:862
  169.2 2.0 collective-permute-start.37
  171.3 18.1 %attend_backward.3 = (bf16[512,768]{1,0:T(8,128)(2,1)}, bf16[512,768]{1,0:T(8,128)(2,1)}, bf16[512,768]{1,0:T(8,128)(2,1)}, bf16[512,768]{1,0:T(8,128)(2,1)}, bf16[16,768]{1,0:T(8,128)(2,1)}) custom-call(s32[32,128]{1,0:T(8,128)} %get-tuple-element.64.table, bf16[512,768]{1,0:T(8,128)(2,1)} %get-tuple-element.65.refs_0_, ...), custom_call_target="tpu_custom_call" | custom-call | flops 70778880 | bytes 196608 | tf_op jit(solution)/shard_map/attend_backward/pallas_call | solution.py:459
  189.4 6.6 %row_dot.5 = (bf16[1,1,4,112,768]{4,3,2,1,0:T(8,128)(2,1)}, bf16[1,1,4,112,768]{4,3,2,1,0:T(8,128)(2,1)}) custom-call(bf16[1,2,4,96,512]{4,3,2,1,0:T(8,128)(2,1)} %bitcast.30, bf16[1,2,4,96,512]{4,3,2,1,0:T(8,128)(2,1)} %bitcast.31, bf16[1,2,4,96,512]{4,3,2,1,0:T(8,128)(2,1)} %bitcast.32, bf16[1,2,4,96,512]{4,3,2,1,0:T(8,128)(2,1)} %bitcast.33, ...), custom_call_target="tpu_custom_call" | custom-call | flops 37748736 | bytes 131072 | tf_op jit(solution)/shard_map/row_dot/pallas_call | solution.py:862
  196.0 4.3 %spread.2.refs_4_ = bf16[2,512,768]{2,1,0:T(8,128)(2,1)} custom-call(bf16[512,768]{1,0:T(8,128)(2,1)} %get-tuple-element.92.first, bf16[512,768]{1,0:T(8,128)(2,1)} %get-tuple-element.93.second, bf16[768,768]{1,0:T(8,128)(2,1)} %get-tuple-element.91.w, bf16[1,1,4,112,768]{4,3,2,1,0:T(8,128)(2,1)} %get-tuple-element.99.refs_0_), custom_call_target="tpu_custom_call" | custom-call | flops 18874368 | bytes 81920 | tf_op jit(solution)/shard_map/spread/pallas_call | solution.py:979
  200.3 4.5 %collective-permute-done.37 = bf16[1,1,4,96,1024]{4,3,2,1,0:T(8,128)(2,1)} collective-permute-done((bf16[1,1,4,96,1024]{4,3,2,1,0:T(8,128)(2,1)}, bf16[1,1,4,96,1024]{4,3,2,1,0:T(8,128)(2,1)}, u32[]{:S(2)}, u32[]{:S(2)}) %collective-permute-start.37) | collective-permute-done | bytes 786464 | tf_op jit(solution)/shard_map/ppermute | solution.py:46
  204.8 3.1 %joined_sums.2.refs_2_ = bf16[4,96,1024]{2,1,0:T(8,128)(2,1)} custom-call(bf16[4,96,1024]{2,1,0:T(8,128)(2,1)} %bitcast.34, bf16[4,96,1024]{2,1,0:T(8,128)(2,1)} %bitcast.35, bf16[4,96,1024]{2,1,0:T(8,128)(2,1)} %bitcast.12.refs_2_, bf16[4,96,1024]{2,1,0:T(8,128)(2,1)} %bitcast.13.refs_3_, bf16[2,512,768]{2,1,0:T(8,128)(2,1)} %spread.2.refs_4_), custom_call_target="tpu_custom_call" | custom-call | flops 24576 | bytes 49152 | tf_op jit(solution)/shard_map/joined_sums/pallas_call | solution.py:949
  208.0 5.9 %all-to-all-done.ref = bf16[4,2,2,96,768]{4,3,2,1,0:T(8,128)(2,1)S(1)} async-done(((bf16[4,2,2,96,768]{4,3,2,1,0:T(8,128)(2,1)}), bf16[4,2,2,96,768]{4,3,2,1,0:T(8,128)(2,1)S(1)}, u32[]{:S(2)}, u32[]{:S(2)}) %all-to-all-start) | async-done | bytes 2359328 | tf_op jit(solution)/shard_map/all_to_all | solution.py:86
  213.9 3.5 %all-to-all-start.2 = ((bf16[4,96,1024]{2,1,0:T(8,128)(2,1)}), bf16[4,96,1024]{2,1,0:T(8,128)(2,1)S(1)}, u32[]{:S(2)}, u32[]{:S(2)}) async-start(bf16[4,96,1024]{2,1,0:T(8,128)(2,1)} %joined_sums.2.refs_2_), calls=%async_computation.2 | async-start | bytes 1572864 | tf_op jit(solution)/shard_map/all_to_all | solution.py:86
  218.4 5.0 %spread.3 = (bf16[512,768]{1,0:T(8,128)(2,1)}, f32[512,768]{1,0:T(8,128)}) custom-call(bf16[512,768]{1,0:T(8,128)(2,1)} %get-tuple-element.89.first, bf16[512,768]{1,0:T(8,128)(2,1)} %get-tuple-element.90.second, bf16[768,768]{1,0:T(8,128)(2,1)} %get-tuple-element.91.w, bf16[2,512,768]{2,1,0:T(8,128)(2,1)} %collective-permute-done.34.refs_0_, ...), custom_call_target="tpu_custom_call" | custom-call | flops 18874368 | bytes 81920 | tf_op jit(solution)/shard_map/spread/pallas_call | solution.py:979
  223.9 2.7 %fold.1 = (bf16[2,96,768]{2,1,0:T(8,128)(2,1)}, bf16[2,96,768]{2,1,0:T(8,128)(2,1)}) custom-call(bf16[4,2,2,96,768]{4,3,2,1,0:T(8,128)(2,1)} %copy-done.1, bf16[512,768]{1,0:T(8,128)(2,1)} %get-tuple-element.105.refs_0_), custom_call_target="tpu_custom_call" | custom-call | flops 18432 | bytes 55296 | tf_op jit(solution)/shard_map/fold/pallas_call | solution.py:924
  226.6 7.8 %collective-permute-done.39 = bf16[1,1,4,112,768]{4,3,2,1,0:T(8,128)(2,1)} collective-permute-done((bf16[1,1,4,112,768]{4,3,2,1,0:T(8,128)(2,1)}, bf16[1,1,4,112,768]{4,3,2,1,0:T(8,128)(2,1)}, u32[]{:S(2)}, u32[]{:S(2)}) %collective-permute-start.39) | collective-permute-done | bytes 688160 | tf_op jit(solution)/shard_map/ppermute | solution.py:40
  234.4 2.4 joined_sums.3.refs_0_
  237.2 4.3 %all-to-all-start.1 = ((bf16[4,112,768]{2,1,0:T(8,128)(2,1)}), bf16[4,112,768]{2,1,0:T(8,128)(2,1)S(1)}, u32[]{:S(2)}, u32[]{:S(2)}) async-start(bf16[4,112,768]{2,1,0:T(8,128)(2,1)} %joined_sums.3.refs_0_), calls=%async_computation.1 | async-start | bytes 1376256 | tf_op jit(solution)/shard_map/all_to_all | solution.py:86
  243.6 5.1 %collective-permute-done.40.b_ref = bf16[2,96,768]{2,1,0:T(8,128)(2,1)S(1)} collective-permute-done((bf16[2,96,768]{2,1,0:T(8,128)(2,1)S(1)}, bf16[2,96,768]{2,1,0:T(8,128)(2,1)S(1)}, u32[]{:S(2)}, u32[]{:S(2)}) %collective-permute-start.40) | collective-permute-done | bytes 294944 | tf_op jit(solution)/shard_map/ppermute | solution.py:35
  249.4 1.8 plus.1
  252.1 2.7 %convert_add_fusion = f32[512,768]{1,0:T(8,128)} fusion(f32[512,768]{1,0:T(8,128)} %get-tuple-element.104, bf16[512,768]{1,0:T(8,128)(2,1)S(1)} %collective-permute-done.38), kind=kLoop, calls=%fused_computation.1 | loop fusion | flops 786432 | bytes 3932160 | tf_op jit(solution)/shard_map/add | solution.py:1289
  254.9 1.7 collective-permute-done.41
  (158 shorter events, 31.8 us)
Async XLA Ops:
  2.2 8.6 %collective-permute-start.4 = (bf16[96,768]{1,0:T(8,128)(2,1)}, bf16[96,768]{1,0:T(8,128)(2,1)S(1)}, u32[]{:S(2)}, u32[]{:S(2)}) collective-permute-start(bf16[96,768]{1,0:T(8,128)(2,1)} %pack_queries.1._.refs_4_), channel_id=1, source_target_pairs={{0,8},{8,16},{16,24},{24,28},{28,20},{20,12},{12,4},{4,0},{1,9},{9... | collective-permute-start | bytes 442376 | tf_op jit(solution)/shard_map/ppermute | solution.py:64
  8.8 42.8 %copy-start.29 = (f32[192]{0:T(256)S(1)}, f32[192]{0:T(256)}, u32[]{:S(2)}) copy-start(f32[192]{0:T(256)} %param.26) | copy-start | bytes 2308
  8.8 42.8 %copy-start.30 = (f32[192]{0:T(256)S(1)}, f32[192]{0:T(256)}, u32[]{:S(2)}) copy-start(f32[192]{0:T(256)} %param.23) | copy-start | bytes 2308
  8.8 9.8 %collective-permute-start.1 = (bf16[96,1792]{1,0:T(8,128)(2,1)}, bf16[96,1792]{1,0:T(8,128)(2,1)S(1)}, u32[]{:S(2)}, u32[]{:S(2)}) collective-permute-start(bf16[96,1792]{1,0:T(8,128)(2,1)} %pack_weights.1.a), channel_id=1, source_target_pairs={{0,2},{1,3},{2,0},{3,1},{4,6},{5,7},{6,4},{7,5},{8,10},{9,11},{10,... | collective-permute-start | bytes 1032200 | tf_op jit(solution)/shard_map/ppermute | solution.py:35
  10.4 5.4 %collective-permute-start.5 = (bf16[96,768]{1,0:T(8,128)(2,1)}, bf16[96,768]{1,0:T(8,128)(2,1)S(1)}, u32[]{:S(2)}, u32[]{:S(2)}) collective-permute-start(bf16[96,768]{1,0:T(8,128)(2,1)} %pack_queries.1._.refs_4_), channel_id=1, source_target_pairs={{0,4},{8,0},{16,8},{24,16},{28,24},{20,28},{12,20},{4,12},{1,5},{9... | collective-permute-start | bytes 442376 | tf_op jit(solution)/shard_map/ppermute | solution.py:64
  10.8 52.0 %copy-start.31 = (bf16[96,768]{1,0:T(8,128)(2,1)}, bf16[96,768]{1,0:T(8,128)(2,1)S(1)}, u32[]{:S(2)}) copy-start(bf16[96,768]{1,0:T(8,128)(2,1)S(1)} %collective-permute-done.4.refs_5_) | copy-start | bytes 442372
  10.8 5.4 %collective-permute-start.6 = (bf16[96,768]{1,0:T(8,128)(2,1)S(1)}, bf16[96,768]{1,0:T(8,128)(2,1)S(1)}, u32[]{:S(2)}, u32[]{:S(2)}) collective-permute-start(bf16[96,768]{1,0:T(8,128)(2,1)S(1)} %collective-permute-done.4.refs_5_), channel_id=1, source_target_pairs={{0,8},{8,16},{16,24},{24,28},{28,20},{20,12},{12,4},{4,0},{1,9},{9... | collective-permute-start | bytes 442376 | tf_op jit(solution)/shard_map/ppermute | solution.py:64
  15.7 7.2 %collective-permute-start.7 = (bf16[96,768]{1,0:T(8,128)(2,1)S(1)}, bf16[96,768]{1,0:T(8,128)(2,1)S(1)}, u32[]{:S(2)}, u32[]{:S(2)}) collective-permute-start(bf16[96,768]{1,0:T(8,128)(2,1)S(1)} %collective-permute-done.5.refs_6_), channel_id=1, source_target_pairs={{0,4},{8,0},{16,8},{24,16},{28,24},{20,28},{12,20},{4,12},{1,5},{9... | collective-permute-start | bytes 442376 | tf_op jit(solution)/shard_map/ppermute | solution.py:64
  16.2 7.2 %collective-permute-start.8 = (bf16[96,768]{1,0:T(8,128)(2,1)S(1)}, bf16[96,768]{1,0:T(8,128)(2,1)S(1)}, u32[]{:S(2)}, u32[]{:S(2)}) collective-permute-start(bf16[96,768]{1,0:T(8,128)(2,1)S(1)} %collective-permute-done.6.refs_7_), channel_id=1, source_target_pairs={{0,8},{8,16},{16,24},{24,28},{28,20},{20,12},{12,4},{4,0},{1,9},{9... | collective-permute-start | bytes 442376 | tf_op jit(solution)/shard_map/ppermute | solution.py:64
  21.4 18.4 %collective-permute-start.2 = (bf16[512,768]{1,0:T(8,128)(2,1)}, bf16[512,768]{1,0:T(8,128)(2,1)}, u32[]{:S(2)}, u32[]{:S(2)}) collective-permute-start(bf16[512,768]{1,0:T(8,128)(2,1)} %held.1), channel_id=1, source_target_pairs={{0,2},{1,3},{2,0},{3,1},{4,6},{5,7},{6,4},{7,5},{8,10},{9,11},{10,... | collective-permute-start | bytes 2359304 | tf_op jit(solution)/shard_map/ppermute | solution.py:35
  22.9 5.1 %collective-permute-start.9 = (bf16[96,768]{1,0:T(8,128)(2,1)S(1)}, bf16[96,768]{1,0:T(8,128)(2,1)S(1)}, u32[]{:S(2)}, u32[]{:S(2)}) collective-permute-start(bf16[96,768]{1,0:T(8,128)(2,1)S(1)} %collective-permute-done.7.refs_8_), channel_id=1, source_target_pairs={{0,4},{8,0},{16,8},{24,16},{28,24},{20,28},{12,20},{4,12},{1,5},{9... | collective-permute-start | bytes 442376 | tf_op jit(solution)/shard_map/ppermute | solution.py:64
  23.4 5.1 %collective-permute-start.10 = (bf16[96,768]{1,0:T(8,128)(2,1)S(1)}, bf16[96,768]{1,0:T(8,128)(2,1)S(1)}, u32[]{:S(2)}, u32[]{:S(2)}) collective-permute-start(bf16[96,768]{1,0:T(8,128)(2,1)S(1)} %collective-permute-done.8.refs_9_.refs_0_), channel_id=1, source_target_pairs={{0,8},{8,16},{16,24},{24,28},{28,20},{20,12},{12,4},{4,0},{1,9},{9... | collective-permute-start | bytes 442376 | tf_op jit(solution)/shard_map/ppermute | solution.py:64
  31.4 15.8 %collective-permute-start.14 = (bf16[96,3584]{1,0:T(8,128)(2,1)}, bf16[96,3584]{1,0:T(8,128)(2,1)S(1)}, u32[]{:S(2)}, u32[]{:S(2)}) collective-permute-start(bf16[96,3584]{1,0:T(8,128)(2,1)} %pair_weights.1.refs_6_), channel_id=1, source_target_pairs={{0,8},{8,16},{16,24},{24,28},{28,20},{20,12},{12,4},{4,0},{1,9},{9... | collective-permute-start | bytes 2064392 | tf_op jit(solution)/shard_map/ppermute | solution.py:64
  32.9 19.3 %collective-permute-start = (bf16[512,768]{1,0:T(8,128)(2,1)S(1)}, bf16[512,768]{1,0:T(8,128)(2,1)}, u32[]{:S(2)}, u32[]{:S(2)}) collective-permute-start(bf16[512,768]{1,0:T(8,128)(2,1)S(1)} %copy-done.3), channel_id=1, source_target_pairs={{0,1},{1,0},{2,3},{3,2},{4,5},{5,4},{6,7},{7,6},{8,9},{9,8},{10,11... | collective-permute-start | bytes 2359304 | tf_op jit(solution)/shard_map/ppermute | solution.py:35
  39.8 18.6 %collective-permute-start.3 = (bf16[512,768]{1,0:T(8,128)(2,1)}, bf16[512,768]{1,0:T(8,128)(2,1)}, u32[]{:S(2)}, u32[]{:S(2)}) collective-permute-start(bf16[512,768]{1,0:T(8,128)(2,1)} %collective-permute-done.2.refs_2_), channel_id=1, source_target_pairs={{0,1},{1,0},{2,3},{3,2},{4,5},{5,4},{6,7},{7,6},{8,9},{9,8},{10,11... | collective-permute-start | bytes 2359304 | tf_op jit(solution)/shard_map/ppermute | solution.py:35
  39.8 18.1 %collective-permute-start.15 = (bf16[96,3584]{1,0:T(8,128)(2,1)}, bf16[96,3584]{1,0:T(8,128)(2,1)S(1)}, u32[]{:S(2)}, u32[]{:S(2)}) collective-permute-start(bf16[96,3584]{1,0:T(8,128)(2,1)} %pair_weights.1.refs_6_), channel_id=1, source_target_pairs={{0,4},{8,0},{16,8},{24,16},{28,24},{20,28},{12,20},{4,12},{1,5},{9... | collective-permute-start | bytes 2064392 | tf_op jit(solution)/shard_map/ppermute | solution.py:64
  47.2 14.1 %collective-permute-start.16 = (bf16[96,3584]{1,0:T(8,128)(2,1)S(1)}, bf16[96,3584]{1,0:T(8,128)(2,1)S(1)}, u32[]{:S(2)}, u32[]{:S(2)}) collective-permute-start(bf16[96,3584]{1,0:T(8,128)(2,1)S(1)} %collective-permute-done.14.refs_7_), channel_id=1, source_target_pairs={{0,8},{8,16},{16,24},{24,28},{28,20},{20,12},{12,4},{4,0},{1,9},{9... | collective-permute-start | bytes 2064392 | tf_op jit(solution)/shard_map/ppermute | solution.py:64
  52.2 26.2 %collective-permute-start.21 = (bf16[96,3584]{1,0:T(8,128)(2,1)}, bf16[96,3584]{1,0:T(8,128)(2,1)}, u32[]{:S(2)}, u32[]{:S(2)}) collective-permute-start(bf16[96,3584]{1,0:T(8,128)(2,1)} %pair_weights.1.refs_6_), channel_id=1, source_target_pairs={{0,1},{1,0},{2,3},{3,2},{4,5},{5,4},{6,7},{7,6},{8,9},{9,8},{10,11... | collective-permute-start | bytes 2064392 | tf_op jit(solution)/shard_map/ppermute | solution.py:35
  52.2 36.7 %collective-permute-start.22 = (bf16[96,3584]{1,0:T(8,128)(2,1)S(1)}, bf16[96,3584]{1,0:T(8,128)(2,1)S(1)}, u32[]{:S(2)}, u32[]{:S(2)}) collective-permute-start(bf16[96,3584]{1,0:T(8,128)(2,1)S(1)} %collective-permute-done.14.refs_7_), channel_id=1, source_target_pairs={{0,1},{1,0},{2,3},{3,2},{4,5},{5,4},{6,7},{7,6},{8,9},{9,8},{10,11... | collective-permute-start | bytes 2064392 | tf_op jit(solution)/shard_map/ppermute | solution.py:35
  57.9 20.8 %collective-permute-start.17 = (bf16[96,3584]{1,0:T(8,128)(2,1)S(1)}, bf16[96,3584]{1,0:T(8,128)(2,1)}, u32[]{:S(2)}, u32[]{:S(2)}) collective-permute-start(bf16[96,3584]{1,0:T(8,128)(2,1)S(1)} %collective-permute-done.15.refs_8_), channel_id=1, source_target_pairs={{0,4},{8,0},{16,8},{24,16},{28,24},{20,28},{12,20},{4,12},{1,5},{9... | collective-permute-start | bytes 2064392 | tf_op jit(solution)/shard_map/ppermute | solution.py:64
  58.5 30.6 %collective-permute-start.23 = (bf16[96,3584]{1,0:T(8,128)(2,1)S(1)}, bf16[96,3584]{1,0:T(8,128)(2,1)}, u32[]{:S(2)}, u32[]{:S(2)}) collective-permute-start(bf16[96,3584]{1,0:T(8,128)(2,1)S(1)} %collective-permute-done.15.refs_8_), channel_id=1, source_target_pairs={{0,1},{1,0},{2,3},{3,2},{4,5},{5,4},{6,7},{7,6},{8,9},{9,8},{10,11... | collective-permute-start | bytes 2064392 | tf_op jit(solution)/shard_map/ppermute | solution.py:35
  61.3 17.9 %collective-permute-start.18 = (bf16[96,3584]{1,0:T(8,128)(2,1)S(1)}, bf16[96,3584]{1,0:T(8,128)(2,1)}, u32[]{:S(2)}, u32[]{:S(2)}) collective-permute-start(bf16[96,3584]{1,0:T(8,128)(2,1)S(1)} %collective-permute-done.16.refs_9_), channel_id=1, source_target_pairs={{0,8},{8,16},{16,24},{24,28},{28,20},{20,12},{12,4},{4,0},{1,9},{9... | collective-permute-start | bytes 2064392 | tf_op jit(solution)/shard_map/ppermute | solution.py:64
  78.5 12.3 %collective-permute-start.12 = (bf16[2,512,256]{2,1,0:T(8,128)(2,1)}, bf16[2,512,256]{2,1,0:T(8,128)(2,1)S(1)}, u32[]{:S(2)}, u32[]{:S(2)}) collective-permute-start(bf16[2,512,256]{2,1,0:T(8,128)(2,1)} %get-tuple-element.71), channel_id=1, source_target_pairs={{0,2},{1,3},{2,0},{3,1},{4,6},{5,7},{6,4},{7,5},{8,10},{9,11},{10,... | collective-permute-start | bytes 1572872 | tf_op jit(solution)/shard_map/ppermute | solution.py:35
  78.7 16.1 %collective-permute-start.19 = (bf16[96,3584]{1,0:T(8,128)(2,1)}, bf16[96,3584]{1,0:T(8,128)(2,1)}, u32[]{:S(2)}, u32[]{:S(2)}) collective-permute-start(bf16[96,3584]{1,0:T(8,128)(2,1)} %collective-permute-done.17.refs_10_), channel_id=1, source_target_pairs={{0,4},{8,0},{16,8},{24,16},{28,24},{20,28},{12,20},{4,12},{1,5},{9... | collective-permute-start | bytes 2064392 | tf_op jit(solution)/shard_map/ppermute | solution.py:64
  79.1 15.8 %collective-permute-start.20 = (bf16[96,3584]{1,0:T(8,128)(2,1)}, bf16[96,3584]{1,0:T(8,128)(2,1)}, u32[]{:S(2)}, u32[]{:S(2)}) collective-permute-start(bf16[96,3584]{1,0:T(8,128)(2,1)} %collective-permute-done.18.refs_11_), channel_id=1, source_target_pairs={{0,8},{8,16},{16,24},{24,28},{28,20},{20,12},{12,4},{4,0},{1,9},{9... | collective-permute-start | bytes 2064392 | tf_op jit(solution)/shard_map/ppermute | solution.py:64
  89.0 1.6 collective-permute-start.11
  89.1 6.9 %collective-permute-start.24 = (bf16[96,3584]{1,0:T(8,128)(2,1)S(1)}, bf16[96,3584]{1,0:T(8,128)(2,1)S(1)}, u32[]{:S(2)}, u32[]{:S(2)}) collective-permute-start(bf16[96,3584]{1,0:T(8,128)(2,1)S(1)} %collective-permute-done.16.refs_9_), channel_id=1, source_target_pairs={{0,1},{1,0},{2,3},{3,2},{4,5},{5,4},{6,7},{7,6},{8,9},{9,8},{10,11... | collective-permute-start | bytes 2064392 | tf_op jit(solution)/shard_map/ppermute | solution.py:35
  90.6 7.0 %collective-permute-start.25 = (bf16[96,3584]{1,0:T(8,128)(2,1)}, bf16[96,3584]{1,0:T(8,128)(2,1)S(1)}, u32[]{:S(2)}, u32[]{:S(2)}) collective-permute-start(bf16[96,3584]{1,0:T(8,128)(2,1)} %collective-permute-done.17.refs_10_), channel_id=1, source_target_pairs={{0,1},{1,0},{2,3},{3,2},{4,5},{5,4},{6,7},{7,6},{8,9},{9,8},{10,11... | collective-permute-start | bytes 2064392 | tf_op jit(solution)/shard_map/ppermute | solution.py:35
  91.3 7.1 %collective-permute-start.26 = (bf16[96,3584]{1,0:T(8,128)(2,1)}, bf16[96,3584]{1,0:T(8,128)(2,1)}, u32[]{:S(2)}, u32[]{:S(2)}) collective-permute-start(bf16[96,3584]{1,0:T(8,128)(2,1)} %collective-permute-done.18.refs_11_), channel_id=1, source_target_pairs={{0,1},{1,0},{2,3},{3,2},{4,5},{5,4},{6,7},{7,6},{8,9},{9,8},{10,11... | collective-permute-start | bytes 2064392 | tf_op jit(solution)/shard_map/ppermute | solution.py:35
  94.7 3.7 %collective-permute-start.27 = (bf16[96,3584]{1,0:T(8,128)(2,1)}, bf16[96,3584]{1,0:T(8,128)(2,1)}, u32[]{:S(2)}, u32[]{:S(2)}) collective-permute-start(bf16[96,3584]{1,0:T(8,128)(2,1)} %collective-permute-done.19.refs_12_), channel_id=1, source_target_pairs={{0,1},{1,0},{2,3},{3,2},{4,5},{5,4},{6,7},{7,6},{8,9},{9,8},{10,11... | collective-permute-start | bytes 2064392 | tf_op jit(solution)/shard_map/ppermute | solution.py:35
  95.0 3.5 %collective-permute-start.28 = (bf16[96,3584]{1,0:T(8,128)(2,1)}, bf16[96,3584]{1,0:T(8,128)(2,1)}, u32[]{:S(2)}, u32[]{:S(2)}) collective-permute-start(bf16[96,3584]{1,0:T(8,128)(2,1)} %collective-permute-done.20.refs_13_), channel_id=1, source_target_pairs={{0,1},{1,0},{2,3},{3,2},{4,5},{5,4},{6,7},{7,6},{8,9},{9,8},{10,11... | collective-permute-start | bytes 2064392 | tf_op jit(solution)/shard_map/ppermute | solution.py:35
  96.0 2.5 collective-permute-start.13
  131.0 15.7 %collective-permute-start.33 = (bf16[4,512,768]{2,1,0:T(8,128)(2,1)}, bf16[4,512,768]{2,1,0:T(8,128)(2,1)S(1)}, u32[]{:S(2)}, u32[]{:S(2)}) collective-permute-start(bf16[4,512,768]{2,1,0:T(8,128)(2,1)} %get-tuple-element.81), channel_id=1, source_target_pairs={{0,1},{1,0},{2,3},{3,2},{4,5},{5,4},{6,7},{7,6},{8,9},{9,8},{10,11... | collective-permute-start | bytes 9437192 | tf_op jit(solution)/shard_map/ppermute | solution.py:35
  131.3 15.5 %collective-permute-start.32 = (bf16[3,2,4,96,512]{4,3,2,1,0:T(8,128)(2,1)}, bf16[3,2,4,96,512]{4,3,2,1,0:T(8,128)(2,1)}, u32[]{:S(2)}, u32[]{:S(2)}) collective-permute-start(bf16[3,2,4,96,512]{4,3,2,1,0:T(8,128)(2,1)} %get-tuple-element.79.refs_0_.refs_2_), channel_id=1, source_target_pairs={{0,1},{1,0},{2,3},{3,2},{4,5},{5,4},{6,7},{7,6},{8,9},{9,8},{10,11... | collective-permute-start | bytes 7077896 | tf_op jit(solution)/shard_map/ppermute | solution.py:35
  131.6 11.3 %collective-permute-start.29 = (bf16[560,256]{1,0:T(8,128)(2,1)}, bf16[560,256]{1,0:T(8,128)(2,1)S(1)}, u32[]{:S(2)}, u32[]{:S(2)}) collective-permute-start(bf16[560,256]{1,0:T(8,128)(2,1)} %get-tuple-element.73), channel_id=1, source_target_pairs={{0,1},{1,0},{2,3},{3,2},{4,5},{5,4},{6,7},{7,6},{8,9},{9,8},{10,11... | collective-permute-start | bytes 860168 | tf_op jit(solution)/shard_map/ppermute | solution.py:35
  131.8 11.2 %collective-permute-start.30 = (bf16[560,256]{1,0:T(8,128)(2,1)}, bf16[560,256]{1,0:T(8,128)(2,1)}, u32[]{:S(2)}, u32[]{:S(2)}) collective-permute-start(bf16[560,256]{1,0:T(8,128)(2,1)} %get-tuple-element.74), channel_id=1, source_target_pairs={{0,2},{1,3},{2,0},{3,1},{4,6},{5,7},{6,4},{7,5},{8,10},{9,11},{10,... | collective-permute-start | bytes 860168 | tf_op jit(solution)/shard_map/ppermute | solution.py:35
  132.3 14.5 %collective-permute-start.31 = (bf16[560,256]{1,0:T(8,128)(2,1)}, bf16[560,256]{1,0:T(8,128)(2,1)}, u32[]{:S(2)}, u32[]{:S(2)}) collective-permute-start(bf16[560,256]{1,0:T(8,128)(2,1)} %get-tuple-element.75), channel_id=1, source_target_pairs={{0,3},{1,2},{2,1},{3,0},{4,7},{5,6},{6,5},{7,4},{8,11},{9,10},{10,... | collective-permute-start | bytes 860168 | tf_op jit(solution)/shard_map/ppermute | solution.py:35
  154.7 59.2 %all-to-all-start = ((bf16[4,2,2,96,768]{4,3,2,1,0:T(8,128)(2,1)}), bf16[4,2,2,96,768]{4,3,2,1,0:T(8,128)(2,1)S(1)}, u32[]{:S(2)}, u32[]{:S(2)}) async-start(bf16[4,2,2,96,768]{4,3,2,1,0:T(8,128)(2,1)} %row_dot.3.refs_12_), calls=%async_computation | async-start | bytes 4718592 | tf_op jit(solution)/shard_map/all_to_all | solution.py:86
  167.7 32.6 %collective-permute-start.35 = (bf16[1,1,4,96,1024]{4,3,2,1,0:T(8,128)(2,1)}, bf16[1,1,4,96,1024]{4,3,2,1,0:T(8,128)(2,1)S(1)}, u32[]{:S(2)}, u32[]{:S(2)}) collective-permute-start(bf16[1,1,4,96,1024]{4,3,2,1,0:T(8,128)(2,1)} %get-tuple-element.102), channel_id=1, source_target_pairs={{0,2},{1,3},{2,0},{3,1},{4,6},{5,7},{6,4},{7,5},{8,10},{9,11},{10,... | collective-permute-start | bytes 2359304 | tf_op jit(solution)/shard_map/ppermute | solution.py:35
  168.3 32.0 %collective-permute-start.36 = (bf16[1,1,4,96,1024]{4,3,2,1,0:T(8,128)(2,1)}, bf16[1,1,4,96,1024]{4,3,2,1,0:T(8,128)(2,1)}, u32[]{:S(2)}, u32[]{:S(2)}) collective-permute-start(bf16[1,1,4,96,1024]{4,3,2,1,0:T(8,128)(2,1)} %get-tuple-element.103), channel_id=1, source_target_pairs={{0,4},{4,0},{8,12},{12,8},{16,20},{20,16},{24,28},{28,24},{1,5},{5... | collective-permute-start | bytes 2359304 | tf_op jit(solution)/shard_map/ppermute | solution.py:40
  169.2 35.6 %collective-permute-start.37 = (bf16[1,1,4,96,1024]{4,3,2,1,0:T(8,128)(2,1)}, bf16[1,1,4,96,1024]{4,3,2,1,0:T(8,128)(2,1)}, u32[]{:S(2)}, u32[]{:S(2)}) collective-permute-start(bf16[1,1,4,96,1024]{4,3,2,1,0:T(8,128)(2,1)} %get-tuple-element.85.refs_11_), channel_id=1, source_target_pairs={{0,6},{1,7},{2,4},{3,5},{4,2},{5,3},{6,0},{7,1},{8,14},{9,15},{10,... | collective-permute-start | bytes 2359304 | tf_op jit(solution)/shard_map/ppermute | solution.py:46
  200.3 18.1 %collective-permute-start.34 = (bf16[2,512,768]{2,1,0:T(8,128)(2,1)}, bf16[2,512,768]{2,1,0:T(8,128)(2,1)}, u32[]{:S(2)}, u32[]{:S(2)}) collective-permute-start(bf16[2,512,768]{2,1,0:T(8,128)(2,1)} %spread.2.refs_4_), channel_id=1, source_target_pairs={{0,1},{1,0},{2,3},{3,2},{4,5},{5,4},{6,7},{7,6},{8,9},{9,8},{10,11... | collective-permute-start | bytes 4718600 | tf_op jit(solution)/shard_map/ppermute | solution.py:35
  213.9 23.3 %all-to-all-start.2 = ((bf16[4,96,1024]{2,1,0:T(8,128)(2,1)}), bf16[4,96,1024]{2,1,0:T(8,128)(2,1)S(1)}, u32[]{:S(2)}, u32[]{:S(2)}) async-start(bf16[4,96,1024]{2,1,0:T(8,128)(2,1)} %joined_sums.2.refs_2_), calls=%async_computation.2 | async-start | bytes 1572864 | tf_op jit(solution)/shard_map/all_to_all | solution.py:86
  217.4 17.0 %collective-permute-start.39 = (bf16[1,1,4,112,768]{4,3,2,1,0:T(8,128)(2,1)}, bf16[1,1,4,112,768]{4,3,2,1,0:T(8,128)(2,1)}, u32[]{:S(2)}, u32[]{:S(2)}) collective-permute-start(bf16[1,1,4,112,768]{4,3,2,1,0:T(8,128)(2,1)} %get-tuple-element.99.refs_0_), channel_id=1, source_target_pairs={{0,4},{4,0},{8,12},{12,8},{16,20},{20,16},{24,28},{28,24},{1,5},{5... | collective-permute-start | bytes 2064392 | tf_op jit(solution)/shard_map/ppermute | solution.py:40
  223.4 28.7 %collective-permute-start.38 = (bf16[512,768]{1,0:T(8,128)(2,1)}, bf16[512,768]{1,0:T(8,128)(2,1)S(1)}, u32[]{:S(2)}, u32[]{:S(2)}) collective-permute-start(bf16[512,768]{1,0:T(8,128)(2,1)} %get-tuple-element.105.refs_0_), channel_id=1, source_target_pairs={{0,2},{1,3},{2,0},{3,1},{4,6},{5,7},{6,4},{7,5},{8,10},{9,11},{10,... | collective-permute-start | bytes 2359304 | tf_op jit(solution)/shard_map/ppermute | solution.py:35
  237.2 20.9 %all-to-all-start.1 = ((bf16[4,112,768]{2,1,0:T(8,128)(2,1)}), bf16[4,112,768]{2,1,0:T(8,128)(2,1)S(1)}, u32[]{:S(2)}, u32[]{:S(2)}) async-start(bf16[4,112,768]{2,1,0:T(8,128)(2,1)} %joined_sums.3.refs_0_), calls=%async_computation.1 | async-start | bytes 1376256 | tf_op jit(solution)/shard_map/all_to_all | solution.py:86
  241.4 7.3 %collective-permute-start.40 = (bf16[2,96,768]{2,1,0:T(8,128)(2,1)S(1)}, bf16[2,96,768]{2,1,0:T(8,128)(2,1)S(1)}, u32[]{:S(2)}, u32[]{:S(2)}) collective-permute-start(bf16[2,96,768]{2,1,0:T(8,128)(2,1)S(1)} %copy-done.13), channel_id=1, source_target_pairs={{0,2},{1,3},{2,0},{3,1},{4,6},{5,7},{6,4},{7,5},{8,10},{9,11},{10,... | collective-permute-start | bytes 884744 | tf_op jit(solution)/shard_map/ppermute | solution.py:35
  251.2 5.4 %collective-permute-start.41 = (bf16[1,96,768]{2,1,0:T(8,128)(2,1)}, bf16[1,96,768]{2,1,0:T(8,128)(2,1)S(1)}, u32[]{:S(2)}, u32[]{:S(2)}) collective-permute-start(bf16[1,96,768]{2,1,0:T(8,128)(2,1)} %get-tuple-element.110), channel_id=1, source_target_pairs={{0,4},{4,0},{8,12},{12,8},{16,20},{20,16},{24,28},{28,24},{1,5},{5... | collective-permute-start | bytes 442376 | tf_op jit(solution)/shard_map/ppermute | solution.py:40
  (32 other events, 345.9 us)

commit v6 on v5

--- a/solution.py
+++ b/solution.py
@@ -21,7 +21,7 @@
 SUM_ROW = 10
 ORDER = (0, 1, 2, 3)
 SUM_ROWS = 16
-BELOW = SUM_ROWS * (D // PAD)
+BELOW = SUM_ROWS * (D // LANES)
 GATE = 5
 
 masked_score = -1e30
@@ -316,13 +316,13 @@
     else:
         outs = take(len(chosen))
         key_sum, value_sum = take(2)
-    rows, up_rows, sems = refs
+    rows, up_rows, up_packed, sems = refs
     own_rows = own_blocks * BLK
     copies = [
         pltpu.make_async_copy(parts[s], rows.at[pl.ds(s * own_rows, own_rows)], sems.at[s])
         for s in range(pieces)
     ] + [
-        pltpu.make_async_copy(ups[at], up_rows.at[at], sems.at[pieces + at])
+        pltpu.make_async_copy(ups[at], up_packed.at[at], sems.at[pieces + at])
         for at in range(len(chosen))
     ]
     late = []
@@ -340,6 +340,12 @@
     query_masks = head_masks(heads, HD**-0.5, bf16)
     up_masks = head_masks(heads, 1.0, bf16)
     out_masks = head_masks(heads, HD**-0.5, f32)
+    half = own_rows // 2
+    for at in range(len(chosen)):
+        up_rows[at, :, :LANES] = up_packed[at, :own_rows, :]
+        last = up_packed[at, own_rows : own_rows + half, :]
+        up_rows[at, :half, LANES:] = last
+        up_rows[at, half:, LANES:] = pltpu.roll(last.astype(f32), HD, 1).astype(bf16)
 
     side = 2 if len(chosen) == 1 else 1
 
@@ -432,7 +438,7 @@
     small = small_ref[...]
     for at in range(len(chosen)):
         parts = [
-            up_rows[at, own_rows + k * SUM_ROWS : own_rows + (k + 1) * SUM_ROWS, :]
+            up_packed[at, own_rows + half + k * SUM_ROWS : own_rows + half + (k + 1) * SUM_ROWS, :]
             for k in range(BELOW // SUM_ROWS)
         ]
         small = small + jnp.concatenate(parts, axis=1).astype(f32)
@@ -470,7 +476,8 @@
         scratch_shapes=scratch
         + [
             pltpu.VMEM((pieces * own_rows, 3 * PAD), bf16),
-            pltpu.VMEM((n, own_rows + BELOW, PAD), bf16),
+            pltpu.VMEM((n, own_rows, PAD), bf16),
+            pltpu.VMEM((n, own_rows + own_rows // 2 + BELOW, LANES), bf16),
             pltpu.SemaphoreType.DMA((pieces + n + 2,)),
         ],
         cost_estimate=cost(30 * work * HD, 12 << 20, work),
@@ -545,6 +552,7 @@
         slope_buf,
         last_buf,
         turned_buf,
+        send_buf,
         sums,
         up_sums,
         in_sems,
@@ -561,7 +569,7 @@
     for s in range(teams):
         source = mixed[s] if places[s] is None else mixed[s].at[places[s]]
         first.append(
-            pltpu.make_async_copy(source, o_buf.at[s, pl.ds(0, x_in.shape[0]), :], in_sems.at[s])
+            pltpu.make_async_copy(source, o_buf.at[s], in_sems.at[s])
         )
     first.append(pltpu.make_async_copy(x_in, x_buf, in_sems.at[teams]))
     upstream_copy = pltpu.make_async_copy(g_in, g_buf, in_sems.at[teams + 1])
@@ -725,12 +733,16 @@
             up_sums[8 * s : 8 * s + 8, :], axis=0, keepdims=True
         )
     for s in (2, 3, 1, 0):
-        o_buf[s, :rows, :] = contract(last_buf[...], out_w[s], (1, 0)).astype(bf16)
-        for k in range(D // PAD):
-            o_buf[s, rows + k * SUM_ROWS : rows + (k + 1) * SUM_ROWS, :] = small[
-                :, k * PAD : (k + 1) * PAD
-            ].astype(bf16)
-        leave(o_buf.at[s], back_out[s])
+        back = contract(last_buf[...], out_w[s], (1, 0))
+        half = rows // 2
+        send_buf[s, :rows, :] = back[:, :LANES].astype(bf16)
+        send_buf[s, rows : rows + half, :] = (
+            back[:half, LANES:] + pltpu.roll(back[half:, LANES:], HD, 1)
+        ).astype(bf16)
+        for k in range(D // LANES):
+            at = rows + half + k * SUM_ROWS
+            send_buf[s, at : at + SUM_ROWS, :] = small[:, k * LANES : (k + 1) * LANES].astype(bf16)
+        leave(send_buf.at[s], back_out[s])
     for copy in leaving:
         copy.wait()
 
@@ -748,14 +760,14 @@
     return pl.pallas_call(
         partial(rows_kernel, [at for _, at in mixed], len(weights)),
         out_shape=[low, pair, pair, turned]
-        + [struct((rows + BELOW, PAD), bf16)] * teams
+        + [struct((rows + rows // 2 + BELOW, LANES), bf16)] * teams
         + [low, struct((16, D), f32)],
         in_specs=[SMEM_SPEC]
         + [ANY_SPEC] * (teams + 2 + len(weights))
         + [VMEM_SPEC] * 2,
         out_specs=[ANY_SPEC] * (5 + teams) + [VMEM_SPEC],
         scratch_shapes=[
-            pltpu.VMEM((teams, rows + BELOW, PAD), bf16),
+            pltpu.VMEM((teams, rows, PAD), bf16),
             pltpu.VMEM((rows, D), bf16),
             pltpu.VMEM((rows, D), bf16),
             pltpu.VMEM((teams, D, PAD), bf16),
@@ -769,6 +781,7 @@
             pltpu.VMEM((teams, rows, hidden), bf16),
             pltpu.VMEM((rows, D), bf16),
             pltpu.VMEM((3, D, rows), bf16),
+            pltpu.VMEM((teams, rows + rows // 2 + BELOW, LANES), bf16),
             pltpu.VMEM((48, D), f32),
             pltpu.VMEM((8 * teams, hidden), f32),
             pltpu.SemaphoreType.DMA((teams + 2,)),

time: 261 us -> 259 us (level)
  waiting for transfers between devices: 65 us -> 62 us
    ppermute x24, waiting for transfers between devices: 18.6 us -> 15.5 us  [swap(): return lax.ppermute(array, 'tensor', [(t, t ^ bit) for t in range(size)])]
  transfers between devices with their start and end apart: 45 -> 45, of which waited for: 20 -> 20; matrix products, arithmetic and copies ran while one was open for 4% -> 4% of each run, Pallas kernels for 35% -> 36%
where the time goes in v6:
time: 259 us; the launch traced here: 257 us
  Pallas kernels  132 us (51%)
  waiting for transfers between devices  62 us (24%)
  starting transfers between devices  43.5 us (17%)
  local copies, waits for them, and re-layouts  14 us (5%)
  other arithmetic  4.36 us (2%)
    pallas_call x1, Pallas kernels, layer_rows(): pl.pallas_call(partial(rows_kernel, [at for _, at in mixed], len(weights)...  31.9 us
    pallas_call x2, Pallas kernels, attend_backward(): pl.pallas_call(partial(attend_back_kernel, heads, chosen, pieces, own_blo...  27.9 us
    ppermute x14, waiting for transfers between devices, ring_send(): lax.ppermute(array, 'dp', [(order[i], order[(i + step) % size]) for i in...  25.2 us
    pallas_call x3, Pallas kernels, row_dot(): pl.pallas_call(kernel, grid=(lows[-1],), out_shape=[struct((far, *lead, p...  21 us
    ppermute x14, starting transfers between devices, ring_send(): lax.ppermute(array, 'dp', [(order[i], order[(i + step) % size]) for i in...  16.9 us
    ppermute x24, waiting for transfers between devices, swap(): return lax.ppermute(array, 'tensor', [(t, t ^ bit) for t in range(size)])  15.5 us
    pallas_call x2, Pallas kernels, attend_forward(): pl.pallas_call(partial(attend_kernel, heads, chosen, pieces, own_blocks),...  14.5 us
    all_to_all x3, starting transfers between devices, far_exchange(): lax.all_to_all(blocks, 'dp', 0, 0, axis_index_groups=groups, tiled=True)  12.6 us
  transfers between devices with their start and end apart: 45, of which 20 were waited for; matrix products, arithmetic and copies ran while one was open for 4% of the time, Pallas kernels for 36%

profile of v6, /device:TPU:0, one launch (start us, length us, event | category | flops | bytes accessed | tf_op | source)
XLA Modules:
  0.0 257.4 jit_solution(15266037259581779950)
XLA Ops:
  0.7 1.5 pack_queries.1._.refs_4_
  2.2 3.0 %collective-permute-start.4 = (bf16[96,768]{1,0:T(8,128)(2,1)}, bf16[96,768]{1,0:T(8,128)(2,1)S(1)}, u32[]{:S(2)}, u32[]{:S(2)}) collective-permute-start(bf16[96,768]{1,0:T(8,128)(2,1)} %pack_queries.1._.refs_4_), channel_id=1, source_target_pairs={{0,8},{8,16},{16,24},{24,28},{28,20},{20,12},{12,4},{4,0},{1,9},{9... | collective-permute-start | bytes 442376 | tf_op jit(solution)/shard_map/ppermute | solution.py:64
  5.2 1.7 copy.38.down
  6.9 1.9 pack_weights.1.a
  8.8 1.6 collective-permute-start.1
  10.8 1.6 collective-permute-start.6
  12.4 3.3 %collective-permute-done.5.refs_6_ = bf16[96,768]{1,0:T(8,128)(2,1)S(1)} collective-permute-done((bf16[96,768]{1,0:T(8,128)(2,1)}, bf16[96,768]{1,0:T(8,128)(2,1)S(1)}, u32[]{:S(2)}, u32[]{:S(2)}) %collective-permute-start.5) | collective-permute-done | bytes 147488 | tf_op jit(solution)/shard_map/ppermute | solution.py:64
  16.2 1.6 collective-permute-start.8
  19.4 2.1 held.1
  23.4 1.6 collective-permute-start.10
  25.0 3.1 %collective-permute-done.9.refs_10_.refs_1_ = bf16[96,768]{1,0:T(8,128)(2,1)S(1)} collective-permute-done((bf16[96,768]{1,0:T(8,128)(2,1)S(1)}, bf16[96,768]{1,0:T(8,128)(2,1)S(1)}, u32[]{:S(2)}, u32[]{:S(2)}) %collective-permute-start.9) | collective-permute-done | bytes 147488 | tf_op jit(solution)/shard_map/ppermute | solution.py:64
  29.4 2.0 pair_weights.1.refs_6_
  31.4 1.6 collective-permute-start.14
  32.9 6.9 %collective-permute-done.2.refs_2_ = bf16[512,768]{1,0:T(8,128)(2,1)} collective-permute-done((bf16[512,768]{1,0:T(8,128)(2,1)}, bf16[512,768]{1,0:T(8,128)(2,1)}, u32[]{:S(2)}, u32[]{:S(2)}) %collective-permute-start.2) | collective-permute-done | bytes 786464 | tf_op jit(solution)/shard_map/ppermute | solution.py:35
  40.4 6.8 %collective-permute-done.14.refs_7_ = bf16[96,3584]{1,0:T(8,128)(2,1)S(1)} collective-permute-done((bf16[96,3584]{1,0:T(8,128)(2,1)}, bf16[96,3584]{1,0:T(8,128)(2,1)S(1)}, u32[]{:S(2)}, u32[]{:S(2)}) %collective-permute-start.14) | collective-permute-done | bytes 688160 | tf_op jit(solution)/shard_map/ppermute | solution.py:64
  47.2 1.6 collective-permute-start.16
  50.1 1.5 block_tables.1
  52.7 5.2 %collective-permute-done.15.refs_8_ = bf16[96,3584]{1,0:T(8,128)(2,1)S(1)} collective-permute-done((bf16[96,3584]{1,0:T(8,128)(2,1)}, bf16[96,3584]{1,0:T(8,128)(2,1)S(1)}, u32[]{:S(2)}, u32[]{:S(2)}) %collective-permute-start.15) | collective-permute-done | bytes 688160 | tf_op jit(solution)/shard_map/ppermute | solution.py:64
  58.5 2.8 %collective-permute-done.16.refs_9_ = bf16[96,3584]{1,0:T(8,128)(2,1)S(1)} collective-permute-done((bf16[96,3584]{1,0:T(8,128)(2,1)S(1)}, bf16[96,3584]{1,0:T(8,128)(2,1)S(1)}, u32[]{:S(2)}, u32[]{:S(2)}) %collective-permute-start.16) | collective-permute-done | bytes 688160 | tf_op jit(solution)/shard_map/ppermute | solution.py:64
  61.3 1.6 collective-permute-start.18
  62.9 8.3 %project_in.1 = (bf16[512,768]{1,0:T(8,128)(2,1)}, bf16[512,768]{1,0:T(8,128)(2,1)}, bf16[512,768]{1,0:T(8,128)(2,1)}, bf16[512,768]{1,0:T(8,128)(2,1)}, bf16[2,...) custom-call(bf16[512,768]{1,0:T(8,128)(2,1)} %refs_4_.1, ...), custom_call_target="tpu_custom_call" | custom-call | flops 4831838208 | bytes 25165824 | tf_op jit(solution)/shard_map/project_in/pallas_call | solution.py:1124
  71.1 7.2 %attend_forward.3 = (bf16[2,512,256]{2,1,0:T(8,128)(2,1)}, f32[512,128]{1,0:T(8,128)}, f32[512,128]{1,0:T(8,128)}) custom-call(s32[32,128]{1,0:T(8,128)} %get-tuple-element.64.table, bf16[512,768]{1,0:T(8,128)(2,1)} %get-tuple-element.65.refs_0_, bf16[512,768]{1,0:T(8,128)(2,1)} %get-tuple-element.66.refs_1_, bf16[512,768]{1,0:T(8,128)(2,1)} %get-tuple-element.67.refs_2_, ...), custom_call_target="tpu_custom_call" | custom-call | flops 4831838208 | bytes 16777216 | tf_op jit(solution)/shard_map/attend_forward/pallas_call | solution.py:278
  79.1 1.6 collective-permute-start.20
  80.7 7.3 %attend_forward.2 = (bf16[2,512,256]{2,1,0:T(8,128)(2,1)}, f32[512,128]{1,0:T(8,128)}, f32[512,128]{1,0:T(8,128)}) custom-call(s32[32,128]{1,0:T(8,128)} %get-tuple-element.64.table, bf16[512,768]{1,0:T(8,128)(2,1)} %get-tuple-element.65.refs_0_, bf16[512,768]{1,0:T(8,128)(2,1)} %get-tuple-element.66.refs_1_, bf16[512,768]{1,0:T(8,128)(2,1)} %get-tuple-element.67.refs_2_, ...), custom_call_target="tpu_custom_call" | custom-call | flops 4831838208 | bytes 16777216 | tf_op jit(solution)/shard_map/attend_forward/pallas_call | solution.py:278
  91.4 3.3 %collective-permute-done.19.refs_12_ = bf16[96,3584]{1,0:T(8,128)(2,1)} collective-permute-done((bf16[96,3584]{1,0:T(8,128)(2,1)}, bf16[96,3584]{1,0:T(8,128)(2,1)}, u32[]{:S(2)}, u32[]{:S(2)}) %collective-permute-start.19) | collective-permute-done | bytes 688160 | tf_op jit(solution)/shard_map/ppermute | solution.py:64
  99.2 31.9 %layer_rows.1 = (bf16[512,768]{1,0:T(8,128)(2,1)}, bf16[4,512,768]{2,1,0:T(8,128)(2,1)}, bf16[4,512,768]{2,1,0:T(8,128)(2,1)}, bf16[3,2,4,96,512]{4,3,2,1,0:T(8,...) custom-call(s32[1]{0:T(128)S(6)} %copy.40.length_ref.length, ...), custom_call_target="tpu_custom_call" | custom-call | flops 176160768 | bytes 393216 | tf_op jit(solution)/shard_map/layer_rows/pallas_call | solution.py:760
  133.5 9.7 %attend_backward.2 = (bf16[512,256]{1,0:T(8,128)(2,1)}, f32[2048,256]{1,0:T(8,128)}, f32[2048,256]{1,0:T(8,128)}) custom-call(s32[32,128]{1,0:T(8,128)} %get-tuple-element.64.table, bf16[512,768]{1,0:T(8,128)(2,1)} %get-tuple-element.65.refs_0_, bf16[512,768]{1,0:T(8,128)(2,1)} %get-tuple-element.66.refs_1_, bf16[512,768]{1,0:T(8,128)(2,1)} %get-tuple-element.67.refs_2_, ...), custom_call_target="tpu_custom_call" | custom-call | flops 23592960 | bytes 196608 | tf_op jit(solution)/shard_map/attend_backward/pallas_call | solution.py:465
  144.0 1.7 copy-done
  145.7 6.3 %row_dot.3.refs_12_ = bf16[4,2,2,96,768]{4,3,2,1,0:T(8,128)(2,1)} custom-call(bf16[3,2,4,96,512]{4,3,2,1,0:T(8,128)(2,1)} %get-tuple-element.79.refs_0_.refs_2_, bf16[3,2,4,96,512]{4,3,2,1,0:T(8,128)(2,1)} %collective-permute-done.32.refs_1_.refs_3_, bf16[4,512,768]{2,1,0:T(8,128)(2,1)} %get-tuple-element.80.refs_2_.refs_3_.refs_4_.refs_5_, ...), custom_call_target="tpu_custom_call" | custom-call | flops 37748736 | bytes 131072 | tf_op jit(solution)/shard_map/row_dot/pallas_call | solution.py:875
  152.0 4.8 %all-to-all-start = ((bf16[4,2,2,96,768]{4,3,2,1,0:T(8,128)(2,1)}), bf16[4,2,2,96,768]{4,3,2,1,0:T(8,128)(2,1)S(1)}, u32[]{:S(2)}, u32[]{:S(2)}) async-start(bf16[4,2,2,96,768]{4,3,2,1,0:T(8,128)(2,1)} %row_dot.3.refs_12_), calls=%async_computation | async-start | bytes 4718592 | tf_op jit(solution)/shard_map/all_to_all | solution.py:86
  156.8 8.2 %row_dot.4 = (bf16[1,1,4,96,1024]{4,3,2,1,0:T(8,128)(2,1)}, bf16[1,1,4,96,1024]{4,3,2,1,0:T(8,128)(2,1)}, bf16[1,1,4,96,1024]{4,3,2,1,0:T(8,128)(2,1)}, bf16[1,1,4,96,1024]{4,3,2,1,0:T(8,128)(2,1)}) custom-call(bf16[3,2,4,96,512]{4,3,2,1,0:T(8,128)(2,1)} %get-tuple-element.79.refs_0_.refs_2_, ...), custom_call_target="tpu_custom_call" | custom-call | flops 50331648 | bytes 131072 | tf_op jit(solution)/shard_map/row_dot/pallas_call | solution.py:875
  166.4 2.1 collective-permute-start.37
  168.5 18.2 %attend_backward.3 = (bf16[512,768]{1,0:T(8,128)(2,1)}, bf16[512,768]{1,0:T(8,128)(2,1)}, bf16[512,768]{1,0:T(8,128)(2,1)}, bf16[512,768]{1,0:T(8,128)(2,1)}, bf16[16,768]{1,0:T(8,128)(2,1)}) custom-call(s32[32,128]{1,0:T(8,128)} %get-tuple-element.64.table, bf16[512,768]{1,0:T(8,128)(2,1)} %get-tuple-element.65.refs_0_, ...), custom_call_target="tpu_custom_call" | custom-call | flops 70778880 | bytes 196608 | tf_op jit(solution)/shard_map/attend_backward/pallas_call | solution.py:465
  186.7 6.6 %row_dot.5 = (bf16[1,1,4,112,768]{4,3,2,1,0:T(8,128)(2,1)}, bf16[1,1,4,112,768]{4,3,2,1,0:T(8,128)(2,1)}) custom-call(bf16[1,2,4,96,512]{4,3,2,1,0:T(8,128)(2,1)} %bitcast.30, bf16[1,2,4,96,512]{4,3,2,1,0:T(8,128)(2,1)} %bitcast.31, bf16[1,2,4,96,512]{4,3,2,1,0:T(8,128)(2,1)} %bitcast.32, bf16[1,2,4,96,512]{4,3,2,1,0:T(8,128)(2,1)} %bitcast.33, ...), custom_call_target="tpu_custom_call" | custom-call | flops 37748736 | bytes 131072 | tf_op jit(solution)/shard_map/row_dot/pallas_call | solution.py:875
  193.3 4.3 %spread.2.refs_4_ = bf16[2,512,768]{2,1,0:T(8,128)(2,1)} custom-call(bf16[512,768]{1,0:T(8,128)(2,1)} %get-tuple-element.92.first, bf16[512,768]{1,0:T(8,128)(2,1)} %get-tuple-element.93.second, bf16[768,768]{1,0:T(8,128)(2,1)} %get-tuple-element.91.w, bf16[1,1,4,112,768]{4,3,2,1,0:T(8,128)(2,1)} %get-tuple-element.99.refs_0_), custom_call_target="tpu_custom_call" | custom-call | flops 18874368 | bytes 81920 | tf_op jit(solution)/shard_map/spread/pallas_call | solution.py:992
  197.6 4.4 %collective-permute-done.37 = bf16[1,1,4,96,1024]{4,3,2,1,0:T(8,128)(2,1)} collective-permute-done((bf16[1,1,4,96,1024]{4,3,2,1,0:T(8,128)(2,1)}, bf16[1,1,4,96,1024]{4,3,2,1,0:T(8,128)(2,1)}, u32[]{:S(2)}, u32[]{:S(2)}) %collective-permute-start.37) | collective-permute-done | bytes 786464 | tf_op jit(solution)/shard_map/ppermute | solution.py:46
  202.0 3.1 %joined_sums.2.refs_2_ = bf16[4,96,1024]{2,1,0:T(8,128)(2,1)} custom-call(bf16[4,96,1024]{2,1,0:T(8,128)(2,1)} %bitcast.34, bf16[4,96,1024]{2,1,0:T(8,128)(2,1)} %bitcast.35, bf16[4,96,1024]{2,1,0:T(8,128)(2,1)} %bitcast.12.refs_2_, bf16[4,96,1024]{2,1,0:T(8,128)(2,1)} %bitcast.13.refs_3_, bf16[2,512,768]{2,1,0:T(8,128)(2,1)} %spread.2.refs_4_), custom_call_target="tpu_custom_call" | custom-call | flops 24576 | bytes 49152 | tf_op jit(solution)/shard_map/joined_sums/pallas_call | solution.py:962
  205.1 6.0 %all-to-all-done.ref = bf16[4,2,2,96,768]{4,3,2,1,0:T(8,128)(2,1)S(1)} async-done(((bf16[4,2,2,96,768]{4,3,2,1,0:T(8,128)(2,1)}), bf16[4,2,2,96,768]{4,3,2,1,0:T(8,128)(2,1)S(1)}, u32[]{:S(2)}, u32[]{:S(2)}) %all-to-all-start) | async-done | bytes 2359328 | tf_op jit(solution)/shard_map/all_to_all | solution.py:86
  211.1 3.5 %all-to-all-start.2 = ((bf16[4,96,1024]{2,1,0:T(8,128)(2,1)}), bf16[4,96,1024]{2,1,0:T(8,128)(2,1)S(1)}, u32[]{:S(2)}, u32[]{:S(2)}) async-start(bf16[4,96,1024]{2,1,0:T(8,128)(2,1)} %joined_sums.2.refs_2_), calls=%async_computation.2 | async-start | bytes 1572864 | tf_op jit(solution)/shard_map/all_to_all | solution.py:86
  215.6 5.0 %spread.3 = (bf16[512,768]{1,0:T(8,128)(2,1)}, f32[512,768]{1,0:T(8,128)}) custom-call(bf16[512,768]{1,0:T(8,128)(2,1)} %get-tuple-element.89.first, bf16[512,768]{1,0:T(8,128)(2,1)} %get-tuple-element.90.second, bf16[768,768]{1,0:T(8,128)(2,1)} %get-tuple-element.91.w, bf16[2,512,768]{2,1,0:T(8,128)(2,1)} %collective-permute-done.34.refs_0_, ...), custom_call_target="tpu_custom_call" | custom-call | flops 18874368 | bytes 81920 | tf_op jit(solution)/shard_map/spread/pallas_call | solution.py:992
  221.1 2.7 %fold.1 = (bf16[2,96,768]{2,1,0:T(8,128)(2,1)}, bf16[2,96,768]{2,1,0:T(8,128)(2,1)}) custom-call(bf16[4,2,2,96,768]{4,3,2,1,0:T(8,128)(2,1)} %copy-done.1, bf16[512,768]{1,0:T(8,128)(2,1)} %get-tuple-element.105.refs_0_), custom_call_target="tpu_custom_call" | custom-call | flops 18432 | bytes 55296 | tf_op jit(solution)/shard_map/fold/pallas_call | solution.py:937
  223.8 7.8 %collective-permute-done.39 = bf16[1,1,4,112,768]{4,3,2,1,0:T(8,128)(2,1)} collective-permute-done((bf16[1,1,4,112,768]{4,3,2,1,0:T(8,128)(2,1)}, bf16[1,1,4,112,768]{4,3,2,1,0:T(8,128)(2,1)}, u32[]{:S(2)}, u32[]{:S(2)}) %collective-permute-start.39) | collective-permute-done | bytes 688160 | tf_op jit(solution)/shard_map/ppermute | solution.py:40
  231.6 2.4 joined_sums.3.refs_0_
  234.4 4.3 %all-to-all-start.1 = ((bf16[4,112,768]{2,1,0:T(8,128)(2,1)}), bf16[4,112,768]{2,1,0:T(8,128)(2,1)S(1)}, u32[]{:S(2)}, u32[]{:S(2)}) async-start(bf16[4,112,768]{2,1,0:T(8,128)(2,1)} %joined_sums.3.refs_0_), calls=%async_computation.1 | async-start | bytes 1376256 | tf_op jit(solution)/shard_map/all_to_all | solution.py:86
  240.8 5.1 %collective-permute-done.40.b_ref = bf16[2,96,768]{2,1,0:T(8,128)(2,1)S(1)} collective-permute-done((bf16[2,96,768]{2,1,0:T(8,128)(2,1)S(1)}, bf16[2,96,768]{2,1,0:T(8,128)(2,1)S(1)}, u32[]{:S(2)}, u32[]{:S(2)}) %collective-permute-start.40) | collective-permute-done | bytes 294944 | tf_op jit(solution)/shard_map/ppermute | solution.py:35
  246.6 1.8 plus.1
  249.3 2.7 %convert_add_fusion = f32[512,768]{1,0:T(8,128)} fusion(f32[512,768]{1,0:T(8,128)} %get-tuple-element.104, bf16[512,768]{1,0:T(8,128)(2,1)S(1)} %collective-permute-done.38), kind=kLoop, calls=%fused_computation.1 | loop fusion | flops 786432 | bytes 3932160 | tf_op jit(solution)/shard_map/add | solution.py:1302
  252.1 1.7 collective-permute-done.41
  (158 shorter events, 30.9 us)
Async XLA Ops:
  2.2 8.6 %collective-permute-start.4 = (bf16[96,768]{1,0:T(8,128)(2,1)}, bf16[96,768]{1,0:T(8,128)(2,1)S(1)}, u32[]{:S(2)}, u32[]{:S(2)}) collective-permute-start(bf16[96,768]{1,0:T(8,128)(2,1)} %pack_queries.1._.refs_4_), channel_id=1, source_target_pairs={{0,8},{8,16},{16,24},{24,28},{28,20},{20,12},{12,4},{4,0},{1,9},{9... | collective-permute-start | bytes 442376 | tf_op jit(solution)/shard_map/ppermute | solution.py:64
  8.8 42.8 %copy-start.29 = (f32[192]{0:T(256)S(1)}, f32[192]{0:T(256)}, u32[]{:S(2)}) copy-start(f32[192]{0:T(256)} %param.26) | copy-start | bytes 2308
  8.8 42.8 %copy-start.30 = (f32[192]{0:T(256)S(1)}, f32[192]{0:T(256)}, u32[]{:S(2)}) copy-start(f32[192]{0:T(256)} %param.23) | copy-start | bytes 2308
  8.8 9.8 %collective-permute-start.1 = (bf16[96,1792]{1,0:T(8,128)(2,1)}, bf16[96,1792]{1,0:T(8,128)(2,1)S(1)}, u32[]{:S(2)}, u32[]{:S(2)}) collective-permute-start(bf16[96,1792]{1,0:T(8,128)(2,1)} %pack_weights.1.a), channel_id=1, source_target_pairs={{0,2},{1,3},{2,0},{3,1},{4,6},{5,7},{6,4},{7,5},{8,10},{9,11},{10,... | collective-permute-start | bytes 1032200 | tf_op jit(solution)/shard_map/ppermute | solution.py:35
  10.4 5.4 %collective-permute-start.5 = (bf16[96,768]{1,0:T(8,128)(2,1)}, bf16[96,768]{1,0:T(8,128)(2,1)S(1)}, u32[]{:S(2)}, u32[]{:S(2)}) collective-permute-start(bf16[96,768]{1,0:T(8,128)(2,1)} %pack_queries.1._.refs_4_), channel_id=1, source_target_pairs={{0,4},{8,0},{16,8},{24,16},{28,24},{20,28},{12,20},{4,12},{1,5},{9... | collective-permute-start | bytes 442376 | tf_op jit(solution)/shard_map/ppermute | solution.py:64
  10.8 52.0 %copy-start.31 = (bf16[96,768]{1,0:T(8,128)(2,1)}, bf16[96,768]{1,0:T(8,128)(2,1)S(1)}, u32[]{:S(2)}) copy-start(bf16[96,768]{1,0:T(8,128)(2,1)S(1)} %collective-permute-done.4.refs_5_) | copy-start | bytes 442372
  10.8 5.4 %collective-permute-start.6 = (bf16[96,768]{1,0:T(8,128)(2,1)S(1)}, bf16[96,768]{1,0:T(8,128)(2,1)S(1)}, u32[]{:S(2)}, u32[]{:S(2)}) collective-permute-start(bf16[96,768]{1,0:T(8,128)(2,1)S(1)} %collective-permute-done.4.refs_5_), channel_id=1, source_target_pairs={{0,8},{8,16},{16,24},{24,28},{28,20},{20,12},{12,4},{4,0},{1,9},{9... | collective-permute-start | bytes 442376 | tf_op jit(solution)/shard_map/ppermute | solution.py:64
  15.7 7.2 %collective-permute-start.7 = (bf16[96,768]{1,0:T(8,128)(2,1)S(1)}, bf16[96,768]{1,0:T(8,128)(2,1)S(1)}, u32[]{:S(2)}, u32[]{:S(2)}) collective-permute-start(bf16[96,768]{1,0:T(8,128)(2,1)S(1)} %collective-permute-done.5.refs_6_), channel_id=1, source_target_pairs={{0,4},{8,0},{16,8},{24,16},{28,24},{20,28},{12,20},{4,12},{1,5},{9... | collective-permute-start | bytes 442376 | tf_op jit(solution)/shard_map/ppermute | solution.py:64
  16.2 7.2 %collective-permute-start.8 = (bf16[96,768]{1,0:T(8,128)(2,1)S(1)}, bf16[96,768]{1,0:T(8,128)(2,1)S(1)}, u32[]{:S(2)}, u32[]{:S(2)}) collective-permute-start(bf16[96,768]{1,0:T(8,128)(2,1)S(1)} %collective-permute-done.6.refs_7_), channel_id=1, source_target_pairs={{0,8},{8,16},{16,24},{24,28},{28,20},{20,12},{12,4},{4,0},{1,9},{9... | collective-permute-start | bytes 442376 | tf_op jit(solution)/shard_map/ppermute | solution.py:64
  21.4 18.4 %collective-permute-start.2 = (bf16[512,768]{1,0:T(8,128)(2,1)}, bf16[512,768]{1,0:T(8,128)(2,1)}, u32[]{:S(2)}, u32[]{:S(2)}) collective-permute-start(bf16[512,768]{1,0:T(8,128)(2,1)} %held.1), channel_id=1, source_target_pairs={{0,2},{1,3},{2,0},{3,1},{4,6},{5,7},{6,4},{7,5},{8,10},{9,11},{10,... | collective-permute-start | bytes 2359304 | tf_op jit(solution)/shard_map/ppermute | solution.py:35
  22.9 5.1 %collective-permute-start.9 = (bf16[96,768]{1,0:T(8,128)(2,1)S(1)}, bf16[96,768]{1,0:T(8,128)(2,1)S(1)}, u32[]{:S(2)}, u32[]{:S(2)}) collective-permute-start(bf16[96,768]{1,0:T(8,128)(2,1)S(1)} %collective-permute-done.7.refs_8_), channel_id=1, source_target_pairs={{0,4},{8,0},{16,8},{24,16},{28,24},{20,28},{12,20},{4,12},{1,5},{9... | collective-permute-start | bytes 442376 | tf_op jit(solution)/shard_map/ppermute | solution.py:64
  23.4 5.1 %collective-permute-start.10 = (bf16[96,768]{1,0:T(8,128)(2,1)S(1)}, bf16[96,768]{1,0:T(8,128)(2,1)S(1)}, u32[]{:S(2)}, u32[]{:S(2)}) collective-permute-start(bf16[96,768]{1,0:T(8,128)(2,1)S(1)} %collective-permute-done.8.refs_9_.refs_0_), channel_id=1, source_target_pairs={{0,8},{8,16},{16,24},{24,28},{28,20},{20,12},{12,4},{4,0},{1,9},{9... | collective-permute-start | bytes 442376 | tf_op jit(solution)/shard_map/ppermute | solution.py:64
  31.4 15.8 %collective-permute-start.14 = (bf16[96,3584]{1,0:T(8,128)(2,1)}, bf16[96,3584]{1,0:T(8,128)(2,1)S(1)}, u32[]{:S(2)}, u32[]{:S(2)}) collective-permute-start(bf16[96,3584]{1,0:T(8,128)(2,1)} %pair_weights.1.refs_6_), channel_id=1, source_target_pairs={{0,8},{8,16},{16,24},{24,28},{28,20},{20,12},{12,4},{4,0},{1,9},{9... | collective-permute-start | bytes 2064392 | tf_op jit(solution)/shard_map/ppermute | solution.py:64
  32.9 19.3 %collective-permute-start = (bf16[512,768]{1,0:T(8,128)(2,1)S(1)}, bf16[512,768]{1,0:T(8,128)(2,1)}, u32[]{:S(2)}, u32[]{:S(2)}) collective-permute-start(bf16[512,768]{1,0:T(8,128)(2,1)S(1)} %copy-done.3), channel_id=1, source_target_pairs={{0,1},{1,0},{2,3},{3,2},{4,5},{5,4},{6,7},{7,6},{8,9},{9,8},{10,11... | collective-permute-start | bytes 2359304 | tf_op jit(solution)/shard_map/ppermute | solution.py:35
  39.8 18.6 %collective-permute-start.3 = (bf16[512,768]{1,0:T(8,128)(2,1)}, bf16[512,768]{1,0:T(8,128)(2,1)}, u32[]{:S(2)}, u32[]{:S(2)}) collective-permute-start(bf16[512,768]{1,0:T(8,128)(2,1)} %collective-permute-done.2.refs_2_), channel_id=1, source_target_pairs={{0,1},{1,0},{2,3},{3,2},{4,5},{5,4},{6,7},{7,6},{8,9},{9,8},{10,11... | collective-permute-start | bytes 2359304 | tf_op jit(solution)/shard_map/ppermute | solution.py:35
  39.8 18.1 %collective-permute-start.15 = (bf16[96,3584]{1,0:T(8,128)(2,1)}, bf16[96,3584]{1,0:T(8,128)(2,1)S(1)}, u32[]{:S(2)}, u32[]{:S(2)}) collective-permute-start(bf16[96,3584]{1,0:T(8,128)(2,1)} %pair_weights.1.refs_6_), channel_id=1, source_target_pairs={{0,4},{8,0},{16,8},{24,16},{28,24},{20,28},{12,20},{4,12},{1,5},{9... | collective-permute-start | bytes 2064392 | tf_op jit(solution)/shard_map/ppermute | solution.py:64
  47.2 14.1 %collective-permute-start.16 = (bf16[96,3584]{1,0:T(8,128)(2,1)S(1)}, bf16[96,3584]{1,0:T(8,128)(2,1)S(1)}, u32[]{:S(2)}, u32[]{:S(2)}) collective-permute-start(bf16[96,3584]{1,0:T(8,128)(2,1)S(1)} %collective-permute-done.14.refs_7_), channel_id=1, source_target_pairs={{0,8},{8,16},{16,24},{24,28},{28,20},{20,12},{12,4},{4,0},{1,9},{9... | collective-permute-start | bytes 2064392 | tf_op jit(solution)/shard_map/ppermute | solution.py:64
  52.2 26.2 %collective-permute-start.21 = (bf16[96,3584]{1,0:T(8,128)(2,1)}, bf16[96,3584]{1,0:T(8,128)(2,1)}, u32[]{:S(2)}, u32[]{:S(2)}) collective-permute-start(bf16[96,3584]{1,0:T(8,128)(2,1)} %pair_weights.1.refs_6_), channel_id=1, source_target_pairs={{0,1},{1,0},{2,3},{3,2},{4,5},{5,4},{6,7},{7,6},{8,9},{9,8},{10,11... | collective-permute-start | bytes 2064392 | tf_op jit(solution)/shard_map/ppermute | solution.py:35
  52.2 36.7 %collective-permute-start.22 = (bf16[96,3584]{1,0:T(8,128)(2,1)S(1)}, bf16[96,3584]{1,0:T(8,128)(2,1)S(1)}, u32[]{:S(2)}, u32[]{:S(2)}) collective-permute-start(bf16[96,3584]{1,0:T(8,128)(2,1)S(1)} %collective-permute-done.14.refs_7_), channel_id=1, source_target_pairs={{0,1},{1,0},{2,3},{3,2},{4,5},{5,4},{6,7},{7,6},{8,9},{9,8},{10,11... | collective-permute-start | bytes 2064392 | tf_op jit(solution)/shard_map/ppermute | solution.py:35
  57.9 20.8 %collective-permute-start.17 = (bf16[96,3584]{1,0:T(8,128)(2,1)S(1)}, bf16[96,3584]{1,0:T(8,128)(2,1)}, u32[]{:S(2)}, u32[]{:S(2)}) collective-permute-start(bf16[96,3584]{1,0:T(8,128)(2,1)S(1)} %collective-permute-done.15.refs_8_), channel_id=1, source_target_pairs={{0,4},{8,0},{16,8},{24,16},{28,24},{20,28},{12,20},{4,12},{1,5},{9... | collective-permute-start | bytes 2064392 | tf_op jit(solution)/shard_map/ppermute | solution.py:64
  58.5 30.6 %collective-permute-start.23 = (bf16[96,3584]{1,0:T(8,128)(2,1)S(1)}, bf16[96,3584]{1,0:T(8,128)(2,1)}, u32[]{:S(2)}, u32[]{:S(2)}) collective-permute-start(bf16[96,3584]{1,0:T(8,128)(2,1)S(1)} %collective-permute-done.15.refs_8_), channel_id=1, source_target_pairs={{0,1},{1,0},{2,3},{3,2},{4,5},{5,4},{6,7},{7,6},{8,9},{9,8},{10,11... | collective-permute-start | bytes 2064392 | tf_op jit(solution)/shard_map/ppermute | solution.py:35
  61.3 17.9 %collective-permute-start.18 = (bf16[96,3584]{1,0:T(8,128)(2,1)S(1)}, bf16[96,3584]{1,0:T(8,128)(2,1)}, u32[]{:S(2)}, u32[]{:S(2)}) collective-permute-start(bf16[96,3584]{1,0:T(8,128)(2,1)S(1)} %collective-permute-done.16.refs_9_), channel_id=1, source_target_pairs={{0,8},{8,16},{16,24},{24,28},{28,20},{20,12},{12,4},{4,0},{1,9},{9... | collective-permute-start | bytes 2064392 | tf_op jit(solution)/shard_map/ppermute | solution.py:64
  78.5 12.2 %collective-permute-start.12 = (bf16[2,512,256]{2,1,0:T(8,128)(2,1)}, bf16[2,512,256]{2,1,0:T(8,128)(2,1)S(1)}, u32[]{:S(2)}, u32[]{:S(2)}) collective-permute-start(bf16[2,512,256]{2,1,0:T(8,128)(2,1)} %get-tuple-element.71), channel_id=1, source_target_pairs={{0,2},{1,3},{2,0},{3,1},{4,6},{5,7},{6,4},{7,5},{8,10},{9,11},{10,... | collective-permute-start | bytes 1572872 | tf_op jit(solution)/shard_map/ppermute | solution.py:35
  78.7 16.1 %collective-permute-start.19 = (bf16[96,3584]{1,0:T(8,128)(2,1)}, bf16[96,3584]{1,0:T(8,128)(2,1)}, u32[]{:S(2)}, u32[]{:S(2)}) collective-permute-start(bf16[96,3584]{1,0:T(8,128)(2,1)} %collective-permute-done.17.refs_10_), channel_id=1, source_target_pairs={{0,4},{8,0},{16,8},{24,16},{28,24},{20,28},{12,20},{4,12},{1,5},{9... | collective-permute-start | bytes 2064392 | tf_op jit(solution)/shard_map/ppermute | solution.py:64
  79.1 15.8 %collective-permute-start.20 = (bf16[96,3584]{1,0:T(8,128)(2,1)}, bf16[96,3584]{1,0:T(8,128)(2,1)}, u32[]{:S(2)}, u32[]{:S(2)}) collective-permute-start(bf16[96,3584]{1,0:T(8,128)(2,1)} %collective-permute-done.18.refs_11_), channel_id=1, source_target_pairs={{0,8},{8,16},{16,24},{24,28},{28,20},{20,12},{12,4},{4,0},{1,9},{9... | collective-permute-start | bytes 2064392 | tf_op jit(solution)/shard_map/ppermute | solution.py:64
  89.0 1.6 collective-permute-start.11
  89.1 6.9 %collective-permute-start.24 = (bf16[96,3584]{1,0:T(8,128)(2,1)S(1)}, bf16[96,3584]{1,0:T(8,128)(2,1)S(1)}, u32[]{:S(2)}, u32[]{:S(2)}) collective-permute-start(bf16[96,3584]{1,0:T(8,128)(2,1)S(1)} %collective-permute-done.16.refs_9_), channel_id=1, source_target_pairs={{0,1},{1,0},{2,3},{3,2},{4,5},{5,4},{6,7},{7,6},{8,9},{9,8},{10,11... | collective-permute-start | bytes 2064392 | tf_op jit(solution)/shard_map/ppermute | solution.py:35
  90.6 7.0 %collective-permute-start.25 = (bf16[96,3584]{1,0:T(8,128)(2,1)}, bf16[96,3584]{1,0:T(8,128)(2,1)S(1)}, u32[]{:S(2)}, u32[]{:S(2)}) collective-permute-start(bf16[96,3584]{1,0:T(8,128)(2,1)} %collective-permute-done.17.refs_10_), channel_id=1, source_target_pairs={{0,1},{1,0},{2,3},{3,2},{4,5},{5,4},{6,7},{7,6},{8,9},{9,8},{10,11... | collective-permute-start | bytes 2064392 | tf_op jit(solution)/shard_map/ppermute | solution.py:35
  91.3 7.2 %collective-permute-start.26 = (bf16[96,3584]{1,0:T(8,128)(2,1)}, bf16[96,3584]{1,0:T(8,128)(2,1)}, u32[]{:S(2)}, u32[]{:S(2)}) collective-permute-start(bf16[96,3584]{1,0:T(8,128)(2,1)} %collective-permute-done.18.refs_11_), channel_id=1, source_target_pairs={{0,1},{1,0},{2,3},{3,2},{4,5},{5,4},{6,7},{7,6},{8,9},{9,8},{10,11... | collective-permute-start | bytes 2064392 | tf_op jit(solution)/shard_map/ppermute | solution.py:35
  94.7 3.7 %collective-permute-start.27 = (bf16[96,3584]{1,0:T(8,128)(2,1)}, bf16[96,3584]{1,0:T(8,128)(2,1)}, u32[]{:S(2)}, u32[]{:S(2)}) collective-permute-start(bf16[96,3584]{1,0:T(8,128)(2,1)} %collective-permute-done.19.refs_12_), channel_id=1, source_target_pairs={{0,1},{1,0},{2,3},{3,2},{4,5},{5,4},{6,7},{7,6},{8,9},{9,8},{10,11... | collective-permute-start | bytes 2064392 | tf_op jit(solution)/shard_map/ppermute | solution.py:35
  95.0 3.5 %collective-permute-start.28 = (bf16[96,3584]{1,0:T(8,128)(2,1)}, bf16[96,3584]{1,0:T(8,128)(2,1)}, u32[]{:S(2)}, u32[]{:S(2)}) collective-permute-start(bf16[96,3584]{1,0:T(8,128)(2,1)} %collective-permute-done.20.refs_13_), channel_id=1, source_target_pairs={{0,1},{1,0},{2,3},{3,2},{4,5},{5,4},{6,7},{7,6},{8,9},{9,8},{10,11... | collective-permute-start | bytes 2064392 | tf_op jit(solution)/shard_map/ppermute | solution.py:35
  96.0 2.5 collective-permute-start.13
  131.1 12.9 %collective-permute-start.33 = (bf16[4,512,768]{2,1,0:T(8,128)(2,1)}, bf16[4,512,768]{2,1,0:T(8,128)(2,1)S(1)}, u32[]{:S(2)}, u32[]{:S(2)}) collective-permute-start(bf16[4,512,768]{2,1,0:T(8,128)(2,1)} %get-tuple-element.81), channel_id=1, source_target_pairs={{0,1},{1,0},{2,3},{3,2},{4,5},{5,4},{6,7},{7,6},{8,9},{9,8},{10,11... | collective-permute-start | bytes 9437192 | tf_op jit(solution)/shard_map/ppermute | solution.py:35
  131.3 12.7 %collective-permute-start.32 = (bf16[3,2,4,96,512]{4,3,2,1,0:T(8,128)(2,1)}, bf16[3,2,4,96,512]{4,3,2,1,0:T(8,128)(2,1)}, u32[]{:S(2)}, u32[]{:S(2)}) collective-permute-start(bf16[3,2,4,96,512]{4,3,2,1,0:T(8,128)(2,1)} %get-tuple-element.79.refs_0_.refs_2_), channel_id=1, source_target_pairs={{0,1},{1,0},{2,3},{3,2},{4,5},{5,4},{6,7},{7,6},{8,9},{9,8},{10,11... | collective-permute-start | bytes 7077896 | tf_op jit(solution)/shard_map/ppermute | solution.py:35
  131.7 11.6 %collective-permute-start.29 = (bf16[864,128]{1,0:T(8,128)(2,1)}, bf16[864,128]{1,0:T(8,128)(2,1)S(1)}, u32[]{:S(2)}, u32[]{:S(2)}) collective-permute-start(bf16[864,128]{1,0:T(8,128)(2,1)} %get-tuple-element.73), channel_id=1, source_target_pairs={{0,1},{1,0},{2,3},{3,2},{4,5},{5,4},{6,7},{7,6},{8,9},{9,8},{10,11... | collective-permute-start | bytes 663560 | tf_op jit(solution)/shard_map/ppermute | solution.py:35
  131.8 11.4 %collective-permute-start.30 = (bf16[864,128]{1,0:T(8,128)(2,1)}, bf16[864,128]{1,0:T(8,128)(2,1)}, u32[]{:S(2)}, u32[]{:S(2)}) collective-permute-start(bf16[864,128]{1,0:T(8,128)(2,1)} %get-tuple-element.74), channel_id=1, source_target_pairs={{0,2},{1,3},{2,0},{3,1},{4,6},{5,7},{6,4},{7,5},{8,10},{9,11},{10,... | collective-permute-start | bytes 663560 | tf_op jit(solution)/shard_map/ppermute | solution.py:35
  132.3 11.7 %collective-permute-start.31 = (bf16[864,128]{1,0:T(8,128)(2,1)}, bf16[864,128]{1,0:T(8,128)(2,1)}, u32[]{:S(2)}, u32[]{:S(2)}) collective-permute-start(bf16[864,128]{1,0:T(8,128)(2,1)} %get-tuple-element.75), channel_id=1, source_target_pairs={{0,3},{1,2},{2,1},{3,0},{4,7},{5,6},{6,5},{7,4},{8,11},{9,10},{10,... | collective-permute-start | bytes 663560 | tf_op jit(solution)/shard_map/ppermute | solution.py:35
  152.0 59.2 %all-to-all-start = ((bf16[4,2,2,96,768]{4,3,2,1,0:T(8,128)(2,1)}), bf16[4,2,2,96,768]{4,3,2,1,0:T(8,128)(2,1)S(1)}, u32[]{:S(2)}, u32[]{:S(2)}) async-start(bf16[4,2,2,96,768]{4,3,2,1,0:T(8,128)(2,1)} %row_dot.3.refs_12_), calls=%async_computation | async-start | bytes 4718592 | tf_op jit(solution)/shard_map/all_to_all | solution.py:86
  165.0 32.6 %collective-permute-start.35 = (bf16[1,1,4,96,1024]{4,3,2,1,0:T(8,128)(2,1)}, bf16[1,1,4,96,1024]{4,3,2,1,0:T(8,128)(2,1)S(1)}, u32[]{:S(2)}, u32[]{:S(2)}) collective-permute-start(bf16[1,1,4,96,1024]{4,3,2,1,0:T(8,128)(2,1)} %get-tuple-element.102), channel_id=1, source_target_pairs={{0,2},{1,3},{2,0},{3,1},{4,6},{5,7},{6,4},{7,5},{8,10},{9,11},{10,... | collective-permute-start | bytes 2359304 | tf_op jit(solution)/shard_map/ppermute | solution.py:35
  165.6 32.1 %collective-permute-start.36 = (bf16[1,1,4,96,1024]{4,3,2,1,0:T(8,128)(2,1)}, bf16[1,1,4,96,1024]{4,3,2,1,0:T(8,128)(2,1)}, u32[]{:S(2)}, u32[]{:S(2)}) collective-permute-start(bf16[1,1,4,96,1024]{4,3,2,1,0:T(8,128)(2,1)} %get-tuple-element.103), channel_id=1, source_target_pairs={{0,4},{4,0},{8,12},{12,8},{16,20},{20,16},{24,28},{28,24},{1,5},{5... | collective-permute-start | bytes 2359304 | tf_op jit(solution)/shard_map/ppermute | solution.py:40
  166.4 35.6 %collective-permute-start.37 = (bf16[1,1,4,96,1024]{4,3,2,1,0:T(8,128)(2,1)}, bf16[1,1,4,96,1024]{4,3,2,1,0:T(8,128)(2,1)}, u32[]{:S(2)}, u32[]{:S(2)}) collective-permute-start(bf16[1,1,4,96,1024]{4,3,2,1,0:T(8,128)(2,1)} %get-tuple-element.85.refs_11_), channel_id=1, source_target_pairs={{0,6},{1,7},{2,4},{3,5},{4,2},{5,3},{6,0},{7,1},{8,14},{9,15},{10,... | collective-permute-start | bytes 2359304 | tf_op jit(solution)/shard_map/ppermute | solution.py:46
  197.6 18.0 %collective-permute-start.34 = (bf16[2,512,768]{2,1,0:T(8,128)(2,1)}, bf16[2,512,768]{2,1,0:T(8,128)(2,1)}, u32[]{:S(2)}, u32[]{:S(2)}) collective-permute-start(bf16[2,512,768]{2,1,0:T(8,128)(2,1)} %spread.2.refs_4_), channel_id=1, source_target_pairs={{0,1},{1,0},{2,3},{3,2},{4,5},{5,4},{6,7},{7,6},{8,9},{9,8},{10,11... | collective-permute-start | bytes 4718600 | tf_op jit(solution)/shard_map/ppermute | solution.py:35
  211.1 23.3 %all-to-all-start.2 = ((bf16[4,96,1024]{2,1,0:T(8,128)(2,1)}), bf16[4,96,1024]{2,1,0:T(8,128)(2,1)S(1)}, u32[]{:S(2)}, u32[]{:S(2)}) async-start(bf16[4,96,1024]{2,1,0:T(8,128)(2,1)} %joined_sums.2.refs_2_), calls=%async_computation.2 | async-start | bytes 1572864 | tf_op jit(solution)/shard_map/all_to_all | solution.py:86
  214.6 17.0 %collective-permute-start.39 = (bf16[1,1,4,112,768]{4,3,2,1,0:T(8,128)(2,1)}, bf16[1,1,4,112,768]{4,3,2,1,0:T(8,128)(2,1)}, u32[]{:S(2)}, u32[]{:S(2)}) collective-permute-start(bf16[1,1,4,112,768]{4,3,2,1,0:T(8,128)(2,1)} %get-tuple-element.99.refs_0_), channel_id=1, source_target_pairs={{0,4},{4,0},{8,12},{12,8},{16,20},{20,16},{24,28},{28,24},{1,5},{5... | collective-permute-start | bytes 2064392 | tf_op jit(solution)/shard_map/ppermute | solution.py:40
  220.6 28.7 %collective-permute-start.38 = (bf16[512,768]{1,0:T(8,128)(2,1)}, bf16[512,768]{1,0:T(8,128)(2,1)S(1)}, u32[]{:S(2)}, u32[]{:S(2)}) collective-permute-start(bf16[512,768]{1,0:T(8,128)(2,1)} %get-tuple-element.105.refs_0_), channel_id=1, source_target_pairs={{0,2},{1,3},{2,0},{3,1},{4,6},{5,7},{6,4},{7,5},{8,10},{9,11},{10,... | collective-permute-start | bytes 2359304 | tf_op jit(solution)/shard_map/ppermute | solution.py:35
  234.4 20.9 %all-to-all-start.1 = ((bf16[4,112,768]{2,1,0:T(8,128)(2,1)}), bf16[4,112,768]{2,1,0:T(8,128)(2,1)S(1)}, u32[]{:S(2)}, u32[]{:S(2)}) async-start(bf16[4,112,768]{2,1,0:T(8,128)(2,1)} %joined_sums.3.refs_0_), calls=%async_computation.1 | async-start | bytes 1376256 | tf_op jit(solution)/shard_map/all_to_all | solution.py:86
  238.7 7.3 %collective-permute-start.40 = (bf16[2,96,768]{2,1,0:T(8,128)(2,1)S(1)}, bf16[2,96,768]{2,1,0:T(8,128)(2,1)S(1)}, u32[]{:S(2)}, u32[]{:S(2)}) collective-permute-start(bf16[2,96,768]{2,1,0:T(8,128)(2,1)S(1)} %copy-done.13), channel_id=1, source_target_pairs={{0,2},{1,3},{2,0},{3,1},{4,6},{5,7},{6,4},{7,5},{8,10},{9,11},{10,... | collective-permute-start | bytes 884744 | tf_op jit(solution)/shard_map/ppermute | solution.py:35
  248.5 5.4 %collective-permute-start.41 = (bf16[1,96,768]{2,1,0:T(8,128)(2,1)}, bf16[1,96,768]{2,1,0:T(8,128)(2,1)S(1)}, u32[]{:S(2)}, u32[]{:S(2)}) collective-permute-start(bf16[1,96,768]{2,1,0:T(8,128)(2,1)} %get-tuple-element.110), channel_id=1, source_target_pairs={{0,4},{4,0},{8,12},{12,8},{16,20},{20,16},{24,28},{28,24},{1,5},{5... | collective-permute-start | bytes 442376 | tf_op jit(solution)/shard_map/ppermute | solution.py:40
  (32 other events, 342.8 us)

commit v7 on v6

--- a/solution.py
+++ b/solution.py
@@ -1274,11 +1274,13 @@
     if halved:
         kept, gone = row_dot([qkv_group], 1, "bits", (), tail)
         away = dp_swap(gone, 1)
-        parts = spread([grads[3], grads[1]], qkv_w, waited=(gone,))
+        parts = spread([grads[3], grads[1]], qkv_w, waited=(gone, *up_away))
         spread_away = swap(parts, 1)
-        up_blocks = joined_sums([a[0, 0] for a in (up_quads[0], *up_away)], (parts,))
-        up_arrived = far_exchange(up_blocks)
-        beyond, here = spread([grads[2], grads[0]], qkv_w, spread_away, after_low, (up_blocks,))
+        up_blocks = joined_sums([a[0, 0] for a in (up_quads[0], *up_away)], (parts,), True)
+        up_part = up_blocks[0].astype(f32)
+        for z in range(1, 4):
+            up_part = up_part + dp_swap(up_blocks[z], 2 * z).astype(f32)
+        beyond, here = spread([grads[2], grads[0]], qkv_w, spread_away, after_low, (up_blocks[0],))
         beyond_away = swap(beyond, 2)
         down_here, down_next = fold(down_blocks, (beyond,))
         down_away = swap(down_next, 2)
@@ -1288,7 +1290,6 @@
         down_here, down_next = plus(down_here, down_away, (blocks,), 2)
         down_away = dp_swap(down_next, 1)
         down_part = down_here[0].astype(f32) + down_away[0].astype(f32)
-        up_part = jnp.sum(up_arrived.astype(f32), axis=0)
         qkv_part, small = qkv_part[:-16], qkv_part[-16:]
     else:
         blocks = row_dot([qkv_group], 1)[0].reshape(D, -1)

time: 259 us -> 255 us (0.985)
  waiting for transfers between devices: 62 us -> 55.3 us
  starting transfers between devices: 43.5 us -> 46.8 us
    all_to_all x3 -> x2, waiting for transfers between devices: 7.23 us -> 0.49 us  [far_exchange(): lax.all_to_all(blocks, 'dp', 0, 0, axis_index_groups=groups, tiled=True)]
    ppermute x3 -> x6, starting transfers between devices: 2.68 us -> 7.88 us  [dp_swap(): return lax.ppermute(array, 'dp', [(t, t ^ bit) for t in range(size)])]
    ppermute x24, waiting for transfers between devices: 15.5 us -> 10.4 us  [swap(): return lax.ppermute(array, 'tensor', [(t, t ^ bit) for t in range(size)])]
    ppermute x1, waiting for transfers between devices: 4.41 us -> 8.7 us  [swap_both(): return lax.ppermute(array, axes, [(t, t ^ 6) for t in range(size)])]
    all_to_all x3 -> x2, starting transfers between devices: 12.6 us -> 9.76 us  [far_exchange(): lax.all_to_all(blocks, 'dp', 0, 0, axis_index_groups=groups, tiled=True)]
    ppermute x3 -> x6, waiting for transfers between devices: 9.57 us -> 10.5 us  [dp_swap(): return lax.ppermute(array, 'dp', [(t, t ^ bit) for t in range(size)])]
  transfers between devices with their start and end apart: 45 -> 47, of which waited for: 20 -> 17; matrix products, arithmetic and copies ran while one was open for 4% -> 4% of each run, Pallas kernels for 36% -> 36%
where the time goes in v7:
time: 255 us; the launch traced here: 254 us
  Pallas kernels  132 us (52%)
  waiting for transfers between devices  55.3 us (22%)
  starting transfers between devices  46.8 us (18%)
  local copies, waits for them, and re-layouts  14.7 us (6%)
  other arithmetic  3.92 us (2%)
    pallas_call x1, Pallas kernels, layer_rows(): pl.pallas_call(partial(rows_kernel, [at for _, at in mixed], len(weights)...  31.9 us
    pallas_call x2, Pallas kernels, attend_backward(): pl.pallas_call(partial(attend_back_kernel, heads, chosen, pieces, own_blo...  27.9 us
    ppermute x14, waiting for transfers between devices, ring_send(): lax.ppermute(array, 'dp', [(order[i], order[(i + step) % size]) for i in...  25.2 us
    pallas_call x3, Pallas kernels, row_dot(): pl.pallas_call(kernel, grid=(lows[-1],), out_shape=[struct((far, *lead, p...  21.1 us
    ppermute x14, starting transfers between devices, ring_send(): lax.ppermute(array, 'dp', [(order[i], order[(i + step) % size]) for i in...  16.9 us
    pallas_call x2, Pallas kernels, attend_forward(): pl.pallas_call(partial(attend_kernel, heads, chosen, pieces, own_blocks),...  14.5 us
    ppermute x6, waiting for transfers between devices, dp_swap(): return lax.ppermute(array, 'dp', [(t, t ^ bit) for t in range(size)])  10.5 us
    ppermute x24, waiting for transfers between devices, swap(): return lax.ppermute(array, 'tensor', [(t, t ^ bit) for t in range(size)])  10.4 us
  transfers between devices with their start and end apart: 47, of which 17 were waited for; matrix products, arithmetic and copies ran while one was open for 4% of the time, Pallas kernels for 36%

profile of v7, /device:TPU:0, one launch (start us, length us, event | category | flops | bytes accessed | tf_op | source)
XLA Modules:
  0.0 254.2 jit_solution(16904627301860499770)
XLA Ops:
  0.7 1.5 pack_queries.1._.refs_4_
  2.2 3.0 %collective-permute-start.4 = (bf16[96,768]{1,0:T(8,128)(2,1)}, bf16[96,768]{1,0:T(8,128)(2,1)S(1)}, u32[]{:S(2)}, u32[]{:S(2)}) collective-permute-start(bf16[96,768]{1,0:T(8,128)(2,1)} %pack_queries.1._.refs_4_), channel_id=1, source_target_pairs={{0,8},{8,16},{16,24},{24,28},{28,20},{20,12},{12,4},{4,0},{1,9},{9... | collective-permute-start | bytes 442376 | tf_op jit(solution)/shard_map/ppermute | solution.py:64
  5.2 1.7 copy.38.down
  6.9 1.9 pack_weights.1.a
  8.9 1.5 collective-permute-start.1
  10.8 1.6 collective-permute-start.6
  12.4 3.3 %collective-permute-done.5.refs_6_ = bf16[96,768]{1,0:T(8,128)(2,1)S(1)} collective-permute-done((bf16[96,768]{1,0:T(8,128)(2,1)}, bf16[96,768]{1,0:T(8,128)(2,1)S(1)}, u32[]{:S(2)}, u32[]{:S(2)}) %collective-permute-start.5) | collective-permute-done | bytes 147488 | tf_op jit(solution)/shard_map/ppermute | solution.py:64
  16.2 1.6 collective-permute-start.8
  19.4 2.1 held.1
  21.4 1.5 collective-permute-start.2
  23.4 1.6 collective-permute-start.10
  25.0 3.1 %collective-permute-done.9.refs_10_.refs_1_ = bf16[96,768]{1,0:T(8,128)(2,1)S(1)} collective-permute-done((bf16[96,768]{1,0:T(8,128)(2,1)S(1)}, bf16[96,768]{1,0:T(8,128)(2,1)S(1)}, u32[]{:S(2)}, u32[]{:S(2)}) %collective-permute-start.9) | collective-permute-done | bytes 147488 | tf_op jit(solution)/shard_map/ppermute | solution.py:64
  29.4 2.0 pair_weights.1.refs_6_
  31.4 1.6 collective-permute-start.14
  33.0 6.9 %collective-permute-done.2.refs_2_ = bf16[512,768]{1,0:T(8,128)(2,1)} collective-permute-done((bf16[512,768]{1,0:T(8,128)(2,1)}, bf16[512,768]{1,0:T(8,128)(2,1)}, u32[]{:S(2)}, u32[]{:S(2)}) %collective-permute-start.2) | collective-permute-done | bytes 786464 | tf_op jit(solution)/shard_map/ppermute | solution.py:35
  40.4 6.8 %collective-permute-done.14.refs_7_ = bf16[96,3584]{1,0:T(8,128)(2,1)S(1)} collective-permute-done((bf16[96,3584]{1,0:T(8,128)(2,1)}, bf16[96,3584]{1,0:T(8,128)(2,1)S(1)}, u32[]{:S(2)}, u32[]{:S(2)}) %collective-permute-start.14) | collective-permute-done | bytes 688160 | tf_op jit(solution)/shard_map/ppermute | solution.py:64
  47.2 1.6 collective-permute-start.16
  50.1 1.5 block_tables.1
  52.8 5.2 %collective-permute-done.15.refs_8_ = bf16[96,3584]{1,0:T(8,128)(2,1)S(1)} collective-permute-done((bf16[96,3584]{1,0:T(8,128)(2,1)}, bf16[96,3584]{1,0:T(8,128)(2,1)S(1)}, u32[]{:S(2)}, u32[]{:S(2)}) %collective-permute-start.15) | collective-permute-done | bytes 688160 | tf_op jit(solution)/shard_map/ppermute | solution.py:64
  58.5 2.8 %collective-permute-done.16.refs_9_ = bf16[96,3584]{1,0:T(8,128)(2,1)S(1)} collective-permute-done((bf16[96,3584]{1,0:T(8,128)(2,1)S(1)}, bf16[96,3584]{1,0:T(8,128)(2,1)S(1)}, u32[]{:S(2)}, u32[]{:S(2)}) %collective-permute-start.16) | collective-permute-done | bytes 688160 | tf_op jit(solution)/shard_map/ppermute | solution.py:64
  61.3 1.6 collective-permute-start.18
  62.9 8.3 %project_in.1 = (bf16[512,768]{1,0:T(8,128)(2,1)}, bf16[512,768]{1,0:T(8,128)(2,1)}, bf16[512,768]{1,0:T(8,128)(2,1)}, bf16[512,768]{1,0:T(8,128)(2,1)}, bf16[2,...) custom-call(bf16[512,768]{1,0:T(8,128)(2,1)} %refs_4_.1, ...), custom_call_target="tpu_custom_call" | custom-call | flops 4831838208 | bytes 25165824 | tf_op jit(solution)/shard_map/project_in/pallas_call | solution.py:1124
  71.2 7.2 %attend_forward.3 = (bf16[2,512,256]{2,1,0:T(8,128)(2,1)}, f32[512,128]{1,0:T(8,128)}, f32[512,128]{1,0:T(8,128)}) custom-call(s32[32,128]{1,0:T(8,128)} %get-tuple-element.68.table, bf16[512,768]{1,0:T(8,128)(2,1)} %get-tuple-element.69.refs_0_, bf16[512,768]{1,0:T(8,128)(2,1)} %get-tuple-element.70.refs_1_, bf16[512,768]{1,0:T(8,128)(2,1)} %get-tuple-element.71.refs_2_, ...), custom_call_target="tpu_custom_call" | custom-call | flops 4831838208 | bytes 16777216 | tf_op jit(solution)/shard_map/attend_forward/pallas_call | solution.py:278
  79.2 1.6 collective-permute-start.20
  80.7 7.2 %attend_forward.2 = (bf16[2,512,256]{2,1,0:T(8,128)(2,1)}, f32[512,128]{1,0:T(8,128)}, f32[512,128]{1,0:T(8,128)}) custom-call(s32[32,128]{1,0:T(8,128)} %get-tuple-element.68.table, bf16[512,768]{1,0:T(8,128)(2,1)} %get-tuple-element.69.refs_0_, bf16[512,768]{1,0:T(8,128)(2,1)} %get-tuple-element.70.refs_1_, bf16[512,768]{1,0:T(8,128)(2,1)} %get-tuple-element.71.refs_2_, ...), custom_call_target="tpu_custom_call" | custom-call | flops 4831838208 | bytes 16777216 | tf_op jit(solution)/shard_map/attend_forward/pallas_call | solution.py:278
  91.4 3.3 %collective-permute-done.19.refs_12_ = bf16[96,3584]{1,0:T(8,128)(2,1)} collective-permute-done((bf16[96,3584]{1,0:T(8,128)(2,1)}, bf16[96,3584]{1,0:T(8,128)(2,1)}, u32[]{:S(2)}, u32[]{:S(2)}) %collective-permute-start.19) | collective-permute-done | bytes 688160 | tf_op jit(solution)/shard_map/ppermute | solution.py:64
  99.1 31.9 %layer_rows.1 = (bf16[512,768]{1,0:T(8,128)(2,1)}, bf16[4,512,768]{2,1,0:T(8,128)(2,1)}, bf16[4,512,768]{2,1,0:T(8,128)(2,1)}, bf16[3,2,4,96,512]{4,3,2,1,0:T(8,...) custom-call(s32[1]{0:T(128)S(6)} %copy.40.length_ref.length, ...), custom_call_target="tpu_custom_call" | custom-call | flops 176160768 | bytes 393216 | tf_op jit(solution)/shard_map/layer_rows/pallas_call | solution.py:760
  133.5 9.7 %attend_backward.2 = (bf16[512,256]{1,0:T(8,128)(2,1)}, f32[2048,256]{1,0:T(8,128)}, f32[2048,256]{1,0:T(8,128)}) custom-call(s32[32,128]{1,0:T(8,128)} %get-tuple-element.68.table, bf16[512,768]{1,0:T(8,128)(2,1)} %get-tuple-element.69.refs_0_, bf16[512,768]{1,0:T(8,128)(2,1)} %get-tuple-element.70.refs_1_, bf16[512,768]{1,0:T(8,128)(2,1)} %get-tuple-element.71.refs_2_, ...), custom_call_target="tpu_custom_call" | custom-call | flops 23592960 | bytes 196608 | tf_op jit(solution)/shard_map/attend_backward/pallas_call | solution.py:465
  144.0 1.7 copy-done
  145.7 6.4 %row_dot.3.refs_12_ = bf16[4,2,2,96,768]{4,3,2,1,0:T(8,128)(2,1)} custom-call(bf16[3,2,4,96,512]{4,3,2,1,0:T(8,128)(2,1)} %get-tuple-element.83.refs_0_.refs_2_, bf16[3,2,4,96,512]{4,3,2,1,0:T(8,128)(2,1)} %collective-permute-done.32.refs_1_.refs_3_, bf16[4,512,768]{2,1,0:T(8,128)(2,1)} %get-tuple-element.84.refs_2_.refs_3_.refs_4_.refs_5_, ...), custom_call_target="tpu_custom_call" | custom-call | flops 37748736 | bytes 131072 | tf_op jit(solution)/shard_map/row_dot/pallas_call | solution.py:875
  152.0 4.8 %all-to-all-start = ((bf16[4,2,2,96,768]{4,3,2,1,0:T(8,128)(2,1)}), bf16[4,2,2,96,768]{4,3,2,1,0:T(8,128)(2,1)S(1)}, u32[]{:S(2)}, u32[]{:S(2)}) async-start(bf16[4,2,2,96,768]{4,3,2,1,0:T(8,128)(2,1)} %row_dot.3.refs_12_), calls=%async_computation | async-start | bytes 4718592 | tf_op jit(solution)/shard_map/all_to_all | solution.py:86
  156.9 8.2 %row_dot.4 = (bf16[1,1,4,96,1024]{4,3,2,1,0:T(8,128)(2,1)}, bf16[1,1,4,96,1024]{4,3,2,1,0:T(8,128)(2,1)}, bf16[1,1,4,96,1024]{4,3,2,1,0:T(8,128)(2,1)}, bf16[1,1,4,96,1024]{4,3,2,1,0:T(8,128)(2,1)}) custom-call(bf16[3,2,4,96,512]{4,3,2,1,0:T(8,128)(2,1)} %get-tuple-element.83.refs_0_.refs_2_, ...), custom_call_target="tpu_custom_call" | custom-call | flops 50331648 | bytes 131072 | tf_op jit(solution)/shard_map/row_dot/pallas_call | solution.py:875
  166.5 2.1 collective-permute-start.36
  168.6 18.2 %attend_backward.3 = (bf16[512,768]{1,0:T(8,128)(2,1)}, bf16[512,768]{1,0:T(8,128)(2,1)}, bf16[512,768]{1,0:T(8,128)(2,1)}, bf16[512,768]{1,0:T(8,128)(2,1)}, bf16[16,768]{1,0:T(8,128)(2,1)}) custom-call(s32[32,128]{1,0:T(8,128)} %get-tuple-element.68.table, bf16[512,768]{1,0:T(8,128)(2,1)} %get-tuple-element.69.refs_0_, ...), custom_call_target="tpu_custom_call" | custom-call | flops 70778880 | bytes 196608 | tf_op jit(solution)/shard_map/attend_backward/pallas_call | solution.py:465
  186.8 6.6 %row_dot.5 = (bf16[1,1,4,112,768]{4,3,2,1,0:T(8,128)(2,1)}, bf16[1,1,4,112,768]{4,3,2,1,0:T(8,128)(2,1)}) custom-call(bf16[1,2,4,96,512]{4,3,2,1,0:T(8,128)(2,1)} %bitcast.31, bf16[1,2,4,96,512]{4,3,2,1,0:T(8,128)(2,1)} %bitcast.32, bf16[1,2,4,96,512]{4,3,2,1,0:T(8,128)(2,1)} %bitcast.33, bf16[1,2,4,96,512]{4,3,2,1,0:T(8,128)(2,1)} %bitcast.34, ...), custom_call_target="tpu_custom_call" | custom-call | flops 37748736 | bytes 131072 | tf_op jit(solution)/shard_map/row_dot/pallas_call | solution.py:875
  193.4 8.7 %collective-permute-done.36.refs_3_ = bf16[1,1,4,96,1024]{4,3,2,1,0:T(8,128)(2,1)} collective-permute-done((bf16[1,1,4,96,1024]{4,3,2,1,0:T(8,128)(2,1)}, bf16[1,1,4,96,1024]{4,3,2,1,0:T(8,128)(2,1)}, u32[]{:S(2)}, u32[]{:S(2)}) %collective-permute-start.36) | collective-permute-done | bytes 786464 | tf_op jit(solution)/shard_map/ppermute | solution.py:46
  202.1 4.3 %spread.2.refs_4_ = bf16[2,512,768]{2,1,0:T(8,128)(2,1)} custom-call(bf16[512,768]{1,0:T(8,128)(2,1)} %get-tuple-element.96.first, bf16[512,768]{1,0:T(8,128)(2,1)} %get-tuple-element.97.second, bf16[768,768]{1,0:T(8,128)(2,1)} %get-tuple-element.95.w, bf16[1,1,4,112,768]{4,3,2,1,0:T(8,128)(2,1)} %get-tuple-element.103.refs_0_, ...), custom_call_target="tpu_custom_call" | custom-call | flops 18874368 | bytes 81920 | tf_op jit(solution)/shard_map/spread/pallas_call | solution.py:992
  207.6 2.9 %joined_sums.2 = (bf16[96,1024]{1,0:T(8,128)(2,1)}, bf16[96,1024]{1,0:T(8,128)(2,1)}, bf16[96,1024]{1,0:T(8,128)(2,1)}, bf16[96,1024]{1,0:T(8,128)(2,1)}) custom-call(bf16[4,96,1024]{2,1,0:T(8,128)(2,1)} %bitcast.35, bf16[4,96,1024]{2,1,0:T(8,128)(2,1)} %bitcast.26, bf16[4,96,1024]{2,1,0:T(8,128)(2,1)} %bitcast.12.refs_2_, ...), custom_call_target="tpu_custom_call" | custom-call | flops 24576 | bytes 49152 | tf_op jit(solution)/shard_map/joined_sums/pallas_call | solution.py:962
  210.5 5.0 %spread.3 = (bf16[512,768]{1,0:T(8,128)(2,1)}, f32[512,768]{1,0:T(8,128)}) custom-call(bf16[512,768]{1,0:T(8,128)(2,1)} %get-tuple-element.93.first, bf16[512,768]{1,0:T(8,128)(2,1)} %get-tuple-element.94.second, bf16[768,768]{1,0:T(8,128)(2,1)} %get-tuple-element.95.w, bf16[2,512,768]{2,1,0:T(8,128)(2,1)} %collective-permute-done.37.refs_0_, ...), custom_call_target="tpu_custom_call" | custom-call | flops 18874368 | bytes 81920 | tf_op jit(solution)/shard_map/spread/pallas_call | solution.py:992
  216.7 3.5 %collective-permute-start.42 = (bf16[96,1024]{1,0:T(8,128)(2,1)}, bf16[96,1024]{1,0:T(8,128)(2,1)S(1)}, u32[]{:S(2)}, u32[]{:S(2)}) collective-permute-start(bf16[96,1024]{1,0:T(8,128)(2,1)} %get-tuple-element.115), channel_id=1, source_target_pairs={{0,24},{4,28},{8,16},{12,20},{16,8},{20,12},{24,0},{28,4},{1,25},{... | collective-permute-start | bytes 589832 | tf_op jit(solution)/shard_map/ppermute | solution.py:40
  221.1 1.4 copy-done.1
  222.5 2.7 %fold.1 = (bf16[2,96,768]{2,1,0:T(8,128)(2,1)}, bf16[2,96,768]{2,1,0:T(8,128)(2,1)}) custom-call(bf16[4,2,2,96,768]{4,3,2,1,0:T(8,128)(2,1)} %copy-done.1, bf16[512,768]{1,0:T(8,128)(2,1)} %get-tuple-element.110.refs_0_), custom_call_target="tpu_custom_call" | custom-call | flops 18432 | bytes 55296 | tf_op jit(solution)/shard_map/fold/pallas_call | solution.py:937
  226.0 2.3 joined_sums.3.refs_0_
  228.4 4.9 %all-to-all-start.1 = ((bf16[4,112,768]{2,1,0:T(8,128)(2,1)}), bf16[4,112,768]{2,1,0:T(8,128)(2,1)S(1)}, u32[]{:S(2)}, u32[]{:S(2)}) async-start(bf16[4,112,768]{2,1,0:T(8,128)(2,1)} %joined_sums.3.refs_0_), calls=%async_computation.1 | async-start | bytes 1376256 | tf_op jit(solution)/shard_map/all_to_all | solution.py:86
  233.3 7.9 %collective-permute-done.41 = bf16[96,1024]{1,0:T(8,128)(2,1)} collective-permute-done((bf16[96,1024]{1,0:T(8,128)(2,1)}, bf16[96,1024]{1,0:T(8,128)(2,1)}, u32[]{:S(2)}, u32[]{:S(2)}) %collective-permute-start.41) | collective-permute-done | bytes 196640 | tf_op jit(solution)/shard_map/ppermute | solution.py:40
  243.8 1.8 plus.1
  245.6 1.5 collective-permute-start.44
  248.4 2.6 %collective-permute-done.44 = bf16[1,96,768]{2,1,0:T(8,128)(2,1)S(1)} collective-permute-done((bf16[1,96,768]{2,1,0:T(8,128)(2,1)}, bf16[1,96,768]{2,1,0:T(8,128)(2,1)S(1)}, u32[]{:S(2)}, u32[]{:S(2)}) %collective-permute-start.44) | collective-permute-done | bytes 147488 | tf_op jit(solution)/shard_map/ppermute | solution.py:40
  (162 shorter events, 31.5 us)
Async XLA Ops:
  2.2 8.6 %collective-permute-start.4 = (bf16[96,768]{1,0:T(8,128)(2,1)}, bf16[96,768]{1,0:T(8,128)(2,1)S(1)}, u32[]{:S(2)}, u32[]{:S(2)}) collective-permute-start(bf16[96,768]{1,0:T(8,128)(2,1)} %pack_queries.1._.refs_4_), channel_id=1, source_target_pairs={{0,8},{8,16},{16,24},{24,28},{28,20},{20,12},{12,4},{4,0},{1,9},{9... | collective-permute-start | bytes 442376 | tf_op jit(solution)/shard_map/ppermute | solution.py:64
  8.9 9.7 %collective-permute-start.1 = (bf16[96,1792]{1,0:T(8,128)(2,1)}, bf16[96,1792]{1,0:T(8,128)(2,1)S(1)}, u32[]{:S(2)}, u32[]{:S(2)}) collective-permute-start(bf16[96,1792]{1,0:T(8,128)(2,1)} %pack_weights.1.a), channel_id=1, source_target_pairs={{0,2},{1,3},{2,0},{3,1},{4,6},{5,7},{6,4},{7,5},{8,10},{9,11},{10,... | collective-permute-start | bytes 1032200 | tf_op jit(solution)/shard_map/ppermute | solution.py:35
  10.4 5.4 %collective-permute-start.5 = (bf16[96,768]{1,0:T(8,128)(2,1)}, bf16[96,768]{1,0:T(8,128)(2,1)S(1)}, u32[]{:S(2)}, u32[]{:S(2)}) collective-permute-start(bf16[96,768]{1,0:T(8,128)(2,1)} %pack_queries.1._.refs_4_), channel_id=1, source_target_pairs={{0,4},{8,0},{16,8},{24,16},{28,24},{20,28},{12,20},{4,12},{1,5},{9... | collective-permute-start | bytes 442376 | tf_op jit(solution)/shard_map/ppermute | solution.py:64
  10.8 52.0 %copy-start.31 = (bf16[96,768]{1,0:T(8,128)(2,1)}, bf16[96,768]{1,0:T(8,128)(2,1)S(1)}, u32[]{:S(2)}) copy-start(bf16[96,768]{1,0:T(8,128)(2,1)S(1)} %collective-permute-done.4.refs_5_) | copy-start | bytes 442372
  10.8 5.4 %collective-permute-start.6 = (bf16[96,768]{1,0:T(8,128)(2,1)S(1)}, bf16[96,768]{1,0:T(8,128)(2,1)S(1)}, u32[]{:S(2)}, u32[]{:S(2)}) collective-permute-start(bf16[96,768]{1,0:T(8,128)(2,1)S(1)} %collective-permute-done.4.refs_5_), channel_id=1, source_target_pairs={{0,8},{8,16},{16,24},{24,28},{28,20},{20,12},{12,4},{4,0},{1,9},{9... | collective-permute-start | bytes 442376 | tf_op jit(solution)/shard_map/ppermute | solution.py:64
  15.7 7.2 %collective-permute-start.7 = (bf16[96,768]{1,0:T(8,128)(2,1)S(1)}, bf16[96,768]{1,0:T(8,128)(2,1)S(1)}, u32[]{:S(2)}, u32[]{:S(2)}) collective-permute-start(bf16[96,768]{1,0:T(8,128)(2,1)S(1)} %collective-permute-done.5.refs_6_), channel_id=1, source_target_pairs={{0,4},{8,0},{16,8},{24,16},{28,24},{20,28},{12,20},{4,12},{1,5},{9... | collective-permute-start | bytes 442376 | tf_op jit(solution)/shard_map/ppermute | solution.py:64
  16.2 7.2 %collective-permute-start.8 = (bf16[96,768]{1,0:T(8,128)(2,1)S(1)}, bf16[96,768]{1,0:T(8,128)(2,1)S(1)}, u32[]{:S(2)}, u32[]{:S(2)}) collective-permute-start(bf16[96,768]{1,0:T(8,128)(2,1)S(1)} %collective-permute-done.6.refs_7_), channel_id=1, source_target_pairs={{0,8},{8,16},{16,24},{24,28},{28,20},{20,12},{12,4},{4,0},{1,9},{9... | collective-permute-start | bytes 442376 | tf_op jit(solution)/shard_map/ppermute | solution.py:64
  21.4 18.4 %collective-permute-start.2 = (bf16[512,768]{1,0:T(8,128)(2,1)}, bf16[512,768]{1,0:T(8,128)(2,1)}, u32[]{:S(2)}, u32[]{:S(2)}) collective-permute-start(bf16[512,768]{1,0:T(8,128)(2,1)} %held.1), channel_id=1, source_target_pairs={{0,2},{1,3},{2,0},{3,1},{4,6},{5,7},{6,4},{7,5},{8,10},{9,11},{10,... | collective-permute-start | bytes 2359304 | tf_op jit(solution)/shard_map/ppermute | solution.py:35
  22.9 5.1 %collective-permute-start.9 = (bf16[96,768]{1,0:T(8,128)(2,1)S(1)}, bf16[96,768]{1,0:T(8,128)(2,1)S(1)}, u32[]{:S(2)}, u32[]{:S(2)}) collective-permute-start(bf16[96,768]{1,0:T(8,128)(2,1)S(1)} %collective-permute-done.7.refs_8_), channel_id=1, source_target_pairs={{0,4},{8,0},{16,8},{24,16},{28,24},{20,28},{12,20},{4,12},{1,5},{9... | collective-permute-start | bytes 442376 | tf_op jit(solution)/shard_map/ppermute | solution.py:64
  23.4 5.1 %collective-permute-start.10 = (bf16[96,768]{1,0:T(8,128)(2,1)S(1)}, bf16[96,768]{1,0:T(8,128)(2,1)S(1)}, u32[]{:S(2)}, u32[]{:S(2)}) collective-permute-start(bf16[96,768]{1,0:T(8,128)(2,1)S(1)} %collective-permute-done.8.refs_9_.refs_0_), channel_id=1, source_target_pairs={{0,8},{8,16},{16,24},{24,28},{28,20},{20,12},{12,4},{4,0},{1,9},{9... | collective-permute-start | bytes 442376 | tf_op jit(solution)/shard_map/ppermute | solution.py:64
  31.4 15.8 %collective-permute-start.14 = (bf16[96,3584]{1,0:T(8,128)(2,1)}, bf16[96,3584]{1,0:T(8,128)(2,1)S(1)}, u32[]{:S(2)}, u32[]{:S(2)}) collective-permute-start(bf16[96,3584]{1,0:T(8,128)(2,1)} %pair_weights.1.refs_6_), channel_id=1, source_target_pairs={{0,8},{8,16},{16,24},{24,28},{28,20},{20,12},{12,4},{4,0},{1,9},{9... | collective-permute-start | bytes 2064392 | tf_op jit(solution)/shard_map/ppermute | solution.py:64
  33.0 19.3 %collective-permute-start = (bf16[512,768]{1,0:T(8,128)(2,1)S(1)}, bf16[512,768]{1,0:T(8,128)(2,1)}, u32[]{:S(2)}, u32[]{:S(2)}) collective-permute-start(bf16[512,768]{1,0:T(8,128)(2,1)S(1)} %copy-done.4), channel_id=1, source_target_pairs={{0,1},{1,0},{2,3},{3,2},{4,5},{5,4},{6,7},{7,6},{8,9},{9,8},{10,11... | collective-permute-start | bytes 2359304 | tf_op jit(solution)/shard_map/ppermute | solution.py:35
  39.9 18.6 %collective-permute-start.3 = (bf16[512,768]{1,0:T(8,128)(2,1)}, bf16[512,768]{1,0:T(8,128)(2,1)}, u32[]{:S(2)}, u32[]{:S(2)}) collective-permute-start(bf16[512,768]{1,0:T(8,128)(2,1)} %collective-permute-done.2.refs_2_), channel_id=1, source_target_pairs={{0,1},{1,0},{2,3},{3,2},{4,5},{5,4},{6,7},{7,6},{8,9},{9,8},{10,11... | collective-permute-start | bytes 2359304 | tf_op jit(solution)/shard_map/ppermute | solution.py:35
  39.9 18.1 %collective-permute-start.15 = (bf16[96,3584]{1,0:T(8,128)(2,1)}, bf16[96,3584]{1,0:T(8,128)(2,1)S(1)}, u32[]{:S(2)}, u32[]{:S(2)}) collective-permute-start(bf16[96,3584]{1,0:T(8,128)(2,1)} %pair_weights.1.refs_6_), channel_id=1, source_target_pairs={{0,4},{8,0},{16,8},{24,16},{28,24},{20,28},{12,20},{4,12},{1,5},{9... | collective-permute-start | bytes 2064392 | tf_op jit(solution)/shard_map/ppermute | solution.py:64
  47.2 14.1 %collective-permute-start.16 = (bf16[96,3584]{1,0:T(8,128)(2,1)S(1)}, bf16[96,3584]{1,0:T(8,128)(2,1)S(1)}, u32[]{:S(2)}, u32[]{:S(2)}) collective-permute-start(bf16[96,3584]{1,0:T(8,128)(2,1)S(1)} %collective-permute-done.14.refs_7_), channel_id=1, source_target_pairs={{0,8},{8,16},{16,24},{24,28},{28,20},{20,12},{12,4},{4,0},{1,9},{9... | collective-permute-start | bytes 2064392 | tf_op jit(solution)/shard_map/ppermute | solution.py:64
  52.3 26.2 %collective-permute-start.21 = (bf16[96,3584]{1,0:T(8,128)(2,1)}, bf16[96,3584]{1,0:T(8,128)(2,1)}, u32[]{:S(2)}, u32[]{:S(2)}) collective-permute-start(bf16[96,3584]{1,0:T(8,128)(2,1)} %pair_weights.1.refs_6_), channel_id=1, source_target_pairs={{0,1},{1,0},{2,3},{3,2},{4,5},{5,4},{6,7},{7,6},{8,9},{9,8},{10,11... | collective-permute-start | bytes 2064392 | tf_op jit(solution)/shard_map/ppermute | solution.py:35
  52.3 36.7 %collective-permute-start.22 = (bf16[96,3584]{1,0:T(8,128)(2,1)S(1)}, bf16[96,3584]{1,0:T(8,128)(2,1)S(1)}, u32[]{:S(2)}, u32[]{:S(2)}) collective-permute-start(bf16[96,3584]{1,0:T(8,128)(2,1)S(1)} %collective-permute-done.14.refs_7_), channel_id=1, source_target_pairs={{0,1},{1,0},{2,3},{3,2},{4,5},{5,4},{6,7},{7,6},{8,9},{9,8},{10,11... | collective-permute-start | bytes 2064392 | tf_op jit(solution)/shard_map/ppermute | solution.py:35
  57.9 20.8 %collective-permute-start.17 = (bf16[96,3584]{1,0:T(8,128)(2,1)S(1)}, bf16[96,3584]{1,0:T(8,128)(2,1)}, u32[]{:S(2)}, u32[]{:S(2)}) collective-permute-start(bf16[96,3584]{1,0:T(8,128)(2,1)S(1)} %collective-permute-done.15.refs_8_), channel_id=1, source_target_pairs={{0,4},{8,0},{16,8},{24,16},{28,24},{20,28},{12,20},{4,12},{1,5},{9... | collective-permute-start | bytes 2064392 | tf_op jit(solution)/shard_map/ppermute | solution.py:64
  58.5 30.6 %collective-permute-start.23 = (bf16[96,3584]{1,0:T(8,128)(2,1)S(1)}, bf16[96,3584]{1,0:T(8,128)(2,1)}, u32[]{:S(2)}, u32[]{:S(2)}) collective-permute-start(bf16[96,3584]{1,0:T(8,128)(2,1)S(1)} %collective-permute-done.15.refs_8_), channel_id=1, source_target_pairs={{0,1},{1,0},{2,3},{3,2},{4,5},{5,4},{6,7},{7,6},{8,9},{9,8},{10,11... | collective-permute-start | bytes 2064392 | tf_op jit(solution)/shard_map/ppermute | solution.py:35
  61.3 17.9 %collective-permute-start.18 = (bf16[96,3584]{1,0:T(8,128)(2,1)S(1)}, bf16[96,3584]{1,0:T(8,128)(2,1)}, u32[]{:S(2)}, u32[]{:S(2)}) collective-permute-start(bf16[96,3584]{1,0:T(8,128)(2,1)S(1)} %collective-permute-done.16.refs_9_), channel_id=1, source_target_pairs={{0,8},{8,16},{16,24},{24,28},{28,20},{20,12},{12,4},{4,0},{1,9},{9... | collective-permute-start | bytes 2064392 | tf_op jit(solution)/shard_map/ppermute | solution.py:64
  78.5 12.2 %collective-permute-start.12 = (bf16[2,512,256]{2,1,0:T(8,128)(2,1)}, bf16[2,512,256]{2,1,0:T(8,128)(2,1)S(1)}, u32[]{:S(2)}, u32[]{:S(2)}) collective-permute-start(bf16[2,512,256]{2,1,0:T(8,128)(2,1)} %get-tuple-element.75), channel_id=1, source_target_pairs={{0,2},{1,3},{2,0},{3,1},{4,6},{5,7},{6,4},{7,5},{8,10},{9,11},{10,... | collective-permute-start | bytes 1572872 | tf_op jit(solution)/shard_map/ppermute | solution.py:35
  78.7 16.0 %collective-permute-start.19 = (bf16[96,3584]{1,0:T(8,128)(2,1)}, bf16[96,3584]{1,0:T(8,128)(2,1)}, u32[]{:S(2)}, u32[]{:S(2)}) collective-permute-start(bf16[96,3584]{1,0:T(8,128)(2,1)} %collective-permute-done.17.refs_10_), channel_id=1, source_target_pairs={{0,4},{8,0},{16,8},{24,16},{28,24},{20,28},{12,20},{4,12},{1,5},{9... | collective-permute-start | bytes 2064392 | tf_op jit(solution)/shard_map/ppermute | solution.py:64
  79.2 15.8 %collective-permute-start.20 = (bf16[96,3584]{1,0:T(8,128)(2,1)}, bf16[96,3584]{1,0:T(8,128)(2,1)}, u32[]{:S(2)}, u32[]{:S(2)}) collective-permute-start(bf16[96,3584]{1,0:T(8,128)(2,1)} %collective-permute-done.18.refs_11_), channel_id=1, source_target_pairs={{0,8},{8,16},{16,24},{24,28},{28,20},{20,12},{12,4},{4,0},{1,9},{9... | collective-permute-start | bytes 2064392 | tf_op jit(solution)/shard_map/ppermute | solution.py:64
  89.0 1.6 collective-permute-start.11
  89.1 6.9 %collective-permute-start.24 = (bf16[96,3584]{1,0:T(8,128)(2,1)S(1)}, bf16[96,3584]{1,0:T(8,128)(2,1)S(1)}, u32[]{:S(2)}, u32[]{:S(2)}) collective-permute-start(bf16[96,3584]{1,0:T(8,128)(2,1)S(1)} %collective-permute-done.16.refs_9_), channel_id=1, source_target_pairs={{0,1},{1,0},{2,3},{3,2},{4,5},{5,4},{6,7},{7,6},{8,9},{9,8},{10,11... | collective-permute-start | bytes 2064392 | tf_op jit(solution)/shard_map/ppermute | solution.py:35
  90.6 7.0 %collective-permute-start.25 = (bf16[96,3584]{1,0:T(8,128)(2,1)}, bf16[96,3584]{1,0:T(8,128)(2,1)S(1)}, u32[]{:S(2)}, u32[]{:S(2)}) collective-permute-start(bf16[96,3584]{1,0:T(8,128)(2,1)} %collective-permute-done.17.refs_10_), channel_id=1, source_target_pairs={{0,1},{1,0},{2,3},{3,2},{4,5},{5,4},{6,7},{7,6},{8,9},{9,8},{10,11... | collective-permute-start | bytes 2064392 | tf_op jit(solution)/shard_map/ppermute | solution.py:35
  91.3 7.2 %collective-permute-start.26 = (bf16[96,3584]{1,0:T(8,128)(2,1)}, bf16[96,3584]{1,0:T(8,128)(2,1)}, u32[]{:S(2)}, u32[]{:S(2)}) collective-permute-start(bf16[96,3584]{1,0:T(8,128)(2,1)} %collective-permute-done.18.refs_11_), channel_id=1, source_target_pairs={{0,1},{1,0},{2,3},{3,2},{4,5},{5,4},{6,7},{7,6},{8,9},{9,8},{10,11... | collective-permute-start | bytes 2064392 | tf_op jit(solution)/shard_map/ppermute | solution.py:35
  94.7 3.7 %collective-permute-start.27 = (bf16[96,3584]{1,0:T(8,128)(2,1)}, bf16[96,3584]{1,0:T(8,128)(2,1)}, u32[]{:S(2)}, u32[]{:S(2)}) collective-permute-start(bf16[96,3584]{1,0:T(8,128)(2,1)} %collective-permute-done.19.refs_12_), channel_id=1, source_target_pairs={{0,1},{1,0},{2,3},{3,2},{4,5},{5,4},{6,7},{7,6},{8,9},{9,8},{10,11... | collective-permute-start | bytes 2064392 | tf_op jit(solution)/shard_map/ppermute | solution.py:35
  95.0 3.5 %collective-permute-start.28 = (bf16[96,3584]{1,0:T(8,128)(2,1)}, bf16[96,3584]{1,0:T(8,128)(2,1)}, u32[]{:S(2)}, u32[]{:S(2)}) collective-permute-start(bf16[96,3584]{1,0:T(8,128)(2,1)} %collective-permute-done.20.refs_13_), channel_id=1, source_target_pairs={{0,1},{1,0},{2,3},{3,2},{4,5},{5,4},{6,7},{7,6},{8,9},{9,8},{10,11... | collective-permute-start | bytes 2064392 | tf_op jit(solution)/shard_map/ppermute | solution.py:35
  96.0 2.5 collective-permute-start.13
  131.1 12.9 %collective-permute-start.33 = (bf16[4,512,768]{2,1,0:T(8,128)(2,1)}, bf16[4,512,768]{2,1,0:T(8,128)(2,1)S(1)}, u32[]{:S(2)}, u32[]{:S(2)}) collective-permute-start(bf16[4,512,768]{2,1,0:T(8,128)(2,1)} %get-tuple-element.85), channel_id=1, source_target_pairs={{0,1},{1,0},{2,3},{3,2},{4,5},{5,4},{6,7},{7,6},{8,9},{9,8},{10,11... | collective-permute-start | bytes 9437192 | tf_op jit(solution)/shard_map/ppermute | solution.py:35
  131.3 12.7 %collective-permute-start.32 = (bf16[3,2,4,96,512]{4,3,2,1,0:T(8,128)(2,1)}, bf16[3,2,4,96,512]{4,3,2,1,0:T(8,128)(2,1)}, u32[]{:S(2)}, u32[]{:S(2)}) collective-permute-start(bf16[3,2,4,96,512]{4,3,2,1,0:T(8,128)(2,1)} %get-tuple-element.83.refs_0_.refs_2_), channel_id=1, source_target_pairs={{0,1},{1,0},{2,3},{3,2},{4,5},{5,4},{6,7},{7,6},{8,9},{9,8},{10,11... | collective-permute-start | bytes 7077896 | tf_op jit(solution)/shard_map/ppermute | solution.py:35
  131.7 11.6 %collective-permute-start.29 = (bf16[864,128]{1,0:T(8,128)(2,1)}, bf16[864,128]{1,0:T(8,128)(2,1)S(1)}, u32[]{:S(2)}, u32[]{:S(2)}) collective-permute-start(bf16[864,128]{1,0:T(8,128)(2,1)} %get-tuple-element.77), channel_id=1, source_target_pairs={{0,1},{1,0},{2,3},{3,2},{4,5},{5,4},{6,7},{7,6},{8,9},{9,8},{10,11... | collective-permute-start | bytes 663560 | tf_op jit(solution)/shard_map/ppermute | solution.py:35
  131.8 11.5 %collective-permute-start.30 = (bf16[864,128]{1,0:T(8,128)(2,1)}, bf16[864,128]{1,0:T(8,128)(2,1)}, u32[]{:S(2)}, u32[]{:S(2)}) collective-permute-start(bf16[864,128]{1,0:T(8,128)(2,1)} %get-tuple-element.78), channel_id=1, source_target_pairs={{0,2},{1,3},{2,0},{3,1},{4,6},{5,7},{6,4},{7,5},{8,10},{9,11},{10,... | collective-permute-start | bytes 663560 | tf_op jit(solution)/shard_map/ppermute | solution.py:35
  132.3 11.7 %collective-permute-start.31 = (bf16[864,128]{1,0:T(8,128)(2,1)}, bf16[864,128]{1,0:T(8,128)(2,1)}, u32[]{:S(2)}, u32[]{:S(2)}) collective-permute-start(bf16[864,128]{1,0:T(8,128)(2,1)} %get-tuple-element.79), channel_id=1, source_target_pairs={{0,3},{1,2},{2,1},{3,0},{4,7},{5,6},{6,5},{7,4},{8,11},{9,10},{10,... | collective-permute-start | bytes 663560 | tf_op jit(solution)/shard_map/ppermute | solution.py:35
  152.0 69.0 %all-to-all-start = ((bf16[4,2,2,96,768]{4,3,2,1,0:T(8,128)(2,1)}), bf16[4,2,2,96,768]{4,3,2,1,0:T(8,128)(2,1)S(1)}, u32[]{:S(2)}, u32[]{:S(2)}) async-start(bf16[4,2,2,96,768]{4,3,2,1,0:T(8,128)(2,1)} %row_dot.3.refs_12_), calls=%async_computation | async-start | bytes 4718592 | tf_op jit(solution)/shard_map/all_to_all | solution.py:86
  165.0 28.4 %collective-permute-start.34 = (bf16[1,1,4,96,1024]{4,3,2,1,0:T(8,128)(2,1)}, bf16[1,1,4,96,1024]{4,3,2,1,0:T(8,128)(2,1)S(1)}, u32[]{:S(2)}, u32[]{:S(2)}) collective-permute-start(bf16[1,1,4,96,1024]{4,3,2,1,0:T(8,128)(2,1)} %get-tuple-element.104), channel_id=1, source_target_pairs={{0,2},{1,3},{2,0},{3,1},{4,6},{5,7},{6,4},{7,5},{8,10},{9,11},{10,... | collective-permute-start | bytes 2359304 | tf_op jit(solution)/shard_map/ppermute | solution.py:35
  165.7 27.8 %collective-permute-start.35 = (bf16[1,1,4,96,1024]{4,3,2,1,0:T(8,128)(2,1)}, bf16[1,1,4,96,1024]{4,3,2,1,0:T(8,128)(2,1)}, u32[]{:S(2)}, u32[]{:S(2)}) collective-permute-start(bf16[1,1,4,96,1024]{4,3,2,1,0:T(8,128)(2,1)} %get-tuple-element.105), channel_id=1, source_target_pairs={{0,4},{4,0},{8,12},{12,8},{16,20},{20,16},{24,28},{28,24},{1,5},{5... | collective-permute-start | bytes 2359304 | tf_op jit(solution)/shard_map/ppermute | solution.py:40
  166.5 35.6 %collective-permute-start.36 = (bf16[1,1,4,96,1024]{4,3,2,1,0:T(8,128)(2,1)}, bf16[1,1,4,96,1024]{4,3,2,1,0:T(8,128)(2,1)}, u32[]{:S(2)}, u32[]{:S(2)}) collective-permute-start(bf16[1,1,4,96,1024]{4,3,2,1,0:T(8,128)(2,1)} %get-tuple-element.89.refs_11_), channel_id=1, source_target_pairs={{0,6},{1,7},{2,4},{3,5},{4,2},{5,3},{6,0},{7,1},{8,14},{9,15},{10,... | collective-permute-start | bytes 2359304 | tf_op jit(solution)/shard_map/ppermute | solution.py:46
  206.4 4.1 %collective-permute-start.37 = (bf16[2,512,768]{2,1,0:T(8,128)(2,1)}, bf16[2,512,768]{2,1,0:T(8,128)(2,1)}, u32[]{:S(2)}, u32[]{:S(2)}) collective-permute-start(bf16[2,512,768]{2,1,0:T(8,128)(2,1)} %spread.2.refs_4_), channel_id=1, source_target_pairs={{0,1},{1,0},{2,3},{3,2},{4,5},{5,4},{6,7},{7,6},{8,9},{9,8},{10,11... | collective-permute-start | bytes 4718600 | tf_op jit(solution)/shard_map/ppermute | solution.py:35
  206.4 18.7 %collective-permute-start.39 = (bf16[1,1,4,112,768]{4,3,2,1,0:T(8,128)(2,1)}, bf16[1,1,4,112,768]{4,3,2,1,0:T(8,128)(2,1)}, u32[]{:S(2)}, u32[]{:S(2)}) collective-permute-start(bf16[1,1,4,112,768]{4,3,2,1,0:T(8,128)(2,1)} %get-tuple-element.103.refs_0_), channel_id=1, source_target_pairs={{0,4},{4,0},{8,12},{12,8},{16,20},{20,16},{24,28},{28,24},{1,5},{5... | collective-permute-start | bytes 2064392 | tf_op jit(solution)/shard_map/ppermute | solution.py:40
  215.5 31.6 %collective-permute-start.38 = (bf16[512,768]{1,0:T(8,128)(2,1)}, bf16[512,768]{1,0:T(8,128)(2,1)S(1)}, u32[]{:S(2)}, u32[]{:S(2)}) collective-permute-start(bf16[512,768]{1,0:T(8,128)(2,1)} %get-tuple-element.110.refs_0_), channel_id=1, source_target_pairs={{0,2},{1,3},{2,0},{3,1},{4,6},{5,7},{6,4},{7,5},{8,10},{9,11},{10,... | collective-permute-start | bytes 2359304 | tf_op jit(solution)/shard_map/ppermute | solution.py:35
  216.7 16.6 %collective-permute-start.42 = (bf16[96,1024]{1,0:T(8,128)(2,1)}, bf16[96,1024]{1,0:T(8,128)(2,1)S(1)}, u32[]{:S(2)}, u32[]{:S(2)}) collective-permute-start(bf16[96,1024]{1,0:T(8,128)(2,1)} %get-tuple-element.115), channel_id=1, source_target_pairs={{0,24},{4,28},{8,16},{12,20},{16,8},{20,12},{24,0},{28,4},{1,25},{... | collective-permute-start | bytes 589832 | tf_op jit(solution)/shard_map/ppermute | solution.py:40
  220.2 21.0 %collective-permute-start.41 = (bf16[96,1024]{1,0:T(8,128)(2,1)}, bf16[96,1024]{1,0:T(8,128)(2,1)}, u32[]{:S(2)}, u32[]{:S(2)}) collective-permute-start(bf16[96,1024]{1,0:T(8,128)(2,1)} %get-tuple-element.114), channel_id=1, source_target_pairs={{0,16},{4,20},{8,24},{12,28},{16,0},{20,4},{24,8},{28,12},{1,17},{... | collective-permute-start | bytes 589832 | tf_op jit(solution)/shard_map/ppermute | solution.py:40
  220.2 21.0 %collective-permute-start.40 = (bf16[96,1024]{1,0:T(8,128)(2,1)}, bf16[96,1024]{1,0:T(8,128)(2,1)}, u32[]{:S(2)}, u32[]{:S(2)}) collective-permute-start(bf16[96,1024]{1,0:T(8,128)(2,1)} %get-tuple-element.113), channel_id=1, source_target_pairs={{0,8},{4,12},{8,0},{12,4},{16,24},{20,28},{24,16},{28,20},{1,9},{5... | collective-permute-start | bytes 589832 | tf_op jit(solution)/shard_map/ppermute | solution.py:40
  225.1 18.7 %collective-permute-start.43 = (bf16[2,96,768]{2,1,0:T(8,128)(2,1)}, bf16[2,96,768]{2,1,0:T(8,128)(2,1)}, u32[]{:S(2)}, u32[]{:S(2)}) collective-permute-start(bf16[2,96,768]{2,1,0:T(8,128)(2,1)} %get-tuple-element.112.refs_2_), channel_id=1, source_target_pairs={{0,2},{1,3},{2,0},{3,1},{4,6},{5,7},{6,4},{7,5},{8,10},{9,11},{10,... | collective-permute-start | bytes 884744 | tf_op jit(solution)/shard_map/ppermute | solution.py:35
  228.4 23.8 %all-to-all-start.1 = ((bf16[4,112,768]{2,1,0:T(8,128)(2,1)}), bf16[4,112,768]{2,1,0:T(8,128)(2,1)S(1)}, u32[]{:S(2)}, u32[]{:S(2)}) async-start(bf16[4,112,768]{2,1,0:T(8,128)(2,1)} %joined_sums.3.refs_0_), calls=%async_computation.1 | async-start | bytes 1376256 | tf_op jit(solution)/shard_map/all_to_all | solution.py:86
  245.6 5.4 %collective-permute-start.44 = (bf16[1,96,768]{2,1,0:T(8,128)(2,1)}, bf16[1,96,768]{2,1,0:T(8,128)(2,1)S(1)}, u32[]{:S(2)}, u32[]{:S(2)}) collective-permute-start(bf16[1,96,768]{2,1,0:T(8,128)(2,1)} %get-tuple-element.118), channel_id=1, source_target_pairs={{0,4},{4,0},{8,12},{12,8},{16,20},{20,16},{24,28},{28,24},{1,5},{5... | collective-permute-start | bytes 442376 | tf_op jit(solution)/shard_map/ppermute | solution.py:40
  (34 other events, 456.1 us)

commit v8 on v7

--- a/solution.py
+++ b/solution.py
@@ -1189,8 +1189,8 @@
     halved = members == 8
     if halved:
         queries = pack_queries(w_query, w_key, w_value)
-        own = pack_weights(w_up, w_out, w_down, queries)
         qkv_pieces = ring_pieces(queries)
+        own = pack_weights(w_up, w_out, w_down, qkv_pieces[2])
         beyond_own = swap(own, 2)
         shard = pair_weights(own, beyond_own, hidden, qkv_pieces[GATE:])
     else:

time: 255 us -> 259 us (1.016)
  waiting for transfers between devices: 55.3 us -> 59.2 us
    ppermute x1, waiting for transfers between devices: 8.7 us -> 0.01 us  [swap_both(): return lax.ppermute(array, axes, [(t, t ^ 6) for t in range(size)])]
    ppermute x6, waiting for transfers between devices: 10.5 us -> 18.9 us  [dp_swap(): return lax.ppermute(array, 'dp', [(t, t ^ bit) for t in range(size)])]
    ppermute x14, waiting for transfers between devices: 25.2 us -> 29.4 us  [ring_send(): lax.ppermute(array, 'dp', [(order[i], order[(i + step) % size]) for i in...]
  transfers between devices with their start and end apart: 47 -> 47, of which waited for: 17 -> 18; matrix products, arithmetic and copies ran while one was open for 4% -> 4% of each run, Pallas kernels for 36% -> 36%
where the time goes in v8:
time: 259 us; the launch traced here: 258 us
  Pallas kernels  132 us (51%)
  waiting for transfers between devices  59.2 us (23%)
  starting transfers between devices  46.6 us (18%)
  local copies, waits for them, and re-layouts  14.7 us (6%)
  other arithmetic  3.92 us (2%)
    pallas_call x1, Pallas kernels, layer_rows(): pl.pallas_call(partial(rows_kernel, [at for _, at in mixed], len(weights)...  31.9 us
    ppermute x14, waiting for transfers between devices, ring_send(): lax.ppermute(array, 'dp', [(order[i], order[(i + step) % size]) for i in...  29.4 us
    pallas_call x2, Pallas kernels, attend_backward(): pl.pallas_call(partial(attend_back_kernel, heads, chosen, pieces, own_blo...  27.9 us
    pallas_call x3, Pallas kernels, row_dot(): pl.pallas_call(kernel, grid=(lows[-1],), out_shape=[struct((far, *lead, p...  21.1 us
    ppermute x6, waiting for transfers between devices, dp_swap(): return lax.ppermute(array, 'dp', [(t, t ^ bit) for t in range(size)])  18.9 us
    ppermute x14, starting transfers between devices, ring_send(): lax.ppermute(array, 'dp', [(order[i], order[(i + step) % size]) for i in...  16.3 us
    pallas_call x2, Pallas kernels, attend_forward(): pl.pallas_call(partial(attend_kernel, heads, chosen, pieces, own_blocks),...  14.5 us
    ppermute x24, starting transfers between devices, swap(): return lax.ppermute(array, 'tensor', [(t, t ^ bit) for t in range(size)])  11.8 us
  transfers between devices with their start and end apart: 47, of which 18 were waited for; matrix products, arithmetic and copies ran while one was open for 4% of the time, Pallas kernels for 36%

profile of v8, /device:TPU:0, one launch (start us, length us, event | category | flops | bytes accessed | tf_op | source)
XLA Modules:
  0.0 257.8 jit_solution(2606538208738343211)
XLA Ops:
  0.7 1.5 pack_queries.1.refs_4_
  2.2 3.0 %collective-permute-start.1 = (bf16[96,768]{1,0:T(8,128)(2,1)}, bf16[96,768]{1,0:T(8,128)(2,1)S(1)}, u32[]{:S(2)}, u32[]{:S(2)}) collective-permute-start(bf16[96,768]{1,0:T(8,128)(2,1)} %pack_queries.1.refs_4_), channel_id=1, source_target_pairs={{0,4},{8,0},{16,8},{24,16},{28,24},{20,28},{12,20},{4,12},{1,5},{9... | collective-permute-start | bytes 442376 | tf_op jit(solution)/shard_map/ppermute | solution.py:64
  5.2 1.7 copy.38.down
  6.9 2.3 collective-permute-done.1._.refs_6_
  9.9 1.9 pack_weights.1.a
  11.8 1.7 collective-permute-start.2
  13.5 1.6 collective-permute-start.6
  15.5 3.1 %collective-permute-done.6.refs_7_ = bf16[96,768]{1,0:T(8,128)(2,1)S(1)} collective-permute-done((bf16[96,768]{1,0:T(8,128)(2,1)S(1)}, bf16[96,768]{1,0:T(8,128)(2,1)S(1)}, u32[]{:S(2)}, u32[]{:S(2)}) %collective-permute-start.6) | collective-permute-done | bytes 147488 | tf_op jit(solution)/shard_map/ppermute | solution.py:64
  18.6 1.6 collective-permute-start.8
  22.0 2.1 held.1
  25.4 1.5 collective-permute-start.9
  27.5 3.1 %collective-permute-done.9.refs_10_.refs_1_ = bf16[96,768]{1,0:T(8,128)(2,1)S(1)} collective-permute-done((bf16[96,768]{1,0:T(8,128)(2,1)S(1)}, bf16[96,768]{1,0:T(8,128)(2,1)S(1)}, u32[]{:S(2)}, u32[]{:S(2)}) %collective-permute-start.9) | collective-permute-done | bytes 147488 | tf_op jit(solution)/shard_map/ppermute | solution.py:64
  30.6 1.5 collective-permute-done.10.refs_11_.refs_2_
  32.8 2.0 pair_weights.1.refs_6_
  36.8 5.4 %collective-permute-done.3.refs_2_ = bf16[512,768]{1,0:T(8,128)(2,1)} collective-permute-done((bf16[512,768]{1,0:T(8,128)(2,1)}, bf16[512,768]{1,0:T(8,128)(2,1)}, u32[]{:S(2)}, u32[]{:S(2)}) %collective-permute-start.3) | collective-permute-done | bytes 786464 | tf_op jit(solution)/shard_map/ppermute | solution.py:35
  42.2 8.3 %collective-permute-done.14.refs_7_ = bf16[96,3584]{1,0:T(8,128)(2,1)S(1)} collective-permute-done((bf16[96,3584]{1,0:T(8,128)(2,1)}, bf16[96,3584]{1,0:T(8,128)(2,1)S(1)}, u32[]{:S(2)}, u32[]{:S(2)}) %collective-permute-start.14) | collective-permute-done | bytes 688160 | tf_op jit(solution)/shard_map/ppermute | solution.py:64
  54.0 1.5 block_tables.1
  56.6 7.2 %collective-permute-done.16.refs_9_ = bf16[96,3584]{1,0:T(8,128)(2,1)S(1)} collective-permute-done((bf16[96,3584]{1,0:T(8,128)(2,1)S(1)}, bf16[96,3584]{1,0:T(8,128)(2,1)S(1)}, u32[]{:S(2)}, u32[]{:S(2)}) %collective-permute-start.16) | collective-permute-done | bytes 688160 | tf_op jit(solution)/shard_map/ppermute | solution.py:64
  64.2 1.6 collective-permute-start.18
  66.2 8.3 %project_in.1 = (bf16[512,768]{1,0:T(8,128)(2,1)}, bf16[512,768]{1,0:T(8,128)(2,1)}, bf16[512,768]{1,0:T(8,128)(2,1)}, bf16[512,768]{1,0:T(8,128)(2,1)}, bf16[2,...) custom-call(bf16[512,768]{1,0:T(8,128)(2,1)} %refs_4_.1, ...), custom_call_target="tpu_custom_call" | custom-call | flops 4831838208 | bytes 25165824 | tf_op jit(solution)/shard_map/project_in/pallas_call | solution.py:1124
  74.5 7.2 %attend_forward.3 = (bf16[2,512,256]{2,1,0:T(8,128)(2,1)}, f32[512,128]{1,0:T(8,128)}, f32[512,128]{1,0:T(8,128)}) custom-call(s32[32,128]{1,0:T(8,128)} %get-tuple-element.68.table, bf16[512,768]{1,0:T(8,128)(2,1)} %get-tuple-element.69.refs_0_, bf16[512,768]{1,0:T(8,128)(2,1)} %get-tuple-element.70.refs_1_, bf16[512,768]{1,0:T(8,128)(2,1)} %get-tuple-element.71.refs_2_, ...), custom_call_target="tpu_custom_call" | custom-call | flops 4831838208 | bytes 16777216 | tf_op jit(solution)/shard_map/attend_forward/pallas_call | solution.py:278
  82.5 1.6 collective-permute-start.20
  84.0 7.2 %attend_forward.2 = (bf16[2,512,256]{2,1,0:T(8,128)(2,1)}, f32[512,128]{1,0:T(8,128)}, f32[512,128]{1,0:T(8,128)}) custom-call(s32[32,128]{1,0:T(8,128)} %get-tuple-element.68.table, bf16[512,768]{1,0:T(8,128)(2,1)} %get-tuple-element.69.refs_0_, bf16[512,768]{1,0:T(8,128)(2,1)} %get-tuple-element.70.refs_1_, bf16[512,768]{1,0:T(8,128)(2,1)} %get-tuple-element.71.refs_2_, ...), custom_call_target="tpu_custom_call" | custom-call | flops 4831838208 | bytes 16777216 | tf_op jit(solution)/shard_map/attend_forward/pallas_call | solution.py:278
  96.0 3.4 %collective-permute-done.20.refs_13_ = bf16[96,3584]{1,0:T(8,128)(2,1)} collective-permute-done((bf16[96,3584]{1,0:T(8,128)(2,1)}, bf16[96,3584]{1,0:T(8,128)(2,1)}, u32[]{:S(2)}, u32[]{:S(2)}) %collective-permute-start.20) | collective-permute-done | bytes 688160 | tf_op jit(solution)/shard_map/ppermute | solution.py:64
  102.9 31.9 %layer_rows.1 = (bf16[512,768]{1,0:T(8,128)(2,1)}, bf16[4,512,768]{2,1,0:T(8,128)(2,1)}, bf16[4,512,768]{2,1,0:T(8,128)(2,1)}, bf16[3,2,4,96,512]{4,3,2,1,0:T(8,...) custom-call(s32[1]{0:T(128)S(6)} %copy.40.length_ref.length, ...), custom_call_target="tpu_custom_call" | custom-call | flops 176160768 | bytes 393216 | tf_op jit(solution)/shard_map/layer_rows/pallas_call | solution.py:760
  135.6 1.5 collective-permute-start.30
  137.3 9.7 %attend_backward.2 = (bf16[512,256]{1,0:T(8,128)(2,1)}, f32[2048,256]{1,0:T(8,128)}, f32[2048,256]{1,0:T(8,128)}) custom-call(s32[32,128]{1,0:T(8,128)} %get-tuple-element.68.table, bf16[512,768]{1,0:T(8,128)(2,1)} %get-tuple-element.69.refs_0_, bf16[512,768]{1,0:T(8,128)(2,1)} %get-tuple-element.70.refs_1_, bf16[512,768]{1,0:T(8,128)(2,1)} %get-tuple-element.71.refs_2_, ...), custom_call_target="tpu_custom_call" | custom-call | flops 23592960 | bytes 196608 | tf_op jit(solution)/shard_map/attend_backward/pallas_call | solution.py:465
  147.8 1.7 copy-done
  149.4 6.4 %row_dot.3.refs_12_ = bf16[4,2,2,96,768]{4,3,2,1,0:T(8,128)(2,1)} custom-call(bf16[3,2,4,96,512]{4,3,2,1,0:T(8,128)(2,1)} %get-tuple-element.83.refs_0_.refs_2_, bf16[3,2,4,96,512]{4,3,2,1,0:T(8,128)(2,1)} %collective-permute-done.32.refs_1_.refs_3_, bf16[4,512,768]{2,1,0:T(8,128)(2,1)} %get-tuple-element.84.refs_2_.refs_3_.refs_4_.refs_5_, ...), custom_call_target="tpu_custom_call" | custom-call | flops 37748736 | bytes 131072 | tf_op jit(solution)/shard_map/row_dot/pallas_call | solution.py:875
  155.8 3.9 %all-to-all-start = ((bf16[4,2,2,96,768]{4,3,2,1,0:T(8,128)(2,1)}), bf16[4,2,2,96,768]{4,3,2,1,0:T(8,128)(2,1)S(1)}, u32[]{:S(2)}, u32[]{:S(2)}) async-start(bf16[4,2,2,96,768]{4,3,2,1,0:T(8,128)(2,1)} %row_dot.3.refs_12_), calls=%async_computation | async-start | bytes 4718592 | tf_op jit(solution)/shard_map/all_to_all | solution.py:86
  159.7 8.2 %row_dot.4 = (bf16[1,1,4,96,1024]{4,3,2,1,0:T(8,128)(2,1)}, bf16[1,1,4,96,1024]{4,3,2,1,0:T(8,128)(2,1)}, bf16[1,1,4,96,1024]{4,3,2,1,0:T(8,128)(2,1)}, bf16[1,1,4,96,1024]{4,3,2,1,0:T(8,128)(2,1)}) custom-call(bf16[3,2,4,96,512]{4,3,2,1,0:T(8,128)(2,1)} %get-tuple-element.83.refs_0_.refs_2_, ...), custom_call_target="tpu_custom_call" | custom-call | flops 50331648 | bytes 131072 | tf_op jit(solution)/shard_map/row_dot/pallas_call | solution.py:875
  167.9 1.6 collective-permute-start.34
  169.4 1.6 collective-permute-start.35
  171.4 18.2 %attend_backward.3 = (bf16[512,768]{1,0:T(8,128)(2,1)}, bf16[512,768]{1,0:T(8,128)(2,1)}, bf16[512,768]{1,0:T(8,128)(2,1)}, bf16[512,768]{1,0:T(8,128)(2,1)}, bf16[16,768]{1,0:T(8,128)(2,1)}) custom-call(s32[32,128]{1,0:T(8,128)} %get-tuple-element.68.table, bf16[512,768]{1,0:T(8,128)(2,1)} %get-tuple-element.69.refs_0_, ...), custom_call_target="tpu_custom_call" | custom-call | flops 70778880 | bytes 196608 | tf_op jit(solution)/shard_map/attend_backward/pallas_call | solution.py:465
  189.6 6.6 %row_dot.5 = (bf16[1,1,4,112,768]{4,3,2,1,0:T(8,128)(2,1)}, bf16[1,1,4,112,768]{4,3,2,1,0:T(8,128)(2,1)}) custom-call(bf16[1,2,4,96,512]{4,3,2,1,0:T(8,128)(2,1)} %bitcast.31, bf16[1,2,4,96,512]{4,3,2,1,0:T(8,128)(2,1)} %bitcast.32, bf16[1,2,4,96,512]{4,3,2,1,0:T(8,128)(2,1)} %bitcast.33, bf16[1,2,4,96,512]{4,3,2,1,0:T(8,128)(2,1)} %bitcast.34, ...), custom_call_target="tpu_custom_call" | custom-call | flops 37748736 | bytes 131072 | tf_op jit(solution)/shard_map/row_dot/pallas_call | solution.py:875
  196.2 9.7 %collective-permute-done.35.refs_2_ = bf16[1,1,4,96,1024]{4,3,2,1,0:T(8,128)(2,1)} collective-permute-done((bf16[1,1,4,96,1024]{4,3,2,1,0:T(8,128)(2,1)}, bf16[1,1,4,96,1024]{4,3,2,1,0:T(8,128)(2,1)}, u32[]{:S(2)}, u32[]{:S(2)}) %collective-permute-start.35) | collective-permute-done | bytes 786464 | tf_op jit(solution)/shard_map/ppermute | solution.py:40
  205.9 4.3 %spread.2.refs_4_ = bf16[2,512,768]{2,1,0:T(8,128)(2,1)} custom-call(bf16[512,768]{1,0:T(8,128)(2,1)} %get-tuple-element.96.first, bf16[512,768]{1,0:T(8,128)(2,1)} %get-tuple-element.97.second, bf16[768,768]{1,0:T(8,128)(2,1)} %get-tuple-element.95.w, bf16[1,1,4,112,768]{4,3,2,1,0:T(8,128)(2,1)} %get-tuple-element.103.refs_0_, ...), custom_call_target="tpu_custom_call" | custom-call | flops 18874368 | bytes 81920 | tf_op jit(solution)/shard_map/spread/pallas_call | solution.py:992
  210.2 1.6 collective-permute-start.39
  211.8 2.9 %joined_sums.2 = (bf16[96,1024]{1,0:T(8,128)(2,1)}, bf16[96,1024]{1,0:T(8,128)(2,1)}, bf16[96,1024]{1,0:T(8,128)(2,1)}, bf16[96,1024]{1,0:T(8,128)(2,1)}) custom-call(bf16[4,96,1024]{2,1,0:T(8,128)(2,1)} %bitcast.35, bf16[4,96,1024]{2,1,0:T(8,128)(2,1)} %bitcast.26, bf16[4,96,1024]{2,1,0:T(8,128)(2,1)} %bitcast.12.refs_2_, ...), custom_call_target="tpu_custom_call" | custom-call | flops 24576 | bytes 49152 | tf_op jit(solution)/shard_map/joined_sums/pallas_call | solution.py:962
  214.7 5.0 %spread.3 = (bf16[512,768]{1,0:T(8,128)(2,1)}, f32[512,768]{1,0:T(8,128)}) custom-call(bf16[512,768]{1,0:T(8,128)(2,1)} %get-tuple-element.93.first, bf16[512,768]{1,0:T(8,128)(2,1)} %get-tuple-element.94.second, bf16[768,768]{1,0:T(8,128)(2,1)} %get-tuple-element.95.w, bf16[2,512,768]{2,1,0:T(8,128)(2,1)} %collective-permute-done.37.refs_0_, ...), custom_call_target="tpu_custom_call" | custom-call | flops 18874368 | bytes 81920 | tf_op jit(solution)/shard_map/spread/pallas_call | solution.py:992
  220.3 3.5 %collective-permute-start.42 = (bf16[96,1024]{1,0:T(8,128)(2,1)}, bf16[96,1024]{1,0:T(8,128)(2,1)S(1)}, u32[]{:S(2)}, u32[]{:S(2)}) collective-permute-start(bf16[96,1024]{1,0:T(8,128)(2,1)} %get-tuple-element.115), channel_id=1, source_target_pairs={{0,24},{4,28},{8,16},{12,20},{16,8},{20,12},{24,0},{28,4},{1,25},{... | collective-permute-start | bytes 589832 | tf_op jit(solution)/shard_map/ppermute | solution.py:40
  226.0 2.7 %fold.1 = (bf16[2,96,768]{2,1,0:T(8,128)(2,1)}, bf16[2,96,768]{2,1,0:T(8,128)(2,1)}) custom-call(bf16[4,2,2,96,768]{4,3,2,1,0:T(8,128)(2,1)} %copy-done.1, bf16[512,768]{1,0:T(8,128)(2,1)} %get-tuple-element.110.refs_0_), custom_call_target="tpu_custom_call" | custom-call | flops 18432 | bytes 55296 | tf_op jit(solution)/shard_map/fold/pallas_call | solution.py:937
  230.2 2.3 joined_sums.3.refs_0_
  232.5 4.9 %all-to-all-start.1 = ((bf16[4,112,768]{2,1,0:T(8,128)(2,1)}), bf16[4,112,768]{2,1,0:T(8,128)(2,1)S(1)}, u32[]{:S(2)}, u32[]{:S(2)}) async-start(bf16[4,112,768]{2,1,0:T(8,128)(2,1)} %joined_sums.3.refs_0_), calls=%async_computation.1 | async-start | bytes 1376256 | tf_op jit(solution)/shard_map/all_to_all | solution.py:86
  237.4 6.8 %collective-permute-done.41 = bf16[96,1024]{1,0:T(8,128)(2,1)} collective-permute-done((bf16[96,1024]{1,0:T(8,128)(2,1)}, bf16[96,1024]{1,0:T(8,128)(2,1)}, u32[]{:S(2)}, u32[]{:S(2)}) %collective-permute-start.41) | collective-permute-done | bytes 196640 | tf_op jit(solution)/shard_map/ppermute | solution.py:40
  246.9 1.8 plus.1
  248.6 1.6 collective-permute-start.44
  251.6 2.4 collective-permute-done.44
  (162 shorter events, 35.1 us)
Async XLA Ops:
  2.2 7.1 %collective-permute-start.1 = (bf16[96,768]{1,0:T(8,128)(2,1)}, bf16[96,768]{1,0:T(8,128)(2,1)S(1)}, u32[]{:S(2)}, u32[]{:S(2)}) collective-permute-start(bf16[96,768]{1,0:T(8,128)(2,1)} %pack_queries.1.refs_4_), channel_id=1, source_target_pairs={{0,4},{8,0},{16,8},{24,16},{28,24},{20,28},{12,20},{4,12},{1,5},{9... | collective-permute-start | bytes 442376 | tf_op jit(solution)/shard_map/ppermute | solution.py:64
  5.2 8.3 %collective-permute-start.5 = (bf16[96,768]{1,0:T(8,128)(2,1)}, bf16[96,768]{1,0:T(8,128)(2,1)S(1)}, u32[]{:S(2)}, u32[]{:S(2)}) collective-permute-start(bf16[96,768]{1,0:T(8,128)(2,1)} %pack_queries.1.refs_4_), channel_id=1, source_target_pairs={{0,8},{8,16},{16,24},{24,28},{28,20},{20,12},{12,4},{4,0},{1,9},{9... | collective-permute-start | bytes 442376 | tf_op jit(solution)/shard_map/ppermute | solution.py:64
  11.8 9.5 %collective-permute-start.2 = (bf16[96,1792]{1,0:T(8,128)(2,1)}, bf16[96,1792]{1,0:T(8,128)(2,1)S(1)}, u32[]{:S(2)}, u32[]{:S(2)}) collective-permute-start(bf16[96,1792]{1,0:T(8,128)(2,1)} %pack_weights.1.a), channel_id=1, source_target_pairs={{0,2},{1,3},{2,0},{3,1},{4,6},{5,7},{6,4},{7,5},{8,10},{9,11},{10,... | collective-permute-start | bytes 1032200 | tf_op jit(solution)/shard_map/ppermute | solution.py:35
  13.5 5.1 %collective-permute-start.6 = (bf16[96,768]{1,0:T(8,128)(2,1)S(1)}, bf16[96,768]{1,0:T(8,128)(2,1)S(1)}, u32[]{:S(2)}, u32[]{:S(2)}) collective-permute-start(bf16[96,768]{1,0:T(8,128)(2,1)S(1)} %collective-permute-done.5.refs_5_), channel_id=1, source_target_pairs={{0,8},{8,16},{16,24},{24,28},{28,20},{20,12},{12,4},{4,0},{1,9},{9... | collective-permute-start | bytes 442376 | tf_op jit(solution)/shard_map/ppermute | solution.py:64
  15.1 10.4 %collective-permute-start.7 = (bf16[96,768]{1,0:T(8,128)(2,1)}, bf16[96,768]{1,0:T(8,128)(2,1)S(1)}, u32[]{:S(2)}, u32[]{:S(2)}) collective-permute-start(bf16[96,768]{1,0:T(8,128)(2,1)} %copy-done.20), channel_id=1, source_target_pairs={{0,4},{8,0},{16,8},{24,16},{28,24},{20,28},{12,20},{4,12},{1,5},{9... | collective-permute-start | bytes 442376 | tf_op jit(solution)/shard_map/ppermute | solution.py:64
  18.6 47.6 %copy-start.33 = (bf16[96,768]{1,0:T(8,128)(2,1)}, bf16[96,768]{1,0:T(8,128)(2,1)S(1)}, u32[]{:S(2)}) copy-start(bf16[96,768]{1,0:T(8,128)(2,1)S(1)} %collective-permute-done.6.refs_7_) | copy-start | bytes 442372
  18.6 8.4 %collective-permute-start.8 = (bf16[96,768]{1,0:T(8,128)(2,1)S(1)}, bf16[96,768]{1,0:T(8,128)(2,1)S(1)}, u32[]{:S(2)}, u32[]{:S(2)}) collective-permute-start(bf16[96,768]{1,0:T(8,128)(2,1)S(1)} %collective-permute-done.6.refs_7_), channel_id=1, source_target_pairs={{0,8},{8,16},{16,24},{24,28},{28,20},{20,12},{12,4},{4,0},{1,9},{9... | collective-permute-start | bytes 442376 | tf_op jit(solution)/shard_map/ppermute | solution.py:64
  24.1 18.1 %collective-permute-start.3 = (bf16[512,768]{1,0:T(8,128)(2,1)}, bf16[512,768]{1,0:T(8,128)(2,1)}, u32[]{:S(2)}, u32[]{:S(2)}) collective-permute-start(bf16[512,768]{1,0:T(8,128)(2,1)} %held.1), channel_id=1, source_target_pairs={{0,2},{1,3},{2,0},{3,1},{4,6},{5,7},{6,4},{7,5},{8,10},{9,11},{10,... | collective-permute-start | bytes 2359304 | tf_op jit(solution)/shard_map/ppermute | solution.py:35
  25.4 5.1 %collective-permute-start.9 = (bf16[96,768]{1,0:T(8,128)(2,1)S(1)}, bf16[96,768]{1,0:T(8,128)(2,1)S(1)}, u32[]{:S(2)}, u32[]{:S(2)}) collective-permute-start(bf16[96,768]{1,0:T(8,128)(2,1)S(1)} %collective-permute-done.7.refs_8_), channel_id=1, source_target_pairs={{0,4},{8,0},{16,8},{24,16},{28,24},{20,28},{12,20},{4,12},{1,5},{9... | collective-permute-start | bytes 442376 | tf_op jit(solution)/shard_map/ppermute | solution.py:64
  27.0 5.1 %collective-permute-start.10 = (bf16[96,768]{1,0:T(8,128)(2,1)S(1)}, bf16[96,768]{1,0:T(8,128)(2,1)S(1)}, u32[]{:S(2)}, u32[]{:S(2)}) collective-permute-start(bf16[96,768]{1,0:T(8,128)(2,1)S(1)} %collective-permute-done.8.refs_9_.refs_0_), channel_id=1, source_target_pairs={{0,8},{8,16},{16,24},{24,28},{28,20},{20,12},{12,4},{4,0},{1,9},{9... | collective-permute-start | bytes 442376 | tf_op jit(solution)/shard_map/ppermute | solution.py:64
  34.8 15.8 %collective-permute-start.14 = (bf16[96,3584]{1,0:T(8,128)(2,1)}, bf16[96,3584]{1,0:T(8,128)(2,1)S(1)}, u32[]{:S(2)}, u32[]{:S(2)}) collective-permute-start(bf16[96,3584]{1,0:T(8,128)(2,1)} %pair_weights.1.refs_6_), channel_id=1, source_target_pairs={{0,8},{8,16},{16,24},{24,28},{28,20},{20,12},{12,4},{4,0},{1,9},{9... | collective-permute-start | bytes 2064392 | tf_op jit(solution)/shard_map/ppermute | solution.py:64
  35.5 15.8 %collective-permute-start.15 = (bf16[96,3584]{1,0:T(8,128)(2,1)}, bf16[96,3584]{1,0:T(8,128)(2,1)S(1)}, u32[]{:S(2)}, u32[]{:S(2)}) collective-permute-start(bf16[96,3584]{1,0:T(8,128)(2,1)} %pair_weights.1.refs_6_), channel_id=1, source_target_pairs={{0,4},{8,0},{16,8},{24,16},{28,24},{20,28},{12,20},{4,12},{1,5},{9... | collective-permute-start | bytes 2064392 | tf_op jit(solution)/shard_map/ppermute | solution.py:64
  36.8 19.3 %collective-permute-start = (bf16[512,768]{1,0:T(8,128)(2,1)S(1)}, bf16[512,768]{1,0:T(8,128)(2,1)}, u32[]{:S(2)}, u32[]{:S(2)}) collective-permute-start(bf16[512,768]{1,0:T(8,128)(2,1)S(1)} %copy-done.4), channel_id=1, source_target_pairs={{0,1},{1,0},{2,3},{3,2},{4,5},{5,4},{6,7},{7,6},{8,9},{9,8},{10,11... | collective-permute-start | bytes 2359304 | tf_op jit(solution)/shard_map/ppermute | solution.py:35
  42.2 23.6 %collective-permute-start.4 = (bf16[512,768]{1,0:T(8,128)(2,1)}, bf16[512,768]{1,0:T(8,128)(2,1)}, u32[]{:S(2)}, u32[]{:S(2)}) collective-permute-start(bf16[512,768]{1,0:T(8,128)(2,1)} %collective-permute-done.3.refs_2_), channel_id=1, source_target_pairs={{0,1},{1,0},{2,3},{3,2},{4,5},{5,4},{6,7},{7,6},{8,9},{9,8},{10,11... | collective-permute-start | bytes 2359304 | tf_op jit(solution)/shard_map/ppermute | solution.py:35
  50.6 13.2 %collective-permute-start.16 = (bf16[96,3584]{1,0:T(8,128)(2,1)S(1)}, bf16[96,3584]{1,0:T(8,128)(2,1)S(1)}, u32[]{:S(2)}, u32[]{:S(2)}) collective-permute-start(bf16[96,3584]{1,0:T(8,128)(2,1)S(1)} %collective-permute-done.14.refs_7_), channel_id=1, source_target_pairs={{0,8},{8,16},{16,24},{24,28},{28,20},{20,12},{12,4},{4,0},{1,9},{9... | collective-permute-start | bytes 2064392 | tf_op jit(solution)/shard_map/ppermute | solution.py:64
  51.3 12.9 %collective-permute-start.17 = (bf16[96,3584]{1,0:T(8,128)(2,1)S(1)}, bf16[96,3584]{1,0:T(8,128)(2,1)}, u32[]{:S(2)}, u32[]{:S(2)}) collective-permute-start(bf16[96,3584]{1,0:T(8,128)(2,1)S(1)} %collective-permute-done.15.refs_8_), channel_id=1, source_target_pairs={{0,4},{8,0},{16,8},{24,16},{28,24},{20,28},{12,20},{4,12},{1,5},{9... | collective-permute-start | bytes 2064392 | tf_op jit(solution)/shard_map/ppermute | solution.py:64
  56.1 25.7 %collective-permute-start.21 = (bf16[96,3584]{1,0:T(8,128)(2,1)}, bf16[96,3584]{1,0:T(8,128)(2,1)}, u32[]{:S(2)}, u32[]{:S(2)}) collective-permute-start(bf16[96,3584]{1,0:T(8,128)(2,1)} %pair_weights.1.refs_6_), channel_id=1, source_target_pairs={{0,1},{1,0},{2,3},{3,2},{4,5},{5,4},{6,7},{7,6},{8,9},{9,8},{10,11... | collective-permute-start | bytes 2064392 | tf_op jit(solution)/shard_map/ppermute | solution.py:35
  56.1 36.2 %collective-permute-start.22 = (bf16[96,3584]{1,0:T(8,128)(2,1)S(1)}, bf16[96,3584]{1,0:T(8,128)(2,1)S(1)}, u32[]{:S(2)}, u32[]{:S(2)}) collective-permute-start(bf16[96,3584]{1,0:T(8,128)(2,1)S(1)} %collective-permute-done.14.refs_7_), channel_id=1, source_target_pairs={{0,1},{1,0},{2,3},{3,2},{4,5},{5,4},{6,7},{7,6},{8,9},{9,8},{10,11... | collective-permute-start | bytes 2064392 | tf_op jit(solution)/shard_map/ppermute | solution.py:35
  63.8 28.6 %collective-permute-start.23 = (bf16[96,3584]{1,0:T(8,128)(2,1)S(1)}, bf16[96,3584]{1,0:T(8,128)(2,1)}, u32[]{:S(2)}, u32[]{:S(2)}) collective-permute-start(bf16[96,3584]{1,0:T(8,128)(2,1)S(1)} %collective-permute-done.15.refs_8_), channel_id=1, source_target_pairs={{0,1},{1,0},{2,3},{3,2},{4,5},{5,4},{6,7},{7,6},{8,9},{9,8},{10,11... | collective-permute-start | bytes 2064392 | tf_op jit(solution)/shard_map/ppermute | solution.py:35
  64.2 18.3 %collective-permute-start.18 = (bf16[96,3584]{1,0:T(8,128)(2,1)S(1)}, bf16[96,3584]{1,0:T(8,128)(2,1)}, u32[]{:S(2)}, u32[]{:S(2)}) collective-permute-start(bf16[96,3584]{1,0:T(8,128)(2,1)S(1)} %collective-permute-done.16.refs_9_), channel_id=1, source_target_pairs={{0,8},{8,16},{16,24},{24,28},{28,20},{20,12},{12,4},{4,0},{1,9},{9... | collective-permute-start | bytes 2064392 | tf_op jit(solution)/shard_map/ppermute | solution.py:64
  65.8 29.7 %collective-permute-start.19 = (bf16[96,3584]{1,0:T(8,128)(2,1)}, bf16[96,3584]{1,0:T(8,128)(2,1)}, u32[]{:S(2)}, u32[]{:S(2)}) collective-permute-start(bf16[96,3584]{1,0:T(8,128)(2,1)} %collective-permute-done.17.refs_10_), channel_id=1, source_target_pairs={{0,4},{8,0},{16,8},{24,16},{28,24},{20,28},{12,20},{4,12},{1,5},{9... | collective-permute-start | bytes 2064392 | tf_op jit(solution)/shard_map/ppermute | solution.py:64
  81.9 13.7 %collective-permute-start.12 = (bf16[2,512,256]{2,1,0:T(8,128)(2,1)}, bf16[2,512,256]{2,1,0:T(8,128)(2,1)S(1)}, u32[]{:S(2)}, u32[]{:S(2)}) collective-permute-start(bf16[2,512,256]{2,1,0:T(8,128)(2,1)} %get-tuple-element.75), channel_id=1, source_target_pairs={{0,2},{1,3},{2,0},{3,1},{4,6},{5,7},{6,4},{7,5},{8,10},{9,11},{10,... | collective-permute-start | bytes 1572872 | tf_op jit(solution)/shard_map/ppermute | solution.py:35
  82.5 16.9 %collective-permute-start.20 = (bf16[96,3584]{1,0:T(8,128)(2,1)}, bf16[96,3584]{1,0:T(8,128)(2,1)}, u32[]{:S(2)}, u32[]{:S(2)}) collective-permute-start(bf16[96,3584]{1,0:T(8,128)(2,1)} %collective-permute-done.18.refs_11_), channel_id=1, source_target_pairs={{0,8},{8,16},{16,24},{24,28},{28,20},{20,12},{12,4},{4,0},{1,9},{9... | collective-permute-start | bytes 2064392 | tf_op jit(solution)/shard_map/ppermute | solution.py:64
  92.3 1.6 collective-permute-start.11
  92.4 7.7 %collective-permute-start.24 = (bf16[96,3584]{1,0:T(8,128)(2,1)S(1)}, bf16[96,3584]{1,0:T(8,128)(2,1)S(1)}, u32[]{:S(2)}, u32[]{:S(2)}) collective-permute-start(bf16[96,3584]{1,0:T(8,128)(2,1)S(1)} %collective-permute-done.16.refs_9_), channel_id=1, source_target_pairs={{0,1},{1,0},{2,3},{3,2},{4,5},{5,4},{6,7},{7,6},{8,9},{9,8},{10,11... | collective-permute-start | bytes 2064392 | tf_op jit(solution)/shard_map/ppermute | solution.py:35
  93.9 8.1 %collective-permute-start.25 = (bf16[96,3584]{1,0:T(8,128)(2,1)}, bf16[96,3584]{1,0:T(8,128)(2,1)S(1)}, u32[]{:S(2)}, u32[]{:S(2)}) collective-permute-start(bf16[96,3584]{1,0:T(8,128)(2,1)} %collective-permute-done.17.refs_10_), channel_id=1, source_target_pairs={{0,1},{1,0},{2,3},{3,2},{4,5},{5,4},{6,7},{7,6},{8,9},{9,8},{10,11... | collective-permute-start | bytes 2064392 | tf_op jit(solution)/shard_map/ppermute | solution.py:35
  95.5 6.6 %collective-permute-start.26 = (bf16[96,3584]{1,0:T(8,128)(2,1)}, bf16[96,3584]{1,0:T(8,128)(2,1)}, u32[]{:S(2)}, u32[]{:S(2)}) collective-permute-start(bf16[96,3584]{1,0:T(8,128)(2,1)} %collective-permute-done.18.refs_11_), channel_id=1, source_target_pairs={{0,1},{1,0},{2,3},{3,2},{4,5},{5,4},{6,7},{7,6},{8,9},{9,8},{10,11... | collective-permute-start | bytes 2064392 | tf_op jit(solution)/shard_map/ppermute | solution.py:35
  95.5 6.6 %collective-permute-start.27 = (bf16[96,3584]{1,0:T(8,128)(2,1)}, bf16[96,3584]{1,0:T(8,128)(2,1)}, u32[]{:S(2)}, u32[]{:S(2)}) collective-permute-start(bf16[96,3584]{1,0:T(8,128)(2,1)} %collective-permute-done.19.refs_12_), channel_id=1, source_target_pairs={{0,1},{1,0},{2,3},{3,2},{4,5},{5,4},{6,7},{7,6},{8,9},{9,8},{10,11... | collective-permute-start | bytes 2064392 | tf_op jit(solution)/shard_map/ppermute | solution.py:35
  99.4 2.7 %collective-permute-start.28 = (bf16[96,3584]{1,0:T(8,128)(2,1)}, bf16[96,3584]{1,0:T(8,128)(2,1)}, u32[]{:S(2)}, u32[]{:S(2)}) collective-permute-start(bf16[96,3584]{1,0:T(8,128)(2,1)} %collective-permute-done.20.refs_13_), channel_id=1, source_target_pairs={{0,1},{1,0},{2,3},{3,2},{4,5},{5,4},{6,7},{7,6},{8,9},{9,8},{10,11... | collective-permute-start | bytes 2064392 | tf_op jit(solution)/shard_map/ppermute | solution.py:35
  100.1 2.0 collective-permute-start.13
  134.8 12.9 %collective-permute-start.33 = (bf16[4,512,768]{2,1,0:T(8,128)(2,1)}, bf16[4,512,768]{2,1,0:T(8,128)(2,1)S(1)}, u32[]{:S(2)}, u32[]{:S(2)}) collective-permute-start(bf16[4,512,768]{2,1,0:T(8,128)(2,1)} %get-tuple-element.85), channel_id=1, source_target_pairs={{0,1},{1,0},{2,3},{3,2},{4,5},{5,4},{6,7},{7,6},{8,9},{9,8},{10,11... | collective-permute-start | bytes 9437192 | tf_op jit(solution)/shard_map/ppermute | solution.py:35
  135.1 12.7 %collective-permute-start.32 = (bf16[3,2,4,96,512]{4,3,2,1,0:T(8,128)(2,1)}, bf16[3,2,4,96,512]{4,3,2,1,0:T(8,128)(2,1)}, u32[]{:S(2)}, u32[]{:S(2)}) collective-permute-start(bf16[3,2,4,96,512]{4,3,2,1,0:T(8,128)(2,1)} %get-tuple-element.83.refs_0_.refs_2_), channel_id=1, source_target_pairs={{0,1},{1,0},{2,3},{3,2},{4,5},{5,4},{6,7},{7,6},{8,9},{9,8},{10,11... | collective-permute-start | bytes 7077896 | tf_op jit(solution)/shard_map/ppermute | solution.py:35
  135.4 11.6 %collective-permute-start.29 = (bf16[864,128]{1,0:T(8,128)(2,1)}, bf16[864,128]{1,0:T(8,128)(2,1)S(1)}, u32[]{:S(2)}, u32[]{:S(2)}) collective-permute-start(bf16[864,128]{1,0:T(8,128)(2,1)} %get-tuple-element.77), channel_id=1, source_target_pairs={{0,1},{1,0},{2,3},{3,2},{4,5},{5,4},{6,7},{7,6},{8,9},{9,8},{10,11... | collective-permute-start | bytes 663560 | tf_op jit(solution)/shard_map/ppermute | solution.py:35
  135.6 11.4 %collective-permute-start.30 = (bf16[864,128]{1,0:T(8,128)(2,1)}, bf16[864,128]{1,0:T(8,128)(2,1)}, u32[]{:S(2)}, u32[]{:S(2)}) collective-permute-start(bf16[864,128]{1,0:T(8,128)(2,1)} %get-tuple-element.78), channel_id=1, source_target_pairs={{0,2},{1,3},{2,0},{3,1},{4,6},{5,7},{6,4},{7,5},{8,10},{9,11},{10,... | collective-permute-start | bytes 663560 | tf_op jit(solution)/shard_map/ppermute | solution.py:35
  137.1 10.7 %collective-permute-start.31 = (bf16[864,128]{1,0:T(8,128)(2,1)}, bf16[864,128]{1,0:T(8,128)(2,1)}, u32[]{:S(2)}, u32[]{:S(2)}) collective-permute-start(bf16[864,128]{1,0:T(8,128)(2,1)} %get-tuple-element.79), channel_id=1, source_target_pairs={{0,3},{1,2},{2,1},{3,0},{4,7},{5,6},{6,5},{7,4},{8,11},{9,10},{10,... | collective-permute-start | bytes 663560 | tf_op jit(solution)/shard_map/ppermute | solution.py:35
  155.8 68.9 %all-to-all-start = ((bf16[4,2,2,96,768]{4,3,2,1,0:T(8,128)(2,1)}), bf16[4,2,2,96,768]{4,3,2,1,0:T(8,128)(2,1)S(1)}, u32[]{:S(2)}, u32[]{:S(2)}) async-start(bf16[4,2,2,96,768]{4,3,2,1,0:T(8,128)(2,1)} %row_dot.3.refs_12_), calls=%async_computation | async-start | bytes 4718592 | tf_op jit(solution)/shard_map/all_to_all | solution.py:86
  167.9 28.3 %collective-permute-start.34 = (bf16[1,1,4,96,1024]{4,3,2,1,0:T(8,128)(2,1)}, bf16[1,1,4,96,1024]{4,3,2,1,0:T(8,128)(2,1)S(1)}, u32[]{:S(2)}, u32[]{:S(2)}) collective-permute-start(bf16[1,1,4,96,1024]{4,3,2,1,0:T(8,128)(2,1)} %get-tuple-element.104), channel_id=1, source_target_pairs={{0,2},{1,3},{2,0},{3,1},{4,6},{5,7},{6,4},{7,5},{8,10},{9,11},{10,... | collective-permute-start | bytes 2359304 | tf_op jit(solution)/shard_map/ppermute | solution.py:35
  169.4 36.5 %collective-permute-start.35 = (bf16[1,1,4,96,1024]{4,3,2,1,0:T(8,128)(2,1)}, bf16[1,1,4,96,1024]{4,3,2,1,0:T(8,128)(2,1)}, u32[]{:S(2)}, u32[]{:S(2)}) collective-permute-start(bf16[1,1,4,96,1024]{4,3,2,1,0:T(8,128)(2,1)} %get-tuple-element.105), channel_id=1, source_target_pairs={{0,4},{4,0},{8,12},{12,8},{16,20},{20,16},{24,28},{28,24},{1,5},{5... | collective-permute-start | bytes 2359304 | tf_op jit(solution)/shard_map/ppermute | solution.py:40
  171.0 34.9 %collective-permute-start.36 = (bf16[1,1,4,96,1024]{4,3,2,1,0:T(8,128)(2,1)}, bf16[1,1,4,96,1024]{4,3,2,1,0:T(8,128)(2,1)}, u32[]{:S(2)}, u32[]{:S(2)}) collective-permute-start(bf16[1,1,4,96,1024]{4,3,2,1,0:T(8,128)(2,1)} %get-tuple-element.89.refs_11_), channel_id=1, source_target_pairs={{0,6},{1,7},{2,4},{3,5},{4,2},{5,3},{6,0},{7,1},{8,14},{9,15},{10,... | collective-permute-start | bytes 2359304 | tf_op jit(solution)/shard_map/ppermute | solution.py:46
  210.2 4.5 %collective-permute-start.37 = (bf16[2,512,768]{2,1,0:T(8,128)(2,1)}, bf16[2,512,768]{2,1,0:T(8,128)(2,1)}, u32[]{:S(2)}, u32[]{:S(2)}) collective-permute-start(bf16[2,512,768]{2,1,0:T(8,128)(2,1)} %spread.2.refs_4_), channel_id=1, source_target_pairs={{0,1},{1,0},{2,3},{3,2},{4,5},{5,4},{6,7},{7,6},{8,9},{9,8},{10,11... | collective-permute-start | bytes 4718600 | tf_op jit(solution)/shard_map/ppermute | solution.py:35
  210.2 18.5 %collective-permute-start.39 = (bf16[1,1,4,112,768]{4,3,2,1,0:T(8,128)(2,1)}, bf16[1,1,4,112,768]{4,3,2,1,0:T(8,128)(2,1)}, u32[]{:S(2)}, u32[]{:S(2)}) collective-permute-start(bf16[1,1,4,112,768]{4,3,2,1,0:T(8,128)(2,1)} %get-tuple-element.103.refs_0_), channel_id=1, source_target_pairs={{0,4},{4,0},{8,12},{12,8},{16,20},{20,16},{24,28},{28,24},{1,5},{5... | collective-permute-start | bytes 2064392 | tf_op jit(solution)/shard_map/ppermute | solution.py:40
  219.7 30.6 %collective-permute-start.38 = (bf16[512,768]{1,0:T(8,128)(2,1)}, bf16[512,768]{1,0:T(8,128)(2,1)S(1)}, u32[]{:S(2)}, u32[]{:S(2)}) collective-permute-start(bf16[512,768]{1,0:T(8,128)(2,1)} %get-tuple-element.110.refs_0_), channel_id=1, source_target_pairs={{0,2},{1,3},{2,0},{3,1},{4,6},{5,7},{6,4},{7,5},{8,10},{9,11},{10,... | collective-permute-start | bytes 2359304 | tf_op jit(solution)/shard_map/ppermute | solution.py:35
  220.3 17.2 %collective-permute-start.42 = (bf16[96,1024]{1,0:T(8,128)(2,1)}, bf16[96,1024]{1,0:T(8,128)(2,1)S(1)}, u32[]{:S(2)}, u32[]{:S(2)}) collective-permute-start(bf16[96,1024]{1,0:T(8,128)(2,1)} %get-tuple-element.115), channel_id=1, source_target_pairs={{0,24},{4,28},{8,16},{12,20},{16,8},{20,12},{24,0},{28,4},{1,25},{... | collective-permute-start | bytes 589832 | tf_op jit(solution)/shard_map/ppermute | solution.py:40
  223.8 20.5 %collective-permute-start.41 = (bf16[96,1024]{1,0:T(8,128)(2,1)}, bf16[96,1024]{1,0:T(8,128)(2,1)}, u32[]{:S(2)}, u32[]{:S(2)}) collective-permute-start(bf16[96,1024]{1,0:T(8,128)(2,1)} %get-tuple-element.114), channel_id=1, source_target_pairs={{0,16},{4,20},{8,24},{12,28},{16,0},{20,4},{24,8},{28,12},{1,17},{... | collective-permute-start | bytes 589832 | tf_op jit(solution)/shard_map/ppermute | solution.py:40
  223.8 20.5 %collective-permute-start.40 = (bf16[96,1024]{1,0:T(8,128)(2,1)}, bf16[96,1024]{1,0:T(8,128)(2,1)}, u32[]{:S(2)}, u32[]{:S(2)}) collective-permute-start(bf16[96,1024]{1,0:T(8,128)(2,1)} %get-tuple-element.113), channel_id=1, source_target_pairs={{0,8},{4,12},{8,0},{12,4},{16,24},{20,28},{24,16},{28,20},{1,9},{5... | collective-permute-start | bytes 589832 | tf_op jit(solution)/shard_map/ppermute | solution.py:40
  228.7 18.1 %collective-permute-start.43 = (bf16[2,96,768]{2,1,0:T(8,128)(2,1)}, bf16[2,96,768]{2,1,0:T(8,128)(2,1)}, u32[]{:S(2)}, u32[]{:S(2)}) collective-permute-start(bf16[2,96,768]{2,1,0:T(8,128)(2,1)} %get-tuple-element.112.refs_2_), channel_id=1, source_target_pairs={{0,2},{1,3},{2,0},{3,1},{4,6},{5,7},{6,4},{7,5},{8,10},{9,11},{10,... | collective-permute-start | bytes 884744 | tf_op jit(solution)/shard_map/ppermute | solution.py:35
  232.5 23.2 %all-to-all-start.1 = ((bf16[4,112,768]{2,1,0:T(8,128)(2,1)}), bf16[4,112,768]{2,1,0:T(8,128)(2,1)S(1)}, u32[]{:S(2)}, u32[]{:S(2)}) async-start(bf16[4,112,768]{2,1,0:T(8,128)(2,1)} %joined_sums.3.refs_0_), calls=%async_computation.1 | async-start | bytes 1376256 | tf_op jit(solution)/shard_map/all_to_all | solution.py:86
  248.6 5.4 %collective-permute-start.44 = (bf16[1,96,768]{2,1,0:T(8,128)(2,1)}, bf16[1,96,768]{2,1,0:T(8,128)(2,1)S(1)}, u32[]{:S(2)}, u32[]{:S(2)}) collective-permute-start(bf16[1,96,768]{2,1,0:T(8,128)(2,1)} %get-tuple-element.118), channel_id=1, source_target_pairs={{0,4},{4,0},{8,12},{12,8},{16,20},{20,16},{24,28},{28,24},{1,5},{5... | collective-permute-start | bytes 442376 | tf_op jit(solution)/shard_map/ppermute | solution.py:40
  (34 other events, 462.8 us)

commit v9 on v7

--- a/solution.py
+++ b/solution.py
@@ -682,7 +682,7 @@
         z = (scaled_buf[at, :] * g1[...] + c1[...]) + wide_buf[at, :] + b_down[...]
         scaled, inv_std = row_stats(z)
         x_buf[at, :] = (scaled * g2[...] + c2[...]).astype(bf16)
-        row = lax.broadcasted_iota(jnp.int32, (tile, D), 0) + i * tile
+        row = lax.broadcasted_iota(jnp.int32, (tile, 1), 0) + i * tile
         upstream = jnp.where(row < live, g_buf[at, :].astype(f32), 0.0)
         grad = norm_backward(upstream, scaled, inv_std, g2[...]).astype(bf16)
         g_buf[at, :] = grad

time: 255 us -> 255 us (level)
  no operation moved by 1% of the time
where the time goes in v9:
time: 255 us; the launch traced here: 254 us
  Pallas kernels  132 us (52%)
  waiting for transfers between devices  55.3 us (22%)
  starting transfers between devices  46.8 us (18%)
  local copies, waits for them, and re-layouts  14.7 us (6%)
  other arithmetic  3.92 us (2%)
    pallas_call x1, Pallas kernels, layer_rows(): pl.pallas_call(partial(rows_kernel, [at for _, at in mixed], len(weights)...  31.9 us
    pallas_call x2, Pallas kernels, attend_backward(): pl.pallas_call(partial(attend_back_kernel, heads, chosen, pieces, own_blo...  27.9 us
    ppermute x14, waiting for transfers between devices, ring_send(): lax.ppermute(array, 'dp', [(order[i], order[(i + step) % size]) for i in...  25.2 us
    pallas_call x3, Pallas kernels, row_dot(): pl.pallas_call(kernel, grid=(lows[-1],), out_shape=[struct((far, *lead, p...  21.1 us
    ppermute x14, starting transfers between devices, ring_send(): lax.ppermute(array, 'dp', [(order[i], order[(i + step) % size]) for i in...  16.9 us
    pallas_call x2, Pallas kernels, attend_forward(): pl.pallas_call(partial(attend_kernel, heads, chosen, pieces, own_blocks),...  14.5 us
    ppermute x6, waiting for transfers between devices, dp_swap(): return lax.ppermute(array, 'dp', [(t, t ^ bit) for t in range(size)])  10.5 us
    ppermute x24, waiting for transfers between devices, swap(): return lax.ppermute(array, 'tensor', [(t, t ^ bit) for t in range(size)])  10.4 us
  transfers between devices with their start and end apart: 47, of which 17 were waited for; matrix products, arithmetic and copies ran while one was open for 4% of the time, Pallas kernels for 36%

profile of v9, /device:TPU:0, one launch (start us, length us, event | category | flops | bytes accessed | tf_op | source)
XLA Modules:
  0.0 254.2 jit_solution(16904627301860499770)
XLA Ops:
  0.7 1.5 pack_queries.1._.refs_4_
  2.2 3.0 %collective-permute-start.4 = (bf16[96,768]{1,0:T(8,128)(2,1)}, bf16[96,768]{1,0:T(8,128)(2,1)S(1)}, u32[]{:S(2)}, u32[]{:S(2)}) collective-permute-start(bf16[96,768]{1,0:T(8,128)(2,1)} %pack_queries.1._.refs_4_), channel_id=1, source_target_pairs={{0,8},{8,16},{16,24},{24,28},{28,20},{20,12},{12,4},{4,0},{1,9},{9... | collective-permute-start | bytes 442376 | tf_op jit(solution)/shard_map/ppermute | solution.py:64
  5.2 1.7 copy.38.down
  6.9 1.9 pack_weights.1.a
  8.9 1.5 collective-permute-start.1
  10.8 1.6 collective-permute-start.6
  12.4 3.3 %collective-permute-done.5.refs_6_ = bf16[96,768]{1,0:T(8,128)(2,1)S(1)} collective-permute-done((bf16[96,768]{1,0:T(8,128)(2,1)}, bf16[96,768]{1,0:T(8,128)(2,1)S(1)}, u32[]{:S(2)}, u32[]{:S(2)}) %collective-permute-start.5) | collective-permute-done | bytes 147488 | tf_op jit(solution)/shard_map/ppermute | solution.py:64
  16.2 1.6 collective-permute-start.8
  19.4 2.1 held.1
  21.4 1.5 collective-permute-start.2
  23.4 1.6 collective-permute-start.10
  25.0 3.1 %collective-permute-done.9.refs_10_.refs_1_ = bf16[96,768]{1,0:T(8,128)(2,1)S(1)} collective-permute-done((bf16[96,768]{1,0:T(8,128)(2,1)S(1)}, bf16[96,768]{1,0:T(8,128)(2,1)S(1)}, u32[]{:S(2)}, u32[]{:S(2)}) %collective-permute-start.9) | collective-permute-done | bytes 147488 | tf_op jit(solution)/shard_map/ppermute | solution.py:64
  29.4 2.0 pair_weights.1.refs_6_
  31.4 1.6 collective-permute-start.14
  33.0 6.9 %collective-permute-done.2.refs_2_ = bf16[512,768]{1,0:T(8,128)(2,1)} collective-permute-done((bf16[512,768]{1,0:T(8,128)(2,1)}, bf16[512,768]{1,0:T(8,128)(2,1)}, u32[]{:S(2)}, u32[]{:S(2)}) %collective-permute-start.2) | collective-permute-done | bytes 786464 | tf_op jit(solution)/shard_map/ppermute | solution.py:35
  40.4 6.8 %collective-permute-done.14.refs_7_ = bf16[96,3584]{1,0:T(8,128)(2,1)S(1)} collective-permute-done((bf16[96,3584]{1,0:T(8,128)(2,1)}, bf16[96,3584]{1,0:T(8,128)(2,1)S(1)}, u32[]{:S(2)}, u32[]{:S(2)}) %collective-permute-start.14) | collective-permute-done | bytes 688160 | tf_op jit(solution)/shard_map/ppermute | solution.py:64
  47.2 1.6 collective-permute-start.16
  50.1 1.5 block_tables.1
  52.8 5.2 %collective-permute-done.15.refs_8_ = bf16[96,3584]{1,0:T(8,128)(2,1)S(1)} collective-permute-done((bf16[96,3584]{1,0:T(8,128)(2,1)}, bf16[96,3584]{1,0:T(8,128)(2,1)S(1)}, u32[]{:S(2)}, u32[]{:S(2)}) %collective-permute-start.15) | collective-permute-done | bytes 688160 | tf_op jit(solution)/shard_map/ppermute | solution.py:64
  58.5 2.8 %collective-permute-done.16.refs_9_ = bf16[96,3584]{1,0:T(8,128)(2,1)S(1)} collective-permute-done((bf16[96,3584]{1,0:T(8,128)(2,1)S(1)}, bf16[96,3584]{1,0:T(8,128)(2,1)S(1)}, u32[]{:S(2)}, u32[]{:S(2)}) %collective-permute-start.16) | collective-permute-done | bytes 688160 | tf_op jit(solution)/shard_map/ppermute | solution.py:64
  61.3 1.6 collective-permute-start.18
  62.9 8.3 %project_in.1 = (bf16[512,768]{1,0:T(8,128)(2,1)}, bf16[512,768]{1,0:T(8,128)(2,1)}, bf16[512,768]{1,0:T(8,128)(2,1)}, bf16[512,768]{1,0:T(8,128)(2,1)}, bf16[2,...) custom-call(bf16[512,768]{1,0:T(8,128)(2,1)} %refs_4_.1, ...), custom_call_target="tpu_custom_call" | custom-call | flops 4831838208 | bytes 25165824 | tf_op jit(solution)/shard_map/project_in/pallas_call | solution.py:1124
  71.2 7.2 %attend_forward.3 = (bf16[2,512,256]{2,1,0:T(8,128)(2,1)}, f32[512,128]{1,0:T(8,128)}, f32[512,128]{1,0:T(8,128)}) custom-call(s32[32,128]{1,0:T(8,128)} %get-tuple-element.68.table, bf16[512,768]{1,0:T(8,128)(2,1)} %get-tuple-element.69.refs_0_, bf16[512,768]{1,0:T(8,128)(2,1)} %get-tuple-element.70.refs_1_, bf16[512,768]{1,0:T(8,128)(2,1)} %get-tuple-element.71.refs_2_, ...), custom_call_target="tpu_custom_call" | custom-call | flops 4831838208 | bytes 16777216 | tf_op jit(solution)/shard_map/attend_forward/pallas_call | solution.py:278
  79.2 1.6 collective-permute-start.20
  80.7 7.2 %attend_forward.2 = (bf16[2,512,256]{2,1,0:T(8,128)(2,1)}, f32[512,128]{1,0:T(8,128)}, f32[512,128]{1,0:T(8,128)}) custom-call(s32[32,128]{1,0:T(8,128)} %get-tuple-element.68.table, bf16[512,768]{1,0:T(8,128)(2,1)} %get-tuple-element.69.refs_0_, bf16[512,768]{1,0:T(8,128)(2,1)} %get-tuple-element.70.refs_1_, bf16[512,768]{1,0:T(8,128)(2,1)} %get-tuple-element.71.refs_2_, ...), custom_call_target="tpu_custom_call" | custom-call | flops 4831838208 | bytes 16777216 | tf_op jit(solution)/shard_map/attend_forward/pallas_call | solution.py:278
  91.4 3.3 %collective-permute-done.19.refs_12_ = bf16[96,3584]{1,0:T(8,128)(2,1)} collective-permute-done((bf16[96,3584]{1,0:T(8,128)(2,1)}, bf16[96,3584]{1,0:T(8,128)(2,1)}, u32[]{:S(2)}, u32[]{:S(2)}) %collective-permute-start.19) | collective-permute-done | bytes 688160 | tf_op jit(solution)/shard_map/ppermute | solution.py:64
  99.1 31.9 %layer_rows.1 = (bf16[512,768]{1,0:T(8,128)(2,1)}, bf16[4,512,768]{2,1,0:T(8,128)(2,1)}, bf16[4,512,768]{2,1,0:T(8,128)(2,1)}, bf16[3,2,4,96,512]{4,3,2,1,0:T(8,...) custom-call(s32[1]{0:T(128)S(6)} %copy.40.length_ref.length, ...), custom_call_target="tpu_custom_call" | custom-call | flops 176160768 | bytes 393216 | tf_op jit(solution)/shard_map/layer_rows/pallas_call | solution.py:760
  133.5 9.7 %attend_backward.2 = (bf16[512,256]{1,0:T(8,128)(2,1)}, f32[2048,256]{1,0:T(8,128)}, f32[2048,256]{1,0:T(8,128)}) custom-call(s32[32,128]{1,0:T(8,128)} %get-tuple-element.68.table, bf16[512,768]{1,0:T(8,128)(2,1)} %get-tuple-element.69.refs_0_, bf16[512,768]{1,0:T(8,128)(2,1)} %get-tuple-element.70.refs_1_, bf16[512,768]{1,0:T(8,128)(2,1)} %get-tuple-element.71.refs_2_, ...), custom_call_target="tpu_custom_call" | custom-call | flops 23592960 | bytes 196608 | tf_op jit(solution)/shard_map/attend_backward/pallas_call | solution.py:465
  144.0 1.7 copy-done
  145.7 6.4 %row_dot.3.refs_12_ = bf16[4,2,2,96,768]{4,3,2,1,0:T(8,128)(2,1)} custom-call(bf16[3,2,4,96,512]{4,3,2,1,0:T(8,128)(2,1)} %get-tuple-element.83.refs_0_.refs_2_, bf16[3,2,4,96,512]{4,3,2,1,0:T(8,128)(2,1)} %collective-permute-done.32.refs_1_.refs_3_, bf16[4,512,768]{2,1,0:T(8,128)(2,1)} %get-tuple-element.84.refs_2_.refs_3_.refs_4_.refs_5_, ...), custom_call_target="tpu_custom_call" | custom-call | flops 37748736 | bytes 131072 | tf_op jit(solution)/shard_map/row_dot/pallas_call | solution.py:875
  152.0 4.8 %all-to-all-start = ((bf16[4,2,2,96,768]{4,3,2,1,0:T(8,128)(2,1)}), bf16[4,2,2,96,768]{4,3,2,1,0:T(8,128)(2,1)S(1)}, u32[]{:S(2)}, u32[]{:S(2)}) async-start(bf16[4,2,2,96,768]{4,3,2,1,0:T(8,128)(2,1)} %row_dot.3.refs_12_), calls=%async_computation | async-start | bytes 4718592 | tf_op jit(solution)/shard_map/all_to_all | solution.py:86
  156.9 8.2 %row_dot.4 = (bf16[1,1,4,96,1024]{4,3,2,1,0:T(8,128)(2,1)}, bf16[1,1,4,96,1024]{4,3,2,1,0:T(8,128)(2,1)}, bf16[1,1,4,96,1024]{4,3,2,1,0:T(8,128)(2,1)}, bf16[1,1,4,96,1024]{4,3,2,1,0:T(8,128)(2,1)}) custom-call(bf16[3,2,4,96,512]{4,3,2,1,0:T(8,128)(2,1)} %get-tuple-element.83.refs_0_.refs_2_, ...), custom_call_target="tpu_custom_call" | custom-call | flops 50331648 | bytes 131072 | tf_op jit(solution)/shard_map/row_dot/pallas_call | solution.py:875
  166.5 2.1 collective-permute-start.36
  168.6 18.2 %attend_backward.3 = (bf16[512,768]{1,0:T(8,128)(2,1)}, bf16[512,768]{1,0:T(8,128)(2,1)}, bf16[512,768]{1,0:T(8,128)(2,1)}, bf16[512,768]{1,0:T(8,128)(2,1)}, bf16[16,768]{1,0:T(8,128)(2,1)}) custom-call(s32[32,128]{1,0:T(8,128)} %get-tuple-element.68.table, bf16[512,768]{1,0:T(8,128)(2,1)} %get-tuple-element.69.refs_0_, ...), custom_call_target="tpu_custom_call" | custom-call | flops 70778880 | bytes 196608 | tf_op jit(solution)/shard_map/attend_backward/pallas_call | solution.py:465
  186.8 6.6 %row_dot.5 = (bf16[1,1,4,112,768]{4,3,2,1,0:T(8,128)(2,1)}, bf16[1,1,4,112,768]{4,3,2,1,0:T(8,128)(2,1)}) custom-call(bf16[1,2,4,96,512]{4,3,2,1,0:T(8,128)(2,1)} %bitcast.31, bf16[1,2,4,96,512]{4,3,2,1,0:T(8,128)(2,1)} %bitcast.32, bf16[1,2,4,96,512]{4,3,2,1,0:T(8,128)(2,1)} %bitcast.33, bf16[1,2,4,96,512]{4,3,2,1,0:T(8,128)(2,1)} %bitcast.34, ...), custom_call_target="tpu_custom_call" | custom-call | flops 37748736 | bytes 131072 | tf_op jit(solution)/shard_map/row_dot/pallas_call | solution.py:875
  193.4 8.7 %collective-permute-done.36.refs_3_ = bf16[1,1,4,96,1024]{4,3,2,1,0:T(8,128)(2,1)} collective-permute-done((bf16[1,1,4,96,1024]{4,3,2,1,0:T(8,128)(2,1)}, bf16[1,1,4,96,1024]{4,3,2,1,0:T(8,128)(2,1)}, u32[]{:S(2)}, u32[]{:S(2)}) %collective-permute-start.36) | collective-permute-done | bytes 786464 | tf_op jit(solution)/shard_map/ppermute | solution.py:46
  202.1 4.3 %spread.2.refs_4_ = bf16[2,512,768]{2,1,0:T(8,128)(2,1)} custom-call(bf16[512,768]{1,0:T(8,128)(2,1)} %get-tuple-element.96.first, bf16[512,768]{1,0:T(8,128)(2,1)} %get-tuple-element.97.second, bf16[768,768]{1,0:T(8,128)(2,1)} %get-tuple-element.95.w, bf16[1,1,4,112,768]{4,3,2,1,0:T(8,128)(2,1)} %get-tuple-element.103.refs_0_, ...), custom_call_target="tpu_custom_call" | custom-call | flops 18874368 | bytes 81920 | tf_op jit(solution)/shard_map/spread/pallas_call | solution.py:992
  207.6 2.9 %joined_sums.2 = (bf16[96,1024]{1,0:T(8,128)(2,1)}, bf16[96,1024]{1,0:T(8,128)(2,1)}, bf16[96,1024]{1,0:T(8,128)(2,1)}, bf16[96,1024]{1,0:T(8,128)(2,1)}) custom-call(bf16[4,96,1024]{2,1,0:T(8,128)(2,1)} %bitcast.35, bf16[4,96,1024]{2,1,0:T(8,128)(2,1)} %bitcast.26, bf16[4,96,1024]{2,1,0:T(8,128)(2,1)} %bitcast.12.refs_2_, ...), custom_call_target="tpu_custom_call" | custom-call | flops 24576 | bytes 49152 | tf_op jit(solution)/shard_map/joined_sums/pallas_call | solution.py:962
  210.5 5.0 %spread.3 = (bf16[512,768]{1,0:T(8,128)(2,1)}, f32[512,768]{1,0:T(8,128)}) custom-call(bf16[512,768]{1,0:T(8,128)(2,1)} %get-tuple-element.93.first, bf16[512,768]{1,0:T(8,128)(2,1)} %get-tuple-element.94.second, bf16[768,768]{1,0:T(8,128)(2,1)} %get-tuple-element.95.w, bf16[2,512,768]{2,1,0:T(8,128)(2,1)} %collective-permute-done.37.refs_0_, ...), custom_call_target="tpu_custom_call" | custom-call | flops 18874368 | bytes 81920 | tf_op jit(solution)/shard_map/spread/pallas_call | solution.py:992
  216.7 3.5 %collective-permute-start.42 = (bf16[96,1024]{1,0:T(8,128)(2,1)}, bf16[96,1024]{1,0:T(8,128)(2,1)S(1)}, u32[]{:S(2)}, u32[]{:S(2)}) collective-permute-start(bf16[96,1024]{1,0:T(8,128)(2,1)} %get-tuple-element.115), channel_id=1, source_target_pairs={{0,24},{4,28},{8,16},{12,20},{16,8},{20,12},{24,0},{28,4},{1,25},{... | collective-permute-start | bytes 589832 | tf_op jit(solution)/shard_map/ppermute | solution.py:40
  221.1 1.4 copy-done.1
  222.5 2.7 %fold.1 = (bf16[2,96,768]{2,1,0:T(8,128)(2,1)}, bf16[2,96,768]{2,1,0:T(8,128)(2,1)}) custom-call(bf16[4,2,2,96,768]{4,3,2,1,0:T(8,128)(2,1)} %copy-done.1, bf16[512,768]{1,0:T(8,128)(2,1)} %get-tuple-element.110.refs_0_), custom_call_target="tpu_custom_call" | custom-call | flops 18432 | bytes 55296 | tf_op jit(solution)/shard_map/fold/pallas_call | solution.py:937
  226.0 2.3 joined_sums.3.refs_0_
  228.4 4.9 %all-to-all-start.1 = ((bf16[4,112,768]{2,1,0:T(8,128)(2,1)}), bf16[4,112,768]{2,1,0:T(8,128)(2,1)S(1)}, u32[]{:S(2)}, u32[]{:S(2)}) async-start(bf16[4,112,768]{2,1,0:T(8,128)(2,1)} %joined_sums.3.refs_0_), calls=%async_computation.1 | async-start | bytes 1376256 | tf_op jit(solution)/shard_map/all_to_all | solution.py:86
  233.3 7.9 %collective-permute-done.41 = bf16[96,1024]{1,0:T(8,128)(2,1)} collective-permute-done((bf16[96,1024]{1,0:T(8,128)(2,1)}, bf16[96,1024]{1,0:T(8,128)(2,1)}, u32[]{:S(2)}, u32[]{:S(2)}) %collective-permute-start.41) | collective-permute-done | bytes 196640 | tf_op jit(solution)/shard_map/ppermute | solution.py:40
  243.8 1.8 plus.1
  245.6 1.5 collective-permute-start.44
  248.4 2.6 %collective-permute-done.44 = bf16[1,96,768]{2,1,0:T(8,128)(2,1)S(1)} collective-permute-done((bf16[1,96,768]{2,1,0:T(8,128)(2,1)}, bf16[1,96,768]{2,1,0:T(8,128)(2,1)S(1)}, u32[]{:S(2)}, u32[]{:S(2)}) %collective-permute-start.44) | collective-permute-done | bytes 147488 | tf_op jit(solution)/shard_map/ppermute | solution.py:40
  (162 shorter events, 31.5 us)
Async XLA Ops:
  2.2 8.6 %collective-permute-start.4 = (bf16[96,768]{1,0:T(8,128)(2,1)}, bf16[96,768]{1,0:T(8,128)(2,1)S(1)}, u32[]{:S(2)}, u32[]{:S(2)}) collective-permute-start(bf16[96,768]{1,0:T(8,128)(2,1)} %pack_queries.1._.refs_4_), channel_id=1, source_target_pairs={{0,8},{8,16},{16,24},{24,28},{28,20},{20,12},{12,4},{4,0},{1,9},{9... | collective-permute-start | bytes 442376 | tf_op jit(solution)/shard_map/ppermute | solution.py:64
  8.9 9.7 %collective-permute-start.1 = (bf16[96,1792]{1,0:T(8,128)(2,1)}, bf16[96,1792]{1,0:T(8,128)(2,1)S(1)}, u32[]{:S(2)}, u32[]{:S(2)}) collective-permute-start(bf16[96,1792]{1,0:T(8,128)(2,1)} %pack_weights.1.a), channel_id=1, source_target_pairs={{0,2},{1,3},{2,0},{3,1},{4,6},{5,7},{6,4},{7,5},{8,10},{9,11},{10,... | collective-permute-start | bytes 1032200 | tf_op jit(solution)/shard_map/ppermute | solution.py:35
  10.4 5.4 %collective-permute-start.5 = (bf16[96,768]{1,0:T(8,128)(2,1)}, bf16[96,768]{1,0:T(8,128)(2,1)S(1)}, u32[]{:S(2)}, u32[]{:S(2)}) collective-permute-start(bf16[96,768]{1,0:T(8,128)(2,1)} %pack_queries.1._.refs_4_), channel_id=1, source_target_pairs={{0,4},{8,0},{16,8},{24,16},{28,24},{20,28},{12,20},{4,12},{1,5},{9... | collective-permute-start | bytes 442376 | tf_op jit(solution)/shard_map/ppermute | solution.py:64
  10.8 52.0 %copy-start.31 = (bf16[96,768]{1,0:T(8,128)(2,1)}, bf16[96,768]{1,0:T(8,128)(2,1)S(1)}, u32[]{:S(2)}) copy-start(bf16[96,768]{1,0:T(8,128)(2,1)S(1)} %collective-permute-done.4.refs_5_) | copy-start | bytes 442372
  10.8 5.4 %collective-permute-start.6 = (bf16[96,768]{1,0:T(8,128)(2,1)S(1)}, bf16[96,768]{1,0:T(8,128)(2,1)S(1)}, u32[]{:S(2)}, u32[]{:S(2)}) collective-permute-start(bf16[96,768]{1,0:T(8,128)(2,1)S(1)} %collective-permute-done.4.refs_5_), channel_id=1, source_target_pairs={{0,8},{8,16},{16,24},{24,28},{28,20},{20,12},{12,4},{4,0},{1,9},{9... | collective-permute-start | bytes 442376 | tf_op jit(solution)/shard_map/ppermute | solution.py:64
  15.7 7.2 %collective-permute-start.7 = (bf16[96,768]{1,0:T(8,128)(2,1)S(1)}, bf16[96,768]{1,0:T(8,128)(2,1)S(1)}, u32[]{:S(2)}, u32[]{:S(2)}) collective-permute-start(bf16[96,768]{1,0:T(8,128)(2,1)S(1)} %collective-permute-done.5.refs_6_), channel_id=1, source_target_pairs={{0,4},{8,0},{16,8},{24,16},{28,24},{20,28},{12,20},{4,12},{1,5},{9... | collective-permute-start | bytes 442376 | tf_op jit(solution)/shard_map/ppermute | solution.py:64
  16.2 7.2 %collective-permute-start.8 = (bf16[96,768]{1,0:T(8,128)(2,1)S(1)}, bf16[96,768]{1,0:T(8,128)(2,1)S(1)}, u32[]{:S(2)}, u32[]{:S(2)}) collective-permute-start(bf16[96,768]{1,0:T(8,128)(2,1)S(1)} %collective-permute-done.6.refs_7_), channel_id=1, source_target_pairs={{0,8},{8,16},{16,24},{24,28},{28,20},{20,12},{12,4},{4,0},{1,9},{9... | collective-permute-start | bytes 442376 | tf_op jit(solution)/shard_map/ppermute | solution.py:64
  21.4 18.4 %collective-permute-start.2 = (bf16[512,768]{1,0:T(8,128)(2,1)}, bf16[512,768]{1,0:T(8,128)(2,1)}, u32[]{:S(2)}, u32[]{:S(2)}) collective-permute-start(bf16[512,768]{1,0:T(8,128)(2,1)} %held.1), channel_id=1, source_target_pairs={{0,2},{1,3},{2,0},{3,1},{4,6},{5,7},{6,4},{7,5},{8,10},{9,11},{10,... | collective-permute-start | bytes 2359304 | tf_op jit(solution)/shard_map/ppermute | solution.py:35
  22.9 5.1 %collective-permute-start.9 = (bf16[96,768]{1,0:T(8,128)(2,1)S(1)}, bf16[96,768]{1,0:T(8,128)(2,1)S(1)}, u32[]{:S(2)}, u32[]{:S(2)}) collective-permute-start(bf16[96,768]{1,0:T(8,128)(2,1)S(1)} %collective-permute-done.7.refs_8_), channel_id=1, source_target_pairs={{0,4},{8,0},{16,8},{24,16},{28,24},{20,28},{12,20},{4,12},{1,5},{9... | collective-permute-start | bytes 442376 | tf_op jit(solution)/shard_map/ppermute | solution.py:64
  23.4 5.1 %collective-permute-start.10 = (bf16[96,768]{1,0:T(8,128)(2,1)S(1)}, bf16[96,768]{1,0:T(8,128)(2,1)S(1)}, u32[]{:S(2)}, u32[]{:S(2)}) collective-permute-start(bf16[96,768]{1,0:T(8,128)(2,1)S(1)} %collective-permute-done.8.refs_9_.refs_0_), channel_id=1, source_target_pairs={{0,8},{8,16},{16,24},{24,28},{28,20},{20,12},{12,4},{4,0},{1,9},{9... | collective-permute-start | bytes 442376 | tf_op jit(solution)/shard_map/ppermute | solution.py:64
  31.4 15.8 %collective-permute-start.14 = (bf16[96,3584]{1,0:T(8,128)(2,1)}, bf16[96,3584]{1,0:T(8,128)(2,1)S(1)}, u32[]{:S(2)}, u32[]{:S(2)}) collective-permute-start(bf16[96,3584]{1,0:T(8,128)(2,1)} %pair_weights.1.refs_6_), channel_id=1, source_target_pairs={{0,8},{8,16},{16,24},{24,28},{28,20},{20,12},{12,4},{4,0},{1,9},{9... | collective-permute-start | bytes 2064392 | tf_op jit(solution)/shard_map/ppermute | solution.py:64
  33.0 19.3 %collective-permute-start = (bf16[512,768]{1,0:T(8,128)(2,1)S(1)}, bf16[512,768]{1,0:T(8,128)(2,1)}, u32[]{:S(2)}, u32[]{:S(2)}) collective-permute-start(bf16[512,768]{1,0:T(8,128)(2,1)S(1)} %copy-done.4), channel_id=1, source_target_pairs={{0,1},{1,0},{2,3},{3,2},{4,5},{5,4},{6,7},{7,6},{8,9},{9,8},{10,11... | collective-permute-start | bytes 2359304 | tf_op jit(solution)/shard_map/ppermute | solution.py:35
  39.9 18.6 %collective-permute-start.3 = (bf16[512,768]{1,0:T(8,128)(2,1)}, bf16[512,768]{1,0:T(8,128)(2,1)}, u32[]{:S(2)}, u32[]{:S(2)}) collective-permute-start(bf16[512,768]{1,0:T(8,128)(2,1)} %collective-permute-done.2.refs_2_), channel_id=1, source_target_pairs={{0,1},{1,0},{2,3},{3,2},{4,5},{5,4},{6,7},{7,6},{8,9},{9,8},{10,11... | collective-permute-start | bytes 2359304 | tf_op jit(solution)/shard_map/ppermute | solution.py:35
  39.9 18.1 %collective-permute-start.15 = (bf16[96,3584]{1,0:T(8,128)(2,1)}, bf16[96,3584]{1,0:T(8,128)(2,1)S(1)}, u32[]{:S(2)}, u32[]{:S(2)}) collective-permute-start(bf16[96,3584]{1,0:T(8,128)(2,1)} %pair_weights.1.refs_6_), channel_id=1, source_target_pairs={{0,4},{8,0},{16,8},{24,16},{28,24},{20,28},{12,20},{4,12},{1,5},{9... | collective-permute-start | bytes 2064392 | tf_op jit(solution)/shard_map/ppermute | solution.py:64
  47.2 14.1 %collective-permute-start.16 = (bf16[96,3584]{1,0:T(8,128)(2,1)S(1)}, bf16[96,3584]{1,0:T(8,128)(2,1)S(1)}, u32[]{:S(2)}, u32[]{:S(2)}) collective-permute-start(bf16[96,3584]{1,0:T(8,128)(2,1)S(1)} %collective-permute-done.14.refs_7_), channel_id=1, source_target_pairs={{0,8},{8,16},{16,24},{24,28},{28,20},{20,12},{12,4},{4,0},{1,9},{9... | collective-permute-start | bytes 2064392 | tf_op jit(solution)/shard_map/ppermute | solution.py:64
  52.3 26.2 %collective-permute-start.21 = (bf16[96,3584]{1,0:T(8,128)(2,1)}, bf16[96,3584]{1,0:T(8,128)(2,1)}, u32[]{:S(2)}, u32[]{:S(2)}) collective-permute-start(bf16[96,3584]{1,0:T(8,128)(2,1)} %pair_weights.1.refs_6_), channel_id=1, source_target_pairs={{0,1},{1,0},{2,3},{3,2},{4,5},{5,4},{6,7},{7,6},{8,9},{9,8},{10,11... | collective-permute-start | bytes 2064392 | tf_op jit(solution)/shard_map/ppermute | solution.py:35
  52.3 36.7 %collective-permute-start.22 = (bf16[96,3584]{1,0:T(8,128)(2,1)S(1)}, bf16[96,3584]{1,0:T(8,128)(2,1)S(1)}, u32[]{:S(2)}, u32[]{:S(2)}) collective-permute-start(bf16[96,3584]{1,0:T(8,128)(2,1)S(1)} %collective-permute-done.14.refs_7_), channel_id=1, source_target_pairs={{0,1},{1,0},{2,3},{3,2},{4,5},{5,4},{6,7},{7,6},{8,9},{9,8},{10,11... | collective-permute-start | bytes 2064392 | tf_op jit(solution)/shard_map/ppermute | solution.py:35
  57.9 20.8 %collective-permute-start.17 = (bf16[96,3584]{1,0:T(8,128)(2,1)S(1)}, bf16[96,3584]{1,0:T(8,128)(2,1)}, u32[]{:S(2)}, u32[]{:S(2)}) collective-permute-start(bf16[96,3584]{1,0:T(8,128)(2,1)S(1)} %collective-permute-done.15.refs_8_), channel_id=1, source_target_pairs={{0,4},{8,0},{16,8},{24,16},{28,24},{20,28},{12,20},{4,12},{1,5},{9... | collective-permute-start | bytes 2064392 | tf_op jit(solution)/shard_map/ppermute | solution.py:64
  58.5 30.6 %collective-permute-start.23 = (bf16[96,3584]{1,0:T(8,128)(2,1)S(1)}, bf16[96,3584]{1,0:T(8,128)(2,1)}, u32[]{:S(2)}, u32[]{:S(2)}) collective-permute-start(bf16[96,3584]{1,0:T(8,128)(2,1)S(1)} %collective-permute-done.15.refs_8_), channel_id=1, source_target_pairs={{0,1},{1,0},{2,3},{3,2},{4,5},{5,4},{6,7},{7,6},{8,9},{9,8},{10,11... | collective-permute-start | bytes 2064392 | tf_op jit(solution)/shard_map/ppermute | solution.py:35
  61.3 17.9 %collective-permute-start.18 = (bf16[96,3584]{1,0:T(8,128)(2,1)S(1)}, bf16[96,3584]{1,0:T(8,128)(2,1)}, u32[]{:S(2)}, u32[]{:S(2)}) collective-permute-start(bf16[96,3584]{1,0:T(8,128)(2,1)S(1)} %collective-permute-done.16.refs_9_), channel_id=1, source_target_pairs={{0,8},{8,16},{16,24},{24,28},{28,20},{20,12},{12,4},{4,0},{1,9},{9... | collective-permute-start | bytes 2064392 | tf_op jit(solution)/shard_map/ppermute | solution.py:64
  78.5 12.2 %collective-permute-start.12 = (bf16[2,512,256]{2,1,0:T(8,128)(2,1)}, bf16[2,512,256]{2,1,0:T(8,128)(2,1)S(1)}, u32[]{:S(2)}, u32[]{:S(2)}) collective-permute-start(bf16[2,512,256]{2,1,0:T(8,128)(2,1)} %get-tuple-element.75), channel_id=1, source_target_pairs={{0,2},{1,3},{2,0},{3,1},{4,6},{5,7},{6,4},{7,5},{8,10},{9,11},{10,... | collective-permute-start | bytes 1572872 | tf_op jit(solution)/shard_map/ppermute | solution.py:35
  78.7 16.0 %collective-permute-start.19 = (bf16[96,3584]{1,0:T(8,128)(2,1)}, bf16[96,3584]{1,0:T(8,128)(2,1)}, u32[]{:S(2)}, u32[]{:S(2)}) collective-permute-start(bf16[96,3584]{1,0:T(8,128)(2,1)} %collective-permute-done.17.refs_10_), channel_id=1, source_target_pairs={{0,4},{8,0},{16,8},{24,16},{28,24},{20,28},{12,20},{4,12},{1,5},{9... | collective-permute-start | bytes 2064392 | tf_op jit(solution)/shard_map/ppermute | solution.py:64
  79.2 15.8 %collective-permute-start.20 = (bf16[96,3584]{1,0:T(8,128)(2,1)}, bf16[96,3584]{1,0:T(8,128)(2,1)}, u32[]{:S(2)}, u32[]{:S(2)}) collective-permute-start(bf16[96,3584]{1,0:T(8,128)(2,1)} %collective-permute-done.18.refs_11_), channel_id=1, source_target_pairs={{0,8},{8,16},{16,24},{24,28},{28,20},{20,12},{12,4},{4,0},{1,9},{9... | collective-permute-start | bytes 2064392 | tf_op jit(solution)/shard_map/ppermute | solution.py:64
  89.0 1.6 collective-permute-start.11
  89.1 6.9 %collective-permute-start.24 = (bf16[96,3584]{1,0:T(8,128)(2,1)S(1)}, bf16[96,3584]{1,0:T(8,128)(2,1)S(1)}, u32[]{:S(2)}, u32[]{:S(2)}) collective-permute-start(bf16[96,3584]{1,0:T(8,128)(2,1)S(1)} %collective-permute-done.16.refs_9_), channel_id=1, source_target_pairs={{0,1},{1,0},{2,3},{3,2},{4,5},{5,4},{6,7},{7,6},{8,9},{9,8},{10,11... | collective-permute-start | bytes 2064392 | tf_op jit(solution)/shard_map/ppermute | solution.py:35
  90.6 7.0 %collective-permute-start.25 = (bf16[96,3584]{1,0:T(8,128)(2,1)}, bf16[96,3584]{1,0:T(8,128)(2,1)S(1)}, u32[]{:S(2)}, u32[]{:S(2)}) collective-permute-start(bf16[96,3584]{1,0:T(8,128)(2,1)} %collective-permute-done.17.refs_10_), channel_id=1, source_target_pairs={{0,1},{1,0},{2,3},{3,2},{4,5},{5,4},{6,7},{7,6},{8,9},{9,8},{10,11... | collective-permute-start | bytes 2064392 | tf_op jit(solution)/shard_map/ppermute | solution.py:35
  91.3 7.2 %collective-permute-start.26 = (bf16[96,3584]{1,0:T(8,128)(2,1)}, bf16[96,3584]{1,0:T(8,128)(2,1)}, u32[]{:S(2)}, u32[]{:S(2)}) collective-permute-start(bf16[96,3584]{1,0:T(8,128)(2,1)} %collective-permute-done.18.refs_11_), channel_id=1, source_target_pairs={{0,1},{1,0},{2,3},{3,2},{4,5},{5,4},{6,7},{7,6},{8,9},{9,8},{10,11... | collective-permute-start | bytes 2064392 | tf_op jit(solution)/shard_map/ppermute | solution.py:35
  94.7 3.7 %collective-permute-start.27 = (bf16[96,3584]{1,0:T(8,128)(2,1)}, bf16[96,3584]{1,0:T(8,128)(2,1)}, u32[]{:S(2)}, u32[]{:S(2)}) collective-permute-start(bf16[96,3584]{1,0:T(8,128)(2,1)} %collective-permute-done.19.refs_12_), channel_id=1, source_target_pairs={{0,1},{1,0},{2,3},{3,2},{4,5},{5,4},{6,7},{7,6},{8,9},{9,8},{10,11... | collective-permute-start | bytes 2064392 | tf_op jit(solution)/shard_map/ppermute | solution.py:35
  95.0 3.5 %collective-permute-start.28 = (bf16[96,3584]{1,0:T(8,128)(2,1)}, bf16[96,3584]{1,0:T(8,128)(2,1)}, u32[]{:S(2)}, u32[]{:S(2)}) collective-permute-start(bf16[96,3584]{1,0:T(8,128)(2,1)} %collective-permute-done.20.refs_13_), channel_id=1, source_target_pairs={{0,1},{1,0},{2,3},{3,2},{4,5},{5,4},{6,7},{7,6},{8,9},{9,8},{10,11... | collective-permute-start | bytes 2064392 | tf_op jit(solution)/shard_map/ppermute | solution.py:35
  96.0 2.5 collective-permute-start.13
  131.1 12.9 %collective-permute-start.33 = (bf16[4,512,768]{2,1,0:T(8,128)(2,1)}, bf16[4,512,768]{2,1,0:T(8,128)(2,1)S(1)}, u32[]{:S(2)}, u32[]{:S(2)}) collective-permute-start(bf16[4,512,768]{2,1,0:T(8,128)(2,1)} %get-tuple-element.85), channel_id=1, source_target_pairs={{0,1},{1,0},{2,3},{3,2},{4,5},{5,4},{6,7},{7,6},{8,9},{9,8},{10,11... | collective-permute-start | bytes 9437192 | tf_op jit(solution)/shard_map/ppermute | solution.py:35
  131.3 12.7 %collective-permute-start.32 = (bf16[3,2,4,96,512]{4,3,2,1,0:T(8,128)(2,1)}, bf16[3,2,4,96,512]{4,3,2,1,0:T(8,128)(2,1)}, u32[]{:S(2)}, u32[]{:S(2)}) collective-permute-start(bf16[3,2,4,96,512]{4,3,2,1,0:T(8,128)(2,1)} %get-tuple-element.83.refs_0_.refs_2_), channel_id=1, source_target_pairs={{0,1},{1,0},{2,3},{3,2},{4,5},{5,4},{6,7},{7,6},{8,9},{9,8},{10,11... | collective-permute-start | bytes 7077896 | tf_op jit(solution)/shard_map/ppermute | solution.py:35
  131.7 11.6 %collective-permute-start.29 = (bf16[864,128]{1,0:T(8,128)(2,1)}, bf16[864,128]{1,0:T(8,128)(2,1)S(1)}, u32[]{:S(2)}, u32[]{:S(2)}) collective-permute-start(bf16[864,128]{1,0:T(8,128)(2,1)} %get-tuple-element.77), channel_id=1, source_target_pairs={{0,1},{1,0},{2,3},{3,2},{4,5},{5,4},{6,7},{7,6},{8,9},{9,8},{10,11... | collective-permute-start | bytes 663560 | tf_op jit(solution)/shard_map/ppermute | solution.py:35
  131.8 11.5 %collective-permute-start.30 = (bf16[864,128]{1,0:T(8,128)(2,1)}, bf16[864,128]{1,0:T(8,128)(2,1)}, u32[]{:S(2)}, u32[]{:S(2)}) collective-permute-start(bf16[864,128]{1,0:T(8,128)(2,1)} %get-tuple-element.78), channel_id=1, source_target_pairs={{0,2},{1,3},{2,0},{3,1},{4,6},{5,7},{6,4},{7,5},{8,10},{9,11},{10,... | collective-permute-start | bytes 663560 | tf_op jit(solution)/shard_map/ppermute | solution.py:35
  132.3 11.7 %collective-permute-start.31 = (bf16[864,128]{1,0:T(8,128)(2,1)}, bf16[864,128]{1,0:T(8,128)(2,1)}, u32[]{:S(2)}, u32[]{:S(2)}) collective-permute-start(bf16[864,128]{1,0:T(8,128)(2,1)} %get-tuple-element.79), channel_id=1, source_target_pairs={{0,3},{1,2},{2,1},{3,0},{4,7},{5,6},{6,5},{7,4},{8,11},{9,10},{10,... | collective-permute-start | bytes 663560 | tf_op jit(solution)/shard_map/ppermute | solution.py:35
  152.0 69.0 %all-to-all-start = ((bf16[4,2,2,96,768]{4,3,2,1,0:T(8,128)(2,1)}), bf16[4,2,2,96,768]{4,3,2,1,0:T(8,128)(2,1)S(1)}, u32[]{:S(2)}, u32[]{:S(2)}) async-start(bf16[4,2,2,96,768]{4,3,2,1,0:T(8,128)(2,1)} %row_dot.3.refs_12_), calls=%async_computation | async-start | bytes 4718592 | tf_op jit(solution)/shard_map/all_to_all | solution.py:86
  165.0 28.4 %collective-permute-start.34 = (bf16[1,1,4,96,1024]{4,3,2,1,0:T(8,128)(2,1)}, bf16[1,1,4,96,1024]{4,3,2,1,0:T(8,128)(2,1)S(1)}, u32[]{:S(2)}, u32[]{:S(2)}) collective-permute-start(bf16[1,1,4,96,1024]{4,3,2,1,0:T(8,128)(2,1)} %get-tuple-element.104), channel_id=1, source_target_pairs={{0,2},{1,3},{2,0},{3,1},{4,6},{5,7},{6,4},{7,5},{8,10},{9,11},{10,... | collective-permute-start | bytes 2359304 | tf_op jit(solution)/shard_map/ppermute | solution.py:35
  165.7 27.8 %collective-permute-start.35 = (bf16[1,1,4,96,1024]{4,3,2,1,0:T(8,128)(2,1)}, bf16[1,1,4,96,1024]{4,3,2,1,0:T(8,128)(2,1)}, u32[]{:S(2)}, u32[]{:S(2)}) collective-permute-start(bf16[1,1,4,96,1024]{4,3,2,1,0:T(8,128)(2,1)} %get-tuple-element.105), channel_id=1, source_target_pairs={{0,4},{4,0},{8,12},{12,8},{16,20},{20,16},{24,28},{28,24},{1,5},{5... | collective-permute-start | bytes 2359304 | tf_op jit(solution)/shard_map/ppermute | solution.py:40
  166.5 35.6 %collective-permute-start.36 = (bf16[1,1,4,96,1024]{4,3,2,1,0:T(8,128)(2,1)}, bf16[1,1,4,96,1024]{4,3,2,1,0:T(8,128)(2,1)}, u32[]{:S(2)}, u32[]{:S(2)}) collective-permute-start(bf16[1,1,4,96,1024]{4,3,2,1,0:T(8,128)(2,1)} %get-tuple-element.89.refs_11_), channel_id=1, source_target_pairs={{0,6},{1,7},{2,4},{3,5},{4,2},{5,3},{6,0},{7,1},{8,14},{9,15},{10,... | collective-permute-start | bytes 2359304 | tf_op jit(solution)/shard_map/ppermute | solution.py:46
  206.4 4.1 %collective-permute-start.37 = (bf16[2,512,768]{2,1,0:T(8,128)(2,1)}, bf16[2,512,768]{2,1,0:T(8,128)(2,1)}, u32[]{:S(2)}, u32[]{:S(2)}) collective-permute-start(bf16[2,512,768]{2,1,0:T(8,128)(2,1)} %spread.2.refs_4_), channel_id=1, source_target_pairs={{0,1},{1,0},{2,3},{3,2},{4,5},{5,4},{6,7},{7,6},{8,9},{9,8},{10,11... | collective-permute-start | bytes 4718600 | tf_op jit(solution)/shard_map/ppermute | solution.py:35
  206.4 18.7 %collective-permute-start.39 = (bf16[1,1,4,112,768]{4,3,2,1,0:T(8,128)(2,1)}, bf16[1,1,4,112,768]{4,3,2,1,0:T(8,128)(2,1)}, u32[]{:S(2)}, u32[]{:S(2)}) collective-permute-start(bf16[1,1,4,112,768]{4,3,2,1,0:T(8,128)(2,1)} %get-tuple-element.103.refs_0_), channel_id=1, source_target_pairs={{0,4},{4,0},{8,12},{12,8},{16,20},{20,16},{24,28},{28,24},{1,5},{5... | collective-permute-start | bytes 2064392 | tf_op jit(solution)/shard_map/ppermute | solution.py:40
  215.5 31.6 %collective-permute-start.38 = (bf16[512,768]{1,0:T(8,128)(2,1)}, bf16[512,768]{1,0:T(8,128)(2,1)S(1)}, u32[]{:S(2)}, u32[]{:S(2)}) collective-permute-start(bf16[512,768]{1,0:T(8,128)(2,1)} %get-tuple-element.110.refs_0_), channel_id=1, source_target_pairs={{0,2},{1,3},{2,0},{3,1},{4,6},{5,7},{6,4},{7,5},{8,10},{9,11},{10,... | collective-permute-start | bytes 2359304 | tf_op jit(solution)/shard_map/ppermute | solution.py:35
  216.7 16.6 %collective-permute-start.42 = (bf16[96,1024]{1,0:T(8,128)(2,1)}, bf16[96,1024]{1,0:T(8,128)(2,1)S(1)}, u32[]{:S(2)}, u32[]{:S(2)}) collective-permute-start(bf16[96,1024]{1,0:T(8,128)(2,1)} %get-tuple-element.115), channel_id=1, source_target_pairs={{0,24},{4,28},{8,16},{12,20},{16,8},{20,12},{24,0},{28,4},{1,25},{... | collective-permute-start | bytes 589832 | tf_op jit(solution)/shard_map/ppermute | solution.py:40
  220.2 21.0 %collective-permute-start.41 = (bf16[96,1024]{1,0:T(8,128)(2,1)}, bf16[96,1024]{1,0:T(8,128)(2,1)}, u32[]{:S(2)}, u32[]{:S(2)}) collective-permute-start(bf16[96,1024]{1,0:T(8,128)(2,1)} %get-tuple-element.114), channel_id=1, source_target_pairs={{0,16},{4,20},{8,24},{12,28},{16,0},{20,4},{24,8},{28,12},{1,17},{... | collective-permute-start | bytes 589832 | tf_op jit(solution)/shard_map/ppermute | solution.py:40
  220.2 21.0 %collective-permute-start.40 = (bf16[96,1024]{1,0:T(8,128)(2,1)}, bf16[96,1024]{1,0:T(8,128)(2,1)}, u32[]{:S(2)}, u32[]{:S(2)}) collective-permute-start(bf16[96,1024]{1,0:T(8,128)(2,1)} %get-tuple-element.113), channel_id=1, source_target_pairs={{0,8},{4,12},{8,0},{12,4},{16,24},{20,28},{24,16},{28,20},{1,9},{5... | collective-permute-start | bytes 589832 | tf_op jit(solution)/shard_map/ppermute | solution.py:40
  225.1 18.7 %collective-permute-start.43 = (bf16[2,96,768]{2,1,0:T(8,128)(2,1)}, bf16[2,96,768]{2,1,0:T(8,128)(2,1)}, u32[]{:S(2)}, u32[]{:S(2)}) collective-permute-start(bf16[2,96,768]{2,1,0:T(8,128)(2,1)} %get-tuple-element.112.refs_2_), channel_id=1, source_target_pairs={{0,2},{1,3},{2,0},{3,1},{4,6},{5,7},{6,4},{7,5},{8,10},{9,11},{10,... | collective-permute-start | bytes 884744 | tf_op jit(solution)/shard_map/ppermute | solution.py:35
  228.4 23.8 %all-to-all-start.1 = ((bf16[4,112,768]{2,1,0:T(8,128)(2,1)}), bf16[4,112,768]{2,1,0:T(8,128)(2,1)S(1)}, u32[]{:S(2)}, u32[]{:S(2)}) async-start(bf16[4,112,768]{2,1,0:T(8,128)(2,1)} %joined_sums.3.refs_0_), calls=%async_computation.1 | async-start | bytes 1376256 | tf_op jit(solution)/shard_map/all_to_all | solution.py:86
  245.6 5.4 %collective-permute-start.44 = (bf16[1,96,768]{2,1,0:T(8,128)(2,1)}, bf16[1,96,768]{2,1,0:T(8,128)(2,1)S(1)}, u32[]{:S(2)}, u32[]{:S(2)}) collective-permute-start(bf16[1,96,768]{2,1,0:T(8,128)(2,1)} %get-tuple-element.118), channel_id=1, source_target_pairs={{0,4},{4,0},{8,12},{12,8},{16,20},{20,16},{24,28},{28,24},{1,5},{5... | collective-permute-start | bytes 442376 | tf_op jit(solution)/shard_map/ppermute | solution.py:40
  (34 other events, 456.1 us)
